TPU v7x, 32 devices: a whole 2x2x4 slice. The times are simulated.
32 devices in a mesh: dp: 8 (over y, x, core), mp: 4 (over z).
Axes of the slice: x: 2, y: 2, z: 4, core: 2. Of those that a mesh axis runs over, the one named last changes fastest.
Arguments:
- hidden_in: bfloat16 [16384, 2048], P('dp', 'mp')
- positions: int32 [16384], P('dp'), may hold values from 0 to 1023, as said below
- head_counts: int32 [4], replicated, may hold values from 4 to 6, as said below
- attention_gain: float32 [2048], P('mp'), may hold values from 0.5 to 1.5
- query_projection_weight: bfloat16 [2048, 1536], P(None, 'mp'), may hold values from -0.125 to 0.125
- key_weight: bfloat16 [2048, 320], replicated, may hold values from -0.125 to 0.125
- value_weight: bfloat16 [2048, 320], replicated, may hold values from -0.125 to 0.125
- query_gain: float32 [64], replicated, may hold values from 0.25 to 1.75
- key_gain: float32 [64], replicated, may hold values from 0.25 to 1.75
- output_weight: bfloat16 [1536, 2048], P(None, 'mp'), may hold values from -0.75 to 0.75
- feedforward_gain: float32 [2048], P('mp'), may hold values from 0.5 to 1.5
- gate_weight: bfloat16 [2048, 4096], P(None, 'mp'), may hold values from -0.125 to 0.125
- up_weight: bfloat16 [2048, 4096], P(None, 'mp'), may hold values from -0.125 to 0.125
- down_projection_weight: bfloat16 [4096, 2048], P('mp'), may hold values from -0.125 to 0.125
- cotangent: bfloat16 [16384, 2048], P('dp', 'mp'), may hold values from -6 to 6
Outputs:
- output: bfloat16 [16384, 2048], P('dp', 'mp')
- input_gradient: float32 [16384, 2048], P('dp', 'mp')
- attention_gain_gradient: float32 [2048], P('mp')
- query_weight_gradient: float32 [2048, 1536], P(None, 'mp')
- key_weight_gradient: float32 [2048, 320], replicated
- value_weight_gradient: float32 [2048, 320], replicated
- query_gain_gradient: float32 [64], replicated
- key_gain_gradient: float32 [64], replicated
- output_projection_gradient: float32 [1536, 2048], P(None, 'mp')
- feedforward_gain_gradient: float32 [2048], P('mp')
- gate_weight_gradient: float32 [2048, 4096], P(None, 'mp')
- up_weight_gradient: float32 [2048, 4096], P(None, 'mp')
- down_weight_gradient: float32 [4096, 2048], P('mp')
Inputs may be any that keep to these rules, and one draw needn't show every extreme that they name: `head_counts`: the counts sum to 20; index m's live heads follow those of lower indices; the largest count is 6 in every draw. `positions`: position ids count up by one along each sequence of 1024 tokens and restart at zero at its start and at up to three points inside it; the first sequence of all has no restart inside it.
All inputs are finite; a program needn't handle non-finite values.
Results may differ from a plain program's by a relative error of at most 0.025.
Values may be sent and summed in bfloat16 or wider, within the bound.
No kernel may reach another device: no remote copies, remote signals or barrier semaphores. Data moves between devices by JAX's collectives and lax.ppermute only.
A program may use at most 256 MiB of HBM per device.

v0:
```python
import math

import jax
import jax.numpy as jnp
from jax import lax
from jax.sharding import PartitionSpec as P

D = 2048
QH = 20
KVH = 5
HD = 64
LEN = 1024
BLK = 512
NBLK = 2


epsilon = 1e-05
rope_base = 10000.0
masked_score = -1e30


def rotary_tables(positions):
    half = HD // 2
    inverse = jnp.exp(-math.log(rope_base) * (2.0 * jnp.arange(half, dtype=jnp.float32)) / HD)
    angles = positions.astype(jnp.float32)[..., None] * inverse
    angles = jnp.concatenate([angles, angles], axis=-1)
    return (jnp.cos(angles), jnp.sin(angles))


def rotate(vectors, cosine, sine):
    half = vectors.shape[-1] // 2
    turned = jnp.concatenate([-vectors[..., half:], vectors[..., :half]], axis=-1)
    return vectors * cosine + turned * sine


def head_norm(vectors, gain):
    return vectors * lax.rsqrt(jnp.mean(vectors * vectors, axis=-1, keepdims=True) + epsilon) * gain


def inner(left_operand, right_operand):
    return lax.dot_general(
        left_operand, right_operand, (((0,), (0,)), ((), ())), preferred_element_type=jnp.float32
    )


def against(left_operand, right_operand):
    return lax.dot_general(
        left_operand, right_operand, (((1,), (1,)), ((), ())), preferred_element_type=jnp.float32
    )


def norm_forward(values, gain):
    squares = lax.psum(jnp.sum(values * values, axis=1), "mp")
    rms = lax.rsqrt(squares / D + epsilon)[:, None]
    normed = (values * rms * gain).astype(jnp.bfloat16)
    return (rms, lax.all_gather(normed, "mp", axis=1, tiled=True))


def norm_backward(values, rms, gain, normed_grad):
    weighted = normed_grad * gain
    dotted = lax.psum(jnp.sum(weighted * values, axis=1), "mp")[:, None]
    grad = weighted * rms - values * (rms * rms * rms) * dotted / D
    gain_grad = jnp.sum(normed_grad * values * rms, axis=0)
    return (grad, gain_grad)


def spread_sum(terms):
    return lax.psum_scatter(
        terms.astype(jnp.bfloat16), "mp", scatter_dimension=1, tiled=True
    ).astype(jnp.float32)


def on_device(
    hidden_in,
    positions,
    head_counts,
    attention_gain,
    query_projection_weight,
    key_weight,
    value_weight,
    query_gain,
    key_gain,
    output_weight,
    feedforward_gain,
    gate_weight,
    up_weight,
    down_projection_weight,
    cotangent,
):
    parts = lax.axis_size("mp")
    rank = lax.axis_index("mp")
    tokens = hidden_in.shape[0]
    share = hidden_in.shape[1]
    slots_here = query_projection_weight.shape[1] // HD
    seqs = tokens // LEN
    scale = 1.0 / math.sqrt(HD)
    ranks = jnp.arange(parts, dtype=jnp.int32)
    offset = jnp.sum(jnp.where(ranks < rank, head_counts, 0))
    count = jnp.sum(jnp.where(ranks == rank, head_counts, 0))
    within = jnp.arange(slots_here, dtype=jnp.int32)
    live = (within < count).astype(jnp.float32)
    groups = jnp.minimum((offset + within) // (QH // KVH), KVH - 1)
    choose = (groups[:, None] == jnp.arange(KVH, dtype=jnp.int32)[None, :]).astype(jnp.float32)
    choose_low = choose.astype(jnp.bfloat16)
    cosine, sine = rotary_tables(positions)

    def turn(raw, gain):
        heads = raw.reshape(tokens, -1, HD)
        return rotate(head_norm(heads, gain), cosine[:, None, :], sine[:, None, :])

    inputs = hidden_in.astype(jnp.float32)
    first_rms, normed_full = norm_forward(inputs, attention_gain)
    queries = jnp.dot(normed_full, query_projection_weight, preferred_element_type=jnp.float32)
    keys = jnp.dot(normed_full, key_weight, preferred_element_type=jnp.float32)
    values_low = jnp.dot(normed_full, value_weight, preferred_element_type=jnp.float32).astype(
        jnp.bfloat16
    )
    turned_queries, query_pull = jax.vjp(turn, queries, query_gain)
    turned_keys, key_pull = jax.vjp(turn, keys, key_gain)
    turned_queries = turned_queries.astype(jnp.bfloat16)
    turned_keys = turned_keys.astype(jnp.bfloat16)
    query_heads = jnp.transpose(turned_queries.reshape(seqs, LEN, slots_here, HD), (0, 2, 1, 3))
    key_heads = jnp.einsum(
        "hg,slgd->shld",
        choose_low,
        turned_keys.reshape(seqs, LEN, KVH, HD),
        preferred_element_type=jnp.float32,
    ).astype(jnp.bfloat16)
    value_heads = jnp.einsum(
        "hg,slgd->shld",
        choose_low,
        values_low.reshape(seqs, LEN, KVH, HD),
        preferred_element_type=jnp.float32,
    ).astype(jnp.bfloat16)
    query_blocks = jnp.moveaxis(query_heads.reshape(seqs, slots_here, NBLK, BLK, HD), 2, 0)
    starts = jnp.arange(NBLK, dtype=jnp.int32) * BLK
    cols = jnp.arange(LEN, dtype=jnp.int32)

    def block_scores(block, start):
        scores = (
            jnp.einsum("shid,shjd->shij", block, key_heads, preferred_element_type=jnp.float32)
            * scale
        )
        rows = start + jnp.arange(BLK, dtype=jnp.int32)
        allowed = cols[None, :] <= rows[:, None]
        return jnp.where(allowed, scores, masked_score)

    def attend_block(block_args):
        block, start = block_args
        scores = block_scores(block, start)
        peak = jnp.max(scores, axis=-1, keepdims=True)
        weights = jnp.exp(scores - peak)
        total = jnp.sum(weights, axis=-1, keepdims=True)
        probs = (weights / total).astype(jnp.bfloat16)
        result = jnp.einsum(
            "shij,shjd->shid", probs, value_heads, preferred_element_type=jnp.float32
        )
        return (result, (peak + jnp.log(total))[..., 0])

    mixed, row_totals = lax.map(attend_block, (query_blocks, starts))
    mixed = jnp.moveaxis(mixed, 0, 2).reshape(seqs, slots_here, LEN, HD).astype(jnp.bfloat16)
    mixed = mixed * live.astype(jnp.bfloat16)[None, :, None, None]
    mixed_local = jnp.transpose(mixed, (0, 2, 1, 3)).reshape(tokens, slots_here * HD)
    all_heads = lax.all_gather(mixed_local, "mp", axis=1, tiled=True)
    branch = jnp.dot(all_heads, output_weight, preferred_element_type=jnp.float32)
    middle = inputs + branch
    second_rms, second_normed_complete = norm_forward(middle, feedforward_gain)
    gate = jnp.dot(second_normed_complete, gate_weight, preferred_element_type=jnp.float32)
    up = jnp.dot(second_normed_complete, up_weight, preferred_element_type=jnp.float32)
    sigma = jax.nn.sigmoid(gate)
    swish = gate * sigma
    hidden = (swish * up).astype(jnp.bfloat16)
    down_terms = jnp.dot(hidden, down_projection_weight, preferred_element_type=jnp.float32)
    output = (
        middle
        + lax.psum_scatter(
            down_terms.astype(jnp.bfloat16), "mp", scatter_dimension=1, tiled=True
        ).astype(jnp.float32)
    ).astype(jnp.bfloat16)
    cotangent_full = lax.all_gather(cotangent, "mp", axis=1, tiled=True)
    down_grad = inner(hidden, cotangent_full)
    hidden_grad = against(cotangent_full, down_projection_weight)
    gate_grad = (hidden_grad * up * sigma * (1.0 + gate * (1.0 - sigma))).astype(jnp.bfloat16)
    up_grad = (hidden_grad * swish).astype(jnp.bfloat16)
    gate_weight_grad = inner(second_normed_complete, gate_grad)
    up_weight_grad = inner(second_normed_complete, up_grad)
    normed_two_grad = spread_sum(against(gate_grad, gate_weight) + against(up_grad, up_weight))
    middle_part, feedforward_gain_grad = norm_backward(
        middle, second_rms, feedforward_gain, normed_two_grad
    )
    middle_grad = cotangent.astype(jnp.float32) + middle_part
    branch_grad = middle_grad.astype(jnp.bfloat16)
    output_weight_grad = inner(all_heads, branch_grad)
    slot_terms = against(branch_grad, output_weight)
    mixed_grad = lax.psum_scatter(
        slot_terms.astype(jnp.bfloat16), "mp", scatter_dimension=1, tiled=True
    ).astype(jnp.float32)
    mixed_grad = (mixed_grad.reshape(tokens, slots_here, HD) * live[None, :, None]).astype(
        jnp.bfloat16
    )
    grad_heads = jnp.transpose(mixed_grad.reshape(seqs, LEN, slots_here, HD), (0, 2, 1, 3))
    grad_blocks = jnp.moveaxis(grad_heads.reshape(seqs, slots_here, NBLK, BLK, HD), 2, 0)

    def back_block(carry, block_args):
        key_total, value_total = carry
        block, grad_block, row_total, start = block_args
        scores = block_scores(block, start)
        probs = jnp.exp(scores - row_total[..., None])
        probs_low = probs.astype(jnp.bfloat16)
        prob_grad = jnp.einsum(
            "shid,shjd->shij", grad_block, value_heads, preferred_element_type=jnp.float32
        )
        delta = jnp.sum(probs * prob_grad, axis=-1, keepdims=True)
        score_grad = (probs * (prob_grad - delta)).astype(jnp.bfloat16)
        query_grad = (
            jnp.einsum("shij,shjd->shid", score_grad, key_heads, preferred_element_type=jnp.float32)
            * scale
        )
        key_total = (
            key_total
            + jnp.einsum("shij,shid->shjd", score_grad, block, preferred_element_type=jnp.float32)
            * scale
        )
        value_total = value_total + jnp.einsum(
            "shij,shid->shjd", probs_low, grad_block, preferred_element_type=jnp.float32
        )
        return ((key_total, value_total), query_grad)

    empty = jnp.zeros((seqs, slots_here, LEN, HD), jnp.float32)
    (key_slot_grad, value_slot_grad), query_block_grads = lax.scan(
        back_block, (empty, empty), (query_blocks, grad_blocks, row_totals, starts)
    )
    query_rot_grad = jnp.moveaxis(query_block_grads, 0, 2).reshape(seqs, slots_here, LEN, HD)
    query_rot_grad = jnp.transpose(query_rot_grad, (0, 2, 1, 3)).reshape(tokens, slots_here, HD)
    key_rot_grad = jnp.einsum("hg,shld->slgd", choose, key_slot_grad).reshape(tokens, KVH, HD)
    value_grad = jnp.einsum("hg,shld->slgd", choose, value_slot_grad).reshape(tokens, KVH * HD)
    query_unrotated_gradient, query_gain_part = query_pull(query_rot_grad)
    key_raw_grad, key_gain_part = key_pull(key_rot_grad)
    summed = (
        lax.psum(key_raw_grad.astype(jnp.bfloat16), "mp").astype(jnp.float32),
        lax.psum(value_grad.astype(jnp.bfloat16), "mp").astype(jnp.float32),
        lax.psum(query_gain_part.astype(jnp.bfloat16), "mp").astype(jnp.float32),
        lax.psum(key_gain_part.astype(jnp.bfloat16), "mp").astype(jnp.float32),
    )
    keys_low = summed[0].astype(jnp.bfloat16)
    values_grad_low = summed[1].astype(jnp.bfloat16)
    queries_low = query_unrotated_gradient.astype(jnp.bfloat16)
    query_weight_grad = inner(normed_full, queries_low)
    key_weight_grad = inner(normed_full, keys_low)
    value_weight_grad = inner(normed_full, values_grad_low)
    normed_grad = spread_sum(against(queries_low, query_projection_weight))
    key_rows = lax.dynamic_slice_in_dim(key_weight, rank * share, share, 0)
    value_rows = lax.dynamic_slice_in_dim(value_weight, rank * share, share, 0)
    normed_grad = normed_grad + against(keys_low, key_rows) + against(values_grad_low, value_rows)
    input_part, attention_gain_grad = norm_backward(inputs, first_rms, attention_gain, normed_grad)
    input_gradient = middle_grad + input_part
    totals = (
        lax.psum(attention_gain_grad.astype(jnp.bfloat16), "dp").astype(jnp.float32),
        lax.psum(query_weight_grad.astype(jnp.bfloat16), "dp").astype(jnp.float32),
        lax.psum(key_weight_grad.astype(jnp.bfloat16), "dp").astype(jnp.float32),
        lax.psum(value_weight_grad.astype(jnp.bfloat16), "dp").astype(jnp.float32),
        lax.psum(summed[2].astype(jnp.bfloat16), "dp").astype(jnp.float32),
        lax.psum(summed[3].astype(jnp.bfloat16), "dp").astype(jnp.float32),
        lax.psum(output_weight_grad.astype(jnp.bfloat16), "dp").astype(jnp.float32),
        lax.psum(feedforward_gain_grad.astype(jnp.bfloat16), "dp").astype(jnp.float32),
        lax.psum(gate_weight_grad.astype(jnp.bfloat16), "dp").astype(jnp.float32),
        lax.psum(up_weight_grad.astype(jnp.bfloat16), "dp").astype(jnp.float32),
        lax.psum(down_grad.astype(jnp.bfloat16), "dp").astype(jnp.float32),
    )
    return (
        output,
        input_gradient,
        totals[0],
        totals[1],
        totals[2],
        totals[3],
        totals[4],
        totals[5],
        totals[6],
        totals[7],
        totals[8],
        totals[9],
        totals[10],
    )


def solution(mesh):
    in_specs = (
        P("dp", "mp"),
        P("dp"),
        P(),
        P("mp"),
        P(None, "mp"),
        P(),
        P(),
        P(),
        P(),
        P(None, "mp"),
        P("mp"),
        P(None, "mp"),
        P(None, "mp"),
        P("mp", None),
        P("dp", "mp"),
    )
    out_specs = (
        P("dp", "mp"),
        P("dp", "mp"),
        P("mp"),
        P(None, "mp"),
        P(),
        P(),
        P(),
        P(),
        P(None, "mp"),
        P("mp"),
        P(None, "mp"),
        P(None, "mp"),
        P("mp", None),
    )
    return jax.shard_map(
        on_device, mesh=mesh, in_specs=in_specs, out_specs=out_specs, check_vma=False
    )
```

profile of v0, /device:TPU:16, one launch (start us, length us, event | category | flops | bytes accessed | tf_op | source)
XLA Modules:
  0.0 2033.6 jit_solution(6352952060460513605)
XLA Ops:
  13.3 9.1 psum.133
  29.9 8.1 fusion.86
  39.4 137.0 %all-gather.5.cloned.1.call-done = bf16[2048,2048]{0,1:T(8,128)(2,1)} async-done(((bf16[2048,512]{0,1:T(8,128)(2,1)}), bf16[2048,2048]{0,1:T(8,128)(2,1)}) %all-gather.5.cloned.1.call-update) | async-done | bytes 8388624 | tf_op jit(solution)/shard_map/all_gather | solution.py:56
  176.4 7.4 convolution_convert_fusion.8
  212.7 6.7 fusion.62
  227.1 6.0 reshape.296
  247.2 6.5 fusion.77
  253.7 5.7 reshape.314
  262.3 75.6 %while.30 = (s32[]{:T(128)}, bf16[2,2,6,512,64]{3,4,2,1,0:T(8,128)(2,1)}, f32[2,2,6,512]{3,2,1,0:T(8,128)S(1)}, s32[2]{0:T(128)S(1)}, bf16[2,2,6,512,64]{3,4,2,1...) while((s32[]{:T(128)}, ...), condition=%wide.region_8.9_spmd.clone.clone, body=%wide.region_5.8_spmd.clone.sunk.clone | while | flops 1686628864 | bytes 190279856 | solution.py:160
  264.0 12.2 fusion.187
  276.2 12.3 fusion.188
  291.6 8.5 bitcast_dynamic-update-slice_fusion.9
  301.8 12.2 fusion.187
  314.0 12.3 fusion.188
  329.4 8.5 bitcast_dynamic-update-slice_fusion.9
  343.7 113.7 %all-gather.7.cloned.1.call-done = bf16[2048,1536]{0,1:T(8,128)(2,1)} async-done(((bf16[2048,384]{0,1:T(8,128)(2,1)}), bf16[2048,1536]{0,1:T(8,128)(2,1)}) %all-gather.7.cloned.1.call-update) | async-done | bytes 6291472 | tf_op jit(solution)/shard_map/all_gather | solution.py:164
  457.3 8.3 multiply_reduce_fusion.1
  465.6 8.1 psum.134
  478.3 149.1 %all-gather.9.cloned.1.call-done = bf16[2048,2048]{0,1:T(8,128)(2,1)} async-done(((bf16[2048,512]{0,1:T(8,128)(2,1)}), bf16[2048,2048]{0,1:T(8,128)(2,1)}) %all-gather.9.cloned.1.call-update) | async-done | bytes 8388624 | tf_op jit(solution)/shard_map/all_gather | solution.py:56
  627.4 15.0 fusion.109
  642.4 11.6 fusion.108
  654.0 122.8 %all-gather.11.cloned.1.call-done = bf16[2048,2048]{1,0:T(8,128)(2,1)} async-done(((bf16[2048,512]{1,0:T(8,128)(2,1)}), bf16[2048,2048]{1,0:T(8,128)(2,1)}) %all-gather.11.cloned.1.call-update) | async-done | bytes 8388624 | tf_op jit(solution)/shard_map/all_gather | solution.py:180
  776.8 23.8 %multiply_convert_fusion.1 = (bf16[2048,1024]{1,0:T(8,128)(2,1)}, bf16[2048,1024]{1,0:T(8,128)(2,1)}, bf16[2048,1024]{1,0:T(8,128)(2,1)}) fusion(f32[2048,1024]{1,0:T(8,128)} %fusion.108, f32[2048,1024]{1,0:T(8,128)} %fusion.109, bf16[2048,2048]{1,0:T(8,128)(2,1)} %all-gather.11.cloned.1.call-done, bf16[1024,2048]{1,0:T(8,128)(2,1)} %param.32), kind=kOutput, calls=%fused_computation.53 | convolution fusion | flops 8621391872 | bytes 41943040 | tf_op jit(solution)/shard_map/dot_general | solution.py:47
  800.6 15.4 fusion.110
  816.0 14.1 add_convert_fusion
  830.2 14.0 convolution_convert_fusion.2
  848.2 127.3 %reduce-scatter.9.cloned.1.call-done = bf16[2048,512]{0,1:T(8,128)(2,1)} async-done(((bf16[2048,2048]{0,1:T(8,128)(2,1)}), bf16[2048,512]{0,1:T(8,128)(2,1)}) %reduce-scatter.9.cloned.1.call-update) | async-done | bytes 2097168 | tf_op jit(solution)/shard_map/reduce_scatter | solution.py:68
  980.1 7.9 psum.135
  988.0 135.7 %reduce-scatter.7.cloned.1.call-done = bf16[2048,512]{0,1:T(8,128)(2,1)} async-done(((bf16[2048,2048]{0,1:T(8,128)(2,1)}), bf16[2048,512]{0,1:T(8,128)(2,1)}) %reduce-scatter.7.cloned.1.call-update) | async-done | bytes 2097168 | tf_op jit(solution)/shard_map/reduce_scatter | solution.py:176
  1123.7 6.0 fusion.39
  1131.7 5.4 convolution_convert_fusion.1
  1137.1 8.6 copy.163
  1149.5 15.1 convolution_convert_fusion.3
  1164.6 12.8 convolution_convert_fusion.4
  1177.4 10.4 convolution_convert_fusion.5
  1187.8 5.2 convolution_convert_fusion.6
  1193.0 64.2 %reduce-scatter.13.cloned.1.call-done = bf16[384,2048]{1,0:T(8,128)(2,1)} async-done(((bf16[1536,2048]{1,0:T(8,128)(2,1)}), bf16[384,2048]{1,0:T(8,128)(2,1)}) %reduce-scatter.13.cloned.1.call-update) | async-done | bytes 1572880
  1261.2 5.6 reshape.310
  1271.0 5.8 reshape.315
  1279.7 164.1 %while.31 = (s32[]{:T(128)}, f32[2,6,1024,64]{2,3,1,0:T(8,128)}, f32[2,6,1024,64]{2,3,1,0:T(8,128)}, f32[2,2,6,512,64]{3,4,2,1,0:T(8,128)}, s32[2]{0:T(128)S(1)}...) while((s32[]{:T(128)}, f32[2,6,1024,64]{2,3,1,0:T(8,128)}, ...), condition=%wide.region_19.20_spmd.clone.clone, body=%wide.region_17.19_spmd.clone.sunk.clone | while | flops 4125747712 | bytes 278057216 | solution.py:230
  1281.5 11.5 fusion.198
  1293.0 13.4 select_add_fusion.7
  1306.5 18.2 multiply_reduce_fusion.10
  1324.7 17.3 multiply_convert_fusion.8
  1350.6 9.7 bitcast_dynamic-update-slice_fusion.11
  1361.9 11.5 fusion.198
  1373.4 14.3 select_add_fusion.7
  1387.8 18.2 multiply_reduce_fusion.10
  1406.0 17.3 multiply_convert_fusion.8
  1427.8 6.0 select_add_fusion.6
  1433.7 9.7 bitcast_dynamic-update-slice_fusion.11
  1484.8 5.8 convolution_convert_fusion.7
  1490.6 90.2 %all-reduce.13.cloned.1.call-done = (bf16[2048,320]{0,1:T(8,128)(2,1)}, bf16[2048,320]{0,1:T(8,128)(2,1)}) async-done(((bf16[2048,320]{0,1:T(8,128)(2,1)}, bf16[2048,320]{0,1:T(8,128)(2,1)}), (bf16[2048,320]{0,1:T(8,128)(2,1)}, bf16[2048,320]{0,1:T(8,128)(2,1)})) %all-reduce.13.cloned.1.call-update) | async-done | bytes 2621456 | tf_op jit(solution)/shard_map/psum | solution.py:240
  1580.8 7.8 convolution_convert_fusion.10
  1588.6 7.4 convolution_convert_fusion.9
  1597.5 6.7 convolution_convert_fusion
  1608.2 8.3 all-reduce.6
  1620.8 213.6 %all-reduce.11.cloned.1.call-done = (bf16[2048,384]{1,0:T(8,128)(2,1)}, bf16[2048,320]{0,1:T(8,128)(2,1)}, bf16[2048,320]{0,1:T(8,128)(2,1)}, bf16[1536,512]{1,0...) async-done(((bf16[2048,384]{1,0:T(8,128)(2,1)}, bf16[2048,320]{0,1:T(8,128)(2,1)}, bf16[2048,320]{0,1:T(8,128)(2,1)}, ...) | async-done | bytes 18350096 | tf_op jit(solution)/shard_map/psum | solution.py:259
  1858.3 123.6 %reduce-scatter.11.cloned.1.call-done = bf16[2048,512]{0,1:T(8,128)(2,1)} async-done(((bf16[2048,2048]{0,1:T(8,128)(2,1)}), bf16[2048,512]{0,1:T(8,128)(2,1)}) %reduce-scatter.11.cloned.1.call-update) | async-done | bytes 2097168 | tf_op jit(solution)/shard_map/reduce_scatter | solution.py:68
  1981.9 7.8 fusion.52
  1989.7 13.7 all-reduce.4
  2005.6 7.9 psum.138
  2013.5 7.7 fusion.49
  2021.2 5.3 copy.146
  (300 shorter events, 206.2 us)
Async XLA Ops:
  7.2 214.8 %copy-start = (bf16[2048,384]{1,0:T(8,128)(2,1)S(1)}, bf16[2048,384]{1,0:T(8,128)(2,1)}, u32[]{:S(2)}) copy-start(bf16[2048,384]{1,0:T(8,128)(2,1)} %param.23) | copy-start | bytes 4718596
  7.2 16.5 copy-start.48
  7.2 169.2 %all-gather.5.cloned.1.call-start = ((), (), s32[]{:S(2)}) async-start(), calls=%async_computation.4 | async-start | bytes 10485760 | tf_op jit(solution)/shard_map/all_gather | solution.py:56
  23.7 3.5 copy-start.52
  23.7 3.6 copy-start.61
  27.1 149.3 %copy-start.43 = (bf16[2048,320]{0,1:T(8,128)(2,1)S(1)}, bf16[2048,320]{0,1:T(8,128)(2,1)}, u32[]{:S(2)}) copy-start(bf16[2048,320]{0,1:T(8,128)(2,1)} %param.25) | copy-start | bytes 3932164
  27.1 430.2 %all-gather.7.cloned.1.call-start = ((), (), s32[]{:S(2)}) async-start(), calls=%async_computation.5 | async-start | bytes 7864320 | tf_op jit(solution)/shard_map/all_gather | solution.py:164
  27.3 156.5 %copy-start.58 = (f32[32]{0:T(128)}, f32[32]{0:T(128)S(1)}, u32[]{:S(2)}) copy-start(f32[32]{0:T(128)S(1)} %multiply_exponential_fusion) | copy-start | bytes 388
  28.6 190.7 %copy-start.50 = (s32[6]{0:T(128)}, s32[6]{0:T(128)S(1)}, u32[]{:S(2)}) copy-start(s32[6]{0:T(128)S(1)} %fusion.101) | copy-start | bytes 76
  38.0 174.6 %copy-start.16 = (f32[2,1024,64]{1,0,2:T(2,128)}, f32[2,1024,64]{1,0,2:T(2,128)S(1)}, u32[]{:S(2)}) copy-start(f32[2,1024,64]{1,0,2:T(2,128)S(1)} %get-tuple-element.371) | copy-start | bytes 1572868
  187.3 3.7 copy-start.63
  196.2 7.5 copy-start.53
  212.7 9.3 slice-start
  264.0 24.5 %copy-start.9 = (bf16[2,6,1024,64]{2,3,1,0:T(8,128)(2,1)S(1)}, bf16[2,6,1024,64]{2,3,1,0:T(8,128)(2,1)}, u32[]{:S(2)}) copy-start(bf16[2,6,1024,64]{2,3,1,0:T(8,128)(2,1)} %get-tuple-element.557) | copy-start | bytes 4718596 | tf_op jit(solution)/shard_map/while
  276.2 15.4 copy-start.2
  301.8 24.5 %copy-start.9 = (bf16[2,6,1024,64]{2,3,1,0:T(8,128)(2,1)S(1)}, bf16[2,6,1024,64]{2,3,1,0:T(8,128)(2,1)}, u32[]{:S(2)}) copy-start(bf16[2,6,1024,64]{2,3,1,0:T(8,128)(2,1)} %get-tuple-element.557) | copy-start | bytes 4718596 | tf_op jit(solution)/shard_map/while
  314.0 15.4 copy-start.2
  342.0 115.4 %copy-start.67 = (bf16[1536,512]{1,0:T(8,128)(2,1)S(1)}, bf16[1536,512]{1,0:T(8,128)(2,1)}, u32[]{:S(2)}) copy-start(bf16[1536,512]{1,0:T(8,128)(2,1)} %param.28) | copy-start | bytes 4718596
  343.6 130.1 %copy-start.47 = (f32[512]{0:T(512)S(1)}, f32[512]{0:T(512)}, u32[]{:S(2)}) copy-start(f32[512]{0:T(512)} %param.29) | copy-start | bytes 6148
  343.6 283.8 %all-gather.9.cloned.1.call-start = ((), (), s32[]{:S(2)}) async-start(), calls=%async_computation.6 | async-start | bytes 10485760 | tf_op jit(solution)/shard_map/all_gather | solution.py:56
  477.7 299.1 %all-gather.11.cloned.1.call-start = ((), (), s32[]{:S(2)}) async-start(), calls=%async_computation.8 | async-start | bytes 10485760 | tf_op jit(solution)/shard_map/all_gather | solution.py:180
  478.3 497.2 %reduce-scatter.9.cloned.1.call-start = ((), (), s32[]{:S(2)}) async-start(), calls=%async_computation.9 | async-start | bytes 10485760 | tf_op jit(solution)/shard_map/reduce_scatter | solution.py:68
  627.4 15.0 copy-start.64
  627.4 15.0 copy-start.65
  800.6 15.4 copy-start.66
  800.6 15.4 copy-start.70
  830.2 293.5 %reduce-scatter.7.cloned.1.call-start = ((), (), s32[]{:S(2)}) async-start(), calls=%async_computation.7 | async-start | bytes 10485760 | tf_op jit(solution)/shard_map/reduce_scatter | solution.py:176
  844.2 413.0 %reduce-scatter.13.cloned.1.call-start = ((), (), s32[]{:S(2)}) async-start(), calls=%async_computation.11 | async-start | bytes 7864320
  1145.8 435.0 %all-reduce.13.cloned.1.call-start = ((), (), s32[]{:S(2)}) async-start(), calls=%async_computation.13 | async-start | bytes 5242880 | tf_op jit(solution)/shard_map/psum | solution.py:240
  1149.5 15.1 copy-start.71
  1149.5 27.8 %slice-start.4 = ((s8[8388608]{0:T(1024)(128)(4,1)}), s8[4194304]{0:T(1024)(128)(4,1)S(1)}, s32[]{:S(2)}) async-start(s8[8388608]{0:T(1024)(128)(4,1)} %bitcast.239), calls=%async_computation.18 | async-start | bytes 8388608
  1164.5 12.8 slice-start.5
  1164.5 12.8 copy-start.72
  1164.5 23.2 %slice-start.6 = ((s8[6291456]{0:T(1024)(128)(4,1)}), s8[4194304]{0:T(1024)(128)(4,1)S(1)}, s32[]{:S(2)}) async-start(s8[6291456]{0:T(1024)(128)(4,1)} %bitcast.241), calls=%async_computation.20 | async-start | bytes 8388608
  1177.3 10.4 copy-start.15
  1177.3 10.4 slice-start.7
  1261.2 5.6 copy-start.60
  1271.0 8.7 copy-start.4
  1271.0 8.7 copy-start.39
  1271.0 8.7 copy-start.69
  1281.5 11.5 copy-start.5
  1281.5 11.5 copy-start.13
  1324.7 21.8 %copy-start.6 = (bf16[2,2,6,512,64]{3,4,2,1,0:T(8,128)(2,1)S(1)}, bf16[2,2,6,512,64]{3,4,2,1,0:T(8,128)(2,1)}, u32[]{:S(2)}) copy-start(bf16[2,2,6,512,64]{3,4,2,1,0:T(8,128)(2,1)} %get-tuple-element.583) | copy-start | bytes 4718596 | tf_op jit(solution)/shard_map/while
  1342.0 4.5 copy-start.1
  1361.9 11.5 copy-start.5
  1361.9 11.5 copy-start.13
  1406.0 21.8 %copy-start.6 = (bf16[2,2,6,512,64]{3,4,2,1,0:T(8,128)(2,1)S(1)}, bf16[2,2,6,512,64]{3,4,2,1,0:T(8,128)(2,1)}, u32[]{:S(2)}) copy-start(bf16[2,2,6,512,64]{3,4,2,1,0:T(8,128)(2,1)} %get-tuple-element.583) | copy-start | bytes 4718596 | tf_op jit(solution)/shard_map/while
  1423.3 4.5 copy-start.1
  1461.9 4.9 copy-start.18
  1477.1 357.3 %all-reduce.11.cloned.1.call-start = ((), (), s32[]{:S(2)}) async-start(), calls=%async_computation.12 | async-start | bytes 36700160 | tf_op jit(solution)/shard_map/psum | solution.py:259
  1477.2 3.8 copy-start.11
  1477.2 7.6 slice-start.2
  1481.0 3.8 slice-start.3
  1580.8 7.8 copy-start.32
  1596.1 385.8 %reduce-scatter.11.cloned.1.call-start = ((), (), s32[]{:S(2)}) async-start(), calls=%async_computation.10 | async-start | bytes 10485760 | tf_op jit(solution)/shard_map/reduce_scatter | solution.py:68
  1604.2 12.3 copy-start.22
  1837.8 3.6 copy-start.27
  1844.9 4.4 copy-start.20
  1849.3 4.4 copy-start.19
  1853.8 128.1 %copy-start.33 = (bf16[2048,320]{0,1:T(8,128)(2,1)S(1)}, bf16[2048,320]{0,1:T(8,128)(2,1)}, u32[]{:S(2)}) copy-start(bf16[2048,320]{0,1:T(8,128)(2,1)} %get-tuple-element.349) | copy-start | bytes 3932164
  1853.8 128.1 %copy-start.41 = (f32[2048]{0:T(1024)S(1)}, f32[2048]{0:T(1024)}, u32[]{:S(2)}) copy-start(f32[2048]{0:T(1024)} %copy-done.40) | copy-start | bytes 24580
  1853.8 128.1 %copy-start.49 = (f32[512]{0:T(512)S(1)}, f32[512]{0:T(512)}, u32[]{:S(2)}) copy-start(f32[512]{0:T(512)} %param.22) | copy-start | bytes 6148
  1858.3 131.4 %copy-start.57 = (bf16[512]{0:T(512)(128)(2,1)S(1)}, bf16[512]{0:T(512)(128)(2,1)}, u32[]{:S(2)}) copy-start(bf16[512]{0:T(512)(128)(2,1)} %get-tuple-element.291) | copy-start | bytes 3076
  1858.3 155.3 %copy-start.46 = (f32[2048]{0:T(1024)S(1)}, f32[2048]{0:T(1024)}, u32[]{:S(2)}) copy-start(f32[2048]{0:T(1024)} %get-tuple-element.373) | copy-start | bytes 24580
  (33 other events, 66.3 us)
Sparse Core Ops, SparseCore 0:
  27.3 149.0 all-gather.4
  343.7 113.5 all-gather.6
  477.8 149.5 all-gather.8
  628.9 147.8 all-gather.10
  830.3 145.1 reduce-scatter.8
  978.3 145.3 reduce-scatter.6
  1145.9 111.2 reduce-scatter.12
  1477.2 103.5 all-reduce.12
  1596.2 238.2 all-reduce.10
  1836.7 145.1 reduce-scatter.10
where the time goes:
time: 2050 us; the launch traced here: 2030 us
  waiting for transfers between devices  1280 us (62%)
  matrix products  377 us (18%)
  other arithmetic  173 us (8%)
  local copies, waits for them, and re-layouts  134 us (7%)
  blocking collectives  55 us (3%)
    all_gather x2, waiting for transfers between devices, norm_forward(): return (rms, lax.all_gather(normed, 'mp', axis=1, tiled=True))  286 us
    reduce_scatter x2, waiting for transfers between devices, spread_sum(): lax.psum_scatter(terms.astype(jnp.bfloat16), 'mp', scatter_dimension=1, t...  251 us
    psum x1, waiting for transfers between devices, on_device(): lax.psum(query_weight_grad.astype(jnp.bfloat16), 'dp').astype(jnp.float32)  214 us
    reduce_scatter x1, waiting for transfers between devices, on_device(): lax.psum_scatter(down_terms.astype(jnp.bfloat16), 'mp', scatter_dimension...  136 us
    all_gather x1, waiting for transfers between devices, on_device(): cotangent_full = lax.all_gather(cotangent, 'mp', axis=1, tiled=True)  123 us
    all_gather x1, waiting for transfers between devices, on_device(): all_heads = lax.all_gather(mixed_local, 'mp', axis=1, tiled=True)  114 us
    psum x1, waiting for transfers between devices, on_device(): lax.psum(key_raw_grad.astype(jnp.bfloat16), 'mp').astype(jnp.float32)  90.2 us
    dot_general x7, matrix products, against(): lax.dot_general(left_operand, right_operand, (((1,), (1,)), ((), ())), pr...  77.6 us
  transfers between devices with their start and end apart: 10, of which 10 were waited for; matrix products, arithmetic and copies ran while one was open for 8% of the time, Pallas kernels for 0%

commit v1 on v0

v1 whole, which is shorter than its diff:
```python
import functools
import math

import jax
import jax.numpy as jnp
from jax import lax
from jax.experimental import pallas as pl
from jax.experimental.pallas import tpu as pltpu
from jax.sharding import PartitionSpec as P

D = 2048
QH = 20
KVH = 5
QPG = QH // KVH
HD = 64
LEN = 1024
HALF = LEN // 2

epsilon = 1e-05
rope_base = 10000.0
masked_score = -1e30
low = jnp.bfloat16
full = jnp.float32


def dot(left, right, left_axis, right_axis):
    return lax.dot_general(
        left, right, (((left_axis,), (right_axis,)), ((), ())), preferred_element_type=full
    )


def swap(pieces, axis):
    n = len(pieces)
    return [pieces[0]] + [
        lax.ppermute(pieces[k], axis, [(i, i ^ k) for i in range(n)]) for k in range(1, n)
    ]


def by_rank(blocks, rank):
    bit = 1
    while bit < len(blocks):
        flag = (rank & bit) != 0
        blocks = [jnp.where(flag, blocks[j ^ bit], blocks[j]) for j in range(len(blocks))]
        bit *= 2
    return blocks


def rotary_tables(positions):
    half = HD // 2
    inverse = jnp.exp(-math.log(rope_base) * (2.0 * jnp.arange(half, dtype=full)) / HD)
    angles = inverse[:, None] * positions.astype(full)[None, :]
    cosine, sine = jnp.cos(angles), jnp.sin(angles)
    return jnp.concatenate([cosine, cosine], 0), jnp.concatenate([sine, sine], 0)


def turn(raw, gain, cosine, sine):
    half = HD // 2
    rms = lax.rsqrt(jnp.mean(raw * raw, axis=1, keepdims=True) + epsilon)
    normed = raw * rms * gain[None, :, None]
    turned = jnp.concatenate([-normed[:, half:], normed[:, :half]], axis=1)
    return normed * cosine[None] + turned * sine[None]


def mm(left, right):
    return jnp.dot(left, right, preferred_element_type=full)


def scores_of(key, query, start, first):
    scores = mm(key, query)
    if first is None:
        return scores
    rows = lax.broadcasted_iota(jnp.int32, scores.shape, 0)
    cols = lax.broadcasted_iota(jnp.int32, scores.shape, 1)
    return jnp.where(rows - cols <= start - first, scores, masked_score)


PARTS = (((0, 0),), ((0, None), (HALF, HALF)))


def attend_kernel(starts, q_ref, k_ref, v_ref, o_ref, sums_ref):
    chunk = q_ref.shape[2] // 2
    scale = 1.0 / math.sqrt(HD)
    key = k_ref[0].astype(full).T.astype(low)
    for part, pieces in enumerate(PARTS):
        span = pl.ds(part * chunk, chunk)
        for head in range(QPG):
            query = q_ref[head, :, span] * jnp.asarray(scale, low)
            scores = [
                scores_of(key[at : at + HALF], query, starts[part], first) for at, first in pieces
            ]
            peak = functools.reduce(
                jnp.maximum, [jnp.max(s, axis=0, keepdims=True) for s in scores]
            )
            total = jnp.zeros_like(peak)
            result = jnp.zeros((HD, chunk), full)
            for (at, _), s in zip(pieces, scores):
                weights = jnp.exp(s - peak)
                total += jnp.sum(weights, axis=0, keepdims=True)
                result += mm(v_ref[0, :, at : at + HALF], weights.astype(low))
            o_ref[head, :, span] = (result / total).astype(low)
            sums_ref[0, head : head + 1, span] = peak + jnp.log(total)


def attend_back_kernel(
    starts, q_ref, k_ref, v_ref, g_ref, sums_ref, dq_ref, dk_ref, dv_ref, dk_acc, dv_acc
):
    chunk = q_ref.shape[2] // 2
    scale = 1.0 / math.sqrt(HD)
    key = k_ref[0].astype(full).T.astype(low)
    value = v_ref[0].astype(full).T.astype(low)
    dk_acc[...] = jnp.zeros_like(dk_acc)
    dv_acc[...] = jnp.zeros_like(dv_acc)
    for part, pieces in enumerate(PARTS):
        span = pl.ds(part * chunk, chunk)
        for head in range(QPG):
            query = q_ref[head, :, span] * jnp.asarray(scale, low)
            grad = g_ref[head, :, span]
            query_rows = query.astype(full).T.astype(low)
            grad_rows = grad.astype(full).T.astype(low)
            sums = sums_ref[0, head : head + 1, span]
            delta = jnp.zeros((1, chunk), full)
            kept = []
            for at, first in pieces:
                probs = jnp.exp(
                    scores_of(key[at : at + HALF], query, starts[part], first) - sums
                )
                product = probs * mm(value[at : at + HALF], grad)
                delta += jnp.sum(product, axis=0, keepdims=True)
                kept.append((probs, product))
            dq = jnp.zeros((HD, chunk), full)
            for (at, _), (probs, product) in zip(pieces, kept):
                score_grad = (product - probs * delta).astype(low)
                dq += mm(k_ref[0, :, at : at + HALF], score_grad)
                dk_acc[at : at + HALF, :] += mm(score_grad, query_rows)
                dv_acc[at : at + HALF, :] += mm(probs.astype(low), grad_rows)
            dq_ref[head, :, span] = dq * scale
    dk_ref[0] = dk_acc[...].T
    dv_ref[0] = dv_acc[...].T


def attention_specs(tokens):
    heads = pl.BlockSpec((QPG, HD, tokens), lambda g, s: (g, 0, 0))
    keys = pl.BlockSpec((1, HD, LEN), lambda g, s: (g, 0, 0))
    sums = pl.BlockSpec((1, QPG, tokens), lambda g, s: (g, 0, 0))
    return heads, keys, sums


def attend(starts, queries, keys, values):
    tokens = queries.shape[2]
    heads, whole, sums = attention_specs(tokens)
    pairs = QH * (tokens // 2) * (LEN + HALF)
    return pl.pallas_call(
        attend_kernel,
        out_shape=(
            jax.ShapeDtypeStruct((QH, HD, tokens), low),
            jax.ShapeDtypeStruct((KVH, QPG, tokens), full),
        ),
        grid_spec=pltpu.PrefetchScalarGridSpec(
            num_scalar_prefetch=1,
            grid=(KVH,),
            in_specs=[heads, whole, whole],
            out_specs=[heads, sums],
        ),
        compiler_params=pltpu.CompilerParams(vmem_limit_bytes=40 << 20),
        cost_estimate=pl.CostEstimate(
            flops=pairs * HD * 16, bytes_accessed=8 << 20, transcendentals=pairs
        ),
    )(starts, queries, keys, values)


def attend_back(starts, queries, keys, values, grads, sums_in):
    tokens = queries.shape[2]
    heads, whole, sums = attention_specs(tokens)
    pairs = QH * (tokens // 2) * (LEN + HALF)
    return pl.pallas_call(
        attend_back_kernel,
        out_shape=(
            jax.ShapeDtypeStruct((QH, HD, tokens), full),
            jax.ShapeDtypeStruct((KVH, HD, LEN), full),
            jax.ShapeDtypeStruct((KVH, HD, LEN), full),
        ),
        grid_spec=pltpu.PrefetchScalarGridSpec(
            num_scalar_prefetch=1,
            grid=(KVH,),
            in_specs=[heads, whole, whole, heads, sums],
            out_specs=[heads, whole, whole],
            scratch_shapes=[pltpu.VMEM((LEN, HD), full), pltpu.VMEM((LEN, HD), full)],
        ),
        compiler_params=pltpu.CompilerParams(vmem_limit_bytes=40 << 20),
        cost_estimate=pl.CostEstimate(
            flops=pairs * HD * 40, bytes_accessed=16 << 20, transcendentals=pairs
        ),
    )(starts, queries, keys, values, grads, sums_in)


def norm_backward(values, rms, gain, normed_grad):
    weighted = normed_grad * gain
    dotted = jnp.sum(weighted * values, axis=1, keepdims=True)
    grad = weighted * rms - values * (rms * rms * rms) * dotted / D
    return grad, jnp.sum(normed_grad * values * rms, axis=0)


def on_device(
    hidden_in,
    positions,
    head_counts,
    attention_gain,
    query_projection_weight,
    key_weight,
    value_weight,
    query_gain,
    key_gain,
    output_weight,
    feedforward_gain,
    gate_weight,
    up_weight,
    down_projection_weight,
    cotangent,
):
    groups = lax.axis_size("dp")
    parts = lax.axis_size("mp")
    group = lax.axis_index("dp")
    rank = lax.axis_index("mp")
    tokens, share = hidden_in.shape
    seqs = tokens // LEN
    ring = parts // seqs
    mine = tokens // parts
    chunk = mine // 2
    units = gate_weight.shape[1] // groups
    slots = query_projection_weight.shape[1]
    place = rank % ring
    ranks = range(parts)

    lower = jnp.arange(parts)[None, :] < jnp.arange(parts)[:, None]
    offsets = jnp.sum(jnp.where(lower, head_counts[None, :], 0), axis=1)

    def selection(order):
        within = jnp.arange(slots, dtype=jnp.int32)
        column = offsets[order][:, None] * HD + within[None, :]
        column = jnp.where(within[None, :] < head_counts[order][:, None] * HD, column, -1)
        return (
            column.reshape(-1)[:, None] == jnp.arange(QH * HD, dtype=jnp.int32)[None, :]
        ).astype(low)

    select_near = selection(rank ^ jnp.arange(parts, dtype=jnp.int32))
    select = selection(jnp.arange(parts, dtype=jnp.int32))

    def rows_of(array, other):
        base = (other // ring) * LEN
        at = other % ring
        first = lax.dynamic_slice_in_dim(array, base + at * chunk, chunk, 0)
        last = lax.dynamic_slice_in_dim(array, base + (2 * ring - 1 - at) * chunk, chunk, 0)
        return jnp.concatenate([first, last], 0)

    def to_tokens(array):
        got = swap([rows_of(array, rank ^ k) for k in ranks], "mp")
        return jnp.concatenate(by_rank(got, rank), axis=1)

    def to_features(array, kind):
        array = array.astype(low)
        pieces = by_rank([array[:, j * share : (j + 1) * share] for j in ranks], rank)
        got = by_rank(swap(pieces, "mp"), rank)
        rows = []
        for seq in range(seqs):
            near = got[seq * ring : (seq + 1) * ring]
            rows += [block[:chunk] for block in near]
            rows += [block[chunk:] for block in near[::-1]]
        return jnp.concatenate(rows, 0).astype(kind)

    def everyone(piece):
        return jnp.concatenate(by_rank(swap([piece] * parts, "mp"), rank), axis=0)

    inputs = to_tokens(hidden_in).astype(full)
    gains = everyone(jnp.stack([attention_gain, feedforward_gain], 1)).T
    attention_gain_all, feedforward_gain_all = gains[0], gains[1]

    rows = D // groups
    query_slice = lax.dynamic_slice_in_dim(query_projection_weight, group * rows, rows, 0)
    query_slice = jnp.concatenate(swap([query_slice] * parts, "mp"), axis=1)
    query_slice = mm(query_slice, select_near).astype(low)
    query_all = lax.all_gather(query_slice, "dp", axis=0, tiled=True)
    heads_here = QH * HD // groups
    chosen = lax.dynamic_slice_in_dim(select, group * heads_here, heads_here, 1)
    output_slice = dot(chosen, output_weight, 0, 0).astype(low)
    output_slice = jnp.concatenate(
        by_rank(swap([output_slice] * parts, "mp"), rank), axis=1
    )
    output_all = lax.all_gather(output_slice, "dp", axis=0, tiled=True)

    def near(piece, axis):
        return jnp.concatenate(swap([piece] * parts, "mp"), axis=axis)

    gate_here = near(lax.dynamic_slice_in_dim(gate_weight, group * units, units, 1), 1)
    up_here = near(lax.dynamic_slice_in_dim(up_weight, group * units, units, 1), 1)
    down_here = near(lax.dynamic_slice_in_dim(down_projection_weight, group * units, units, 0), 0)

    cotangent_mine = to_tokens(cotangent)
    cotangent_full = lax.all_gather(cotangent_mine, "dp", axis=0, tiled=True)

    cosine, sine = rotary_tables(rows_of(positions, rank))
    first_rms = lax.rsqrt(jnp.mean(inputs * inputs, axis=1, keepdims=True) + epsilon)
    normed = (inputs * first_rms * attention_gain_all).astype(low)
    keys = dot(key_weight, normed, 0, 1).reshape(KVH, HD, mine)
    values_mine = dot(value_weight, normed, 0, 1).astype(low).reshape(KVH, HD, mine)
    turned_keys, key_pull = jax.vjp(lambda v, g: turn(v, g, cosine, sine), keys, key_gain)
    pair_mine = jnp.concatenate([turned_keys.astype(low), values_mine], 0)

    near_pairs = [pair_mine] + [
        lax.ppermute(pair_mine, "mp", [(i, i ^ k) for i in ranks]) for k in range(1, ring)
    ]
    near_pairs = by_rank(near_pairs, place)
    pair = jnp.concatenate(
        [p[:, :, :chunk] for p in near_pairs] + [p[:, :, chunk:] for p in near_pairs[::-1]], axis=2
    )
    key_heads, value_heads = pair[:KVH], pair[KVH:]

    queries = dot(query_all, normed, 0, 1).reshape(QH, HD, mine)
    turned_queries, query_pull = jax.vjp(
        lambda v, g: turn(v, g, cosine, sine), queries, query_gain
    )
    turned_queries = turned_queries.astype(low)
    starts = jnp.stack([place * chunk, (2 * ring - 1 - place) * chunk]).astype(jnp.int32)
    mixed, row_totals = attend(starts, turned_queries, key_heads, value_heads)
    mixed = mixed.reshape(QH * HD, mine)
    middle = inputs + dot(mixed, output_all, 0, 0)

    second_rms = lax.rsqrt(jnp.mean(middle * middle, axis=1, keepdims=True) + epsilon)
    second_normed = (middle * second_rms * feedforward_gain_all).astype(low)
    second_full = lax.all_gather(second_normed, "dp", axis=0, tiled=True)
    gate = mm(second_full, gate_here)
    up = mm(second_full, up_here)
    sigma = jax.nn.sigmoid(gate)
    swish = gate * sigma
    hidden = (swish * up).astype(low)
    hidden_grad = dot(cotangent_full, down_here, 1, 1)
    gate_grad = (hidden_grad * up * sigma * (1.0 + gate * (1.0 - sigma))).astype(low)
    up_grad = (hidden_grad * swish).astype(low)
    normed_two_terms = dot(gate_grad, gate_here, 1, 1) + dot(up_grad, up_here, 1, 1)
    normed_two_grad = lax.psum_scatter(
        normed_two_terms.astype(low), "dp", scatter_dimension=0, tiled=True
    ).astype(full)
    down_terms = mm(hidden, down_here)
    down_sum = lax.psum_scatter(
        down_terms.astype(low), "dp", scatter_dimension=0, tiled=True
    ).astype(full)
    output = to_features(middle + down_sum, low)

    def reduce_units(grad, axis):
        pieces = [lax.slice_in_dim(grad, k * units, (k + 1) * units, axis=axis) for k in ranks]
        got = swap(pieces, "mp")
        return sum(piece.astype(full) for piece in got).astype(low)

    def columns_back(piece):
        wide = lax.all_gather(piece, "dp", axis=0, tiled=False)
        return jnp.transpose(wide, (1, 0, 2)).reshape(D, -1).astype(full)

    down_grad = reduce_units(dot(hidden, cotangent_full, 0, 0).astype(low), 0)
    down_grad = lax.all_gather(down_grad, "dp", axis=0, tiled=True).astype(full)
    gate_weight_grad = columns_back(reduce_units(dot(second_full, gate_grad, 0, 0).astype(low), 1))
    up_weight_grad = columns_back(reduce_units(dot(second_full, up_grad, 0, 0).astype(low), 1))

    middle_part, feedforward_gain_grad = norm_backward(
        middle, second_rms, feedforward_gain_all, normed_two_grad
    )
    middle_grad = cotangent_mine.astype(full) + middle_part
    branch_grad = middle_grad.astype(low)

    output_grad = mm(mixed, branch_grad).astype(low)
    output_grad = lax.psum_scatter(output_grad, "dp", scatter_dimension=0, tiled=True)
    pieces = by_rank([output_grad[:, j * share : (j + 1) * share] for j in ranks], rank)
    output_grad = sum(piece.astype(full) for piece in swap(pieces, "mp")).astype(low)
    output_grad = lax.all_gather(output_grad, "dp", axis=0, tiled=True)
    output_weight_grad = mm(select, output_grad)

    mixed_grad = dot(output_all, branch_grad, 1, 1).astype(low).reshape(QH, HD, mine)
    query_rot_grad, key_rot_grad, value_grad = attend_back(
        starts, turned_queries, key_heads, value_heads, mixed_grad, row_totals
    )
    queries_low, query_gain_grad = query_pull(query_rot_grad)
    queries_low = queries_low.astype(low).reshape(QH * HD, mine)
    pair_grad = jnp.concatenate([key_rot_grad, value_grad], 0)
    blocks = [
        jnp.concatenate(
            [
                pair_grad[:, :, j * chunk : (j + 1) * chunk],
                pair_grad[:, :, (2 * ring - 1 - j) * chunk : (2 * ring - j) * chunk],
            ],
            axis=2,
        )
        for j in range(ring)
    ]
    blocks = by_rank(blocks, place)
    pair_grad = blocks[0]
    for k in range(1, ring):
        pair_grad += lax.ppermute(
            blocks[k].astype(low), "mp", [(i, i ^ k) for i in ranks]
        ).astype(full)
    keys_grad, key_gain_grad = key_pull(pair_grad[:KVH])
    pair_low = jnp.concatenate(
        [keys_grad.astype(low), pair_grad[KVH:].astype(low)], 0
    ).reshape(2 * KVH * HD, mine)

    query_weight_grad = dot(normed, queries_low, 0, 1).astype(low)
    query_weight_grad = lax.psum_scatter(
        query_weight_grad, "dp", scatter_dimension=0, tiled=True
    )
    query_weight_grad = dot(query_weight_grad, select_near, 1, 1).astype(low)
    pieces = [query_weight_grad[:, k * slots : (k + 1) * slots] for k in ranks]
    query_weight_grad = sum(piece.astype(full) for piece in swap(pieces, "mp")).astype(low)
    query_weight_grad = lax.all_gather(query_weight_grad, "dp", axis=0, tiled=True).astype(full)

    pair_weight_grad = dot(normed, pair_low, 0, 1).astype(low)
    pair_weight_grad = lax.psum_scatter(pair_weight_grad, "dp", scatter_dimension=0, tiled=True)
    pair_weight_grad = sum(
        piece.astype(full) for piece in swap([pair_weight_grad] * parts, "mp")
    ).astype(low)
    pair_weight_grad = lax.all_gather(pair_weight_grad, "dp", axis=0, tiled=True).astype(full)

    normed_grad = (
        dot(queries_low, query_all, 0, 1)
        + dot(pair_low[: KVH * HD], key_weight, 0, 1)
        + dot(pair_low[KVH * HD :], value_weight, 0, 1)
    )
    input_part, attention_gain_grad = norm_backward(
        inputs, first_rms, attention_gain_all, normed_grad
    )
    input_gradient = to_features(middle_grad + input_part, full)

    small = jnp.concatenate(
        [attention_gain_grad, feedforward_gain_grad, query_gain_grad, key_gain_grad]
    )
    small = lax.psum(small, ("dp", "mp"))
    return (
        output,
        input_gradient,
        lax.dynamic_slice_in_dim(small[:D], rank * share, share, 0),
        query_weight_grad,
        pair_weight_grad[:, : KVH * HD],
        pair_weight_grad[:, KVH * HD :],
        small[2 * D : 2 * D + HD],
        small[2 * D + HD :],
        output_weight_grad,
        lax.dynamic_slice_in_dim(small[D : 2 * D], rank * share, share, 0),
        gate_weight_grad,
        up_weight_grad,
        down_grad,
    )


def solution(mesh):
    in_specs = (
        P("dp", "mp"),
        P("dp"),
        P(),
        P("mp"),
        P(None, "mp"),
        P(),
        P(),
        P(),
        P(),
        P(None, "mp"),
        P("mp"),
        P(None, "mp"),
        P(None, "mp"),
        P("mp", None),
        P("dp", "mp"),
    )
    out_specs = (
        P("dp", "mp"),
        P("dp", "mp"),
        P("mp"),
        P(None, "mp"),
        P(),
        P(),
        P(),
        P(),
        P(None, "mp"),
        P("mp"),
        P(None, "mp"),
        P(None, "mp"),
        P("mp", None),
    )
    return jax.shard_map(
        on_device, mesh=mesh, in_specs=in_specs, out_specs=out_specs, check_vma=False
    )
```

time: 2050 us -> 1180 us (0.58)
  waiting for transfers between devices: 1280 us -> 628 us
  matrix products: 377 us -> 223 us
  other arithmetic: 173 us -> 71.5 us
  local copies, waits for them, and re-layouts: 134 us -> 37.3 us
  starting transfers between devices: 0.41 us -> 82.8 us
  Pallas kernels: 0 us -> 53.2 us
    all_gather x4 -> x10, waiting for transfers between devices: 523 us -> 8.91 us  [the longest x1 8.86 us: on_device(): lax.all_gather(query_weight_grad, 'dp', axis=0, tiled=True).astype(full)]
    ppermute x0 -> x50, waiting for transfers between devices: none -> 401 us  [the longest x48 372 us: swap(): lax.ppermute(pieces[k], axis, [(i, i ^ k) for i in range(n)])]
    psum x2 -> x0, waiting for transfers between devices: 304 us -> none  [the longest x1 214 us: on_device(): lax.psum(query_weight_grad.astype(jnp.bfloat16), 'dp').astype(jnp.float32)]
    reduce_scatter x3 -> x5, waiting for transfers between devices: 387 us -> 218 us  [the longest x1 115 us: on_device(): lax.psum_scatter(down_terms.astype(low), 'dp', scatter_dimension=0, tiled...]
    dot_general x39 -> x24, matrix products: 377 us -> 223 us  [the longest x18 153 us: dot(): lax.dot_general(left, right, (((left_axis,), (right_axis,)), ((), ())), p...]
    ppermute x0 -> x50, starting transfers between devices: none -> 81.9 us  [the longest x48 80.3 us: swap(): lax.ppermute(pieces[k], axis, [(i, i ^ k) for i in range(n)])]
    unnamed x11 -> x15, waiting for transfers between devices: 64.9 us -> 0.25 us
    pallas_call x0 -> x2, Pallas kernels: none -> 53.2 us  [the longest x1 32.5 us: attend_back(): pl.pallas_call(attend_back_kernel, out_shape=(jax.ShapeDtypeStruct((QH, H...]
  transfers between devices with their start and end apart: 10 -> 65, of which waited for: 10 -> 38; matrix products, arithmetic and copies ran while one was open for 8% -> 20% of each run, Pallas kernels for 0% -> 2%
where the time goes in v1:
time: 1180 us; the launch traced here: 1170 us
  waiting for transfers between devices  628 us (53%)
  matrix products  223 us (19%)
  starting transfers between devices  82.8 us (7%)
  other arithmetic  71.5 us (6%)
  blocking collectives  60.6 us (5%)
  Pallas kernels  53.2 us (5%)
  local copies, waits for them, and re-layouts  37.3 us (3%)
  between operations  15.9 us (1%)
    ppermute x48, waiting for transfers between devices, swap(): lax.ppermute(pieces[k], axis, [(i, i ^ k) for i in range(n)])  372 us
    dot_general x18, matrix products, dot(): lax.dot_general(left, right, (((left_axis,), (right_axis,)), ((), ())), p...  153 us
    reduce_scatter x1, waiting for transfers between devices, on_device(): lax.psum_scatter(down_terms.astype(low), 'dp', scatter_dimension=0, tiled...  115 us
    reduce_scatter x1, waiting for transfers between devices, on_device(): lax.psum_scatter(normed_two_terms.astype(low), 'dp', scatter_dimension=0,...  102 us
    ppermute x48, starting transfers between devices, swap(): lax.ppermute(pieces[k], axis, [(i, i ^ k) for i in range(n)])  80.3 us
    dot_general x6, matrix products, mm(): return jnp.dot(left, right, preferred_element_type=full)  70.1 us
    psum x1, blocking collectives, on_device(): small = lax.psum(small, ('dp', 'mp'))  60.6 us
    pallas_call x1, Pallas kernels, attend_back(): pl.pallas_call(attend_back_kernel, out_shape=(jax.ShapeDtypeStruct((QH, H...  32.5 us
  transfers between devices with their start and end apart: 65, of which 38 were waited for; matrix products, arithmetic and copies ran while one was open for 20% of the time, Pallas kernels for 2%

profile of v1, /device:TPU:16, one launch (start us, length us, event | category | flops | bytes accessed | tf_op | source)
XLA Modules:
  0.0 1172.1 jit_solution(6590275563262519670)
XLA Ops:
  15.4 9.4 collective-permute-done.5
  43.6 6.3 collective-permute-done.11
  49.9 3.8 collective-permute-done.10
  61.9 28.1 %collective-permute-done.25 = bf16[512,512]{1,0:T(8,128)(2,1)S(1)} collective-permute-done((bf16[512,512]{1,0:T(8,128)(2,1)S(1)}, bf16[512,512]{1,0:T(8,128)(2,1)S(1)}, u32[]{:S(2)}, u32[]{:S(2)}) %collective-permute-start.25) | collective-permute-done | bytes 524320 | tf_op jit(solution)/shard_map/ppermute | solution.py:35
  90.0 9.2 collective-permute-done.26
  113.9 17.3 %collective-permute-done.2 = bf16[512,512]{1,0:T(8,128)(2,1)S(1)} collective-permute-done((bf16[512,512]{1,0:T(8,128)(2,1)S(1)}, bf16[512,512]{1,0:T(8,128)(2,1)S(1)}, u32[]{:S(2)}, u32[]{:S(2)}) %collective-permute-start.2) | collective-permute-done | bytes 524320 | tf_op jit(solution)/shard_map/ppermute | solution.py:35
  131.2 14.6 %collective-permute-done.1 = bf16[512,512]{1,0:T(8,128)(2,1)S(1)} collective-permute-done((bf16[512,512]{1,0:T(8,128)(2,1)S(1)}, bf16[512,512]{1,0:T(8,128)(2,1)S(1)}, u32[]{:S(2)}, u32[]{:S(2)}) %collective-permute-start.1) | collective-permute-done | bytes 524320 | tf_op jit(solution)/shard_map/ppermute | solution.py:35
  145.9 11.4 collective-permute-done
  163.7 14.6 %collective-permute-done.9 = bf16[10,64,512]{2,1,0:T(8,128)(2,1)S(1)} collective-permute-done((bf16[10,64,512]{2,1,0:T(8,128)(2,1)S(1)}, bf16[10,64,512]{2,1,0:T(8,128)(2,1)S(1)}, u32[]{:S(2)}, u32[]{:S(2)}) %collective-permute-start.9) | collective-permute-done | bytes 655392 | tf_op jit(solution)/shard_map/ppermute | solution.py:309
  178.8 6.2 fusion.66
  188.3 20.6 %shard_map.246 = (bf16[20,64,512]{2,1,0:T(8,128)(2,1)S(1)}, f32[5,4,512]{2,1,0:T(4,128)S(1)}) custom-call(s32[2]{0:T(128)S(1)} %pad_add_fusion.2.starts, bf16[20,64,512]{2,1,0:T(8,128)(2,1)S(1)} %fusion.25.q_ref, bf16[5,64,1024]{2,1,0:T(8,128)(2,1)S(1)} %get-tuple-element.139.k_ref, bf16[5,64,1024]{2,1,0:T(8,128)(2,1)S(1)} %get-tuple-element.138.v_ref), custom_call_target="tpu_custom_call" | custom-call | flops 8053063680 | bytes 8388608 | tf_op jit(solution)/shard_map/pallas_call | solution.py:152
  210.0 7.8 multiply_reduce_fusion
  217.8 3.9 multiply_convert_fusion.3
  232.4 44.3 %collective-permute-done.21 = bf16[128,2048]{1,0:T(8,128)(2,1)S(1)} collective-permute-done((bf16[128,2048]{1,0:T(8,128)(2,1)S(1)}, bf16[128,2048]{1,0:T(8,128)(2,1)S(1)}, u32[]{:S(2)}, u32[]{:S(2)}) %collective-permute-start.21) | collective-permute-done | bytes 524320 | tf_op jit(solution)/shard_map/ppermute | solution.py:35
  276.7 12.6 %collective-permute-done.20 = bf16[128,2048]{1,0:T(8,128)(2,1)S(1)} collective-permute-done((bf16[128,2048]{1,0:T(8,128)(2,1)S(1)}, bf16[128,2048]{1,0:T(8,128)(2,1)S(1)}, u32[]{:S(2)}, u32[]{:S(2)}) %collective-permute-start.20) | collective-permute-done | bytes 524320 | tf_op jit(solution)/shard_map/ppermute | solution.py:35
  291.7 4.3 collective-permute-start.14
  296.0 14.9 %fusion.45 = f32[4096,512]{1,0:T(8,128)} fusion(bf16[4096,2048]{1,0:T(8,128)(2,1)} %all-gather.19.cloned.1.call-done, bf16[128,2048]{1,0:T(8,128)(2,1)S(1)} %collective-permute-done.21, bf16[128,2048]{1,0:T(8,128)(2,1)S(1)} %collective-permute-done.20, bf16[128,2048]{1,0:T(8,128)(2,1)} %copy-done.78, bf16[128,2048]{1,0:T(8,128)(2,1)S(1)} %constant_dynamic-slice_fusion.8), kind=kOutput, calls=%fused_computation.173 | convolution fusion | flops 8598323200 | bytes 27262976 | tf_op jit(solution)/shard_map/dot_general | solution.py:27
  310.9 14.3 %collective-permute-done.18 = bf16[2048,128]{1,0:T(8,128)(2,1)} collective-permute-done((bf16[2048,128]{1,0:T(8,128)(2,1)S(1)}, bf16[2048,128]{1,0:T(8,128)(2,1)}, u32[]{:S(2)}, u32[]{:S(2)}) %collective-permute-start.18) | collective-permute-done | bytes 524320 | tf_op jit(solution)/shard_map/ppermute | solution.py:35
  325.2 9.1 collective-permute-done.17
  334.2 14.8 %fusion.47 = f32[4096,512]{1,0:T(8,128)} fusion(bf16[4096,2048]{1,0:T(8,128)(2,1)} %all-gather.17.cloned.1.call-done, bf16[2048,128]{1,0:T(8,128)(2,1)} %collective-permute-done.18, bf16[2048,128]{1,0:T(8,128)(2,1)} %collective-permute-done.17, bf16[2048,128]{1,0:T(8,128)(2,1)} %collective-permute-done.16, ...), kind=kOutput, calls=%fused_computation.175 | convolution fusion | flops 8598323200 | bytes 27262976 | tf_op jit(solution)/shard_map/dot_general | solution.py:65
  349.1 6.5 collective-permute-done.14
  355.6 23.8 %multiply_convert_fusion.1 = (bf16[4096,512]{1,0:T(8,128)(2,1)}, bf16[4096,512]{1,0:T(8,128)(2,1)}, bf16[4096,512]{1,0:T(8,128)(2,1)}) fusion(f32[4096,512]{1,0:T(8,128)} %fusion.45, f32[4096,512]{1,0:T(8,128)} %fusion.47, bf16[4096,2048]{1,0:T(8,128)(2,1)} %all-gather.17.cloned.1.call-done, bf16[2048,128]{1,0:T(8,128)(2,1)} %collective-permute-done.15, ...), kind=kOutput, calls=%fused_computation.17 | convolution fusion | flops 8629780480 | bytes 48234496 | tf_op jit(solution)/shard_map/dot_general | solution.py:65
  379.4 18.0 %fusion.46 = f32[4096,2048]{1,0:T(8,128)} fusion(bf16[4096,512]{1,0:T(8,128)(2,1)} %get-tuple-element.79, bf16[2048,128]{1,0:T(8,128)(2,1)} %collective-permute-done.18, bf16[2048,128]{1,0:T(8,128)(2,1)} %collective-permute-done.17, bf16[2048,128]{1,0:T(8,128)(2,1)} %collective-permute-done.16, bf16[2048,128]{1,0:T(8,128)(2,1)S(1)} %constant_dynamic-slice_fusion.9), kind=kOutput, calls=%fused_computation.174 | convolution fusion | flops 8598323200 | bytes 39845888 | tf_op jit(solution)/shard_map/dot_general | solution.py:27
  397.4 22.5 %add_convert_fusion = bf16[4096,2048]{1,0:T(8,128)(2,1)} fusion(f32[4096,2048]{1,0:T(8,128)} %fusion.46, bf16[4096,512]{1,0:T(8,128)(2,1)} %get-tuple-element.78, bf16[2048,128]{1,0:T(8,128)(2,1)} %collective-permute-done.15, bf16[2048,128]{1,0:T(8,128)(2,1)} %collective-permute-done.14, bf16[2048,128]{1,0:T(8,128)(2,1)} %collective-permute-done.13, ...), kind=kOutput, calls=%fused_computation.4 | convolution fusion | flops 8615100416 | bytes 56623104 | tf_op jit(solution)/shard_map/dot_general | solution.py:27
  421.0 15.7 %convolution_convert_fusion = bf16[4096,2048]{1,0:T(8,128)(2,1)} fusion(bf16[4096,512]{1,0:T(8,128)(2,1)} %get-tuple-element.80, bf16[128,2048]{1,0:T(8,128)(2,1)S(1)} %collective-permute-done.21, bf16[128,2048]{1,0:T(8,128)(2,1)S(1)} %collective-permute-done.20, bf16[128,2048]{1,0:T(8,128)(2,1)S(1)} %copy-done.79, ...), kind=kOutput, calls=%fused_computation.5 | convolution fusion | flops 8606711808 | bytes 23068672 | tf_op jit(solution)/shard_map/dot_general | solution.py:65
  436.8 102.5 %reduce-scatter.8.cloned.1.call-done = bf16[512,2048]{1,0:T(8,128)(2,1)} async-done(((bf16[4096,2048]{1,0:T(8,128)(2,1)}), bf16[512,2048]{1,0:T(8,128)(2,1)}) %reduce-scatter.8.cloned.1.call-update) | async-done | bytes 2097168 | tf_op jit(solution)/shard_map/reduce_scatter | solution.py:339
  539.3 4.3 fusion.9
  543.6 115.1 %reduce-scatter.6.cloned.1.call-done = bf16[512,2048]{1,0:T(8,128)(2,1)} async-done(((bf16[4096,2048]{1,0:T(8,128)(2,1)}), bf16[512,2048]{1,0:T(8,128)(2,1)}) %reduce-scatter.6.cloned.1.call-update) | async-done | bytes 2097168 | tf_op jit(solution)/shard_map/reduce_scatter | solution.py:343
  658.7 5.5 fusion.6
  664.2 7.0 convolution_convert_fusion.4
  671.2 32.5 %shard_map.247 = (f32[20,64,512]{2,1,0:T(8,128)S(1)}, f32[5,64,1024]{2,1,0:T(8,128)S(1)}, f32[5,64,1024]{2,1,0:T(8,128)S(1)}) custom-call(s32[2]{0:T(128)S(1)} %pad_add_fusion.2.starts, bf16[20,64,512]{2,1,0:T(8,128)(2,1)S(1)} %copy-done.3, bf16[5,64,1024]{2,1,0:T(8,128)(2,1)S(1)} %copy-done.5, bf16[5,64,1024]{2,1,0:T(8,128)(2,1)S(1)} %get-tuple-element.138.v_ref, ...), custom_call_target="tpu_custom_call" | custom-call | flops 20132659200 | bytes 16777216 | tf_op jit(solution)/shard_map/pallas_call | solution.py:175
  706.1 14.9 %collective-permute-done.28 = bf16[10,64,512]{2,1,0:T(8,128)(2,1)S(1)} collective-permute-done((bf16[10,64,512]{2,1,0:T(8,128)(2,1)S(1)}, bf16[10,64,512]{2,1,0:T(8,128)(2,1)S(1)}, u32[]{:S(2)}, u32[]{:S(2)}) %collective-permute-start.28) | collective-permute-done | bytes 655392 | tf_op jit(solution)/shard_map/ppermute | solution.py:395
  723.1 4.5 convolution_convert_fusion.3
  727.8 13.6 %convolution_convert_fusion.7 = bf16[2048,512]{1,0:T(8,128)(2,1)S(1)} fusion(bf16[4096,2048]{1,0:T(8,128)(2,1)} %all-gather.17.cloned.1.call-done, bf16[4096,512]{1,0:T(8,128)(2,1)} %get-tuple-element.78), kind=kOutput, calls=%fused_computation.58 | convolution fusion | flops 8590983168 | bytes 23068672 | tf_op jit(solution)/shard_map/dot_general | solution.py:27
  746.1 17.5 %collective-permute-done.41 = bf16[2048,128]{1,0:T(8,128)(2,1)S(1)} collective-permute-done((bf16[2048,128]{1,0:T(8,128)(2,1)S(1)}, bf16[2048,128]{1,0:T(8,128)(2,1)S(1)}, u32[]{:S(2)}, u32[]{:S(2)}) %collective-permute-start.41) | collective-permute-done | bytes 524320 | tf_op jit(solution)/shard_map/ppermute | solution.py:35
  763.7 16.9 %collective-permute-done.43 = bf16[2048,128]{1,0:T(8,128)(2,1)S(1)} collective-permute-done((bf16[2048,128]{1,0:T(8,128)(2,1)S(1)}, bf16[2048,128]{1,0:T(8,128)(2,1)S(1)}, u32[]{:S(2)}, u32[]{:S(2)}) %collective-permute-start.43) | collective-permute-done | bytes 524320 | tf_op jit(solution)/shard_map/ppermute | solution.py:35
  780.6 6.6 collective-permute-done.42
  788.4 13.7 %convolution_convert_fusion.6 = bf16[2048,512]{1,0:T(8,128)(2,1)S(1)} fusion(bf16[4096,2048]{1,0:T(8,128)(2,1)} %all-gather.17.cloned.1.call-done, bf16[4096,512]{1,0:T(8,128)(2,1)} %get-tuple-element.79), kind=kOutput, calls=%fused_computation.57 | convolution fusion | flops 8590983168 | bytes 23068672 | tf_op jit(solution)/shard_map/dot_general | solution.py:27
  808.5 17.4 %collective-permute-done.44 = bf16[2048,128]{1,0:T(8,128)(2,1)S(1)} collective-permute-done((bf16[2048,128]{1,0:T(8,128)(2,1)S(1)}, bf16[2048,128]{1,0:T(8,128)(2,1)S(1)}, u32[]{:S(2)}, u32[]{:S(2)}) %collective-permute-start.44) | collective-permute-done | bytes 524320 | tf_op jit(solution)/shard_map/ppermute | solution.py:35
  825.8 17.5 %collective-permute-done.46 = bf16[2048,128]{1,0:T(8,128)(2,1)S(1)} collective-permute-done((bf16[2048,128]{1,0:T(8,128)(2,1)S(1)}, bf16[2048,128]{1,0:T(8,128)(2,1)S(1)}, u32[]{:S(2)}, u32[]{:S(2)}) %collective-permute-start.46) | collective-permute-done | bytes 524320 | tf_op jit(solution)/shard_map/ppermute | solution.py:35
  843.3 5.7 collective-permute-done.45
  850.2 13.8 %convolution_convert_fusion.5 = bf16[512,2048]{1,0:T(8,128)(2,1)S(1)} fusion(bf16[4096,512]{1,0:T(8,128)(2,1)} %get-tuple-element.80, bf16[4096,2048]{1,0:T(8,128)(2,1)} %all-gather.19.cloned.1.call-done), kind=kOutput, calls=%fused_computation.56 | convolution fusion | flops 8590983168 | bytes 23068672 | tf_op jit(solution)/shard_map/dot_general | solution.py:27
  870.0 16.1 %collective-permute-done.47 = bf16[128,2048]{1,0:T(8,128)(2,1)S(1)} collective-permute-done((bf16[128,2048]{1,0:T(8,128)(2,1)S(1)}, bf16[128,2048]{1,0:T(8,128)(2,1)S(1)}, u32[]{:S(2)}, u32[]{:S(2)}) %collective-permute-start.47) | collective-permute-done | bytes 524320 | tf_op jit(solution)/shard_map/ppermute | solution.py:35
  886.2 18.7 %collective-permute-done.49 = bf16[128,2048]{1,0:T(8,128)(2,1)S(1)} collective-permute-done((bf16[128,2048]{1,0:T(8,128)(2,1)S(1)}, bf16[128,2048]{1,0:T(8,128)(2,1)S(1)}, u32[]{:S(2)}, u32[]{:S(2)}) %collective-permute-start.49) | collective-permute-done | bytes 524320 | tf_op jit(solution)/shard_map/ppermute | solution.py:35
  904.9 4.8 collective-permute-done.48
  910.9 7.8 convolution_convert_fusion.1
  924.8 5.9 convolution_convert_fusion.2
  932.3 4.3 collective-permute-start.36
  936.6 6.8 copy_bitcast_fusion.1
  943.4 10.4 collective-permute-done.37
  957.0 7.7 copy_bitcast_fusion
  964.6 7.3 convert_element_type.298
  977.0 7.0 fusion.82
  984.0 8.7 collective-permute-done.24
  992.7 19.1 %collective-permute-done.22 = bf16[512,512]{1,0:T(8,128)(2,1)S(1)} collective-permute-done((bf16[512,512]{1,0:T(8,128)(2,1)S(1)}, bf16[512,512]{1,0:T(8,128)(2,1)S(1)}, u32[]{:S(2)}, u32[]{:S(2)}) %collective-permute-start.22) | collective-permute-done | bytes 524320 | tf_op jit(solution)/shard_map/ppermute | solution.py:35
  1011.9 4.7 collective-permute-done.23
  1028.3 6.4 fusion.20
  1039.1 4.3 fusion.17
  1049.0 60.6 %psum.7 = f32[4224]{0:T(1024)S(1)} all-reduce(f32[4224]{0:T(1024)S(1)} %concatenate.125), channel_id=1, replica_groups=mesh['dp'=8,'mp'=4] {'dp','mp'}, use_global_device_ids=true, to_apply=%region_15.16 | all-reduce | flops 4224 | bytes 33792 | tf_op jit(solution)/shard_map/psum | solution.py:432
  1119.8 5.2 collective-permute-start.33
  1125.5 6.2 collective-permute-done.34
  1137.8 4.2 fusion.68
  1147.6 5.3 fusion.49
  1153.0 8.9 all-gather.21.cloned.1.call-done
  (389 shorter events, 162.5 us)
Async XLA Ops:
  7.2 171.6 %all-gather.13.cloned.1.call-start = ((), (), s32[]{:S(2)}) async-start(), calls=%async_computation.5 | async-start | bytes 5898240 | tf_op jit(solution)/shard_map/all_gather | solution.py:281
  8.6 16.3 %collective-permute-start.5 = (bf16[256,384]{1,0:T(8,128)(2,1)S(1)}, bf16[256,384]{1,0:T(8,128)(2,1)S(1)}, u32[]{:S(2)}, u32[]{:S(2)}) collective-permute-start(bf16[256,384]{1,0:T(8,128)(2,1)S(1)} %constant_dynamic-slice_fusion.11), channel_id=1, source_target_pairs={{0,3},{1,2},{2,1},{3,0},{4,7},{5,6},{6,5},{7,4},{8,11},{9,10},{10,... | collective-permute-start | bytes 589832 | tf_op jit(solution)/shard_map/ppermute | solution.py:35
  9.1 16.8 %collective-permute-start.4 = (bf16[256,384]{1,0:T(8,128)(2,1)S(1)}, bf16[256,384]{1,0:T(8,128)(2,1)S(1)}, u32[]{:S(2)}, u32[]{:S(2)}) collective-permute-start(bf16[256,384]{1,0:T(8,128)(2,1)S(1)} %constant_dynamic-slice_fusion.11), channel_id=1, source_target_pairs={{0,2},{1,3},{2,0},{3,1},{4,6},{5,7},{6,4},{7,5},{8,10},{9,11},{10,... | collective-permute-start | bytes 589832 | tf_op jit(solution)/shard_map/ppermute | solution.py:35
  12.6 13.3 %collective-permute-start.3 = (bf16[256,384]{1,0:T(8,128)(2,1)S(1)}, bf16[256,384]{1,0:T(8,128)(2,1)S(1)}, u32[]{:S(2)}, u32[]{:S(2)}) collective-permute-start(bf16[256,384]{1,0:T(8,128)(2,1)S(1)} %constant_dynamic-slice_fusion.11), channel_id=1, source_target_pairs={{0,1},{1,0},{2,3},{3,2},{4,5},{5,4},{6,7},{7,6},{8,9},{9,8},{10,11... | collective-permute-start | bytes 589832 | tf_op jit(solution)/shard_map/ppermute | solution.py:35
  28.6 181.4 %all-gather.15.cloned.1.call-start = ((), (), s32[]{:S(2)}) async-start(), calls=%async_computation.6 | async-start | bytes 5898240 | tf_op jit(solution)/shard_map/all_gather | solution.py:288
  34.9 8.7 collective-permute-start.12
  38.5 11.4 collective-permute-start.11
  38.5 15.2 %collective-permute-start.10 = (bf16[160,512]{1,0:T(8,128)(2,1)S(1)}, bf16[160,512]{1,0:T(8,128)(2,1)S(1)}, u32[]{:S(2)}, u32[]{:S(2)}) collective-permute-start(bf16[160,512]{1,0:T(8,128)(2,1)S(1)} %fusion.30), channel_id=1, source_target_pairs={{0,3},{1,2},{2,1},{3,0},{4,7},{5,6},{6,5},{7,4},{8,11},{9,10},{10,... | collective-permute-start | bytes 491528 | tf_op jit(solution)/shard_map/ppermute | solution.py:35
  54.7 241.3 %all-gather.19.cloned.1.call-start = ((), (), s32[]{:S(2)}) async-start(), calls=%async_computation.9 | async-start | bytes 18874368 | tf_op jit(solution)/shard_map/all_gather | solution.py:298
  58.1 31.9 %collective-permute-start.25 = (bf16[512,512]{1,0:T(8,128)(2,1)S(1)}, bf16[512,512]{1,0:T(8,128)(2,1)S(1)}, u32[]{:S(2)}, u32[]{:S(2)}) collective-permute-start(bf16[512,512]{1,0:T(8,128)(2,1)S(1)} %pad_maximum_fusion.14), channel_id=1, source_target_pairs={{0,3},{1,2},{2,1},{3,0},{4,7},{5,6},{6,5},{7,4},{8,11},{9,10},{10,... | collective-permute-start | bytes 1572872 | tf_op jit(solution)/shard_map/ppermute | solution.py:35
  58.8 40.5 %collective-permute-start.26 = (bf16[512,512]{1,0:T(8,128)(2,1)S(1)}, bf16[512,512]{1,0:T(8,128)(2,1)S(1)}, u32[]{:S(2)}, u32[]{:S(2)}) collective-permute-start(bf16[512,512]{1,0:T(8,128)(2,1)S(1)} %pad_maximum_fusion.15), channel_id=1, source_target_pairs={{0,2},{1,3},{2,0},{3,1},{4,6},{5,7},{6,4},{7,5},{8,10},{9,11},{10,... | collective-permute-start | bytes 1572872 | tf_op jit(solution)/shard_map/ppermute | solution.py:35
  59.7 39.5 %collective-permute-start.27 = (bf16[512,512]{1,0:T(8,128)(2,1)S(1)}, bf16[512,512]{1,0:T(8,128)(2,1)S(1)}, u32[]{:S(2)}, u32[]{:S(2)}) collective-permute-start(bf16[512,512]{1,0:T(8,128)(2,1)S(1)} %pad_maximum_fusion.16), channel_id=1, source_target_pairs={{0,1},{1,0},{2,3},{3,2},{4,5},{5,4},{6,7},{7,6},{8,9},{9,8},{10,11... | collective-permute-start | bytes 1572872 | tf_op jit(solution)/shard_map/ppermute | solution.py:35
  102.8 231.4 %all-gather.17.cloned.1.call-start = ((), (), s32[]{:S(2)}) async-start(), calls=%async_computation.7 | async-start | bytes 18874368 | tf_op jit(solution)/shard_map/all_gather | solution.py:329
  102.9 9.4 collective-permute-start.8
  106.3 7.5 collective-permute-start.7
  106.4 7.4 collective-permute-start.6
  107.9 23.3 %collective-permute-start.2 = (bf16[512,512]{1,0:T(8,128)(2,1)S(1)}, bf16[512,512]{1,0:T(8,128)(2,1)S(1)}, u32[]{:S(2)}, u32[]{:S(2)}) collective-permute-start(bf16[512,512]{1,0:T(8,128)(2,1)S(1)} %pad_maximum_fusion.12), channel_id=1, source_target_pairs={{0,1},{1,0},{2,3},{3,2},{4,5},{5,4},{6,7},{7,6},{8,9},{9,8},{10,11... | collective-permute-start | bytes 1572872 | tf_op jit(solution)/shard_map/ppermute | solution.py:35
  110.9 35.0 %collective-permute-start.1 = (bf16[512,512]{1,0:T(8,128)(2,1)S(1)}, bf16[512,512]{1,0:T(8,128)(2,1)S(1)}, u32[]{:S(2)}, u32[]{:S(2)}) collective-permute-start(bf16[512,512]{1,0:T(8,128)(2,1)S(1)} %pad_maximum_fusion.11), channel_id=1, source_target_pairs={{0,2},{1,3},{2,0},{3,1},{4,6},{5,7},{6,4},{7,5},{8,10},{9,11},{10,... | collective-permute-start | bytes 1572872 | tf_op jit(solution)/shard_map/ppermute | solution.py:35
  112.3 44.9 %collective-permute-start = (bf16[512,512]{1,0:T(8,128)(2,1)S(1)}, bf16[512,512]{1,0:T(8,128)(2,1)S(1)}, u32[]{:S(2)}, u32[]{:S(2)}) collective-permute-start(bf16[512,512]{1,0:T(8,128)(2,1)S(1)} %pad_maximum_fusion.10), channel_id=1, source_target_pairs={{0,3},{1,2},{2,1},{3,0},{4,7},{5,6},{6,5},{7,4},{8,11},{9,10},{10,... | collective-permute-start | bytes 1572872 | tf_op jit(solution)/shard_map/ppermute | solution.py:35
  163.6 14.7 %collective-permute-start.9 = (bf16[10,64,512]{2,1,0:T(8,128)(2,1)S(1)}, bf16[10,64,512]{2,1,0:T(8,128)(2,1)S(1)}, u32[]{:S(2)}, u32[]{:S(2)}) collective-permute-start(bf16[10,64,512]{2,1,0:T(8,128)(2,1)S(1)} %pad_maximum_fusion.7), channel_id=1, source_target_pairs={{0,1},{1,0},{2,3},{3,2},{4,5},{5,4},{6,7},{7,6},{8,9},{9,8},{10,11... | collective-permute-start | bytes 1966088 | tf_op jit(solution)/shard_map/ppermute | solution.py:309
  221.8 317.5 %reduce-scatter.8.cloned.1.call-start = ((), (), s32[]{:S(2)}) async-start(), calls=%async_computation.10 | async-start | bytes 18874368 | tf_op jit(solution)/shard_map/reduce_scatter | solution.py:339
  222.9 53.8 %collective-permute-start.21 = (bf16[128,2048]{1,0:T(8,128)(2,1)S(1)}, bf16[128,2048]{1,0:T(8,128)(2,1)S(1)}, u32[]{:S(2)}, u32[]{:S(2)}) collective-permute-start(bf16[128,2048]{1,0:T(8,128)(2,1)S(1)} %constant_dynamic-slice_fusion.8), channel_id=1, source_target_pairs={{0,3},{1,2},{2,1},{3,0},{4,7},{5,6},{6,5},{7,4},{8,11},{9,10},{10,... | collective-permute-start | bytes 1572872 | tf_op jit(solution)/shard_map/ppermute | solution.py:35
  223.5 65.8 %collective-permute-start.20 = (bf16[128,2048]{1,0:T(8,128)(2,1)S(1)}, bf16[128,2048]{1,0:T(8,128)(2,1)S(1)}, u32[]{:S(2)}, u32[]{:S(2)}) collective-permute-start(bf16[128,2048]{1,0:T(8,128)(2,1)S(1)} %constant_dynamic-slice_fusion.8), channel_id=1, source_target_pairs={{0,2},{1,3},{2,0},{3,1},{4,6},{5,7},{6,4},{7,5},{8,10},{9,11},{10,... | collective-permute-start | bytes 1572872 | tf_op jit(solution)/shard_map/ppermute | solution.py:35
  225.7 65.2 %collective-permute-start.19 = (bf16[128,2048]{1,0:T(8,128)(2,1)S(1)}, bf16[128,2048]{1,0:T(8,128)(2,1)S(1)}, u32[]{:S(2)}, u32[]{:S(2)}) collective-permute-start(bf16[128,2048]{1,0:T(8,128)(2,1)S(1)} %constant_dynamic-slice_fusion.8), channel_id=1, source_target_pairs={{0,1},{1,0},{2,3},{3,2},{4,5},{5,4},{6,7},{7,6},{8,9},{9,8},{10,11... | collective-permute-start | bytes 1572872 | tf_op jit(solution)/shard_map/ppermute | solution.py:35
  227.5 97.6 %collective-permute-start.18 = (bf16[2048,128]{1,0:T(8,128)(2,1)S(1)}, bf16[2048,128]{1,0:T(8,128)(2,1)}, u32[]{:S(2)}, u32[]{:S(2)}) collective-permute-start(bf16[2048,128]{1,0:T(8,128)(2,1)S(1)} %constant_dynamic-slice_fusion.9), channel_id=1, source_target_pairs={{0,3},{1,2},{2,1},{3,0},{4,7},{5,6},{6,5},{7,4},{8,11},{9,10},{10,... | collective-permute-start | bytes 1572872 | tf_op jit(solution)/shard_map/ppermute | solution.py:35
  228.1 106.1 %collective-permute-start.17 = (bf16[2048,128]{1,0:T(8,128)(2,1)S(1)}, bf16[2048,128]{1,0:T(8,128)(2,1)}, u32[]{:S(2)}, u32[]{:S(2)}) collective-permute-start(bf16[2048,128]{1,0:T(8,128)(2,1)S(1)} %constant_dynamic-slice_fusion.9), channel_id=1, source_target_pairs={{0,2},{1,3},{2,0},{3,1},{4,6},{5,7},{6,4},{7,5},{8,10},{9,11},{10,... | collective-permute-start | bytes 1572872 | tf_op jit(solution)/shard_map/ppermute | solution.py:35
  276.7 57.6 %collective-permute-start.16 = (bf16[2048,128]{1,0:T(8,128)(2,1)S(1)}, bf16[2048,128]{1,0:T(8,128)(2,1)}, u32[]{:S(2)}, u32[]{:S(2)}) collective-permute-start(bf16[2048,128]{1,0:T(8,128)(2,1)S(1)} %constant_dynamic-slice_fusion.9), channel_id=1, source_target_pairs={{0,1},{1,0},{2,3},{3,2},{4,5},{5,4},{6,7},{7,6},{8,9},{9,8},{10,11... | collective-permute-start | bytes 1572872 | tf_op jit(solution)/shard_map/ppermute | solution.py:35
  289.2 59.8 %collective-permute-start.15 = (bf16[2048,128]{1,0:T(8,128)(2,1)S(1)}, bf16[2048,128]{1,0:T(8,128)(2,1)}, u32[]{:S(2)}, u32[]{:S(2)}) collective-permute-start(bf16[2048,128]{1,0:T(8,128)(2,1)S(1)} %constant_dynamic-slice_fusion.10), channel_id=1, source_target_pairs={{0,3},{1,2},{2,1},{3,0},{4,7},{5,6},{6,5},{7,4},{8,11},{9,10},{10,... | collective-permute-start | bytes 1572872 | tf_op jit(solution)/shard_map/ppermute | solution.py:35
  291.7 63.9 %collective-permute-start.14 = (bf16[2048,128]{1,0:T(8,128)(2,1)S(1)}, bf16[2048,128]{1,0:T(8,128)(2,1)}, u32[]{:S(2)}, u32[]{:S(2)}) collective-permute-start(bf16[2048,128]{1,0:T(8,128)(2,1)S(1)} %constant_dynamic-slice_fusion.10), channel_id=1, source_target_pairs={{0,2},{1,3},{2,0},{3,1},{4,6},{5,7},{6,4},{7,5},{8,10},{9,11},{10,... | collective-permute-start | bytes 1572872 | tf_op jit(solution)/shard_map/ppermute | solution.py:35
  325.2 30.4 %collective-permute-start.13 = (bf16[2048,128]{1,0:T(8,128)(2,1)S(1)}, bf16[2048,128]{1,0:T(8,128)(2,1)}, u32[]{:S(2)}, u32[]{:S(2)}) collective-permute-start(bf16[2048,128]{1,0:T(8,128)(2,1)S(1)} %constant_dynamic-slice_fusion.10), channel_id=1, source_target_pairs={{0,1},{1,0},{2,3},{3,2},{4,5},{5,4},{6,7},{7,6},{8,9},{9,8},{10,11... | collective-permute-start | bytes 1572872 | tf_op jit(solution)/shard_map/ppermute | solution.py:35
  420.0 238.7 %reduce-scatter.6.cloned.1.call-start = ((), (), s32[]{:S(2)}) async-start(), calls=%async_computation.8 | async-start | bytes 18874368 | tf_op jit(solution)/shard_map/reduce_scatter | solution.py:343
  436.7 494.4 %reduce-scatter.12.cloned.1.call-start = ((), (), s32[]{:S(2)}) async-start(), calls=%async_computation.13 | async-start | bytes 2949120 | tf_op jit(solution)/shard_map/reduce_scatter | solution.py:413
  704.5 16.5 %collective-permute-start.28 = (bf16[10,64,512]{2,1,0:T(8,128)(2,1)S(1)}, bf16[10,64,512]{2,1,0:T(8,128)(2,1)S(1)}, u32[]{:S(2)}, u32[]{:S(2)}) collective-permute-start(bf16[10,64,512]{2,1,0:T(8,128)(2,1)S(1)} %select_convert_fusion), channel_id=1, source_target_pairs={{0,1},{1,0},{2,3},{3,2},{4,5},{5,4},{6,7},{7,6},{8,9},{9,8},{10,11... | collective-permute-start | bytes 1966088 | tf_op jit(solution)/shard_map/ppermute | solution.py:395
  727.7 208.9 %all-gather.29.cloned.1.call-start = ((), (), s32[]{:S(2)}) async-start(), calls=%async_computation.18 | async-start | bytes 4718592 | tf_op jit(solution)/shard_map/all_gather | solution.py:354
  741.7 22.0 %collective-permute-start.41 = (bf16[2048,128]{1,0:T(8,128)(2,1)S(1)}, bf16[2048,128]{1,0:T(8,128)(2,1)S(1)}, u32[]{:S(2)}, u32[]{:S(2)}) collective-permute-start(bf16[2048,128]{1,0:T(8,128)(2,1)S(1)} %get-tuple-element.101), channel_id=1, source_target_pairs={{0,1},{1,0},{2,3},{3,2},{4,5},{5,4},{6,7},{7,6},{8,9},{9,8},{10,11... | collective-permute-start | bytes 1572872 | tf_op jit(solution)/shard_map/ppermute | solution.py:35
  743.2 37.3 %collective-permute-start.43 = (bf16[2048,128]{1,0:T(8,128)(2,1)S(1)}, bf16[2048,128]{1,0:T(8,128)(2,1)S(1)}, u32[]{:S(2)}, u32[]{:S(2)}) collective-permute-start(bf16[2048,128]{1,0:T(8,128)(2,1)S(1)} %get-tuple-element.102), channel_id=1, source_target_pairs={{0,3},{1,2},{2,1},{3,0},{4,7},{5,6},{6,5},{7,4},{8,11},{9,10},{10,... | collective-permute-start | bytes 1572872 | tf_op jit(solution)/shard_map/ppermute | solution.py:35
  743.2 44.0 %collective-permute-start.42 = (bf16[2048,128]{1,0:T(8,128)(2,1)S(1)}, bf16[2048,128]{1,0:T(8,128)(2,1)S(1)}, u32[]{:S(2)}, u32[]{:S(2)}) collective-permute-start(bf16[2048,128]{1,0:T(8,128)(2,1)S(1)} %get-tuple-element.103), channel_id=1, source_target_pairs={{0,2},{1,3},{2,0},{3,1},{4,6},{5,7},{6,4},{7,5},{8,10},{9,11},{10,... | collective-permute-start | bytes 1572872 | tf_op jit(solution)/shard_map/ppermute | solution.py:35
  788.3 168.7 %all-gather.31.cloned.1.call-start = ((), (), s32[]{:S(2)}) async-start(), calls=%async_computation.19 | async-start | bytes 4718592 | tf_op jit(solution)/shard_map/all_gather | solution.py:354
  802.3 23.5 %collective-permute-start.44 = (bf16[2048,128]{1,0:T(8,128)(2,1)S(1)}, bf16[2048,128]{1,0:T(8,128)(2,1)S(1)}, u32[]{:S(2)}, u32[]{:S(2)}) collective-permute-start(bf16[2048,128]{1,0:T(8,128)(2,1)S(1)} %get-tuple-element.98), channel_id=1, source_target_pairs={{0,1},{1,0},{2,3},{3,2},{4,5},{5,4},{6,7},{7,6},{8,9},{9,8},{10,11... | collective-permute-start | bytes 1572872 | tf_op jit(solution)/shard_map/ppermute | solution.py:35
  806.0 37.3 %collective-permute-start.46 = (bf16[2048,128]{1,0:T(8,128)(2,1)S(1)}, bf16[2048,128]{1,0:T(8,128)(2,1)S(1)}, u32[]{:S(2)}, u32[]{:S(2)}) collective-permute-start(bf16[2048,128]{1,0:T(8,128)(2,1)S(1)} %get-tuple-element.99), channel_id=1, source_target_pairs={{0,3},{1,2},{2,1},{3,0},{4,7},{5,6},{6,5},{7,4},{8,11},{9,10},{10,... | collective-permute-start | bytes 1572872 | tf_op jit(solution)/shard_map/ppermute | solution.py:35
  806.3 42.7 %collective-permute-start.45 = (bf16[2048,128]{1,0:T(8,128)(2,1)S(1)}, bf16[2048,128]{1,0:T(8,128)(2,1)S(1)}, u32[]{:S(2)}, u32[]{:S(2)}) collective-permute-start(bf16[2048,128]{1,0:T(8,128)(2,1)S(1)} %get-tuple-element.100), channel_id=1, source_target_pairs={{0,2},{1,3},{2,0},{3,1},{4,6},{5,7},{6,4},{7,5},{8,10},{9,11},{10,... | collective-permute-start | bytes 1572872 | tf_op jit(solution)/shard_map/ppermute | solution.py:35
  850.2 114.5 %all-gather.27.cloned.1.call-start = ((), (), s32[]{:S(2)}) async-start(), calls=%async_computation.17 | async-start | bytes 4718592 | tf_op jit(solution)/shard_map/all_gather | solution.py:358
  864.1 22.0 %collective-permute-start.47 = (bf16[128,2048]{1,0:T(8,128)(2,1)S(1)}, bf16[128,2048]{1,0:T(8,128)(2,1)S(1)}, u32[]{:S(2)}, u32[]{:S(2)}) collective-permute-start(bf16[128,2048]{1,0:T(8,128)(2,1)S(1)} %get-tuple-element.95), channel_id=1, source_target_pairs={{0,1},{1,0},{2,3},{3,2},{4,5},{5,4},{6,7},{7,6},{8,9},{9,8},{10,11... | collective-permute-start | bytes 1572872 | tf_op jit(solution)/shard_map/ppermute | solution.py:35
  867.6 37.3 %collective-permute-start.49 = (bf16[128,2048]{1,0:T(8,128)(2,1)S(1)}, bf16[128,2048]{1,0:T(8,128)(2,1)S(1)}, u32[]{:S(2)}, u32[]{:S(2)}) collective-permute-start(bf16[128,2048]{1,0:T(8,128)(2,1)S(1)} %get-tuple-element.96), channel_id=1, source_target_pairs={{0,3},{1,2},{2,1},{3,0},{4,7},{5,6},{6,5},{7,4},{8,11},{9,10},{10,... | collective-permute-start | bytes 1572872 | tf_op jit(solution)/shard_map/ppermute | solution.py:35
  868.1 41.5 %collective-permute-start.48 = (bf16[128,2048]{1,0:T(8,128)(2,1)S(1)}, bf16[128,2048]{1,0:T(8,128)(2,1)S(1)}, u32[]{:S(2)}, u32[]{:S(2)}) collective-permute-start(bf16[128,2048]{1,0:T(8,128)(2,1)S(1)} %get-tuple-element.97), channel_id=1, source_target_pairs={{0,2},{1,3},{2,0},{3,1},{4,6},{5,7},{6,4},{7,5},{8,10},{9,11},{10,... | collective-permute-start | bytes 1572872 | tf_op jit(solution)/shard_map/ppermute | solution.py:35
  910.8 111.3 %reduce-scatter.14.cloned.1.call-start = ((), (), s32[]{:S(2)}) async-start(), calls=%async_computation.15 | async-start | bytes 5898240 | tf_op jit(solution)/shard_map/reduce_scatter | solution.py:369
  918.7 190.9 %reduce-scatter.10.cloned.1.call-start = ((), (), s32[]{:S(2)}) async-start(), calls=%async_computation.11 | async-start | bytes 5898240 | tf_op jit(solution)/shard_map/reduce_scatter | solution.py:404
  930.8 207.0 %all-gather.23.cloned.1.call-start = ((), (), s32[]{:S(2)}) async-start(), calls=%async_computation.14 | async-start | bytes 2949120 | tf_op jit(solution)/shard_map/all_gather | solution.py:417
  931.1 22.7 %collective-permute-start.37 = (bf16[256,640]{1,0:T(8,128)(2,1)}, bf16[256,640]{1,0:T(8,128)(2,1)S(1)}, u32[]{:S(2)}, u32[]{:S(2)}) collective-permute-start(bf16[256,640]{1,0:T(8,128)(2,1)} %reduce-scatter.12.cloned.1.call-done), channel_id=1, source_target_pairs={{0,3},{1,2},{2,1},{3,0},{4,7},{5,6},{6,5},{7,4},{8,11},{9,10},{10,... | collective-permute-start | bytes 983048 | tf_op jit(solution)/shard_map/ppermute | solution.py:35
  932.3 23.7 %collective-permute-start.36 = (bf16[256,640]{1,0:T(8,128)(2,1)}, bf16[256,640]{1,0:T(8,128)(2,1)S(1)}, u32[]{:S(2)}, u32[]{:S(2)}) collective-permute-start(bf16[256,640]{1,0:T(8,128)(2,1)} %reduce-scatter.12.cloned.1.call-done), channel_id=1, source_target_pairs={{0,2},{1,3},{2,0},{3,1},{4,6},{5,7},{6,4},{7,5},{8,10},{9,11},{10,... | collective-permute-start | bytes 983048 | tf_op jit(solution)/shard_map/ppermute | solution.py:35
  936.6 19.4 %collective-permute-start.35 = (bf16[256,640]{1,0:T(8,128)(2,1)}, bf16[256,640]{1,0:T(8,128)(2,1)S(1)}, u32[]{:S(2)}, u32[]{:S(2)}) collective-permute-start(bf16[256,640]{1,0:T(8,128)(2,1)} %reduce-scatter.12.cloned.1.call-done), channel_id=1, source_target_pairs={{0,1},{1,0},{2,3},{3,2},{4,5},{5,4},{6,7},{7,6},{8,9},{9,8},{10,11... | collective-permute-start | bytes 983048 | tf_op jit(solution)/shard_map/ppermute | solution.py:35
  956.9 190.7 %all-gather.25.cloned.1.call-start = ((), (), s32[]{:S(2)}) async-start(), calls=%async_computation.16 | async-start | bytes 1474560 | tf_op jit(solution)/shard_map/all_gather | solution.py:372
  972.1 20.6 %collective-permute-start.24 = (bf16[512,512]{1,0:T(8,128)(2,1)S(1)}, bf16[512,512]{1,0:T(8,128)(2,1)S(1)}, u32[]{:S(2)}, u32[]{:S(2)}) collective-permute-start(bf16[512,512]{1,0:T(8,128)(2,1)S(1)} %get-tuple-element.121), channel_id=1, source_target_pairs={{0,1},{1,0},{2,3},{3,2},{4,5},{5,4},{6,7},{7,6},{8,9},{9,8},{10,11... | collective-permute-start | bytes 1572872 | tf_op jit(solution)/shard_map/ppermute | solution.py:35
  974.5 37.3 %collective-permute-start.22 = (bf16[512,512]{1,0:T(8,128)(2,1)S(1)}, bf16[512,512]{1,0:T(8,128)(2,1)S(1)}, u32[]{:S(2)}, u32[]{:S(2)}) collective-permute-start(bf16[512,512]{1,0:T(8,128)(2,1)S(1)} %get-tuple-element.122), channel_id=1, source_target_pairs={{0,3},{1,2},{2,1},{3,0},{4,7},{5,6},{6,5},{7,4},{8,11},{9,10},{10,... | collective-permute-start | bytes 1572872 | tf_op jit(solution)/shard_map/ppermute | solution.py:35
  975.4 41.2 %collective-permute-start.23 = (bf16[512,512]{1,0:T(8,128)(2,1)S(1)}, bf16[512,512]{1,0:T(8,128)(2,1)S(1)}, u32[]{:S(2)}, u32[]{:S(2)}) collective-permute-start(bf16[512,512]{1,0:T(8,128)(2,1)S(1)} %get-tuple-element.123), channel_id=1, source_target_pairs={{0,2},{1,3},{2,0},{3,1},{4,6},{5,7},{6,4},{7,5},{8,10},{9,11},{10,... | collective-permute-start | bytes 1572872 | tf_op jit(solution)/shard_map/ppermute | solution.py:35
  1023.5 11.2 collective-permute-start.38
  1026.8 8.0 collective-permute-start.39
  1027.3 10.9 collective-permute-start.40
  1039.0 122.8 %all-gather.21.cloned.1.call-start = ((), (), s32[]{:S(2)}) async-start(), calls=%async_computation.12 | async-start | bytes 1769472 | tf_op jit(solution)/shard_map/all_gather | solution.py:410
  1044.5 89.6 %collective-permute-start.31 = (bf16[512,512]{1,0:T(8,128)(2,1)}, bf16[512,512]{1,0:T(8,128)(2,1)S(1)}, u32[]{:S(2)}, u32[]{:S(2)}) collective-permute-start(bf16[512,512]{1,0:T(8,128)(2,1)} %get-tuple-element.104), channel_id=1, source_target_pairs={{0,1},{1,0},{2,3},{3,2},{4,5},{5,4},{6,7},{7,6},{8,9},{9,8},{10,11... | collective-permute-start | bytes 1572872 | tf_op jit(solution)/shard_map/ppermute | solution.py:35
  1044.5 89.7 %collective-permute-start.29 = (bf16[512,512]{1,0:T(8,128)(2,1)}, bf16[512,512]{1,0:T(8,128)(2,1)S(1)}, u32[]{:S(2)}, u32[]{:S(2)}) collective-permute-start(bf16[512,512]{1,0:T(8,128)(2,1)} %get-tuple-element.105), channel_id=1, source_target_pairs={{0,3},{1,2},{2,1},{3,0},{4,7},{5,6},{6,5},{7,4},{8,11},{9,10},{10,... | collective-permute-start | bytes 1572872 | tf_op jit(solution)/shard_map/ppermute | solution.py:35
  1045.2 89.0 %collective-permute-start.30 = (bf16[512,512]{1,0:T(8,128)(2,1)S(1)}, bf16[512,512]{1,0:T(8,128)(2,1)S(1)}, u32[]{:S(2)}, u32[]{:S(2)}) collective-permute-start(bf16[512,512]{1,0:T(8,128)(2,1)S(1)} %get-tuple-element.106), channel_id=1, source_target_pairs={{0,2},{1,3},{2,0},{3,1},{4,6},{5,7},{6,4},{7,5},{8,10},{9,11},{10,... | collective-permute-start | bytes 1572872 | tf_op jit(solution)/shard_map/ppermute | solution.py:35
  1116.1 15.6 %collective-permute-start.34 = (bf16[256,384]{1,0:T(8,128)(2,1)S(1)}, bf16[256,384]{1,0:T(8,128)(2,1)S(1)}, u32[]{:S(2)}, u32[]{:S(2)}) collective-permute-start(bf16[256,384]{1,0:T(8,128)(2,1)S(1)} %get-tuple-element.143), channel_id=1, source_target_pairs={{0,3},{1,2},{2,1},{3,0},{4,7},{5,6},{6,5},{7,4},{8,11},{9,10},{10,... | collective-permute-start | bytes 589832 | tf_op jit(solution)/shard_map/ppermute | solution.py:35
  1119.8 13.6 %collective-permute-start.33 = (bf16[256,384]{1,0:T(8,128)(2,1)S(1)}, bf16[256,384]{1,0:T(8,128)(2,1)S(1)}, u32[]{:S(2)}, u32[]{:S(2)}) collective-permute-start(bf16[256,384]{1,0:T(8,128)(2,1)S(1)} %get-tuple-element.144), channel_id=1, source_target_pairs={{0,2},{1,3},{2,0},{3,1},{4,6},{5,7},{6,4},{7,5},{8,10},{9,11},{10,... | collective-permute-start | bytes 589832 | tf_op jit(solution)/shard_map/ppermute | solution.py:35
  (81 other events, 1096.4 us)
Sparse Core Ops, SparseCore 0:
  28.7 44.1 all-gather.12
  75.3 41.1 all-gather.14
  118.9 89.8 all-gather.18
  221.9 89.8 all-gather.16
  420.1 119.1 reduce-scatter.7
  542.7 115.9 reduce-scatter.5
  727.8 43.6 reduce-scatter.11
  788.4 38.9 all-gather.28
  850.3 38.6 all-gather.30
  911.0 38.4 all-gather.26
  952.8 56.5 reduce-scatter.13
  1013.1 56.6 reduce-scatter.9
  1072.2 30.1 all-gather.22
  1104.2 24.5 all-gather.24
  1134.3 27.4 all-gather.20

commit v2 on v1

--- a/solution.py
+++ b/solution.py
@@ -4,6 +4,7 @@
 import jax
 import jax.numpy as jnp
 from jax import lax
+from jax.experimental.layout import Layout, with_layout_constraint
 from jax.experimental import pallas as pl
 from jax.experimental.pallas import tpu as pltpu
 from jax.sharding import PartitionSpec as P
@@ -43,6 +44,172 @@
         blocks = [jnp.where(flag, blocks[j ^ bit], blocks[j]) for j in range(len(blocks))]
         bit *= 2
     return blocks
+
+
+def exchange(array, axis, mask, n):
+    return lax.ppermute(array, axis, [(i, i ^ mask) for i in range(n)])
+
+
+def by_rows(array):
+    return with_layout_constraint(array, Layout(tuple(range(array.ndim))))
+
+
+def added(*terms):
+    return sum(term.astype(full) for term in terms).astype(low)
+
+
+class Order:
+    def __init__(self, token):
+        self.token = token
+
+    def __call__(self, *arrays):
+        self.token, *arrays = lax.optimization_barrier((self.token, *arrays))
+        return arrays
+
+
+class RelayGather:
+    def __init__(self, piece, axis, n):
+        self.axis, self.n, self.step, self.own = axis, n, 1, piece
+        self.ups, self.downs = [], []
+        self.send(piece, piece)
+
+    def send(self, up, down):
+        n, step = self.n, self.step
+        right = [(i, i + 1) for i in range(step - 1, n - 1)]
+        left = [(i, i - 1) for i in range(n - step, 0, -1)]
+        self.flying = [lax.ppermute(up, self.axis, right), lax.ppermute(down, self.axis, left)]
+
+    def take(self, up, down):
+        self.ups.append(up)
+        self.downs.append(down)
+        self.step += 1
+        if self.step < self.n:
+            self.send(up, down)
+
+    def finish(self, order):
+        while self.step < self.n:
+            self.take(*order(*self.flying))
+        n = self.n
+        return [self.own] + [self.ups[k - 1] + self.downs[n - k - 1] for k in range(1, n)]
+
+
+CUBE = 8
+
+
+def at_index(array, index):
+    return lax.dynamic_index_in_dim(array, index, 0, keepdims=False)
+
+
+class Spread:
+    def __init__(self, piece, axis, n, group):
+        self.axis, self.n, self.chip, self.piece = axis, n, group // 2, piece
+        if n == CUBE:
+            self.flying = [self.move(piece, 2), self.move(piece, 4)]
+        else:
+            self.flying = [lax.all_gather(piece, axis, axis=0, tiled=True)]
+        self.buffer = []
+
+    def move(self, array, mask):
+        return exchange(array, self.axis, mask, self.n)
+
+    def second(self, *got):
+        self.flying = got
+        if self.n == CUBE:
+            near, far = got
+            half = self.piece.shape[0] // 2
+            self.flying = [self.move(near[:half], 4), self.move(far[half:], 2)]
+            mine = jnp.zeros((4, *self.piece.shape), self.piece.dtype)
+            for k, block in enumerate((self.piece, near, far)):
+                mine = lax.dynamic_update_slice(mine, block[None], (self.chip ^ k, 0, 0))
+            self.buffer = [mine]
+
+    def third(self, *got):
+        if self.n != CUBE:
+            self.parts, self.flying = list(got), []
+            return
+        rows = self.piece.shape[0]
+        (mine,) = self.buffer
+        for k, block in enumerate(got):
+            mine = lax.dynamic_update_slice(
+                mine, block[None], (self.chip ^ 3, k * (rows // 2), 0)
+            )
+        mine = mine.reshape(4 * rows, -1)
+        self.parts = [mine]
+        self.flying = [self.move(mine, 1)]
+
+    def last(self, *got):
+        self.parts += got
+
+
+class Collect:
+    def __init__(self, other, axis, n, group):
+        self.axis, self.n, self.chip = axis, n, group // 2
+        if n == CUBE:
+            self.flying = [self.move(other, 1)]
+        else:
+            self.flying = [lax.psum_scatter(other, axis, scatter_dimension=0, tiled=True)]
+
+    def move(self, array, mask):
+        return exchange(array, self.axis, mask, self.n)
+
+    def second(self, mine, *got, launch=True):
+        self.flying = got
+        if self.n != CUBE:
+            return
+        mine = mine.reshape(4, mine.shape[0] // 4, -1)
+        got = got[0].reshape(mine.shape)
+        half = self.half = mine.shape[1] // 2
+        self.sums = added(mine, got)
+        block = lambda k: at_index(self.sums, self.chip ^ k)
+        self.flying = [
+            jnp.concatenate([block(3)[:half], block(1)[:half]], 0),
+            jnp.concatenate([block(3)[half:], block(2)[half:]], 0),
+        ]
+        if launch:
+            self.launch(*self.flying)
+
+    def launch(self, *ready):
+        self.flying = ready
+        if self.n == CUBE:
+            self.flying = [self.move(ready[0], 2), self.move(ready[1], 4)]
+
+    def third(self, *got):
+        if self.n != CUBE:
+            self.flying = got
+            return
+        half = self.half
+        block = lambda k: at_index(self.sums, self.chip ^ k)
+        self.direct = [got[0][half:], got[1][half:]]
+        self.flying = [
+            self.move(added(block(2)[:half], got[0][:half]), 4),
+            self.move(added(block(1)[half:], got[1][:half]), 2),
+        ]
+
+    def last(self, *got):
+        if self.n != CUBE:
+            return got[0]
+        half = self.half
+        own = at_index(self.sums, self.chip)
+        return jnp.concatenate(
+            [
+                added(own[:half], self.direct[0], got[0]),
+                added(own[half:], self.direct[1], got[1]),
+            ],
+            0,
+        )
+
+
+EXTRA = 128
+
+
+def order_split(order, first, *lists):
+    first = list(first)
+    got = order(*first, *[array for arrays in lists for array in arrays])
+    result, at = list(got[: len(first)]), len(first)
+    for arrays in lists:
+        result.append(list(got[at : at + len(arrays)]))
+        at += len(arrays)
+    return result
 
 
 def rotary_tables(positions):
@@ -163,7 +330,7 @@
         ),
         compiler_params=pltpu.CompilerParams(vmem_limit_bytes=40 << 20),
         cost_estimate=pl.CostEstimate(
-            flops=pairs * HD * 16, bytes_accessed=8 << 20, transcendentals=pairs
+            flops=pairs, bytes_accessed=1 << 20, transcendentals=0
         ),
     )(starts, queries, keys, values)
 
@@ -188,9 +355,39 @@
         ),
         compiler_params=pltpu.CompilerParams(vmem_limit_bytes=40 << 20),
         cost_estimate=pl.CostEstimate(
-            flops=pairs * HD * 40, bytes_accessed=16 << 20, transcendentals=pairs
+            flops=pairs, bytes_accessed=1 << 20, transcendentals=0
         ),
     )(starts, queries, keys, values, grads, sums_in)
+
+
+def widen_kernel(wide_ref, down_ref, gate_out, up_out, down_out):
+    units = gate_out.shape[1]
+    gate_out[...] = wide_ref[0, :, :units].astype(full)
+    up_out[...] = wide_ref[0, :, units:].astype(full)
+    down_out[...] = down_ref[...].astype(full)
+
+
+def widen(wide, down):
+    groups, rows, columns = wide.shape
+    units = columns // 2
+    if units % 128:
+        pairs = jnp.transpose(wide, (1, 0, 2)).reshape(rows, groups, 2, units).astype(full)
+        gate, up = (pairs[:, :, k].reshape(rows, -1) for k in range(2))
+        return gate, up, down.astype(full)
+    shape = jax.ShapeDtypeStruct((rows, groups * units), full)
+    column = pl.BlockSpec((rows, units), lambda g: (0, g))
+    return pl.pallas_call(
+        widen_kernel,
+        out_shape=(shape, shape, jax.ShapeDtypeStruct(down.shape, full)),
+        grid=(groups,),
+        in_specs=[
+            pl.BlockSpec((1, rows, columns), lambda g: (g, 0, 0)),
+            pl.BlockSpec((units, down.shape[1]), lambda g: (g, 0)),
+        ],
+        out_specs=[column, column, pl.BlockSpec((units, down.shape[1]), lambda g: (g, 0))],
+        compiler_params=pltpu.CompilerParams(vmem_limit_bytes=32 << 20),
+        cost_estimate=pl.CostEstimate(flops=0, bytes_accessed=1 << 16, transcendentals=0),
+    )(wide, down)
 
 
 def norm_backward(values, rms, gain, normed_grad):
@@ -252,132 +449,201 @@
         last = lax.dynamic_slice_in_dim(array, base + (2 * ring - 1 - at) * chunk, chunk, 0)
         return jnp.concatenate([first, last], 0)
 
-    def to_tokens(array):
-        got = swap([rows_of(array, rank ^ k) for k in ranks], "mp")
-        return jnp.concatenate(by_rank(got, rank), axis=1)
-
-    def to_features(array, kind):
-        array = array.astype(low)
-        pieces = by_rank([array[:, j * share : (j + 1) * share] for j in ranks], rank)
-        got = by_rank(swap(pieces, "mp"), rank)
-        rows = []
-        for seq in range(seqs):
-            near = got[seq * ring : (seq + 1) * ring]
-            rows += [block[:chunk] for block in near]
-            rows += [block[chunk:] for block in near[::-1]]
-        return jnp.concatenate(rows, 0).astype(kind)
-
-    def everyone(piece):
-        return jnp.concatenate(by_rank(swap([piece] * parts, "mp"), rank), axis=0)
-
-    inputs = to_tokens(hidden_in).astype(full)
-    gains = everyone(jnp.stack([attention_gain, feedforward_gain], 1)).T
-    attention_gain_all, feedforward_gain_all = gains[0], gains[1]
-
+    order = Order(head_counts)
     rows = D // groups
+    heads_here = QH * HD // groups
+
     query_slice = lax.dynamic_slice_in_dim(query_projection_weight, group * rows, rows, 0)
-    query_slice = jnp.concatenate(swap([query_slice] * parts, "mp"), axis=1)
+    gains = jnp.stack([attention_gain, feedforward_gain])
+    gains_high = gains.astype(low)
+    gains_low = (gains - gains_high.astype(full)).astype(low)
+    lines = -(-share // slots)
+    gains = jnp.pad(
+        jnp.concatenate([gains_high, gains_low], 0), ((0, 0), (0, lines * slots - share))
+    )
+    query_slice = jnp.concatenate([query_slice, gains.reshape(4 * lines, slots)], 0)
+    query_slice = swap([query_slice] * parts, "mp")
+    cosine, sine = rotary_tables(rows_of(positions, rank))
+    chosen = lax.dynamic_slice_in_dim(select, group * heads_here, heads_here, 1)
+    output_slice = dot(chosen, output_weight, 0, 0).astype(low)
+    pack = jnp.concatenate(
+        [
+            lax.dynamic_slice_in_dim(gate_weight, group * units, units, 1),
+            lax.dynamic_slice_in_dim(up_weight, group * units, units, 1),
+            lax.dynamic_slice_in_dim(down_projection_weight, group * units, units, 0).T,
+        ],
+        1,
+    )
+    inputs = [rows_of(hidden_in, rank ^ k) for k in ranks]
+    late = inputs[parts - 1]
+    inputs = inputs[:1] + [exchange(inputs[k], "mp", k, parts) for k in range(1, parts - 1)]
+    cotangent = [rows_of(cotangent, rank ^ k) for k in ranks]
+    got = order(
+        select_near, select, late, cosine, sine, output_slice, pack,
+        *query_slice, *cotangent, *inputs
+    )
+    select_near, select, late, cosine, sine, output_slice, pack = got[:7]
+    query_slice, cotangent = (got[7 + k * parts : 7 + (k + 1) * parts] for k in range(2))
+    inputs = got[7 + 2 * parts :]
+
+    inputs.append(exchange(late, "mp", parts - 1, parts))
+    output_slice = swap([output_slice] * parts, "mp")
+    gains = by_rank([piece[rows:].reshape(4, -1)[:, :share] for piece in query_slice], rank)
+    gains = jnp.concatenate(gains, 1).astype(full)
+    attention_gain_all, feedforward_gain_all = gains[0] + gains[2], gains[1] + gains[3]
+    query_slice = jnp.concatenate([piece[:rows] for piece in query_slice], axis=1)
     query_slice = mm(query_slice, select_near).astype(low)
     query_all = lax.all_gather(query_slice, "dp", axis=0, tiled=True)
-    heads_here = QH * HD // groups
-    chosen = lax.dynamic_slice_in_dim(select, group * heads_here, heads_here, 1)
-    output_slice = dot(chosen, output_weight, 0, 0).astype(low)
-    output_slice = jnp.concatenate(
-        by_rank(swap([output_slice] * parts, "mp"), rank), axis=1
-    )
-    output_all = lax.all_gather(output_slice, "dp", axis=0, tiled=True)
-
-    def near(piece, axis):
-        return jnp.concatenate(swap([piece] * parts, "mp"), axis=axis)
-
-    gate_here = near(lax.dynamic_slice_in_dim(gate_weight, group * units, units, 1), 1)
-    up_here = near(lax.dynamic_slice_in_dim(up_weight, group * units, units, 1), 1)
-    down_here = near(lax.dynamic_slice_in_dim(down_projection_weight, group * units, units, 0), 0)
-
-    cotangent_mine = to_tokens(cotangent)
-    cotangent_full = lax.all_gather(cotangent_mine, "dp", axis=0, tiled=True)
-
-    cosine, sine = rotary_tables(rows_of(positions, rank))
+    got = order(*inputs, *output_slice)
+    inputs, output_slice = got[:parts], got[parts:]
+
+    inputs = jnp.concatenate(by_rank(inputs, rank), axis=1).astype(full)
     first_rms = lax.rsqrt(jnp.mean(inputs * inputs, axis=1, keepdims=True) + epsilon)
     normed = (inputs * first_rms * attention_gain_all).astype(low)
     keys = dot(key_weight, normed, 0, 1).reshape(KVH, HD, mine)
     values_mine = dot(value_weight, normed, 0, 1).astype(low).reshape(KVH, HD, mine)
     turned_keys, key_pull = jax.vjp(lambda v, g: turn(v, g, cosine, sine), keys, key_gain)
     pair_mine = jnp.concatenate([turned_keys.astype(low), values_mine], 0)
-
-    near_pairs = [pair_mine] + [
-        lax.ppermute(pair_mine, "mp", [(i, i ^ k) for i in ranks]) for k in range(1, ring)
-    ]
+    pair_mine, normed = order(pair_mine, normed)
+
+    near_pairs = [pair_mine] + [exchange(pair_mine, "mp", k, parts) for k in range(1, ring)]
+    output_slice = jnp.concatenate(by_rank(output_slice, rank), axis=1)
+    output_all = lax.all_gather(output_slice, "dp", axis=0, tiled=True)
+    queries = dot(query_all, normed, 0, 1).reshape(QH, HD, mine)
+    turned_queries, query_pull = jax.vjp(
+        lambda v, g: turn(v, g, cosine, sine), queries, query_gain
+    )
+    got = order(turned_queries.astype(low), *near_pairs, *cotangent)
+    turned_queries, near_pairs, cotangent = got[0], got[1 : ring + 1], got[ring + 1 :]
+
+    cotangent = swap(cotangent, "mp")
     near_pairs = by_rank(near_pairs, place)
     pair = jnp.concatenate(
         [p[:, :, :chunk] for p in near_pairs] + [p[:, :, chunk:] for p in near_pairs[::-1]], axis=2
     )
     key_heads, value_heads = pair[:KVH], pair[KVH:]
-
-    queries = dot(query_all, normed, 0, 1).reshape(QH, HD, mine)
-    turned_queries, query_pull = jax.vjp(
-        lambda v, g: turn(v, g, cosine, sine), queries, query_gain
-    )
-    turned_queries = turned_queries.astype(low)
     starts = jnp.stack([place * chunk, (2 * ring - 1 - place) * chunk]).astype(jnp.int32)
     mixed, row_totals = attend(starts, turned_queries, key_heads, value_heads)
     mixed = mixed.reshape(QH * HD, mine)
     middle = inputs + dot(mixed, output_all, 0, 0)
-
     second_rms = lax.rsqrt(jnp.mean(middle * middle, axis=1, keepdims=True) + epsilon)
     second_normed = (middle * second_rms * feedforward_gain_all).astype(low)
-    second_full = lax.all_gather(second_normed, "dp", axis=0, tiled=True)
-    gate = mm(second_full, gate_here)
-    up = mm(second_full, up_here)
-    sigma = jax.nn.sigmoid(gate)
-    swish = gate * sigma
-    hidden = (swish * up).astype(low)
-    hidden_grad = dot(cotangent_full, down_here, 1, 1)
-    gate_grad = (hidden_grad * up * sigma * (1.0 + gate * (1.0 - sigma))).astype(low)
-    up_grad = (hidden_grad * swish).astype(low)
-    normed_two_terms = dot(gate_grad, gate_here, 1, 1) + dot(up_grad, up_here, 1, 1)
-    normed_two_grad = lax.psum_scatter(
-        normed_two_terms.astype(low), "dp", scatter_dimension=0, tiled=True
-    ).astype(full)
-    down_terms = mm(hidden, down_here)
-    down_sum = lax.psum_scatter(
-        down_terms.astype(low), "dp", scatter_dimension=0, tiled=True
-    ).astype(full)
-    output = to_features(middle + down_sum, low)
-
-    def reduce_units(grad, axis):
-        pieces = [lax.slice_in_dim(grad, k * units, (k + 1) * units, axis=axis) for k in ranks]
-        got = swap(pieces, "mp")
-        return sum(piece.astype(full) for piece in got).astype(low)
-
-    def columns_back(piece):
-        wide = lax.all_gather(piece, "dp", axis=0, tiled=False)
-        return jnp.transpose(wide, (1, 0, 2)).reshape(D, -1).astype(full)
-
-    down_grad = reduce_units(dot(hidden, cotangent_full, 0, 0).astype(low), 0)
-    down_grad = lax.all_gather(down_grad, "dp", axis=0, tiled=True).astype(full)
-    gate_weight_grad = columns_back(reduce_units(dot(second_full, gate_grad, 0, 0).astype(low), 1))
-    up_weight_grad = columns_back(reduce_units(dot(second_full, up_grad, 0, 0).astype(low), 1))
-
+    second_normed, pack, *cotangent = order(second_normed, pack, *cotangent)
+
+    second = Spread(second_normed, "dp", groups, group)
+    weights = RelayGather(pack, "mp", parts)
+    cotangent_mine = jnp.concatenate(by_rank(cotangent, rank), axis=1)
+    cube = groups == CUBE
+    if cube:
+        flag = group % 2 != 0
+        pairs = [normed[:, k * rows : (k + 1) * rows] for k in range(groups)]
+        normed_own, normed_other = (
+            jnp.concatenate(
+                [jnp.where(flag, pairs[k ^ 1 ^ a], pairs[k ^ a]) for k in range(0, groups, 2)], 1
+            )
+            for a in (0, 1)
+        )
+    else:
+        normed_own = normed_other = normed
+    *got, up, down, cotangent_mine, normed_own, normed_other = order(
+        *second.flying, *weights.flying, cotangent_mine, normed_own, normed_other
+    )
+    second.second(*got)
+    weights.take(up, down)
+    cotangent_mine, got, (up, down), second.buffer = order_split(
+        order, [cotangent_mine], second.flying, weights.flying, second.buffer
+    )
+    cotangent_full = lax.all_gather(cotangent_mine, "dp", axis=0, tiled=True)
+    second.third(*got)
+    weights.take(up, down)
+    got, (up, down) = order_split(order, [], second.flying, weights.flying)
+    second.last(*got)
+    weights.take(up, down)
+    pack = weights.finish(order)
+    wide = jnp.concatenate(
+        [block[:, :units] for block in pack] + [block[:, units : 2 * units] for block in pack], 1
+    )
+    down_here = jnp.concatenate([block[:, 2 * units :] for block in pack], 1)
+    half = parts * units
+
+    raised = [mm(part, wide) for part in second.parts]
+    hidden = [
+        (v[:, :half] * jax.nn.sigmoid(v[:, :half]) * v[:, half:]).astype(low) for v in raised
+    ]
+    down_terms = [dot(h, down_here, 1, 1).astype(low) for h in hidden]
+    down_terms, raised, hidden, (cotangent_full,) = order_split(
+        order, [], down_terms, raised, hidden, [cotangent_full]
+    )
+    def cores(array, at):
+        if not cube:
+            return array
+        array = array.reshape(4, 2, mine, D)
+        return lax.dynamic_index_in_dim(array, at, 1, keepdims=False).reshape(4 * mine, D)
+
+    cot = [cores(cotangent_full, at) for at in ((group % 2, 1 - group % 2) if cube else (0,))]
+
+    def back(part, v):
+        hidden_grad = mm(part, down_here)
+        gate, up = v[:, :half], v[:, half:]
+        sigma = jax.nn.sigmoid(gate)
+        gate_grad = hidden_grad * up * sigma * (1.0 + gate * (1.0 - sigma))
+        return jnp.concatenate([gate_grad.astype(low), (hidden_grad * gate * sigma).astype(low)], 1)
+
+    grads = [back(cot[-1], raised[-1])]
+    other = dot(grads[0], wide, 1, 1).astype(low)
+    other, grads[0], *raised = order(other, grads[0], *raised)
+
+    second_sum = Collect(other, "dp", groups, group)
+    own = other
+    if len(raised) > 1:
+        grads.insert(0, back(cot[0], raised[0]))
+        own = dot(grads[0], wide, 1, 1).astype(low)
+    own, *grads, hidden, got = order_split(order, [own, *grads], hidden, second_sum.flying)
+
+    second_sum.second(own, *got)
+    wide_grad = sum(dot(part, grad, 0, 0) for part, grad in zip(second.parts, grads)).astype(low)
+    down_grad = sum(dot(part, h, 0, 0) for part, h in zip(cot, hidden)).astype(low)
+    down_sum = Collect(down_terms[-1], "dp", groups, group)
+    down_grad, wide_grad, got, flying = order_split(
+        order, [down_grad, wide_grad], second_sum.flying, down_sum.flying
+    )
+
+    second_sum.third(*got)
+
+    def block_of(k):
+        at = k * units
+        return jnp.concatenate(
+            [
+                wide_grad[:, at : at + units],
+                wide_grad[:, half + at : half + at + units],
+                down_grad[:, at : at + units],
+            ],
+            1,
+        )
+
+    pack = jnp.zeros((parts, D, 3 * units), low)
+    for k in ranks:
+        pack = lax.dynamic_update_slice(
+            pack, block_of(k)[None], ((rank - k) % parts, 0, 0)
+        )
+    pack = lax.psum_scatter(pack, "mp", scatter_dimension=0, tiled=False)
+    down_sum.second(down_terms[0], *flying, launch=False)
+    *got, flying = order_split(order, second_sum.flying, down_sum.flying)
+
+    normed_two_grad = second_sum.last(*got).astype(full)
+    down_sum.launch(*flying)
     middle_part, feedforward_gain_grad = norm_backward(
         middle, second_rms, feedforward_gain_all, normed_two_grad
     )
     middle_grad = cotangent_mine.astype(full) + middle_part
+    lane = lax.broadcasted_iota(jnp.int32, (D, EXTRA), 1)
+    wide_extra = jnp.where(lane == 0, feedforward_gain_grad[:, None], 0.0)
     branch_grad = middle_grad.astype(low)
-
+    mixed_grad = dot(output_all, branch_grad, 1, 1).astype(low).reshape(QH, HD, mine)
     output_grad = mm(mixed, branch_grad).astype(low)
-    output_grad = lax.psum_scatter(output_grad, "dp", scatter_dimension=0, tiled=True)
-    pieces = by_rank([output_grad[:, j * share : (j + 1) * share] for j in ranks], rank)
-    output_grad = sum(piece.astype(full) for piece in swap(pieces, "mp")).astype(low)
-    output_grad = lax.all_gather(output_grad, "dp", axis=0, tiled=True)
-    output_weight_grad = mm(select, output_grad)
-
-    mixed_grad = dot(output_all, branch_grad, 1, 1).astype(low).reshape(QH, HD, mine)
     query_rot_grad, key_rot_grad, value_grad = attend_back(
         starts, turned_queries, key_heads, value_heads, mixed_grad, row_totals
     )
-    queries_low, query_gain_grad = query_pull(query_rot_grad)
-    queries_low = queries_low.astype(low).reshape(QH * HD, mine)
     pair_grad = jnp.concatenate([key_rot_grad, value_grad], 0)
     blocks = [
         jnp.concatenate(
@@ -390,60 +656,148 @@
         for j in range(ring)
     ]
     blocks = by_rank(blocks, place)
-    pair_grad = blocks[0]
-    for k in range(1, ring):
-        pair_grad += lax.ppermute(
-            blocks[k].astype(low), "mp", [(i, i ^ k) for i in ranks]
-        ).astype(full)
+    away = [block.astype(low) for block in blocks[1:]]
+    query_rot_grad, *away, got = order_split(
+        order, [query_rot_grad, *away], down_sum.flying
+    )
+    down_sum.third(*got)
+
+    away = [exchange(block, "mp", k + 1, parts) for k, block in enumerate(away)]
+    queries_low, query_gain_grad = query_pull(query_rot_grad)
+    queries_low = queries_low.astype(low).reshape(QH * HD, mine)
+    queries_low, pack, output_grad, wide_extra, *away, got = order_split(
+        order, [queries_low, pack, output_grad, wide_extra, *away], down_sum.flying
+    )
+    down_total = down_sum.last(*got)
+    output_grad = lax.psum_scatter(output_grad, "dp", scatter_dimension=0, tiled=True)
+    pack = by_rows(pack)
+    wide_grad = by_rows(lax.all_gather(by_rows(pack[:, : 2 * units]), "dp", axis=0, tiled=False))
+    down_grad = by_rows(
+        lax.all_gather(by_rows(pack[:, 2 * units :].T), "dp", axis=0, tiled=True)
+    )
+    pair_grad = sum([blocks[0]] + [block.astype(full) for block in away])
     keys_grad, key_gain_grad = key_pull(pair_grad[:KVH])
     pair_low = jnp.concatenate(
         [keys_grad.astype(low), pair_grad[KVH:].astype(low)], 0
     ).reshape(2 * KVH * HD, mine)
-
-    query_weight_grad = dot(normed, queries_low, 0, 1).astype(low)
-    query_weight_grad = lax.psum_scatter(
-        query_weight_grad, "dp", scatter_dimension=0, tiled=True
-    )
-    query_weight_grad = dot(query_weight_grad, select_near, 1, 1).astype(low)
-    pieces = [query_weight_grad[:, k * slots : (k + 1) * slots] for k in ranks]
-    query_weight_grad = sum(piece.astype(full) for piece in swap(pieces, "mp")).astype(low)
-    query_weight_grad = lax.all_gather(query_weight_grad, "dp", axis=0, tiled=True).astype(full)
-
-    pair_weight_grad = dot(normed, pair_low, 0, 1).astype(low)
-    pair_weight_grad = lax.psum_scatter(pair_weight_grad, "dp", scatter_dimension=0, tiled=True)
-    pair_weight_grad = sum(
-        piece.astype(full) for piece in swap([pair_weight_grad] * parts, "mp")
-    ).astype(low)
-    pair_weight_grad = lax.all_gather(pair_weight_grad, "dp", axis=0, tiled=True).astype(full)
-
+    all_low = jnp.concatenate([queries_low, pair_low], 0)
+    heads_gain = jnp.stack([query_gain_grad, key_gain_grad])
+    top = wide_extra[:2] + jnp.pad(heads_gain, ((0, 0), (EXTRA - HD, 0)))
+    extra = jnp.concatenate([top, wide_extra[2:]], 0)
+    wide_low = jnp.concatenate([all_low, jnp.zeros((EXTRA, mine), low)], 0)
+
+    def projections(normed_part, extra_part):
+        extra_part = jnp.pad(extra_part, ((0, 0), (wide_low.shape[0] - EXTRA, 0)))
+        return (dot(normed_part, wide_low, 0, 1) + extra_part).astype(low)
+
+    own = other = extra
+    if cube:
+        pairs = extra.reshape(4, 2, rows, EXTRA)
+        own, other = (
+            lax.dynamic_index_in_dim(pairs, at, 1, keepdims=False).reshape(4 * rows, EXTRA)
+            for at in (group % 2, 1 - group % 2)
+        )
+    other = projections(normed_other, other)
+    output = [(middle + down_total.astype(full)).astype(low)]
+    other, own, wide_low, all_low, normed_own, *output = order(
+        other, own, wide_low, all_low, normed_own, *output
+    )
+    output = by_rank([output[0][:, j * share : (j + 1) * share] for j in ranks], rank)
+
+    def by_feature(array):
+        return by_rank([array[:, j * share : (j + 1) * share] for j in ranks], rank)
+
+    projection_sum = Collect(other, "dp", groups, group)
+    output = swap(output, "mp")
+    own = projections(normed_own, own) if cube else other
+    queries_low, pair_low = all_low[: QH * HD], all_low[QH * HD :]
     normed_grad = (
         dot(queries_low, query_all, 0, 1)
         + dot(pair_low[: KVH * HD], key_weight, 0, 1)
         + dot(pair_low[KVH * HD :], value_weight, 0, 1)
     )
-    input_part, attention_gain_grad = norm_backward(
+    input_part, _ = norm_backward(
         inputs, first_rms, attention_gain_all, normed_grad
     )
-    input_gradient = to_features(middle_grad + input_part, full)
-
-    small = jnp.concatenate(
-        [attention_gain_grad, feedforward_gain_grad, query_gain_grad, key_gain_grad]
-    )
-    small = lax.psum(small, ("dp", "mp"))
+    input_gradient = (middle_grad + input_part).astype(low)
+    input_gradient, own, got, output = order_split(
+        order, [input_gradient, own], projection_sum.flying, output
+    )
+    projection_sum.second(own, *got)
+
+    def by_tokens(got, kind):
+        got = by_rank(got, rank)
+        rows = []
+        for seq in range(seqs):
+            near = got[seq * ring : (seq + 1) * ring]
+            rows += [block[:chunk] for block in near]
+            rows += [block[chunk:] for block in near[::-1]]
+        return jnp.concatenate(rows, 0).astype(kind)
+
+    output_grad = swap(by_feature(output_grad), "mp")
+    output_grad, got = order_split(order, [], output_grad, projection_sum.flying)
+    output_grad = lax.all_gather(added(*output_grad), "dp", axis=0, tiled=True)
+    projection_sum.third(*got)
+
+    got = order(*projection_sum.flying, input_gradient)
+    projection_total, input_gradient = projection_sum.last(*got[:-1]), got[-1]
+
+    query_total, pair_total, extra = jnp.split(
+        projection_total, [QH * HD, (QH + 2 * KVH) * HD], axis=1
+    )
+    here = lambda weight: lax.dynamic_slice_in_dim(weight, group * rows, rows, 0).astype(full)
+    product = jnp.sum(here(query_all) * query_total.astype(full), axis=1)
+    product += jnp.sum(here(key_weight) * pair_total[:, : KVH * HD].astype(full), axis=1)
+    product += jnp.sum(here(value_weight) * pair_total[:, KVH * HD :].astype(full), axis=1)
+    product = product / lax.dynamic_slice_in_dim(attention_gain_all, group * rows, rows, 0)
+    column = lax.broadcasted_iota(jnp.int32, extra.shape, 1)
+    extra = jnp.where(column == 2, product[:, None].astype(low), extra)
+    query_part = dot(query_total, select_near, 1, 1).astype(low)
+    projection = swap(
+        [
+            jnp.concatenate([query_part[:, k * slots : (k + 1) * slots], pair_total, extra], 1)
+            for k in ranks
+        ],
+        "mp",
+    )
+    *projection, wide_grad, down_grad, input_gradient, output_grad = order(
+        *projection, wide_grad, down_grad, input_gradient, output_grad
+    )
+
+    projection = lax.all_gather(added(*projection), "dp", axis=0, tiled=True)
+    output_weight_grad = mm(select, output_grad)
+    input_gradient = swap(by_feature(input_gradient), "mp")
+    gate_weight_grad, up_weight_grad, down_weight_grad = widen(wide_grad, down_grad)
+    output = by_tokens(output, low)
+    got = order(
+        projection, gate_weight_grad, up_weight_grad, down_weight_grad, output,
+        output_weight_grad, *input_gradient
+    )
+    projection, gate_weight_grad, up_weight_grad, down_weight_grad, output = got[:5]
+    output_weight_grad = got[5]
+    input_gradient = by_tokens(got[6:], full)
+
+    widths = [slots, KVH * HD, KVH * HD, EXTRA]
+    cuts = [sum(widths[: k + 1]) for k in range(3)]
+    query_weight_grad, key_weight_grad, value_weight_grad, extra = jnp.split(
+        projection, cuts, axis=1
+    )
+    extra = extra.astype(full)
+    own_share = lax.dynamic_slice_in_dim(extra, rank * share, share, 0)
     return (
         output,
         input_gradient,
-        lax.dynamic_slice_in_dim(small[:D], rank * share, share, 0),
-        query_weight_grad,
-        pair_weight_grad[:, : KVH * HD],
-        pair_weight_grad[:, KVH * HD :],
-        small[2 * D : 2 * D + HD],
-        small[2 * D + HD :],
+        own_share[:, 2],
+        query_weight_grad.astype(full),
+        key_weight_grad.astype(full),
+        value_weight_grad.astype(full),
+        extra[0, EXTRA - HD :],
+        extra[1, EXTRA - HD :],
         output_weight_grad,
-        lax.dynamic_slice_in_dim(small[D : 2 * D], rank * share, share, 0),
+        own_share[:, 0],
         gate_weight_grad,
         up_weight_grad,
-        down_grad,
+        down_weight_grad,
     )
 
 

time: 1180 us -> 897 us (0.76)
  waiting for transfers between devices: 628 us -> 314 us
  other arithmetic: 71.5 us -> 155 us
  local copies, waits for them, and re-layouts: 37.3 us -> 98.9 us
  blocking collectives: 60.6 us -> 0 us
  matrix products: 223 us -> 176 us
  starting transfers between devices: 82.8 us -> 65.9 us
    ppermute x48 -> x21, waiting for transfers between devices: 372 us -> 148 us  [swap(): lax.ppermute(pieces[k], axis, [(i, i ^ k) for i in range(n)])]
    reduce_scatter x4 -> x1, waiting for transfers between devices: 218 us -> 5.63 us  [on_device(): pack = lax.psum_scatter(pack, 'mp', scatter_dimension=0, tiled=False)]
    ppermute x2 -> x31, waiting for transfers between devices: 29.5 us -> 160 us  [the longest x25 109 us: exchange(): return lax.ppermute(array, axis, [(i, i ^ mask) for i in range(n)])]
    psum x1 -> x0, blocking collectives: 60.6 us -> none  [on_device(): small = lax.psum(small, ('dp', 'mp'))]
    ppermute x48 -> x21, starting transfers between devices: 80.3 us -> 25.9 us  [swap(): lax.ppermute(pieces[k], axis, [(i, i ^ k) for i in range(n)])]
    ppermute x2 -> x31, starting transfers between devices: 1.64 us -> 39.4 us  [the longest x25 22.2 us: exchange(): return lax.ppermute(array, axis, [(i, i ^ mask) for i in range(n)])]
    dot_general x18 -> x20, matrix products: 153 us -> 116 us  [dot(): lax.dot_general(left, right, (((left_axis,), (right_axis,)), ((), ())), p...]
    convert_element_type x14 -> x27, other arithmetic: 38.9 us -> 67.5 us  [the longest x11 41.5 us: added(): return sum((term.astype(full) for term in terms)).astype(low)]
  transfers between devices with their start and end apart: 65 -> 61, of which waited for: 38 -> 31; matrix products, arithmetic and copies ran while one was open for 20% -> 36% of each run, Pallas kernels for 2% -> 7%
where the time goes in v2:
time: 897 us; the launch traced here: 890 us
  waiting for transfers between devices  314 us (35%)
  matrix products  176 us (20%)
  other arithmetic  155 us (17%)
  local copies, waits for them, and re-layouts  98.9 us (11%)
  starting transfers between devices  65.9 us (7%)
  Pallas kernels  63.6 us (7%)
  between operations  16.4 us (2%)
    ppermute x21, waiting for transfers between devices, swap(): lax.ppermute(pieces[k], axis, [(i, i ^ k) for i in range(n)])  148 us
    dot_general x20, matrix products, dot(): lax.dot_general(left, right, (((left_axis,), (right_axis,)), ((), ())), p...  116 us
    ppermute x25, waiting for transfers between devices, exchange(): return lax.ppermute(array, axis, [(i, i ^ mask) for i in range(n)])  109 us
    dot_general x7, matrix products, mm(): return jnp.dot(left, right, preferred_element_type=full)  60.3 us
    ppermute x3, waiting for transfers between devices, send(): lax.ppermute(up, self.axis, right)  49.5 us
    convert_element_type x11, other arithmetic, added(): return sum((term.astype(full) for term in terms)).astype(low)  41.5 us
    unnamed x249, local copies, waits for them, and re-layouts  35.6 us
    pallas_call x1, Pallas kernels, attend_back(): pl.pallas_call(attend_back_kernel, out_shape=(jax.ShapeDtypeStruct((QH, H...  33 us
  transfers between devices with their start and end apart: 61, of which 31 were waited for; matrix products, arithmetic and copies ran while one was open for 36% of the time, Pallas kernels for 7%

profile of v2, /device:TPU:16, one launch (start us, length us, event | category | flops | bytes accessed | tf_op | source)
XLA Modules:
  0.0 889.8 jit_solution(2720914381821850421)
XLA Ops:
  13.1 3.4 constant_dynamic-slice_fusion.8
  27.1 3.6 iota_compare_fusion
  43.3 8.1 collective-permute-done.4
  59.0 3.3 collective-permute-start.6
  63.9 14.8 %collective-permute-done.6 = bf16[160,512]{1,0:T(8,128)(2,1)S(1)} collective-permute-done((bf16[160,512]{1,0:T(8,128)(2,1)S(1)}, bf16[160,512]{1,0:T(8,128)(2,1)S(1)}, u32[]{:S(2)}, u32[]{:S(2)}) %collective-permute-start.6) | collective-permute-done | bytes 163872 | tf_op jit(solution)/shard_map/ppermute | solution.py:36
  78.7 13.9 %collective-permute-done.7 = bf16[160,512]{1,0:T(8,128)(2,1)S(1)} collective-permute-done((bf16[160,512]{1,0:T(8,128)(2,1)S(1)}, bf16[160,512]{1,0:T(8,128)(2,1)S(1)}, u32[]{:S(2)}, u32[]{:S(2)}) %collective-permute-start.7) | collective-permute-done | bytes 163872 | tf_op jit(solution)/shard_map/ppermute | solution.py:36
  107.5 5.5 fusion.100
  116.4 6.1 collective-permute-done.9
  127.7 21.1 %shard_map.246 = (bf16[20,64,512]{2,1,0:T(8,128)(2,1)S(1)}, f32[5,4,512]{2,1,0:T(4,128)S(1)}) custom-call(s32[2]{0:T(128)S(1)} %pad_add_fusion.2.starts, bf16[20,64,512]{2,1,0:T(8,128)(2,1)S(1)} %fusion.21.q_ref, bf16[5,64,1024]{2,1,0:T(8,128)(2,1)S(1)} %get-tuple-element.461.k_ref, bf16[5,64,1024]{2,1,0:T(8,128)(2,1)S(1)} %get-tuple-element.460.v_ref), custom_call_target="tpu_custom_call" | custom-call | flops 7864320 | bytes 1048576 | tf_op jit(solution)/shard_map/pallas_call | solution.py:319
  150.5 6.4 multiply_reduce_fusion
  160.6 8.0 collective-permute-done.12
  173.4 3.9 collective-permute-start.16
  184.6 20.7 %collective-permute-done.15 = bf16[2048,384]{0,1:T(8,128)(2,1)} collective-permute-done((bf16[2048,384]{0,1:T(8,128)(2,1)}, bf16[2048,384]{0,1:T(8,128)(2,1)}, u32[]{:S(2)}, u32[]{:S(2)}) %collective-permute-start.15) | collective-permute-done | bytes 1572896 | tf_op jit(solution)/shard_map/ppermute | solution.py:80
  207.2 4.9 collective-permute-done.13
  215.2 6.3 collective-permute-start.20
  221.6 4.5 broadcast_in_dim.65
  232.2 3.2 bitcast_dynamic-update-slice_fusion.1
  235.4 3.2 bitcast_dynamic-update-slice_fusion
  238.5 9.5 %collective-permute-done.17 = bf16[256,2048]{1,0:T(8,128)(2,1)S(1)} collective-permute-done((bf16[256,2048]{1,0:T(8,128)(2,1)S(1)}, bf16[256,2048]{1,0:T(8,128)(2,1)S(1)}, u32[]{:S(2)}, u32[]{:S(2)}) %collective-permute-start.17) | collective-permute-done | bytes 1048608 | tf_op jit(solution)/shard_map/ppermute | solution.py:50
  260.1 28.8 %collective-permute-done.22 = bf16[2048,384]{0,1:T(8,128)(2,1)S(1)} collective-permute-done((bf16[2048,384]{0,1:T(8,128)(2,1)}, bf16[2048,384]{0,1:T(8,128)(2,1)S(1)}, u32[]{:S(2)}, u32[]{:S(2)}) %collective-permute-start.22) | collective-permute-done | bytes 1572896 | tf_op jit(solution)/shard_map/ppermute | solution.py:80
  288.8 3.3 add.516
  296.2 12.8 %fusion.102 = f32[2048,1024]{1,0:T(8,128)S(1)} fusion(bf16[2048,2048]{1,0:T(8,128)(2,1)} %collective-permute-done.21, bf16[2048,1024]{0,1:T(8,128)(2,1)S(1)} %get-tuple-element.459), kind=kOutput, calls=%fused_computation.437 | convolution fusion | flops 8589934592 | bytes 20971520 | tf_op jit(solution)/shard_map/dot_general | solution.py:232
  309.0 3.3 copy-done.39
  313.7 12.2 %fusion.101 = f32[2048,1024]{1,0:T(8,128)S(1)} fusion(bf16[2048,2048]{1,0:T(8,128)(2,1)} %bitcast.20, bf16[2048,1024]{0,1:T(8,128)(2,1)S(1)} %get-tuple-element.459), kind=kOutput, calls=%fused_computation.436 | convolution fusion | flops 8589934592 | bytes 20971520 | tf_op jit(solution)/shard_map/dot_general | solution.py:232
  329.2 6.9 convolution_convert_fusion.3
  336.2 6.7 convolution_convert_fusion.4
  342.9 9.4 %constant_dynamic-slice_fusion.5 = (bf16[4,1,512,2048]{3,2,1,0:T(8,128)(2,1)S(1)}, bf16[4,1,512,2048]{3,2,1,0:T(8,128)(2,1)}) fusion(bf16[4,2,512,2048]{3,2,1,0:T(8,128)(2,1)} %bitcast.210, s32[]{:T(128)S(6)} %select_n.685, s32[]{:T(128)S(6)} %select_n.684), kind=kLoop, calls=%fused_computation.349 | loop fusion | bytes 33554440 | tf_op jit(solution)/shard_map/jit(dynamic_index_in_dim)/dynamic_slice | solution.py:581
  352.3 12.6 %multiply_convert_fusion.3 = (bf16[2048,512]{1,0:T(8,128)(2,1)S(1)}, bf16[2048,512]{1,0:T(8,128)(2,1)S(1)}) fusion(f32[2048,1024]{1,0:T(8,128)} %copy-done.39, bf16[2048,2048]{1,0:T(8,128)(2,1)S(1)} %bitcast.226, bf16[2048,128]{0,1:T(8,128)(2,1)S(1)} %get-tuple-element.458, bf16[2048,128]{0,1:T(8,128)(2,1)S(1)} %get-tuple-element.456, ...), kind=kOutput, calls=%fused_computation.54 | convolution fusion | flops 4316987392 | bytes 23068672 | tf_op jit(solution)/shard_map/dot_general | solution.py:232
  368.6 10.8 %convolution_convert_fusion.2 = bf16[2048,2048]{1,0:T(8,128)(2,1)} fusion(bf16[2048,1024]{0,1:T(8,128)(2,1)S(1)} %copy-done.95, bf16[2048,512]{1,0:T(8,128)(2,1)S(1)} %get-tuple-element.363, bf16[2048,512]{1,0:T(8,128)(2,1)S(1)} %get-tuple-element.362), kind=kOutput, calls=%fused_computation.20 | convolution fusion | flops 8602517504 | bytes 16777216 | tf_op jit(solution)/shard_map/dot_general | solution.py:28
  379.9 12.0 %multiply_convert_fusion.1 = (bf16[2048,512]{1,0:T(8,128)(2,1)S(1)}, bf16[2048,512]{1,0:T(8,128)(2,1)S(1)}) fusion(f32[2048,1024]{1,0:T(8,128)} %copy-done.38, bf16[2048,2048]{1,0:T(8,128)(2,1)} %bitcast.222, bf16[2048,128]{0,1:T(8,128)(2,1)S(1)} %get-tuple-element.458, bf16[2048,128]{0,1:T(8,128)(2,1)S(1)} %get-tuple-element.456, ...), kind=kOutput, calls=%fused_computation.51 | convolution fusion | flops 4316987392 | bytes 23068672 | tf_op jit(solution)/shard_map/dot_general | solution.py:232
  394.6 10.7 %convolution_convert_fusion.1 = bf16[2048,2048]{1,0:T(8,128)(2,1)S(1)} fusion(bf16[2048,1024]{0,1:T(8,128)(2,1)} %copy-done.94, bf16[2048,512]{1,0:T(8,128)(2,1)S(1)} %get-tuple-element.361, bf16[2048,512]{1,0:T(8,128)(2,1)S(1)} %get-tuple-element.360), kind=kOutput, calls=%fused_computation.19 | convolution fusion | flops 8602517504 | bytes 16777216 | tf_op jit(solution)/shard_map/dot_general | solution.py:28
  405.3 5.7 add_convert_fusion.1
  418.9 8.5 fusion.103
  427.3 7.6 add_convert_fusion.7
  435.0 13.4 %fusion.104 = f32[2048,1024]{1,0:T(8,128)} fusion(bf16[2048,2048]{1,0:T(8,128)(2,1)} %collective-permute-done.21, bf16[2048,1024]{1,0:T(8,128)(2,1)S(1)} %copy-done.51), kind=kOutput, calls=%fused_computation.439 | convolution fusion | flops 8589934592 | bytes 20971520 | tf_op jit(solution)/shard_map/dot_general | solution.py:28
  448.4 12.9 %add_convert_fusion.5 = bf16[2048,1024]{1,0:T(8,128)(2,1)S(1)} fusion(f32[2048,1024]{1,0:T(8,128)} %fusion.104, bf16[2048,2048]{1,0:T(8,128)(2,1)} %bitcast.20, bf16[2048,1024]{1,0:T(8,128)(2,1)S(1)} %copy-done.52), kind=kOutput, calls=%fused_computation.9 | convolution fusion | flops 8594128896 | bytes 25165824 | tf_op jit(solution)/shard_map/dot_general | solution.py:28
  461.4 3.7 collective-permute-done.25
  466.2 3.2 broadcast_in_dim.126
  478.8 8.5 add_convert_fusion
  492.0 10.1 %collective-permute-done.28 = bf16[256,2048]{1,0:T(8,128)(2,1)S(1)} collective-permute-done((bf16[256,2048]{1,0:T(8,128)(2,1)S(1)}, bf16[256,2048]{1,0:T(8,128)(2,1)S(1)}, u32[]{:S(2)}, u32[]{:S(2)}) %collective-permute-start.28) | collective-permute-done | bytes 1048608 | tf_op jit(solution)/shard_map/ppermute | solution.py:50
  504.5 3.4 fusion.33
  515.2 33.0 %shard_map.247 = (f32[20,64,512]{2,1,0:T(8,128)S(1)}, f32[5,64,1024]{2,1,0:T(8,128)S(1)}, f32[5,64,1024]{2,1,0:T(8,128)S(1)}) custom-call(s32[2]{0:T(128)S(1)} %copy-done.11, bf16[20,64,512]{2,1,0:T(8,128)(2,1)S(1)} %copy-done.3, bf16[5,64,1024]{2,1,0:T(8,128)(2,1)S(1)} %copy-done.8, bf16[5,64,1024]{2,1,0:T(8,128)(2,1)S(1)} %copy-done.6, ...), custom_call_target="tpu_custom_call" | custom-call | flops 7864320 | bytes 1048576 | tf_op jit(solution)/shard_map/pallas_call | solution.py:342
  551.8 4.8 convolution_convert_fusion
  568.6 25.3 %collective-permute-done.32 = bf16[10,64,512]{2,1,0:T(8,128)(2,1)S(1)} collective-permute-done((bf16[10,64,512]{2,1,0:T(8,128)(2,1)S(1)}, bf16[10,64,512]{2,1,0:T(8,128)(2,1)S(1)}, u32[]{:S(2)}, u32[]{:S(2)}) %collective-permute-start.32) | collective-permute-done | bytes 655392 | tf_op jit(solution)/shard_map/ppermute | solution.py:50
  594.7 5.6 reduce-scatter.3.cloned.1.call-done
  613.1 5.0 fusion.25
  620.6 5.5 add_convert_fusion.4
  637.3 5.1 fusion.40
  651.0 3.4 collective-permute-done.37
  654.5 25.8 %collective-permute-done.38 = bf16[512,512]{1,0:T(8,128)(2,1)S(1)} collective-permute-done((bf16[512,512]{1,0:T(8,128)(2,1)S(1)}, bf16[512,512]{1,0:T(8,128)(2,1)S(1)}, u32[]{:S(2)}, u32[]{:S(2)}) %collective-permute-start.38) | collective-permute-done | bytes 524320 | tf_op jit(solution)/shard_map/ppermute | solution.py:36
  681.1 4.1 add_convert_fusion.2
  697.2 23.0 %collective-permute-done.43 = bf16[256,2048]{1,0:T(8,128)(2,1)} collective-permute-done((bf16[256,2048]{1,0:T(8,128)(2,1)}, bf16[256,2048]{1,0:T(8,128)(2,1)}, u32[]{:S(2)}, u32[]{:S(2)}) %collective-permute-start.43) | collective-permute-done | bytes 1048608 | tf_op jit(solution)/shard_map/ppermute | solution.py:50
  731.3 12.1 %collective-permute-done.44 = bf16[128,2048]{1,0:T(8,128)(2,1)} collective-permute-done((bf16[128,2048]{1,0:T(8,128)(2,1)}, bf16[128,2048]{1,0:T(8,128)(2,1)}, u32[]{:S(2)}, u32[]{:S(2)}) %collective-permute-start.44) | collective-permute-done | bytes 524320 | tf_op jit(solution)/shard_map/ppermute | solution.py:50
  756.6 18.2 %collective-permute-done.46 = bf16[256,1152]{1,0:T(8,128)(2,1)} collective-permute-done((bf16[256,1152]{1,0:T(8,128)(2,1)}, bf16[256,1152]{1,0:T(8,128)(2,1)}, u32[]{:S(2)}, u32[]{:S(2)}) %collective-permute-start.46) | collective-permute-done | bytes 589856 | tf_op jit(solution)/shard_map/ppermute | solution.py:36
  774.8 20.0 %collective-permute-done.47 = bf16[256,1152]{1,0:T(8,128)(2,1)} collective-permute-done((bf16[256,1152]{1,0:T(8,128)(2,1)}, bf16[256,1152]{1,0:T(8,128)(2,1)}, u32[]{:S(2)}, u32[]{:S(2)}) %collective-permute-start.47) | collective-permute-done | bytes 589856 | tf_op jit(solution)/shard_map/ppermute | solution.py:36
  794.8 10.7 %collective-permute-done.48 = bf16[256,1152]{1,0:T(8,128)(2,1)} collective-permute-done((bf16[256,1152]{1,0:T(8,128)(2,1)}, bf16[256,1152]{1,0:T(8,128)(2,1)}, u32[]{:S(2)}, u32[]{:S(2)}) %collective-permute-start.48) | collective-permute-done | bytes 589856 | tf_op jit(solution)/shard_map/ppermute | solution.py:36
  814.7 3.8 copy-done.4
  818.5 9.5 %shard_map.248 = (f32[2048,1024]{1,0:T(8,128)}, f32[2048,1024]{1,0:T(8,128)}, f32[1024,2048]{1,0:T(8,128)}) custom-call(bf16[8,2048,256]{2,1,0:T(8,128)(2,1)S(1)} %bitcast.195, bf16[1024,2048]{1,0:T(8,128)(2,1)S(1)} %copy-done.9), custom_call_target="tpu_custom_call" | custom-call | bytes 65536 | tf_op jit(solution)/shard_map/pallas_call | solution.py:379
  828.0 3.9 fusion.105
  833.1 15.7 %collective-permute-done.50 = bf16[512,512]{1,0:T(8,128)(2,1)} collective-permute-done((bf16[512,512]{1,0:T(8,128)(2,1)S(1)}, bf16[512,512]{1,0:T(8,128)(2,1)}, u32[]{:S(2)}, u32[]{:S(2)}) %collective-permute-start.50) | collective-permute-done | bytes 524320 | tf_op jit(solution)/shard_map/ppermute | solution.py:36
  848.8 10.0 %collective-permute-done.51 = bf16[512,512]{1,0:T(8,128)(2,1)} collective-permute-done((bf16[512,512]{1,0:T(8,128)(2,1)S(1)}, bf16[512,512]{1,0:T(8,128)(2,1)}, u32[]{:S(2)}, u32[]{:S(2)}) %collective-permute-start.51) | collective-permute-done | bytes 524320 | tf_op jit(solution)/shard_map/ppermute | solution.py:36
  858.8 4.4 slice_convert_fusion
  863.1 3.3 slice_convert_fusion.2
  877.7 3.5 copy.66
  (541 shorter events, 260.8 us)
Async XLA Ops:
  7.2 100.3 %all-gather.9.cloned.1.call-start = ((), (), s32[]{:S(2)}) async-start(), calls=%async_computation.2 | async-start | bytes 5898240 | tf_op jit(solution)/shard_map/all_gather | solution.py:496
  9.6 33.8 %collective-permute-start = (bf16[264,384]{1,0:T(8,128)(2,1)}, bf16[264,384]{1,0:T(8,128)(2,1)}, u32[]{:S(2)}, u32[]{:S(2)}) collective-permute-start(bf16[264,384]{1,0:T(8,128)(2,1)} %pad_maximum_fusion.38), channel_id=1, source_target_pairs={{0,1},{1,0},{2,3},{3,2},{4,5},{5,4},{6,7},{7,6},{8,9},{9,8},{10,11... | collective-permute-start | bytes 608264 | tf_op jit(solution)/shard_map/ppermute | solution.py:36
  11.1 32.2 %collective-permute-start.1 = (bf16[264,384]{1,0:T(8,128)(2,1)}, bf16[264,384]{1,0:T(8,128)(2,1)}, u32[]{:S(2)}, u32[]{:S(2)}) collective-permute-start(bf16[264,384]{1,0:T(8,128)(2,1)} %pad_maximum_fusion.38), channel_id=1, source_target_pairs={{0,2},{1,3},{2,0},{3,1},{4,6},{5,7},{6,4},{7,5},{8,10},{9,11},{10,... | collective-permute-start | bytes 608264 | tf_op jit(solution)/shard_map/ppermute | solution.py:36
  11.5 31.9 %collective-permute-start.2 = (bf16[264,384]{1,0:T(8,128)(2,1)}, bf16[264,384]{1,0:T(8,128)(2,1)}, u32[]{:S(2)}, u32[]{:S(2)}) collective-permute-start(bf16[264,384]{1,0:T(8,128)(2,1)} %pad_maximum_fusion.38), channel_id=1, source_target_pairs={{0,3},{1,2},{2,1},{3,0},{4,7},{5,6},{6,5},{7,4},{8,11},{9,10},{10,... | collective-permute-start | bytes 608264 | tf_op jit(solution)/shard_map/ppermute | solution.py:36
  17.3 26.1 %collective-permute-start.3 = (bf16[512,512]{1,0:T(8,128)(2,1)}, bf16[512,512]{1,0:T(8,128)(2,1)}, u32[]{:S(2)}, u32[]{:S(2)}) collective-permute-start(bf16[512,512]{1,0:T(8,128)(2,1)} %pad_maximum_fusion.36), channel_id=1, source_target_pairs={{0,1},{1,0},{2,3},{3,2},{4,5},{5,4},{6,7},{7,6},{8,9},{9,8},{10,11... | collective-permute-start | bytes 1572872 | tf_op jit(solution)/shard_map/ppermute | solution.py:50
  20.6 30.9 %collective-permute-start.4 = (bf16[512,512]{1,0:T(8,128)(2,1)}, bf16[512,512]{1,0:T(8,128)(2,1)}, u32[]{:S(2)}, u32[]{:S(2)}) collective-permute-start(bf16[512,512]{1,0:T(8,128)(2,1)} %pad_maximum_fusion.37), channel_id=1, source_target_pairs={{0,2},{1,3},{2,0},{3,1},{4,6},{5,7},{6,4},{7,5},{8,10},{9,11},{10,... | collective-permute-start | bytes 1572872 | tf_op jit(solution)/shard_map/ppermute | solution.py:50
  39.2 76.2 %copy-start.58 = (f32[64,512]{1,0:T(8,128)}, f32[64,512]{1,0:T(8,128)S(1)}, u32[]{:S(2)}) copy-start(f32[64,512]{1,0:T(8,128)S(1)} %get-tuple-element.175) | copy-start | bytes 393220
  39.2 76.2 %copy-start.60 = (f32[64,512]{1,0:T(8,128)}, f32[64,512]{1,0:T(8,128)S(1)}, u32[]{:S(2)}) copy-start(f32[64,512]{1,0:T(8,128)S(1)} %get-tuple-element.176) | copy-start | bytes 393220
  57.3 93.2 %all-gather.11.cloned.1.call-start = ((), (), s32[]{:S(2)}) async-start(), calls=%async_computation.3 | async-start | bytes 5898240 | tf_op jit(solution)/shard_map/all_gather | solution.py:511
  57.4 37.9 %collective-permute-start.5 = (bf16[512,512]{1,0:T(8,128)(2,1)S(1)}, bf16[512,512]{1,0:T(8,128)(2,1)S(1)}, u32[]{:S(2)}, u32[]{:S(2)}) collective-permute-start(bf16[512,512]{1,0:T(8,128)(2,1)S(1)} %pad_maximum_fusion.30), channel_id=1, source_target_pairs={{0,3},{1,2},{2,1},{3,0},{4,7},{5,6},{6,5},{7,4},{8,11},{9,10},{10,... | collective-permute-start | bytes 1572872 | tf_op jit(solution)/shard_map/ppermute | solution.py:50
  59.0 19.7 %collective-permute-start.6 = (bf16[160,512]{1,0:T(8,128)(2,1)S(1)}, bf16[160,512]{1,0:T(8,128)(2,1)S(1)}, u32[]{:S(2)}, u32[]{:S(2)}) collective-permute-start(bf16[160,512]{1,0:T(8,128)(2,1)S(1)} %fusion.42), channel_id=1, source_target_pairs={{0,1},{1,0},{2,3},{3,2},{4,5},{5,4},{6,7},{7,6},{8,9},{9,8},{10,11... | collective-permute-start | bytes 491528 | tf_op jit(solution)/shard_map/ppermute | solution.py:36
  62.3 30.3 %collective-permute-start.7 = (bf16[160,512]{1,0:T(8,128)(2,1)S(1)}, bf16[160,512]{1,0:T(8,128)(2,1)S(1)}, u32[]{:S(2)}, u32[]{:S(2)}) collective-permute-start(bf16[160,512]{1,0:T(8,128)(2,1)S(1)} %fusion.42), channel_id=1, source_target_pairs={{0,2},{1,3},{2,0},{3,1},{4,6},{5,7},{6,4},{7,5},{8,10},{9,11},{10,... | collective-permute-start | bytes 491528 | tf_op jit(solution)/shard_map/ppermute | solution.py:36
  63.3 32.0 %collective-permute-start.8 = (bf16[160,512]{1,0:T(8,128)(2,1)S(1)}, bf16[160,512]{1,0:T(8,128)(2,1)S(1)}, u32[]{:S(2)}, u32[]{:S(2)}) collective-permute-start(bf16[160,512]{1,0:T(8,128)(2,1)S(1)} %fusion.42), channel_id=1, source_target_pairs={{0,3},{1,2},{2,1},{3,0},{4,7},{5,6},{6,5},{7,4},{8,11},{9,10},{10,... | collective-permute-start | bytes 491528 | tf_op jit(solution)/shard_map/ppermute | solution.py:36
  96.3 246.6 %all-gather.13.cloned.1.call-start = ((), (), s32[]{:S(2)}) async-start(), calls=%async_computation.4 | async-start | bytes 18874368 | tf_op jit(solution)/shard_map/all_gather | solution.py:556
  99.6 58.0 %copy-start.90 = (f32[1,2048]{1,0:T(1,128)}, f32[1,2048]{1,0:T(1,128)S(1)}, u32[]{:S(2)}) copy-start(f32[1,2048]{1,0:T(1,128)S(1)} %get-tuple-element.490) | copy-start | bytes 24580
  107.5 14.9 %collective-permute-start.9 = (bf16[10,64,512]{2,1,0:T(8,128)(2,1)}, bf16[10,64,512]{2,1,0:T(8,128)(2,1)}, u32[]{:S(2)}, u32[]{:S(2)}) collective-permute-start(bf16[10,64,512]{2,1,0:T(8,128)(2,1)} %pad_maximum_fusion.27), channel_id=1, source_target_pairs={{0,1},{1,0},{2,3},{3,2},{4,5},{5,4},{6,7},{7,6},{8,9},{9,8},{10,11... | collective-permute-start | bytes 1966088 | tf_op jit(solution)/shard_map/ppermute | solution.py:50
  122.5 36.5 %collective-permute-start.10 = (bf16[512,512]{1,0:T(8,128)(2,1)}, bf16[512,512]{1,0:T(8,128)(2,1)}, u32[]{:S(2)}, u32[]{:S(2)}) collective-permute-start(bf16[512,512]{1,0:T(8,128)(2,1)} %pad_maximum_fusion.32), channel_id=1, source_target_pairs={{0,1},{1,0},{2,3},{3,2},{4,5},{5,4},{6,7},{7,6},{8,9},{9,8},{10,11... | collective-permute-start | bytes 1572872 | tf_op jit(solution)/shard_map/ppermute | solution.py:36
  122.7 37.8 %collective-permute-start.11 = (bf16[512,512]{1,0:T(8,128)(2,1)}, bf16[512,512]{1,0:T(8,128)(2,1)}, u32[]{:S(2)}, u32[]{:S(2)}) collective-permute-start(bf16[512,512]{1,0:T(8,128)(2,1)} %pad_maximum_fusion.33), channel_id=1, source_target_pairs={{0,2},{1,3},{2,0},{3,1},{4,6},{5,7},{6,4},{7,5},{8,10},{9,11},{10,... | collective-permute-start | bytes 1572872 | tf_op jit(solution)/shard_map/ppermute | solution.py:36
  125.4 43.2 %collective-permute-start.12 = (bf16[512,512]{1,0:T(8,128)(2,1)}, bf16[512,512]{1,0:T(8,128)(2,1)}, u32[]{:S(2)}, u32[]{:S(2)}) collective-permute-start(bf16[512,512]{1,0:T(8,128)(2,1)} %pad_maximum_fusion.34), channel_id=1, source_target_pairs={{0,3},{1,2},{2,1},{3,0},{4,7},{5,6},{6,5},{7,4},{8,11},{9,10},{10,... | collective-permute-start | bytes 1572872 | tf_op jit(solution)/shard_map/ppermute | solution.py:36
  168.6 43.5 %collective-permute-start.13 = (bf16[512,2048]{1,0:T(8,128)(2,1)S(1)}, bf16[512,2048]{1,0:T(8,128)(2,1)}, u32[]{:S(2)}, u32[]{:S(2)}) collective-permute-start(bf16[512,2048]{1,0:T(8,128)(2,1)S(1)} %multiply_convert_fusion.4), channel_id=1, source_target_pairs={{0,8},{4,12},{8,0},{12,4},{16,24},{20,28},{24,16},{28,20},{1,9},{5... | collective-permute-start | bytes 6291464 | tf_op jit(solution)/shard_map/ppermute | solution.py:50
  170.1 43.3 %collective-permute-start.14 = (bf16[512,2048]{1,0:T(8,128)(2,1)S(1)}, bf16[512,2048]{1,0:T(8,128)(2,1)}, u32[]{:S(2)}, u32[]{:S(2)}) collective-permute-start(bf16[512,2048]{1,0:T(8,128)(2,1)S(1)} %multiply_convert_fusion.4), channel_id=1, source_target_pairs={{0,16},{4,20},{8,24},{12,28},{16,0},{20,4},{24,8},{28,12},{1,17},{... | collective-permute-start | bytes 6291464 | tf_op jit(solution)/shard_map/ppermute | solution.py:50
  171.5 33.8 %collective-permute-start.15 = (bf16[2048,384]{0,1:T(8,128)(2,1)}, bf16[2048,384]{0,1:T(8,128)(2,1)}, u32[]{:S(2)}, u32[]{:S(2)}) collective-permute-start(bf16[2048,384]{0,1:T(8,128)(2,1)} %pad_maximum_fusion.11), channel_id=1, source_target_pairs={{0,1},{1,2},{2,3},{4,5},{5,6},{6,7},{8,9},{9,10},{10,11},{12,13},{... | collective-permute-start | bytes 4718600 | tf_op jit(solution)/shard_map/ppermute | solution.py:80
  173.4 33.8 %collective-permute-start.16 = (bf16[2048,384]{0,1:T(8,128)(2,1)}, bf16[2048,384]{0,1:T(8,128)(2,1)}, u32[]{:S(2)}, u32[]{:S(2)}) collective-permute-start(bf16[2048,384]{0,1:T(8,128)(2,1)} %pad_maximum_fusion.11), channel_id=1, source_target_pairs={{3,2},{2,1},{1,0},{7,6},{6,5},{5,4},{11,10},{10,9},{9,8},{15,14},{... | collective-permute-start | bytes 4718600 | tf_op jit(solution)/shard_map/ppermute | solution.py:80
  213.3 37.2 %collective-permute-start.19 = (bf16[2048,384]{0,1:T(8,128)(2,1)}, bf16[2048,384]{0,1:T(8,128)(2,1)}, u32[]{:S(2)}, u32[]{:S(2)}) collective-permute-start(bf16[2048,384]{0,1:T(8,128)(2,1)} %collective-permute-done.15), channel_id=1, source_target_pairs={{1,2},{2,3},{5,6},{6,7},{9,10},{10,11},{13,14},{14,15},{17,18},{18... | collective-permute-start | bytes 4718600 | tf_op jit(solution)/shard_map/ppermute | solution.py:80
  215.2 35.2 %collective-permute-start.20 = (bf16[2048,384]{0,1:T(8,128)(2,1)}, bf16[2048,384]{0,1:T(8,128)(2,1)}, u32[]{:S(2)}, u32[]{:S(2)}) collective-permute-start(bf16[2048,384]{0,1:T(8,128)(2,1)} %collective-permute-done.16), channel_id=1, source_target_pairs={{2,1},{1,0},{6,5},{5,4},{10,9},{9,8},{14,13},{13,12},{18,17},{17,1... | collective-permute-start | bytes 4718600 | tf_op jit(solution)/shard_map/ppermute | solution.py:80
  228.8 19.3 %collective-permute-start.17 = (bf16[256,2048]{1,0:T(8,128)(2,1)S(1)}, bf16[256,2048]{1,0:T(8,128)(2,1)S(1)}, u32[]{:S(2)}, u32[]{:S(2)}) collective-permute-start(bf16[256,2048]{1,0:T(8,128)(2,1)S(1)} %slice.535), channel_id=1, source_target_pairs={{0,16},{4,20},{8,24},{12,28},{16,0},{20,4},{24,8},{28,12},{1,17},{... | collective-permute-start | bytes 3145736 | tf_op jit(solution)/shard_map/ppermute | solution.py:50
  231.5 18.9 %collective-permute-start.18 = (bf16[256,2048]{1,0:T(8,128)(2,1)S(1)}, bf16[256,2048]{1,0:T(8,128)(2,1)S(1)}, u32[]{:S(2)}, u32[]{:S(2)}) collective-permute-start(bf16[256,2048]{1,0:T(8,128)(2,1)S(1)} %slice.536), channel_id=1, source_target_pairs={{0,8},{4,12},{8,0},{12,4},{16,24},{20,28},{24,16},{28,20},{1,9},{5... | collective-permute-start | bytes 3145736 | tf_op jit(solution)/shard_map/ppermute | solution.py:50
  250.5 349.8 %reduce-scatter.3.cloned.1.call-start = ((), (), s32[]{:S(2)}) async-start(), calls=%async_computation.5 | async-start | bytes 7864320 | tf_op jit(solution)/shard_map/reduce_scatter | solution.py:629
  252.7 36.2 %collective-permute-start.21 = (bf16[2048,2048]{1,0:T(8,128)(2,1)}, bf16[2048,2048]{1,0:T(8,128)(2,1)}, u32[]{:S(2)}, u32[]{:S(2)}) collective-permute-start(bf16[2048,2048]{1,0:T(8,128)(2,1)} %bitcast.20), channel_id=1, source_target_pairs={{0,4},{4,0},{8,12},{12,8},{16,20},{20,16},{24,28},{28,24},{1,5},{5... | collective-permute-start | bytes 25165832 | tf_op jit(solution)/shard_map/ppermute | solution.py:50
  252.7 36.2 %collective-permute-start.22 = (bf16[2048,384]{0,1:T(8,128)(2,1)}, bf16[2048,384]{0,1:T(8,128)(2,1)S(1)}, u32[]{:S(2)}, u32[]{:S(2)}) collective-permute-start(bf16[2048,384]{0,1:T(8,128)(2,1)} %collective-permute-done.19), channel_id=1, source_target_pairs={{2,3},{6,7},{10,11},{14,15},{18,19},{22,23},{26,27},{30,31}} | collective-permute-start | bytes 4718600 | tf_op jit(solution)/shard_map/ppermute | solution.py:80
  254.0 34.8 %collective-permute-start.23 = (bf16[2048,384]{0,1:T(8,128)(2,1)}, bf16[2048,384]{0,1:T(8,128)(2,1)}, u32[]{:S(2)}, u32[]{:S(2)}) collective-permute-start(bf16[2048,384]{0,1:T(8,128)(2,1)} %collective-permute-done.20), channel_id=1, source_target_pairs={{1,0},{5,4},{9,8},{13,12},{17,16},{21,20},{25,24},{29,28}} | collective-permute-start | bytes 4718600 | tf_op jit(solution)/shard_map/ppermute | solution.py:80
  379.4 25.8 %collective-permute-start.24 = (bf16[2048,2048]{1,0:T(8,128)(2,1)}, bf16[2048,2048]{1,0:T(8,128)(2,1)}, u32[]{:S(2)}, u32[]{:S(2)}) collective-permute-start(bf16[2048,2048]{1,0:T(8,128)(2,1)} %convolution_convert_fusion.2), channel_id=1, source_target_pairs={{0,4},{4,0},{8,12},{12,8},{16,20},{20,16},{24,28},{28,24},{1,5},{5... | collective-permute-start | bytes 25165832 | tf_op jit(solution)/shard_map/ppermute | solution.py:50
  379.4 81.9 %collective-permute-start.27 = (bf16[2048,2048]{1,0:T(8,128)(2,1)}, bf16[2048,2048]{1,0:T(8,128)(2,1)S(1)}, u32[]{:S(2)}, u32[]{:S(2)}) collective-permute-start(bf16[2048,2048]{1,0:T(8,128)(2,1)} %convolution_convert_fusion.3), channel_id=1, source_target_pairs={{0,4},{4,0},{8,12},{12,8},{16,20},{20,16},{24,28},{28,24},{1,5},{5... | collective-permute-start | bytes 25165832 | tf_op jit(solution)/shard_map/ppermute | solution.py:50
  413.2 48.2 %collective-permute-start.26 = (bf16[512,2048]{1,0:T(8,128)(2,1)}, bf16[512,2048]{1,0:T(8,128)(2,1)}, u32[]{:S(2)}, u32[]{:S(2)}) collective-permute-start(bf16[512,2048]{1,0:T(8,128)(2,1)} %pad_maximum_fusion.6), channel_id=1, source_target_pairs={{0,16},{4,20},{8,24},{12,28},{16,0},{20,4},{24,8},{28,12},{1,17},{... | collective-permute-start | bytes 6291464 | tf_op jit(solution)/shard_map/ppermute | solution.py:50
  417.2 47.9 %collective-permute-start.25 = (bf16[512,2048]{1,0:T(8,128)(2,1)}, bf16[512,2048]{1,0:T(8,128)(2,1)}, u32[]{:S(2)}, u32[]{:S(2)}) collective-permute-start(bf16[512,2048]{1,0:T(8,128)(2,1)} %pad_maximum_fusion.5), channel_id=1, source_target_pairs={{0,8},{4,12},{8,0},{12,4},{16,24},{20,28},{24,16},{28,20},{1,9},{5... | collective-permute-start | bytes 6291464 | tf_op jit(solution)/shard_map/ppermute | solution.py:50
  474.9 217.6 %reduce-scatter.5.cloned.1.call-start = ((), (), s32[]{:S(2)}) async-start(), calls=%async_computation.6 | async-start | bytes 5898240 | tf_op jit(solution)/shard_map/reduce_scatter | solution.py:672
  477.9 24.3 %collective-permute-start.28 = (bf16[256,2048]{1,0:T(8,128)(2,1)S(1)}, bf16[256,2048]{1,0:T(8,128)(2,1)S(1)}, u32[]{:S(2)}, u32[]{:S(2)}) collective-permute-start(bf16[256,2048]{1,0:T(8,128)(2,1)S(1)} %get-tuple-element.375), channel_id=1, source_target_pairs={{0,16},{4,20},{8,24},{12,28},{16,0},{20,4},{24,8},{28,12},{1,17},{... | collective-permute-start | bytes 3145736 | tf_op jit(solution)/shard_map/ppermute | solution.py:50
  478.0 24.2 %collective-permute-start.29 = (bf16[256,2048]{1,0:T(8,128)(2,1)S(1)}, bf16[256,2048]{1,0:T(8,128)(2,1)S(1)}, u32[]{:S(2)}, u32[]{:S(2)}) collective-permute-start(bf16[256,2048]{1,0:T(8,128)(2,1)S(1)} %get-tuple-element.374), channel_id=1, source_target_pairs={{0,8},{4,12},{8,0},{12,4},{16,24},{20,28},{24,16},{28,20},{1,9},{5... | collective-permute-start | bytes 3145736 | tf_op jit(solution)/shard_map/ppermute | solution.py:50
  502.3 54.3 %collective-permute-start.30 = (bf16[512,2048]{1,0:T(8,128)(2,1)}, bf16[512,2048]{1,0:T(8,128)(2,1)}, u32[]{:S(2)}, u32[]{:S(2)}) collective-permute-start(bf16[512,2048]{1,0:T(8,128)(2,1)} %pad_maximum_fusion.7), channel_id=1, source_target_pairs={{0,8},{4,12},{8,0},{12,4},{16,24},{20,28},{24,16},{28,20},{1,9},{5... | collective-permute-start | bytes 6291464 | tf_op jit(solution)/shard_map/ppermute | solution.py:50
  503.2 53.3 %collective-permute-start.31 = (bf16[512,2048]{1,0:T(8,128)(2,1)}, bf16[512,2048]{1,0:T(8,128)(2,1)}, u32[]{:S(2)}, u32[]{:S(2)}) collective-permute-start(bf16[512,2048]{1,0:T(8,128)(2,1)} %pad_maximum_fusion.8), channel_id=1, source_target_pairs={{0,16},{4,20},{8,24},{12,28},{16,0},{20,4},{24,8},{28,12},{1,17},{... | collective-permute-start | bytes 6291464 | tf_op jit(solution)/shard_map/ppermute | solution.py:50
  559.6 34.3 %collective-permute-start.33 = (bf16[256,2048]{1,0:T(8,128)(2,1)S(1)}, bf16[256,2048]{1,0:T(8,128)(2,1)}, u32[]{:S(2)}, u32[]{:S(2)}) collective-permute-start(bf16[256,2048]{1,0:T(8,128)(2,1)S(1)} %get-tuple-element.367), channel_id=1, source_target_pairs={{0,16},{4,20},{8,24},{12,28},{16,0},{20,4},{24,8},{28,12},{1,17},{... | collective-permute-start | bytes 3145736 | tf_op jit(solution)/shard_map/ppermute | solution.py:50
  560.4 34.3 %collective-permute-start.34 = (bf16[256,2048]{1,0:T(8,128)(2,1)S(1)}, bf16[256,2048]{1,0:T(8,128)(2,1)}, u32[]{:S(2)}, u32[]{:S(2)}) collective-permute-start(bf16[256,2048]{1,0:T(8,128)(2,1)S(1)} %get-tuple-element.366), channel_id=1, source_target_pairs={{0,8},{4,12},{8,0},{12,4},{16,24},{20,28},{24,16},{28,20},{1,9},{5... | collective-permute-start | bytes 3145736 | tf_op jit(solution)/shard_map/ppermute | solution.py:50
  562.8 31.0 %collective-permute-start.32 = (bf16[10,64,512]{2,1,0:T(8,128)(2,1)S(1)}, bf16[10,64,512]{2,1,0:T(8,128)(2,1)S(1)}, u32[]{:S(2)}, u32[]{:S(2)}) collective-permute-start(bf16[10,64,512]{2,1,0:T(8,128)(2,1)S(1)} %copy-done.81), channel_id=1, source_target_pairs={{0,1},{1,0},{2,3},{3,2},{4,5},{5,4},{6,7},{7,6},{8,9},{9,8},{10,11... | collective-permute-start | bytes 1966088 | tf_op jit(solution)/shard_map/ppermute | solution.py:50
  600.3 156.3 %all-gather.15.cloned.1.call-start = ((), (), s32[]{:S(2)}) async-start(), calls=%async_computation.7 | async-start | bytes 4718592 | tf_op jit(solution)/shard_map/all_gather | solution.py:676
  620.5 185.0 %all-gather.17.cloned.1.call-start = ((), (), s32[]{:S(2)}) async-start(), calls=%async_computation.8 | async-start | bytes 1474560 | tf_op jit(solution)/shard_map/all_gather | solution.py:739
  629.2 51.1 %collective-permute-start.35 = (bf16[1024,2048]{1,0:T(8,128)(2,1)}, bf16[1024,2048]{1,0:T(8,128)(2,1)}, u32[]{:S(2)}, u32[]{:S(2)}) collective-permute-start(bf16[1024,2048]{1,0:T(8,128)(2,1)} %add_convert_fusion.4), channel_id=1, source_target_pairs={{0,4},{4,0},{8,12},{12,8},{16,20},{20,16},{24,28},{28,24},{1,5},{5... | collective-permute-start | bytes 12582920 | tf_op jit(solution)/shard_map/ppermute | solution.py:50
  631.1 20.0 %collective-permute-start.36 = (bf16[512,512]{1,0:T(8,128)(2,1)S(1)}, bf16[512,512]{1,0:T(8,128)(2,1)S(1)}, u32[]{:S(2)}, u32[]{:S(2)}) collective-permute-start(bf16[512,512]{1,0:T(8,128)(2,1)S(1)} %get-tuple-element.414), channel_id=1, source_target_pairs={{0,1},{1,0},{2,3},{3,2},{4,5},{5,4},{6,7},{7,6},{8,9},{9,8},{10,11... | collective-permute-start | bytes 1572872 | tf_op jit(solution)/shard_map/ppermute | solution.py:36
  631.6 22.9 %collective-permute-start.37 = (bf16[512,512]{1,0:T(8,128)(2,1)S(1)}, bf16[512,512]{1,0:T(8,128)(2,1)S(1)}, u32[]{:S(2)}, u32[]{:S(2)}) collective-permute-start(bf16[512,512]{1,0:T(8,128)(2,1)S(1)} %get-tuple-element.415), channel_id=1, source_target_pairs={{0,2},{1,3},{2,0},{3,1},{4,6},{5,7},{6,4},{7,5},{8,10},{9,11},{10,... | collective-permute-start | bytes 1572872 | tf_op jit(solution)/shard_map/ppermute | solution.py:36
  631.6 48.7 %collective-permute-start.38 = (bf16[512,512]{1,0:T(8,128)(2,1)S(1)}, bf16[512,512]{1,0:T(8,128)(2,1)S(1)}, u32[]{:S(2)}, u32[]{:S(2)}) collective-permute-start(bf16[512,512]{1,0:T(8,128)(2,1)S(1)} %get-tuple-element.412), channel_id=1, source_target_pairs={{0,3},{1,2},{2,1},{3,0},{4,7},{5,6},{6,5},{7,4},{8,11},{9,10},{10,... | collective-permute-start | bytes 1572872 | tf_op jit(solution)/shard_map/ppermute | solution.py:36
  688.5 31.7 %collective-permute-start.43 = (bf16[256,2048]{1,0:T(8,128)(2,1)}, bf16[256,2048]{1,0:T(8,128)(2,1)}, u32[]{:S(2)}, u32[]{:S(2)}) collective-permute-start(bf16[256,2048]{1,0:T(8,128)(2,1)} %pad_maximum_fusion.22), channel_id=1, source_target_pairs={{0,16},{4,20},{8,24},{12,28},{16,0},{20,4},{24,8},{28,12},{1,17},{... | collective-permute-start | bytes 3145736 | tf_op jit(solution)/shard_map/ppermute | solution.py:50
  690.9 29.3 %collective-permute-start.42 = (bf16[256,2048]{1,0:T(8,128)(2,1)}, bf16[256,2048]{1,0:T(8,128)(2,1)}, u32[]{:S(2)}, u32[]{:S(2)}) collective-permute-start(bf16[256,2048]{1,0:T(8,128)(2,1)} %pad_maximum_fusion.21), channel_id=1, source_target_pairs={{0,8},{4,12},{8,0},{12,4},{16,24},{20,28},{24,16},{28,20},{1,9},{5... | collective-permute-start | bytes 3145736 | tf_op jit(solution)/shard_map/ppermute | solution.py:50
  693.6 26.6 %collective-permute-start.39 = (bf16[160,512]{1,0:T(8,128)(2,1)S(1)}, bf16[160,512]{1,0:T(8,128)(2,1)S(1)}, u32[]{:S(2)}, u32[]{:S(2)}) collective-permute-start(bf16[160,512]{1,0:T(8,128)(2,1)S(1)} %get-tuple-element.474), channel_id=1, source_target_pairs={{0,1},{1,0},{2,3},{3,2},{4,5},{5,4},{6,7},{7,6},{8,9},{9,8},{10,11... | collective-permute-start | bytes 491528 | tf_op jit(solution)/shard_map/ppermute | solution.py:36
  693.7 26.5 %collective-permute-start.40 = (bf16[160,512]{1,0:T(8,128)(2,1)S(1)}, bf16[160,512]{1,0:T(8,128)(2,1)S(1)}, u32[]{:S(2)}, u32[]{:S(2)}) collective-permute-start(bf16[160,512]{1,0:T(8,128)(2,1)S(1)} %get-tuple-element.475), channel_id=1, source_target_pairs={{0,2},{1,3},{2,0},{3,1},{4,6},{5,7},{6,4},{7,5},{8,10},{9,11},{10,... | collective-permute-start | bytes 491528 | tf_op jit(solution)/shard_map/ppermute | solution.py:36
  694.7 25.5 %collective-permute-start.41 = (bf16[160,512]{1,0:T(8,128)(2,1)S(1)}, bf16[160,512]{1,0:T(8,128)(2,1)S(1)}, u32[]{:S(2)}, u32[]{:S(2)}) collective-permute-start(bf16[160,512]{1,0:T(8,128)(2,1)S(1)} %get-tuple-element.472), channel_id=1, source_target_pairs={{0,3},{1,2},{2,1},{3,0},{4,7},{5,6},{6,5},{7,4},{8,11},{9,10},{10,... | collective-permute-start | bytes 491528 | tf_op jit(solution)/shard_map/ppermute | solution.py:36
  721.0 84.5 %all-gather.21.cloned.1.call-start = ((), (), s32[]{:S(2)}) async-start(), calls=%async_computation.10 | async-start | bytes 9437184 | tf_op jit(solution)/shard_map/all_gather | solution.py:674
  723.3 135.4 %all-gather.19.cloned.1.call-start = ((), (), s32[]{:S(2)}) async-start(), calls=%async_computation.9 | async-start | bytes 5308416 | tf_op jit(solution)/shard_map/all_gather | solution.py:767
  726.3 17.1 %collective-permute-start.44 = (bf16[128,2048]{1,0:T(8,128)(2,1)}, bf16[128,2048]{1,0:T(8,128)(2,1)}, u32[]{:S(2)}, u32[]{:S(2)}) collective-permute-start(bf16[128,2048]{1,0:T(8,128)(2,1)} %get-tuple-element.385), channel_id=1, source_target_pairs={{0,16},{4,20},{8,24},{12,28},{16,0},{20,4},{24,8},{28,12},{1,17},{... | collective-permute-start | bytes 1572872 | tf_op jit(solution)/shard_map/ppermute | solution.py:50
  727.7 17.7 %collective-permute-start.45 = (bf16[128,2048]{1,0:T(8,128)(2,1)}, bf16[128,2048]{1,0:T(8,128)(2,1)}, u32[]{:S(2)}, u32[]{:S(2)}) collective-permute-start(bf16[128,2048]{1,0:T(8,128)(2,1)} %get-tuple-element.384), channel_id=1, source_target_pairs={{0,8},{4,12},{8,0},{12,4},{16,24},{20,28},{24,16},{28,20},{1,9},{5... | collective-permute-start | bytes 1572872 | tf_op jit(solution)/shard_map/ppermute | solution.py:50
  753.1 21.7 %collective-permute-start.46 = (bf16[256,1152]{1,0:T(8,128)(2,1)}, bf16[256,1152]{1,0:T(8,128)(2,1)}, u32[]{:S(2)}, u32[]{:S(2)}) collective-permute-start(bf16[256,1152]{1,0:T(8,128)(2,1)} %get-tuple-element.487), channel_id=1, source_target_pairs={{0,1},{1,0},{2,3},{3,2},{4,5},{5,4},{6,7},{7,6},{8,9},{9,8},{10,11... | collective-permute-start | bytes 1769480 | tf_op jit(solution)/shard_map/ppermute | solution.py:36
  753.1 41.7 %collective-permute-start.47 = (bf16[256,1152]{1,0:T(8,128)(2,1)}, bf16[256,1152]{1,0:T(8,128)(2,1)}, u32[]{:S(2)}, u32[]{:S(2)}) collective-permute-start(bf16[256,1152]{1,0:T(8,128)(2,1)} %get-tuple-element.488), channel_id=1, source_target_pairs={{0,2},{1,3},{2,0},{3,1},{4,6},{5,7},{6,4},{7,5},{8,10},{9,11},{10,... | collective-permute-start | bytes 1769480 | tf_op jit(solution)/shard_map/ppermute | solution.py:36
  755.4 50.1 %collective-permute-start.48 = (bf16[256,1152]{1,0:T(8,128)(2,1)}, bf16[256,1152]{1,0:T(8,128)(2,1)}, u32[]{:S(2)}, u32[]{:S(2)}) collective-permute-start(bf16[256,1152]{1,0:T(8,128)(2,1)} %get-tuple-element.486), channel_id=1, source_target_pairs={{0,3},{1,2},{2,1},{3,0},{4,7},{5,6},{6,5},{7,4},{8,11},{9,10},{10,... | collective-permute-start | bytes 1769480 | tf_op jit(solution)/shard_map/ppermute | solution.py:36
  811.2 21.9 %collective-permute-start.49 = (bf16[512,512]{1,0:T(8,128)(2,1)S(1)}, bf16[512,512]{1,0:T(8,128)(2,1)}, u32[]{:S(2)}, u32[]{:S(2)}) collective-permute-start(bf16[512,512]{1,0:T(8,128)(2,1)S(1)} %get-tuple-element.408), channel_id=1, source_target_pairs={{0,1},{1,0},{2,3},{3,2},{4,5},{5,4},{6,7},{7,6},{8,9},{9,8},{10,11... | collective-permute-start | bytes 1572872 | tf_op jit(solution)/shard_map/ppermute | solution.py:36
  811.2 37.6 %collective-permute-start.50 = (bf16[512,512]{1,0:T(8,128)(2,1)S(1)}, bf16[512,512]{1,0:T(8,128)(2,1)}, u32[]{:S(2)}, u32[]{:S(2)}) collective-permute-start(bf16[512,512]{1,0:T(8,128)(2,1)S(1)} %get-tuple-element.409), channel_id=1, source_target_pairs={{0,2},{1,3},{2,0},{3,1},{4,6},{5,7},{6,4},{7,5},{8,10},{9,11},{10,... | collective-permute-start | bytes 1572872 | tf_op jit(solution)/shard_map/ppermute | solution.py:36
  813.9 44.8 %collective-permute-start.51 = (bf16[512,512]{1,0:T(8,128)(2,1)S(1)}, bf16[512,512]{1,0:T(8,128)(2,1)}, u32[]{:S(2)}, u32[]{:S(2)}) collective-permute-start(bf16[512,512]{1,0:T(8,128)(2,1)S(1)} %get-tuple-element.406), channel_id=1, source_target_pairs={{0,3},{1,2},{2,1},{3,0},{4,7},{5,6},{6,5},{7,4},{8,11},{9,10},{10,... | collective-permute-start | bytes 1572872 | tf_op jit(solution)/shard_map/ppermute | solution.py:36
  (113 other events, 719.0 us)
Sparse Core Ops, SparseCore 0:
  57.5 44.0 all-gather.8
  104.0 41.1 all-gather.10
  250.6 88.3 all-gather.12
  475.0 125.2 reduce-scatter.2
  604.1 56.5 reduce-scatter.4
  662.6 43.4 all-gather.14
  721.1 26.5 all-gather.16
  750.3 53.5 all-gather.20
  808.4 38.3 all-gather.18

commit v3 on v2

--- a/solution.py
+++ b/solution.py
@@ -141,6 +141,48 @@
         self.parts += got
 
 
+TOGETHER = (((3, 0), (1, 0)), ((3, 1), (2, 1)), ((0, 0), (0, 1), (2, 0), (1, 1)))
+APART = (((3, 0),), ((3, 1),), ((1, 0),), ((2, 1),), ((0, 0), (0, 1), (2, 0), (1, 1)))
+
+
+def chip_sums(mine, got, chip, plan):
+    half, columns = mine.shape[0] // 8, mine.shape[1]
+    flat = [place for places in plan for place in places]
+    index = jnp.stack([(chip ^ block) * 2 + part for block, part in flat]).astype(jnp.int32)
+    firsts = [sum(len(places) for places in plan[:k]) for k in range(len(plan))]
+
+    def kernel(index_ref, mine_ref, got_ref, *outs):
+        step = pl.program_id(0)
+        total = (mine_ref[...].astype(full) + got_ref[...].astype(full)).astype(low)
+        for first, places, out in zip(firsts, plan, outs):
+
+            @pl.when((step >= first) & (step < first + len(places)))
+            def _():
+                out[...] = total
+
+    source = pl.BlockSpec((half, columns), lambda g, index: (index[g], 0))
+
+    def target(first, count):
+        return pl.BlockSpec(
+            (half, columns), lambda g, index: (jnp.clip(g - first, 0, count - 1), 0)
+        )
+
+    return pl.pallas_call(
+        kernel,
+        out_shape=[
+            jax.ShapeDtypeStruct((len(places) * half, columns), low) for places in plan
+        ],
+        grid_spec=pltpu.PrefetchScalarGridSpec(
+            num_scalar_prefetch=1,
+            grid=(len(flat),),
+            in_specs=[source, source],
+            out_specs=[target(f, len(places)) for f, places in zip(firsts, plan)],
+        ),
+        compiler_params=pltpu.CompilerParams(vmem_limit_bytes=40 << 20),
+        cost_estimate=pl.CostEstimate(flops=0, bytes_accessed=1 << 16, transcendentals=0),
+    )(index, mine, got)
+
+
 class Collect:
     def __init__(self, other, axis, n, group):
         self.axis, self.n, self.chip = axis, n, group // 2
@@ -152,21 +194,17 @@
     def move(self, array, mask):
         return exchange(array, self.axis, mask, self.n)
 
-    def second(self, mine, *got, launch=True):
-        self.flying = got
+    def second(self, mine, *got, apart=False):
+        self.flying, self.held = got, []
         if self.n != CUBE:
             return
-        mine = mine.reshape(4, mine.shape[0] // 4, -1)
-        got = got[0].reshape(mine.shape)
-        half = self.half = mine.shape[1] // 2
-        self.sums = added(mine, got)
-        block = lambda k: at_index(self.sums, self.chip ^ k)
-        self.flying = [
-            jnp.concatenate([block(3)[:half], block(1)[:half]], 0),
-            jnp.concatenate([block(3)[half:], block(2)[half:]], 0),
-        ]
-        if launch:
-            self.launch(*self.flying)
+        self.half = mine.shape[0] // 8
+        *sent, self.keep = chip_sums(mine, got[0], self.chip, APART if apart else TOGETHER)
+        self.apart = apart
+        if apart:
+            self.flying, self.held = sent[:2], sent[2:]
+        else:
+            self.launch(*sent)
 
     def launch(self, *ready):
         self.flying = ready
@@ -174,26 +212,32 @@
             self.flying = [self.move(ready[0], 2), self.move(ready[1], 4)]
 
     def third(self, *got):
+        self.flying = got
         if self.n != CUBE:
-            self.flying = got
             return
         half = self.half
-        block = lambda k: at_index(self.sums, self.chip ^ k)
-        self.direct = [got[0][half:], got[1][half:]]
+        if not self.apart:
+            self.direct = [got[0][half:], got[1][half:]]
         self.flying = [
-            self.move(added(block(2)[:half], got[0][:half]), 4),
-            self.move(added(block(1)[half:], got[1][:half]), 2),
+            self.move(added(self.keep[2 * half : 3 * half], got[0][:half]), 4),
+            self.move(added(self.keep[3 * half :], got[1][:half]), 2),
         ]
+
+    def fourth(self, *got):
+        self.flying = got
+        if self.n == CUBE:
+            self.relayed = got
+            self.flying = [self.move(self.held[0], 2), self.move(self.held[1], 4)]
 
     def last(self, *got):
         if self.n != CUBE:
             return got[0]
         half = self.half
-        own = at_index(self.sums, self.chip)
+        direct, got = (got, self.relayed) if self.apart else (self.direct, got)
         return jnp.concatenate(
             [
-                added(own[:half], self.direct[0], got[0]),
-                added(own[half:], self.direct[1], got[1]),
+                added(self.keep[:half], direct[0], got[0]),
+                added(self.keep[half : 2 * half], direct[1], got[1]),
             ],
             0,
         )
@@ -360,34 +404,66 @@
     )(starts, queries, keys, values, grads, sums_in)
 
 
-def widen_kernel(wide_ref, down_ref, gate_out, up_out, down_out):
+def by_ranks(wide, down, rank, parts):
+    rows, units = wide.shape[0], wide.shape[1] // (2 * parts)
+    place = lambda r: (rank - r) % parts
+    if units % 128:
+        blocks = jnp.concatenate(
+            [a.reshape(rows, -1, parts, units) for a in (wide, down)], 1
+        )
+        blocks = jnp.transpose(blocks, (2, 0, 1, 3)).reshape(parts, rows, 3 * units)
+        return jnp.stack([blocks[place(r)] for r in range(parts)])
+
+    def kernel(index_ref, gate_ref, up_ref, down_ref, out_ref):
+        for k, ref in enumerate((gate_ref, up_ref, down_ref)):
+            out_ref[0, :, k * units : (k + 1) * units] = ref[...]
+
+    def column(first):
+        return pl.BlockSpec((rows, units), lambda r, index: (0, first + index[r]))
+
+    return pl.pallas_call(
+        kernel,
+        out_shape=jax.ShapeDtypeStruct((parts, rows, 3 * units), low),
+        grid_spec=pltpu.PrefetchScalarGridSpec(
+            num_scalar_prefetch=1,
+            grid=(parts,),
+            in_specs=[column(0), column(parts), column(0)],
+            out_specs=pl.BlockSpec((1, rows, 3 * units), lambda r, index: (r, 0, 0)),
+        ),
+        compiler_params=pltpu.CompilerParams(vmem_limit_bytes=32 << 20),
+        cost_estimate=pl.CostEstimate(flops=0, bytes_accessed=1 << 16, transcendentals=0),
+    )(place(jnp.arange(parts, dtype=jnp.int32)), wide, wide, down)
+
+
+def widen_kernel(pack_ref, gate_out, up_out, down_out):
     units = gate_out.shape[1]
-    gate_out[...] = wide_ref[0, :, :units].astype(full)
-    up_out[...] = wide_ref[0, :, units:].astype(full)
-    down_out[...] = down_ref[...].astype(full)
-
-
-def widen(wide, down):
-    groups, rows, columns = wide.shape
-    units = columns // 2
+    gate_out[...] = pack_ref[0, :, :units].astype(full)
+    up_out[...] = pack_ref[0, :, units : 2 * units].astype(full)
+    down_out[...] = pack_ref[0, :, 2 * units :].astype(full).T
+
+
+def widen(pack):
+    groups, rows, columns = pack.shape
+    units = columns // 3
     if units % 128:
-        pairs = jnp.transpose(wide, (1, 0, 2)).reshape(rows, groups, 2, units).astype(full)
-        gate, up = (pairs[:, :, k].reshape(rows, -1) for k in range(2))
-        return gate, up, down.astype(full)
+        gate, up, down = (
+            jnp.transpose(pack[:, :, k * units : (k + 1) * units], (1, 0, 2))
+            .reshape(rows, -1)
+            .astype(full)
+            for k in range(3)
+        )
+        return gate, up, down.T
     shape = jax.ShapeDtypeStruct((rows, groups * units), full)
     column = pl.BlockSpec((rows, units), lambda g: (0, g))
     return pl.pallas_call(
         widen_kernel,
-        out_shape=(shape, shape, jax.ShapeDtypeStruct(down.shape, full)),
+        out_shape=(shape, shape, jax.ShapeDtypeStruct((groups * units, rows), full)),
         grid=(groups,),
-        in_specs=[
-            pl.BlockSpec((1, rows, columns), lambda g: (g, 0, 0)),
-            pl.BlockSpec((units, down.shape[1]), lambda g: (g, 0)),
-        ],
-        out_specs=[column, column, pl.BlockSpec((units, down.shape[1]), lambda g: (g, 0))],
+        in_specs=[pl.BlockSpec((1, rows, columns), lambda g: (g, 0, 0))],
+        out_specs=[column, column, pl.BlockSpec((units, rows), lambda g: (g, 0))],
         compiler_params=pltpu.CompilerParams(vmem_limit_bytes=32 << 20),
         cost_estimate=pl.CostEstimate(flops=0, bytes_accessed=1 << 16, transcendentals=0),
-    )(wide, down)
+    )(pack)
 
 
 def norm_backward(values, rms, gain, normed_grad):
@@ -543,10 +619,17 @@
             )
             for a in (0, 1)
         )
+        pairs = mixed.reshape(4, 2, heads_here, mine)
+        mixed_own, mixed_other = (
+            lax.dynamic_index_in_dim(pairs, at, 1, keepdims=False).reshape(-1, mine)
+            for at in (group % 2, 1 - group % 2)
+        )
     else:
         normed_own = normed_other = normed
-    *got, up, down, cotangent_mine, normed_own, normed_other = order(
-        *second.flying, *weights.flying, cotangent_mine, normed_own, normed_other
+        mixed_own = mixed_other = mixed
+    *got, up, down, cotangent_mine, normed_own, normed_other, mixed_own, mixed_other = order(
+        *second.flying, *weights.flying, cotangent_mine, normed_own, normed_other,
+        mixed_own, mixed_other
     )
     second.second(*got)
     weights.take(up, down)
@@ -610,24 +693,9 @@
 
     second_sum.third(*got)
 
-    def block_of(k):
-        at = k * units
-        return jnp.concatenate(
-            [
-                wide_grad[:, at : at + units],
-                wide_grad[:, half + at : half + at + units],
-                down_grad[:, at : at + units],
-            ],
-            1,
-        )
-
-    pack = jnp.zeros((parts, D, 3 * units), low)
-    for k in ranks:
-        pack = lax.dynamic_update_slice(
-            pack, block_of(k)[None], ((rank - k) % parts, 0, 0)
-        )
+    pack = by_ranks(wide_grad, down_grad, rank, parts)
     pack = lax.psum_scatter(pack, "mp", scatter_dimension=0, tiled=False)
-    down_sum.second(down_terms[0], *flying, launch=False)
+    down_sum.second(down_terms[0], *flying, apart=True)
     *got, flying = order_split(order, second_sum.flying, down_sum.flying)
 
     normed_two_grad = second_sum.last(*got).astype(full)
@@ -640,7 +708,9 @@
     wide_extra = jnp.where(lane == 0, feedforward_gain_grad[:, None], 0.0)
     branch_grad = middle_grad.astype(low)
     mixed_grad = dot(output_all, branch_grad, 1, 1).astype(low).reshape(QH, HD, mine)
-    output_grad = mm(mixed, branch_grad).astype(low)
+    output_other = mm(mixed_other, branch_grad).astype(low)
+    output_own = mm(mixed_own, branch_grad).astype(low) if cube else output_other
+    output_sum = Collect(output_other, "dp", groups, group)
     query_rot_grad, key_rot_grad, value_grad = attend_back(
         starts, turned_queries, key_heads, value_heads, mixed_grad, row_totals
     )
@@ -657,24 +727,20 @@
     ]
     blocks = by_rank(blocks, place)
     away = [block.astype(low) for block in blocks[1:]]
-    query_rot_grad, *away, got = order_split(
-        order, [query_rot_grad, *away], down_sum.flying
+    query_rot_grad, output_own, *away, got, flying = order_split(
+        order, [query_rot_grad, output_own, *away], down_sum.flying, output_sum.flying
     )
     down_sum.third(*got)
+    output_sum.second(output_own, *flying)
 
     away = [exchange(block, "mp", k + 1, parts) for k, block in enumerate(away)]
     queries_low, query_gain_grad = query_pull(query_rot_grad)
     queries_low = queries_low.astype(low).reshape(QH * HD, mine)
-    queries_low, pack, output_grad, wide_extra, *away, got = order_split(
-        order, [queries_low, pack, output_grad, wide_extra, *away], down_sum.flying
-    )
-    down_total = down_sum.last(*got)
-    output_grad = lax.psum_scatter(output_grad, "dp", scatter_dimension=0, tiled=True)
-    pack = by_rows(pack)
-    wide_grad = by_rows(lax.all_gather(by_rows(pack[:, : 2 * units]), "dp", axis=0, tiled=False))
-    down_grad = by_rows(
-        lax.all_gather(by_rows(pack[:, 2 * units :].T), "dp", axis=0, tiled=True)
-    )
+    queries_low, pack, wide_extra, *away, out_relayed, got = order_split(
+        order, [queries_low, pack, wide_extra, *away], down_sum.flying, output_sum.flying
+    )
+    output_sum.third(*got)
+    pack = by_rows(lax.all_gather(by_rows(pack), "dp", axis=0, tiled=False))
     pair_grad = sum([blocks[0]] + [block.astype(full) for block in away])
     keys_grad, key_gain_grad = key_pull(pair_grad[:KVH])
     pair_low = jnp.concatenate(
@@ -698,17 +764,12 @@
             for at in (group % 2, 1 - group % 2)
         )
     other = projections(normed_other, other)
-    output = [(middle + down_total.astype(full)).astype(low)]
-    other, own, wide_low, all_low, normed_own, *output = order(
-        other, own, wide_low, all_low, normed_own, *output
-    )
-    output = by_rank([output[0][:, j * share : (j + 1) * share] for j in ranks], rank)
+    other, own, wide_low, all_low, normed_own = order(other, own, wide_low, all_low, normed_own)
 
     def by_feature(array):
         return by_rank([array[:, j * share : (j + 1) * share] for j in ranks], rank)
 
     projection_sum = Collect(other, "dp", groups, group)
-    output = swap(output, "mp")
     own = projections(normed_own, own) if cube else other
     queries_low, pair_low = all_low[: QH * HD], all_low[QH * HD :]
     normed_grad = (
@@ -720,10 +781,11 @@
         inputs, first_rms, attention_gain_all, normed_grad
     )
     input_gradient = (middle_grad + input_part).astype(low)
-    input_gradient, own, got, output = order_split(
-        order, [input_gradient, own], projection_sum.flying, output
+    input_gradient, own, got, flying = order_split(
+        order, [input_gradient, own], projection_sum.flying, output_sum.flying
     )
     projection_sum.second(own, *got)
+    output_grad = output_sum.last(*flying)
 
     def by_tokens(got, kind):
         got = by_rank(got, rank)
@@ -734,13 +796,19 @@
             rows += [block[chunk:] for block in near[::-1]]
         return jnp.concatenate(rows, 0).astype(kind)
 
+    input_gradient = swap(by_feature(input_gradient), "mp")
+    input_gradient, got, out_relayed = order_split(
+        order, [], input_gradient, projection_sum.flying, out_relayed
+    )
+    projection_sum.third(*got)
+
     output_grad = swap(by_feature(output_grad), "mp")
-    output_grad, got = order_split(order, [], output_grad, projection_sum.flying)
-    output_grad = lax.all_gather(added(*output_grad), "dp", axis=0, tiled=True)
-    projection_sum.third(*got)
-
-    got = order(*projection_sum.flying, input_gradient)
-    projection_total, input_gradient = projection_sum.last(*got[:-1]), got[-1]
+    output_grad, got, out_relayed = order_split(
+        order, [], output_grad, projection_sum.flying, out_relayed
+    )
+    output_grad = jnp.pad(added(*output_grad), ((0, rows - heads_here), (0, 0)))
+    projection_total = projection_sum.last(*got)
+    down_sum.fourth(*out_relayed)
 
     query_total, pair_total, extra = jnp.split(
         projection_total, [QH * HD, (QH + 2 * KVH) * HD], axis=1
@@ -760,28 +828,27 @@
         ],
         "mp",
     )
-    *projection, wide_grad, down_grad, input_gradient, output_grad = order(
-        *projection, wide_grad, down_grad, input_gradient, output_grad
-    )
-
-    projection = lax.all_gather(added(*projection), "dp", axis=0, tiled=True)
+    pack, projection, flying = order_split(order, [pack], projection, down_sum.flying)
+
+    projection = jnp.concatenate([added(*projection), output_grad], 1)
+    projection = lax.all_gather(projection, "dp", axis=0, tiled=True)
+    output = (middle + down_sum.last(*flying).astype(full)).astype(low)
+    output = swap(by_feature(output), "mp")
+    gate_weight_grad, up_weight_grad, down_weight_grad = widen(pack)
+    input_gradient = by_tokens(input_gradient, full)
+    got = order(
+        projection, gate_weight_grad, up_weight_grad, down_weight_grad, input_gradient, *output
+    )
+    projection, gate_weight_grad, up_weight_grad, down_weight_grad, input_gradient = got[:5]
+    output = by_tokens(got[5:], low)
+
+    widths = [slots, KVH * HD, KVH * HD, EXTRA]
+    cuts = [sum(widths[: k + 1]) for k in range(4)]
+    query_weight_grad, key_weight_grad, value_weight_grad, extra, output_grad = jnp.split(
+        projection, cuts, axis=1
+    )
+    output_grad = output_grad.reshape(groups, rows, -1)[:, :heads_here].reshape(QH * HD, -1)
     output_weight_grad = mm(select, output_grad)
-    input_gradient = swap(by_feature(input_gradient), "mp")
-    gate_weight_grad, up_weight_grad, down_weight_grad = widen(wide_grad, down_grad)
-    output = by_tokens(output, low)
-    got = order(
-        projection, gate_weight_grad, up_weight_grad, down_weight_grad, output,
-        output_weight_grad, *input_gradient
-    )
-    projection, gate_weight_grad, up_weight_grad, down_weight_grad, output = got[:5]
-    output_weight_grad = got[5]
-    input_gradient = by_tokens(got[6:], full)
-
-    widths = [slots, KVH * HD, KVH * HD, EXTRA]
-    cuts = [sum(widths[: k + 1]) for k in range(3)]
-    query_weight_grad, key_weight_grad, value_weight_grad, extra = jnp.split(
-        projection, cuts, axis=1
-    )
     extra = extra.astype(full)
     own_share = lax.dynamic_slice_in_dim(extra, rank * share, share, 0)
     return (

time: 897 us -> 864 us (0.963)
  other arithmetic: 155 us -> 108 us
  Pallas kernels: 63.6 us -> 93 us
  local copies, waits for them, and re-layouts: 98.9 us -> 83.4 us
  waiting for transfers between devices: 314 us -> 304 us
    pallas_call x0 -> x5, Pallas kernels: none -> 31.1 us  [the longest x4 27.8 us: chip_sums(): pl.pallas_call(kernel, out_shape=[jax.ShapeDtypeStruct((len(places) * hal...]
    convert_element_type x11 -> x10, other arithmetic: 41.5 us -> 20.3 us  [added(): return sum((term.astype(full) for term in terms)).astype(low)]
    ppermute x25 -> x32, waiting for transfers between devices: 109 us -> 89.2 us  [exchange(): return lax.ppermute(array, axis, [(i, i ^ mask) for i in range(n)])]
    ppermute x21, waiting for transfers between devices: 148 us -> 163 us  [swap(): lax.ppermute(pieces[k], axis, [(i, i ^ k) for i in range(n)])]
    ppermute x25 -> x32, starting transfers between devices: 22.2 us -> 31.3 us  [exchange(): return lax.ppermute(array, axis, [(i, i ^ mask) for i in range(n)])]
    unnamed x249 -> x291, local copies, waits for them, and re-layouts: 35.6 us -> 32.3 us
    dot_general x7 -> x8, matrix products: 60.3 us -> 62.4 us  [mm(): return jnp.dot(left, right, preferred_element_type=full)]
  transfers between devices with their start and end apart: 61 -> 65, of which waited for: 31 -> 39; matrix products, arithmetic and copies ran while one was open for 36% -> 31% of each run, Pallas kernels for 7% -> 10%
where the time goes in v3:
time: 864 us; the launch traced here: 857 us
  waiting for transfers between devices  304 us (35%)
  matrix products  178 us (21%)
  other arithmetic  108 us (12%)
  Pallas kernels  93 us (11%)
  local copies, waits for them, and re-layouts  83.4 us (10%)
  starting transfers between devices  74.4 us (9%)
  between operations  16.7 us (2%)
    ppermute x21, waiting for transfers between devices, swap(): lax.ppermute(pieces[k], axis, [(i, i ^ k) for i in range(n)])  163 us
    dot_general x20, matrix products, dot(): lax.dot_general(left, right, (((left_axis,), (right_axis,)), ((), ())), p...  115 us
    ppermute x32, waiting for transfers between devices, exchange(): return lax.ppermute(array, axis, [(i, i ^ mask) for i in range(n)])  89.2 us
    dot_general x8, matrix products, mm(): return jnp.dot(left, right, preferred_element_type=full)  62.4 us
    ppermute x3, waiting for transfers between devices, send(): lax.ppermute(up, self.axis, right)  50.1 us
    pallas_call x1, Pallas kernels, attend_back(): pl.pallas_call(attend_back_kernel, out_shape=(jax.ShapeDtypeStruct((QH, H...  32.5 us
    unnamed x291, local copies, waits for them, and re-layouts  32.3 us
    ppermute x32, starting transfers between devices, exchange(): return lax.ppermute(array, axis, [(i, i ^ mask) for i in range(n)])  31.3 us
  transfers between devices with their start and end apart: 65, of which 39 were waited for; matrix products, arithmetic and copies ran while one was open for 31% of the time, Pallas kernels for 10%

profile of v3, /device:TPU:16, one launch (start us, length us, event | category | flops | bytes accessed | tf_op | source)
XLA Modules:
  0.0 857.1 jit_solution(159672715780458660)
XLA Ops:
  13.1 3.5 constant_dynamic-slice_fusion.10
  27.2 3.6 iota_compare_fusion
  43.5 8.0 collective-permute-done.4
  59.0 3.3 collective-permute-start.6
  63.9 14.8 %collective-permute-done.6 = bf16[160,512]{1,0:T(8,128)(2,1)S(1)} collective-permute-done((bf16[160,512]{1,0:T(8,128)(2,1)S(1)}, bf16[160,512]{1,0:T(8,128)(2,1)S(1)}, u32[]{:S(2)}, u32[]{:S(2)}) %collective-permute-start.6) | collective-permute-done | bytes 163872 | tf_op jit(solution)/shard_map/ppermute | solution.py:36
  78.7 13.9 %collective-permute-done.7 = bf16[160,512]{1,0:T(8,128)(2,1)S(1)} collective-permute-done((bf16[160,512]{1,0:T(8,128)(2,1)S(1)}, bf16[160,512]{1,0:T(8,128)(2,1)S(1)}, u32[]{:S(2)}, u32[]{:S(2)}) %collective-permute-start.7) | collective-permute-done | bytes 163872 | tf_op jit(solution)/shard_map/ppermute | solution.py:36
  107.8 5.5 fusion.86
  116.6 6.0 collective-permute-done.9
  127.9 20.8 %shard_map.246 = (bf16[20,64,512]{2,1,0:T(8,128)(2,1)S(1)}, f32[5,4,512]{2,1,0:T(4,128)S(1)}) custom-call(s32[2]{0:T(128)S(1)} %pad_add_fusion.2.starts, bf16[20,64,512]{2,1,0:T(8,128)(2,1)S(1)} %fusion.21.q_ref, bf16[5,64,1024]{2,1,0:T(8,128)(2,1)S(1)} %get-tuple-element.490.k_ref, bf16[5,64,1024]{2,1,0:T(8,128)(2,1)S(1)} %get-tuple-element.489.v_ref), custom_call_target="tpu_custom_call" | custom-call | flops 7864320 | bytes 1048576 | tf_op jit(solution)/shard_map/pallas_call | solution.py:363
  150.5 5.8 multiply_reduce_fusion
  160.8 7.9 collective-permute-done.12
  173.5 3.9 collective-permute-start.16
  185.8 19.3 %collective-permute-done.15 = bf16[2048,384]{0,1:T(8,128)(2,1)} collective-permute-done((bf16[2048,384]{0,1:T(8,128)(2,1)S(1)}, bf16[2048,384]{0,1:T(8,128)(2,1)}, u32[]{:S(2)}, u32[]{:S(2)}) %collective-permute-start.15) | collective-permute-done | bytes 1572896 | tf_op jit(solution)/shard_map/ppermute | solution.py:80
  207.0 5.3 collective-permute-done.13
  215.4 6.3 collective-permute-start.20
  221.6 4.5 broadcast_in_dim.51
  226.1 3.2 bitcast_dynamic-update-slice_fusion.2
  233.9 3.2 bitcast_dynamic-update-slice_fusion.1
  237.1 3.2 bitcast_dynamic-update-slice_fusion
  240.3 9.4 %collective-permute-done.17 = bf16[256,2048]{1,0:T(8,128)(2,1)S(1)} collective-permute-done((bf16[256,2048]{1,0:T(8,128)(2,1)S(1)}, bf16[256,2048]{1,0:T(8,128)(2,1)S(1)}, u32[]{:S(2)}, u32[]{:S(2)}) %collective-permute-start.17) | collective-permute-done | bytes 1048608 | tf_op jit(solution)/shard_map/ppermute | solution.py:50
  261.0 30.9 %collective-permute-done.22 = bf16[2048,384]{0,1:T(8,128)(2,1)S(1)} collective-permute-done((bf16[2048,384]{0,1:T(8,128)(2,1)}, bf16[2048,384]{0,1:T(8,128)(2,1)S(1)}, u32[]{:S(2)}, u32[]{:S(2)}) %collective-permute-start.22) | collective-permute-done | bytes 1572896 | tf_op jit(solution)/shard_map/ppermute | solution.py:80
  291.9 3.3 add.513
  298.4 12.8 %fusion.88 = f32[2048,1024]{1,0:T(8,128)S(1)} fusion(bf16[2048,2048]{1,0:T(8,128)(2,1)} %copy-done.127, bf16[2048,1024]{0,1:T(8,128)(2,1)S(1)} %get-tuple-element.482), kind=kOutput, calls=%fused_computation.400 | convolution fusion | flops 8589934592 | bytes 20971520 | tf_op jit(solution)/shard_map/dot_general | solution.py:276
  311.2 3.3 copy-done.41
  315.9 12.1 %fusion.87 = f32[2048,1024]{1,0:T(8,128)S(1)} fusion(bf16[2048,2048]{1,0:T(8,128)(2,1)} %bitcast.31, bf16[2048,1024]{0,1:T(8,128)(2,1)S(1)} %get-tuple-element.482), kind=kOutput, calls=%fused_computation.399 | convolution fusion | flops 8589934592 | bytes 20971520 | tf_op jit(solution)/shard_map/dot_general | solution.py:276
  331.3 7.1 convolution_convert_fusion.2
  338.4 6.7 convolution_convert_fusion.3.mine_ref
  345.1 9.4 %constant_dynamic-slice_fusion.6 = (bf16[4,1,512,2048]{3,2,1,0:T(8,128)(2,1)}, bf16[4,1,512,2048]{3,2,1,0:T(8,128)(2,1)S(1)}) fusion(bf16[4,2,512,2048]{3,2,1,0:T(8,128)(2,1)} %bitcast.115, s32[]{:T(128)S(6)} %select_n.642, s32[]{:T(128)S(6)} %select_n.643), kind=kLoop, calls=%fused_computation.310 | loop fusion | bytes 33554440 | tf_op jit(solution)/shard_map/jit(dynamic_index_in_dim)/dynamic_slice | solution.py:664
  354.5 12.5 %multiply_convert_fusion.3 = (bf16[2048,512]{1,0:T(8,128)(2,1)S(1)}, bf16[2048,512]{1,0:T(8,128)(2,1)S(1)}) fusion(f32[2048,1024]{1,0:T(8,128)} %copy-done.41, bf16[2048,2048]{1,0:T(8,128)(2,1)S(1)} %bitcast.128, bf16[2048,128]{0,1:T(8,128)(2,1)S(1)} %get-tuple-element.481, bf16[2048,128]{0,1:T(8,128)(2,1)S(1)} %get-tuple-element.479, ...), kind=kOutput, calls=%fused_computation.50 | convolution fusion | flops 4316987392 | bytes 23068672 | tf_op jit(solution)/shard_map/dot_general | solution.py:276
  370.8 10.8 %convolution_convert_fusion.1 = bf16[2048,2048]{1,0:T(8,128)(2,1)} fusion(bf16[2048,1024]{0,1:T(8,128)(2,1)S(1)} %copy-done.114, bf16[2048,512]{1,0:T(8,128)(2,1)S(1)} %get-tuple-element.410, bf16[2048,512]{1,0:T(8,128)(2,1)S(1)} %get-tuple-element.409), kind=kOutput, calls=%fused_computation.16 | convolution fusion | flops 8602517504 | bytes 16777216 | tf_op jit(solution)/shard_map/dot_general | solution.py:28
  382.3 11.9 %multiply_convert_fusion.1 = (bf16[2048,512]{1,0:T(8,128)(2,1)S(1)}, bf16[2048,512]{1,0:T(8,128)(2,1)S(1)}) fusion(f32[2048,1024]{1,0:T(8,128)} %copy-done.40, bf16[2048,2048]{1,0:T(8,128)(2,1)} %bitcast.124, bf16[2048,128]{0,1:T(8,128)(2,1)S(1)} %get-tuple-element.481, bf16[2048,128]{0,1:T(8,128)(2,1)S(1)} %get-tuple-element.479, ...), kind=kOutput, calls=%fused_computation.47 | convolution fusion | flops 4316987392 | bytes 23068672 | tf_op jit(solution)/shard_map/dot_general | solution.py:276
  394.2 10.8 %convolution_convert_fusion.mine_ref = bf16[2048,2048]{1,0:T(8,128)(2,1)} fusion(bf16[2048,1024]{0,1:T(8,128)(2,1)S(1)} %copy-done.115, bf16[2048,512]{1,0:T(8,128)(2,1)S(1)} %get-tuple-element.408, bf16[2048,512]{1,0:T(8,128)(2,1)S(1)} %get-tuple-element.407), kind=kOutput, calls=%fused_computation.15 | convolution fusion | flops 8602517504 | bytes 16777216 | tf_op jit(solution)/shard_map/dot_general | solution.py:28
  405.6 10.7 %shard_map.247 = (bf16[512,2048]{1,0:T(8,128)(2,1)S(1)}, bf16[512,2048]{1,0:T(8,128)(2,1)S(1)}, bf16[1024,2048]{1,0:T(8,128)(2,1)S(1)}) custom-call(s32[8]{0:T(128)S(1)} %stack.97.index_ref, bf16[2048,2048]{1,0:T(8,128)(2,1)} %convolution_convert_fusion.mine_ref, bf16[2048,2048]{1,0:T(8,128)(2,1)} %collective-permute-done.24.got_ref), custom_call_target="tpu_custom_call" | custom-call | bytes 65536 | tf_op jit(solution)/shard_map/pallas_call | solution.py:170
  418.2 8.3 fusion.89
  426.5 6.5 add_convert_fusion.4.down_ref
  433.0 13.5 %fusion.90 = f32[2048,1024]{1,0:T(8,128)} fusion(bf16[2048,2048]{1,0:T(8,128)(2,1)} %copy-done.127, bf16[2048,1024]{1,0:T(8,128)(2,1)S(1)} %copy-done.53), kind=kOutput, calls=%fused_computation.402 | convolution fusion | flops 8589934592 | bytes 20971520 | tf_op jit(solution)/shard_map/dot_general | solution.py:28
  446.5 12.7 %add_convert_fusion.2.gate_ref.up_ref = bf16[2048,1024]{1,0:T(8,128)(2,1)S(1)} fusion(f32[2048,1024]{1,0:T(8,128)} %fusion.90, bf16[2048,2048]{1,0:T(8,128)(2,1)} %bitcast.31, bf16[2048,1024]{1,0:T(8,128)(2,1)S(1)} %pad_maximum_fusion.1), kind=kOutput, calls=%fused_computation.6 | convolution fusion | flops 8594128896 | bytes 25165824 | tf_op jit(solution)/shard_map/dot_general | solution.py:28
  459.2 5.0 collective-permute-done.25
  464.9 3.2 shard_map.250
  470.9 4.0 add_convert_fusion.11
  477.0 11.9 %shard_map.248 = (bf16[256,2048]{1,0:T(8,128)(2,1)S(1)}, bf16[256,2048]{1,0:T(8,128)(2,1)S(1)}, bf16[256,2048]{1,0:T(8,128)(2,1)S(1)}, bf16[256,2048]{1,0:T(8,128)(2,1)S(1)}, bf16[1024,2048]{1,0:T(8,128)(2,1)S(1)}) custom-call(s32[8]{0:T(128)S(1)} %stack.98.index_ref, bf16[2048,2048]{1,0:T(8,128)(2,1)} %convolution_convert_fusion.3.mine_ref, ...), custom_call_target="tpu_custom_call" | custom-call | bytes 65536 | tf_op jit(solution)/shard_map/pallas_call | solution.py:170
  489.0 10.2 %collective-permute-done.28 = bf16[256,2048]{1,0:T(8,128)(2,1)} collective-permute-done((bf16[256,2048]{1,0:T(8,128)(2,1)}, bf16[256,2048]{1,0:T(8,128)(2,1)}, u32[]{:S(2)}, u32[]{:S(2)}) %collective-permute-start.28) | collective-permute-done | bytes 1048608 | tf_op jit(solution)/shard_map/ppermute | solution.py:50
  499.4 3.6 add_convert_fusion.10
  512.8 5.4 convolution_convert_fusion.6
  518.3 32.5 %shard_map.249 = (f32[20,64,512]{2,1,0:T(8,128)S(1)}, f32[5,64,1024]{2,1,0:T(8,128)S(1)}, f32[5,64,1024]{2,1,0:T(8,128)S(1)}) custom-call(s32[2]{0:T(128)S(1)} %copy-done.15, bf16[20,64,512]{2,1,0:T(8,128)(2,1)S(1)} %copy-done.4, bf16[5,64,1024]{2,1,0:T(8,128)(2,1)S(1)} %copy-done.8, bf16[5,64,1024]{2,1,0:T(8,128)(2,1)S(1)} %copy-done.6, ...), custom_call_target="tpu_custom_call" | custom-call | flops 7864320 | bytes 1048576 | tf_op jit(solution)/shard_map/pallas_call | solution.py:386
  571.0 5.4 collective-permute-done.36
  577.2 18.0 %collective-permute-done.33 = bf16[10,64,512]{2,1,0:T(8,128)(2,1)S(1)} collective-permute-done((bf16[10,64,512]{2,1,0:T(8,128)(2,1)S(1)}, bf16[10,64,512]{2,1,0:T(8,128)(2,1)S(1)}, u32[]{:S(2)}, u32[]{:S(2)}) %collective-permute-start.33) | collective-permute-done | bytes 655392 | tf_op jit(solution)/shard_map/ppermute | solution.py:50
  604.8 5.7 add_convert_fusion.1
  614.1 5.1 fusion.25
  639.3 17.5 %collective-permute-done.41 = bf16[512,512]{1,0:T(8,128)(2,1)S(1)} collective-permute-done((bf16[512,512]{1,0:T(8,128)(2,1)S(1)}, bf16[512,512]{1,0:T(8,128)(2,1)S(1)}, u32[]{:S(2)}, u32[]{:S(2)}) %collective-permute-start.41) | collective-permute-done | bytes 524320 | tf_op jit(solution)/shard_map/ppermute | solution.py:36
  656.8 15.2 %collective-permute-done.42 = bf16[512,512]{1,0:T(8,128)(2,1)S(1)} collective-permute-done((bf16[512,512]{1,0:T(8,128)(2,1)S(1)}, bf16[512,512]{1,0:T(8,128)(2,1)S(1)}, u32[]{:S(2)}, u32[]{:S(2)}) %collective-permute-start.42) | collective-permute-done | bytes 524320 | tf_op jit(solution)/shard_map/ppermute | solution.py:36
  672.0 11.1 %collective-permute-done.43 = bf16[512,512]{1,0:T(8,128)(2,1)S(1)} collective-permute-done((bf16[512,512]{1,0:T(8,128)(2,1)S(1)}, bf16[512,512]{1,0:T(8,128)(2,1)S(1)}, u32[]{:S(2)}, u32[]{:S(2)}) %collective-permute-start.43) | collective-permute-done | bytes 524320 | tf_op jit(solution)/shard_map/ppermute | solution.py:36
  692.1 3.5 collective-permute-done.46
  715.8 9.2 %collective-permute-done.54 = bf16[256,2048]{1,0:T(8,128)(2,1)S(1)} collective-permute-done((bf16[256,2048]{1,0:T(8,128)(2,1)S(1)}, bf16[256,2048]{1,0:T(8,128)(2,1)S(1)}, u32[]{:S(2)}, u32[]{:S(2)}) %collective-permute-start.54) | collective-permute-done | bytes 1048608 | tf_op jit(solution)/shard_map/ppermute | solution.py:50
  725.9 7.5 collective-permute-done.51
  733.4 19.0 %collective-permute-done.52 = bf16[256,1152]{1,0:T(8,128)(2,1)S(1)} collective-permute-done((bf16[256,1152]{1,0:T(8,128)(2,1)S(1)}, bf16[256,1152]{1,0:T(8,128)(2,1)S(1)}, u32[]{:S(2)}, u32[]{:S(2)}) %collective-permute-start.52) | collective-permute-done | bytes 589856 | tf_op jit(solution)/shard_map/ppermute | solution.py:36
  753.2 11.0 %collective-permute-done.53 = bf16[256,1152]{1,0:T(8,128)(2,1)} collective-permute-done((bf16[256,1152]{1,0:T(8,128)(2,1)S(1)}, bf16[256,1152]{1,0:T(8,128)(2,1)}, u32[]{:S(2)}, u32[]{:S(2)}) %collective-permute-start.53) | collective-permute-done | bytes 589856 | tf_op jit(solution)/shard_map/ppermute | solution.py:36
  780.8 8.6 %shard_map.253 = (f32[2048,1024]{1,0:T(8,128)}, f32[2048,1024]{1,0:T(8,128)}, f32[1024,2048]{1,0:T(8,128)}) custom-call(bf16[8,2048,384]{2,1,0:T(8,128)(2,1)S(1)} %bitcast.106), custom_call_target="tpu_custom_call" | custom-call | bytes 65536 | tf_op jit(solution)/shard_map/pallas_call | solution.py:458
  792.5 18.4 %collective-permute-done.57 = bf16[512,512]{1,0:T(8,128)(2,1)} collective-permute-done((bf16[512,512]{1,0:T(8,128)(2,1)S(1)}, bf16[512,512]{1,0:T(8,128)(2,1)}, u32[]{:S(2)}, u32[]{:S(2)}) %collective-permute-start.57) | collective-permute-done | bytes 524320 | tf_op jit(solution)/shard_map/ppermute | solution.py:36
  810.9 9.8 %collective-permute-done.58 = bf16[512,512]{1,0:T(8,128)(2,1)} collective-permute-done((bf16[512,512]{1,0:T(8,128)(2,1)S(1)}, bf16[512,512]{1,0:T(8,128)(2,1)}, u32[]{:S(2)}, u32[]{:S(2)}) %collective-permute-start.58) | collective-permute-done | bytes 524320 | tf_op jit(solution)/shard_map/ppermute | solution.py:36
  820.7 5.6 slice_convert_fusion
  835.3 3.4 copy.62
  838.7 3.4 copy.63
  842.7 6.5 fusion.91
  (584 shorter events, 246.2 us)
Async XLA Ops:
  7.2 100.6 %all-gather.7.cloned.1.call-start = ((), (), s32[]{:S(2)}) async-start(), calls=%async_computation.1 | async-start | bytes 5898240 | tf_op jit(solution)/shard_map/all_gather | solution.py:572
  9.6 33.9 %collective-permute-start = (bf16[264,384]{1,0:T(8,128)(2,1)}, bf16[264,384]{1,0:T(8,128)(2,1)}, u32[]{:S(2)}, u32[]{:S(2)}) collective-permute-start(bf16[264,384]{1,0:T(8,128)(2,1)} %pad_maximum_fusion.32), channel_id=1, source_target_pairs={{0,1},{1,0},{2,3},{3,2},{4,5},{5,4},{6,7},{7,6},{8,9},{9,8},{10,11... | collective-permute-start | bytes 608264 | tf_op jit(solution)/shard_map/ppermute | solution.py:36
  11.1 32.3 %collective-permute-start.1 = (bf16[264,384]{1,0:T(8,128)(2,1)}, bf16[264,384]{1,0:T(8,128)(2,1)}, u32[]{:S(2)}, u32[]{:S(2)}) collective-permute-start(bf16[264,384]{1,0:T(8,128)(2,1)} %pad_maximum_fusion.32), channel_id=1, source_target_pairs={{0,2},{1,3},{2,0},{3,1},{4,6},{5,7},{6,4},{7,5},{8,10},{9,11},{10,... | collective-permute-start | bytes 608264 | tf_op jit(solution)/shard_map/ppermute | solution.py:36
  11.5 32.0 %collective-permute-start.2 = (bf16[264,384]{1,0:T(8,128)(2,1)}, bf16[264,384]{1,0:T(8,128)(2,1)}, u32[]{:S(2)}, u32[]{:S(2)}) collective-permute-start(bf16[264,384]{1,0:T(8,128)(2,1)} %pad_maximum_fusion.32), channel_id=1, source_target_pairs={{0,3},{1,2},{2,1},{3,0},{4,7},{5,6},{6,5},{7,4},{8,11},{9,10},{10,... | collective-permute-start | bytes 608264 | tf_op jit(solution)/shard_map/ppermute | solution.py:36
  17.4 26.1 %collective-permute-start.3 = (bf16[512,512]{1,0:T(8,128)(2,1)}, bf16[512,512]{1,0:T(8,128)(2,1)}, u32[]{:S(2)}, u32[]{:S(2)}) collective-permute-start(bf16[512,512]{1,0:T(8,128)(2,1)} %pad_maximum_fusion.30), channel_id=1, source_target_pairs={{0,1},{1,0},{2,3},{3,2},{4,5},{5,4},{6,7},{7,6},{8,9},{9,8},{10,11... | collective-permute-start | bytes 1572872 | tf_op jit(solution)/shard_map/ppermute | solution.py:50
  20.7 30.8 %collective-permute-start.4 = (bf16[512,512]{1,0:T(8,128)(2,1)}, bf16[512,512]{1,0:T(8,128)(2,1)}, u32[]{:S(2)}, u32[]{:S(2)}) collective-permute-start(bf16[512,512]{1,0:T(8,128)(2,1)} %pad_maximum_fusion.31), channel_id=1, source_target_pairs={{0,2},{1,3},{2,0},{3,1},{4,6},{5,7},{6,4},{7,5},{8,10},{9,11},{10,... | collective-permute-start | bytes 1572872 | tf_op jit(solution)/shard_map/ppermute | solution.py:50
  57.4 93.1 %all-gather.9.cloned.1.call-start = ((), (), s32[]{:S(2)}) async-start(), calls=%async_computation.2 | async-start | bytes 5898240 | tf_op jit(solution)/shard_map/all_gather | solution.py:587
  57.4 37.9 %collective-permute-start.5 = (bf16[512,512]{1,0:T(8,128)(2,1)S(1)}, bf16[512,512]{1,0:T(8,128)(2,1)}, u32[]{:S(2)}, u32[]{:S(2)}) collective-permute-start(bf16[512,512]{1,0:T(8,128)(2,1)S(1)} %pad_maximum_fusion.24), channel_id=1, source_target_pairs={{0,3},{1,2},{2,1},{3,0},{4,7},{5,6},{6,5},{7,4},{8,11},{9,10},{10,... | collective-permute-start | bytes 1572872 | tf_op jit(solution)/shard_map/ppermute | solution.py:50
  59.0 19.7 %collective-permute-start.6 = (bf16[160,512]{1,0:T(8,128)(2,1)S(1)}, bf16[160,512]{1,0:T(8,128)(2,1)S(1)}, u32[]{:S(2)}, u32[]{:S(2)}) collective-permute-start(bf16[160,512]{1,0:T(8,128)(2,1)S(1)} %fusion.27), channel_id=1, source_target_pairs={{0,1},{1,0},{2,3},{3,2},{4,5},{5,4},{6,7},{7,6},{8,9},{9,8},{10,11... | collective-permute-start | bytes 491528 | tf_op jit(solution)/shard_map/ppermute | solution.py:36
  62.3 30.3 %collective-permute-start.7 = (bf16[160,512]{1,0:T(8,128)(2,1)S(1)}, bf16[160,512]{1,0:T(8,128)(2,1)S(1)}, u32[]{:S(2)}, u32[]{:S(2)}) collective-permute-start(bf16[160,512]{1,0:T(8,128)(2,1)S(1)} %fusion.27), channel_id=1, source_target_pairs={{0,2},{1,3},{2,0},{3,1},{4,6},{5,7},{6,4},{7,5},{8,10},{9,11},{10,... | collective-permute-start | bytes 491528 | tf_op jit(solution)/shard_map/ppermute | solution.py:36
  63.3 32.0 %collective-permute-start.8 = (bf16[160,512]{1,0:T(8,128)(2,1)S(1)}, bf16[160,512]{1,0:T(8,128)(2,1)S(1)}, u32[]{:S(2)}, u32[]{:S(2)}) collective-permute-start(bf16[160,512]{1,0:T(8,128)(2,1)S(1)} %fusion.27), channel_id=1, source_target_pairs={{0,3},{1,2},{2,1},{3,0},{4,7},{5,6},{6,5},{7,4},{8,11},{9,10},{10,... | collective-permute-start | bytes 491528 | tf_op jit(solution)/shard_map/ppermute | solution.py:36
  96.3 248.8 %all-gather.11.cloned.1.call-start = ((), (), s32[]{:S(2)}) async-start(), calls=%async_computation.3 | async-start | bytes 18874368 | tf_op jit(solution)/shard_map/all_gather | solution.py:639
  107.7 14.9 %collective-permute-start.9 = (bf16[10,64,512]{2,1,0:T(8,128)(2,1)}, bf16[10,64,512]{2,1,0:T(8,128)(2,1)}, u32[]{:S(2)}, u32[]{:S(2)}) collective-permute-start(bf16[10,64,512]{2,1,0:T(8,128)(2,1)} %pad_maximum_fusion.21), channel_id=1, source_target_pairs={{0,1},{1,0},{2,3},{3,2},{4,5},{5,4},{6,7},{7,6},{8,9},{9,8},{10,11... | collective-permute-start | bytes 1966088 | tf_op jit(solution)/shard_map/ppermute | solution.py:50
  122.6 36.3 %collective-permute-start.10 = (bf16[512,512]{1,0:T(8,128)(2,1)}, bf16[512,512]{1,0:T(8,128)(2,1)}, u32[]{:S(2)}, u32[]{:S(2)}) collective-permute-start(bf16[512,512]{1,0:T(8,128)(2,1)} %pad_maximum_fusion.26), channel_id=1, source_target_pairs={{0,1},{1,0},{2,3},{3,2},{4,5},{5,4},{6,7},{7,6},{8,9},{9,8},{10,11... | collective-permute-start | bytes 1572872 | tf_op jit(solution)/shard_map/ppermute | solution.py:36
  122.9 37.9 %collective-permute-start.11 = (bf16[512,512]{1,0:T(8,128)(2,1)}, bf16[512,512]{1,0:T(8,128)(2,1)}, u32[]{:S(2)}, u32[]{:S(2)}) collective-permute-start(bf16[512,512]{1,0:T(8,128)(2,1)} %pad_maximum_fusion.27), channel_id=1, source_target_pairs={{0,2},{1,3},{2,0},{3,1},{4,6},{5,7},{6,4},{7,5},{8,10},{9,11},{10,... | collective-permute-start | bytes 1572872 | tf_op jit(solution)/shard_map/ppermute | solution.py:36
  125.6 43.1 %collective-permute-start.12 = (bf16[512,512]{1,0:T(8,128)(2,1)}, bf16[512,512]{1,0:T(8,128)(2,1)}, u32[]{:S(2)}, u32[]{:S(2)}) collective-permute-start(bf16[512,512]{1,0:T(8,128)(2,1)} %pad_maximum_fusion.28), channel_id=1, source_target_pairs={{0,3},{1,2},{2,1},{3,0},{4,7},{5,6},{6,5},{7,4},{8,11},{9,10},{10,... | collective-permute-start | bytes 1572872 | tf_op jit(solution)/shard_map/ppermute | solution.py:36
  168.7 43.6 %collective-permute-start.13 = (bf16[512,2048]{1,0:T(8,128)(2,1)}, bf16[512,2048]{1,0:T(8,128)(2,1)}, u32[]{:S(2)}, u32[]{:S(2)}) collective-permute-start(bf16[512,2048]{1,0:T(8,128)(2,1)} %multiply_convert_fusion.4), channel_id=1, source_target_pairs={{0,8},{4,12},{8,0},{12,4},{16,24},{20,28},{24,16},{28,20},{1,9},{5... | collective-permute-start | bytes 6291464 | tf_op jit(solution)/shard_map/ppermute | solution.py:50
  170.1 43.3 %collective-permute-start.14 = (bf16[512,2048]{1,0:T(8,128)(2,1)}, bf16[512,2048]{1,0:T(8,128)(2,1)}, u32[]{:S(2)}, u32[]{:S(2)}) collective-permute-start(bf16[512,2048]{1,0:T(8,128)(2,1)} %multiply_convert_fusion.4), channel_id=1, source_target_pairs={{0,16},{4,20},{8,24},{12,28},{16,0},{20,4},{24,8},{28,12},{1,17},{... | collective-permute-start | bytes 6291464 | tf_op jit(solution)/shard_map/ppermute | solution.py:50
  171.6 33.5 %collective-permute-start.15 = (bf16[2048,384]{0,1:T(8,128)(2,1)S(1)}, bf16[2048,384]{0,1:T(8,128)(2,1)}, u32[]{:S(2)}, u32[]{:S(2)}) collective-permute-start(bf16[2048,384]{0,1:T(8,128)(2,1)S(1)} %copy-done.44), channel_id=1, source_target_pairs={{0,1},{1,2},{2,3},{4,5},{5,6},{6,7},{8,9},{9,10},{10,11},{12,13},{... | collective-permute-start | bytes 4718600 | tf_op jit(solution)/shard_map/ppermute | solution.py:80
  173.5 33.5 %collective-permute-start.16 = (bf16[2048,384]{0,1:T(8,128)(2,1)S(1)}, bf16[2048,384]{0,1:T(8,128)(2,1)}, u32[]{:S(2)}, u32[]{:S(2)}) collective-permute-start(bf16[2048,384]{0,1:T(8,128)(2,1)S(1)} %copy-done.44), channel_id=1, source_target_pairs={{3,2},{2,1},{1,0},{7,6},{6,5},{5,4},{11,10},{10,9},{9,8},{15,14},{... | collective-permute-start | bytes 4718600 | tf_op jit(solution)/shard_map/ppermute | solution.py:80
  213.4 38.9 %collective-permute-start.19 = (bf16[2048,384]{0,1:T(8,128)(2,1)}, bf16[2048,384]{0,1:T(8,128)(2,1)}, u32[]{:S(2)}, u32[]{:S(2)}) collective-permute-start(bf16[2048,384]{0,1:T(8,128)(2,1)} %collective-permute-done.15), channel_id=1, source_target_pairs={{1,2},{2,3},{5,6},{6,7},{9,10},{10,11},{13,14},{14,15},{17,18},{18... | collective-permute-start | bytes 4718600 | tf_op jit(solution)/shard_map/ppermute | solution.py:80
  215.4 36.9 %collective-permute-start.20 = (bf16[2048,384]{0,1:T(8,128)(2,1)}, bf16[2048,384]{0,1:T(8,128)(2,1)}, u32[]{:S(2)}, u32[]{:S(2)}) collective-permute-start(bf16[2048,384]{0,1:T(8,128)(2,1)} %collective-permute-done.16), channel_id=1, source_target_pairs={{2,1},{1,0},{6,5},{5,4},{10,9},{9,8},{14,13},{13,12},{18,17},{17,1... | collective-permute-start | bytes 4718600 | tf_op jit(solution)/shard_map/ppermute | solution.py:80
  230.6 19.1 %collective-permute-start.17 = (bf16[256,2048]{1,0:T(8,128)(2,1)S(1)}, bf16[256,2048]{1,0:T(8,128)(2,1)S(1)}, u32[]{:S(2)}, u32[]{:S(2)}) collective-permute-start(bf16[256,2048]{1,0:T(8,128)(2,1)S(1)} %slice.424), channel_id=1, source_target_pairs={{0,16},{4,20},{8,24},{12,28},{16,0},{20,4},{24,8},{28,12},{1,17},{... | collective-permute-start | bytes 3145736 | tf_op jit(solution)/shard_map/ppermute | solution.py:50
  233.4 18.9 %collective-permute-start.18 = (bf16[256,2048]{1,0:T(8,128)(2,1)S(1)}, bf16[256,2048]{1,0:T(8,128)(2,1)}, u32[]{:S(2)}, u32[]{:S(2)}) collective-permute-start(bf16[256,2048]{1,0:T(8,128)(2,1)S(1)} %slice.425), channel_id=1, source_target_pairs={{0,8},{4,12},{8,0},{12,4},{16,24},{20,28},{24,16},{28,20},{1,9},{5... | collective-permute-start | bytes 3145736 | tf_op jit(solution)/shard_map/ppermute | solution.py:50
  252.3 346.9 %reduce-scatter.2.cloned.1.call-start = ((), (), s32[]{:S(2)}) async-start(), calls=%async_computation.4 | async-start | bytes 7864320 | tf_op jit(solution)/shard_map/reduce_scatter | solution.py:697
  255.7 36.2 %collective-permute-start.21 = (bf16[2048,2048]{1,0:T(8,128)(2,1)}, bf16[2048,2048]{1,0:T(8,128)(2,1)S(1)}, u32[]{:S(2)}, u32[]{:S(2)}) collective-permute-start(bf16[2048,2048]{1,0:T(8,128)(2,1)} %bitcast.31), channel_id=1, source_target_pairs={{0,4},{4,0},{8,12},{12,8},{16,20},{20,16},{24,28},{28,24},{1,5},{5... | collective-permute-start | bytes 25165832 | tf_op jit(solution)/shard_map/ppermute | solution.py:50
  255.7 36.2 %collective-permute-start.22 = (bf16[2048,384]{0,1:T(8,128)(2,1)}, bf16[2048,384]{0,1:T(8,128)(2,1)S(1)}, u32[]{:S(2)}, u32[]{:S(2)}) collective-permute-start(bf16[2048,384]{0,1:T(8,128)(2,1)} %collective-permute-done.19), channel_id=1, source_target_pairs={{2,3},{6,7},{10,11},{14,15},{18,19},{22,23},{26,27},{30,31}} | collective-permute-start | bytes 4718600 | tf_op jit(solution)/shard_map/ppermute | solution.py:80
  257.1 34.8 %collective-permute-start.23 = (bf16[2048,384]{0,1:T(8,128)(2,1)}, bf16[2048,384]{0,1:T(8,128)(2,1)S(1)}, u32[]{:S(2)}, u32[]{:S(2)}) collective-permute-start(bf16[2048,384]{0,1:T(8,128)(2,1)} %collective-permute-done.20), channel_id=1, source_target_pairs={{1,0},{5,4},{9,8},{13,12},{17,16},{21,20},{25,24},{29,28}} | collective-permute-start | bytes 4718600 | tf_op jit(solution)/shard_map/ppermute | solution.py:80
  381.6 24.0 %collective-permute-start.24 = (bf16[2048,2048]{1,0:T(8,128)(2,1)}, bf16[2048,2048]{1,0:T(8,128)(2,1)}, u32[]{:S(2)}, u32[]{:S(2)}) collective-permute-start(bf16[2048,2048]{1,0:T(8,128)(2,1)} %convolution_convert_fusion.1), channel_id=1, source_target_pairs={{0,4},{4,0},{8,12},{12,8},{16,20},{20,16},{24,28},{28,24},{1,5},{5... | collective-permute-start | bytes 25165832 | tf_op jit(solution)/shard_map/ppermute | solution.py:50
  381.9 77.3 %collective-permute-start.27 = (bf16[2048,2048]{1,0:T(8,128)(2,1)}, bf16[2048,2048]{1,0:T(8,128)(2,1)}, u32[]{:S(2)}, u32[]{:S(2)}) collective-permute-start(bf16[2048,2048]{1,0:T(8,128)(2,1)} %convolution_convert_fusion.2), channel_id=1, source_target_pairs={{0,4},{4,0},{8,12},{12,8},{16,20},{20,16},{24,28},{28,24},{1,5},{5... | collective-permute-start | bytes 25165832 | tf_op jit(solution)/shard_map/ppermute | solution.py:50
  416.4 47.9 %collective-permute-start.25 = (bf16[512,2048]{1,0:T(8,128)(2,1)S(1)}, bf16[512,2048]{1,0:T(8,128)(2,1)}, u32[]{:S(2)}, u32[]{:S(2)}) collective-permute-start(bf16[512,2048]{1,0:T(8,128)(2,1)S(1)} %get-tuple-element.257), channel_id=1, source_target_pairs={{0,8},{4,12},{8,0},{12,4},{16,24},{20,28},{24,16},{28,20},{1,9},{5... | collective-permute-start | bytes 6291464 | tf_op jit(solution)/shard_map/ppermute | solution.py:50
  417.5 47.4 %collective-permute-start.26 = (bf16[512,2048]{1,0:T(8,128)(2,1)S(1)}, bf16[512,2048]{1,0:T(8,128)(2,1)}, u32[]{:S(2)}, u32[]{:S(2)}) collective-permute-start(bf16[512,2048]{1,0:T(8,128)(2,1)S(1)} %get-tuple-element.258), channel_id=1, source_target_pairs={{0,16},{4,20},{8,24},{12,28},{16,0},{20,4},{24,8},{28,12},{1,17},{... | collective-permute-start | bytes 6291464 | tf_op jit(solution)/shard_map/ppermute | solution.py:50
  470.9 293.4 %all-gather.15.cloned.1.call-start = ((), (), s32[]{:S(2)}) async-start(), calls=%async_computation.6 | async-start | bytes 14155776 | tf_op jit(solution)/shard_map/all_gather | solution.py:743
  474.9 24.3 %collective-permute-start.28 = (bf16[256,2048]{1,0:T(8,128)(2,1)}, bf16[256,2048]{1,0:T(8,128)(2,1)}, u32[]{:S(2)}, u32[]{:S(2)}) collective-permute-start(bf16[256,2048]{1,0:T(8,128)(2,1)} %get-tuple-element.420), channel_id=1, source_target_pairs={{0,16},{4,20},{8,24},{12,28},{16,0},{20,4},{24,8},{28,12},{1,17},{... | collective-permute-start | bytes 3145736 | tf_op jit(solution)/shard_map/ppermute | solution.py:50
  475.6 23.8 %collective-permute-start.29 = (bf16[256,2048]{1,0:T(8,128)(2,1)S(1)}, bf16[256,2048]{1,0:T(8,128)(2,1)}, u32[]{:S(2)}, u32[]{:S(2)}) collective-permute-start(bf16[256,2048]{1,0:T(8,128)(2,1)S(1)} %get-tuple-element.419), channel_id=1, source_target_pairs={{0,8},{4,12},{8,0},{12,4},{16,24},{20,28},{24,16},{28,20},{1,9},{5... | collective-permute-start | bytes 3145736 | tf_op jit(solution)/shard_map/ppermute | solution.py:50
  510.1 46.3 %collective-permute-start.32 = (bf16[640,2048]{1,0:T(8,128)(2,1)}, bf16[640,2048]{1,0:T(8,128)(2,1)S(1)}, u32[]{:S(2)}, u32[]{:S(2)}) collective-permute-start(bf16[640,2048]{1,0:T(8,128)(2,1)} %convolution_convert_fusion.4), channel_id=1, source_target_pairs={{0,4},{4,0},{8,12},{12,8},{16,20},{20,16},{24,28},{28,24},{1,5},{5... | collective-permute-start | bytes 7864328 | tf_op jit(solution)/shard_map/ppermute | solution.py:50
  510.2 46.3 %collective-permute-start.30 = (bf16[256,2048]{1,0:T(8,128)(2,1)S(1)}, bf16[256,2048]{1,0:T(8,128)(2,1)}, u32[]{:S(2)}, u32[]{:S(2)}) collective-permute-start(bf16[256,2048]{1,0:T(8,128)(2,1)S(1)} %get-tuple-element.273), channel_id=1, source_target_pairs={{0,8},{4,12},{8,0},{12,4},{16,24},{20,28},{24,16},{28,20},{1,9},{5... | collective-permute-start | bytes 3145736 | tf_op jit(solution)/shard_map/ppermute | solution.py:50
  511.6 44.9 %collective-permute-start.31 = (bf16[256,2048]{1,0:T(8,128)(2,1)S(1)}, bf16[256,2048]{1,0:T(8,128)(2,1)}, u32[]{:S(2)}, u32[]{:S(2)}) collective-permute-start(bf16[256,2048]{1,0:T(8,128)(2,1)S(1)} %get-tuple-element.274), channel_id=1, source_target_pairs={{0,16},{4,20},{8,24},{12,28},{16,0},{20,4},{24,8},{28,12},{1,17},{... | collective-permute-start | bytes 3145736 | tf_op jit(solution)/shard_map/ppermute | solution.py:50
  558.7 17.7 %collective-permute-start.36 = (bf16[160,2048]{1,0:T(8,128)(2,1)S(1)}, bf16[160,2048]{1,0:T(8,128)(2,1)S(1)}, u32[]{:S(2)}, u32[]{:S(2)}) collective-permute-start(bf16[160,2048]{1,0:T(8,128)(2,1)S(1)} %get-tuple-element.285), channel_id=1, source_target_pairs={{0,8},{4,12},{8,0},{12,4},{16,24},{20,28},{24,16},{28,20},{1,9},{5... | collective-permute-start | bytes 1966088 | tf_op jit(solution)/shard_map/ppermute | solution.py:50
  559.5 17.6 %collective-permute-start.37 = (bf16[160,2048]{1,0:T(8,128)(2,1)S(1)}, bf16[160,2048]{1,0:T(8,128)(2,1)S(1)}, u32[]{:S(2)}, u32[]{:S(2)}) collective-permute-start(bf16[160,2048]{1,0:T(8,128)(2,1)S(1)} %get-tuple-element.286), channel_id=1, source_target_pairs={{0,16},{4,20},{8,24},{12,28},{16,0},{20,4},{24,8},{28,12},{1,17},{... | collective-permute-start | bytes 1966088 | tf_op jit(solution)/shard_map/ppermute | solution.py:50
  562.7 35.6 %collective-permute-start.34 = (bf16[256,2048]{1,0:T(8,128)(2,1)S(1)}, bf16[256,2048]{1,0:T(8,128)(2,1)S(1)}, u32[]{:S(2)}, u32[]{:S(2)}) collective-permute-start(bf16[256,2048]{1,0:T(8,128)(2,1)S(1)} %get-tuple-element.416), channel_id=1, source_target_pairs={{0,16},{4,20},{8,24},{12,28},{16,0},{20,4},{24,8},{28,12},{1,17},{... | collective-permute-start | bytes 3145736 | tf_op jit(solution)/shard_map/ppermute | solution.py:50
  564.1 35.2 %collective-permute-start.35 = (bf16[256,2048]{1,0:T(8,128)(2,1)S(1)}, bf16[256,2048]{1,0:T(8,128)(2,1)}, u32[]{:S(2)}, u32[]{:S(2)}) collective-permute-start(bf16[256,2048]{1,0:T(8,128)(2,1)S(1)} %get-tuple-element.415), channel_id=1, source_target_pairs={{0,8},{4,12},{8,0},{12,4},{16,24},{20,28},{24,16},{28,20},{1,9},{5... | collective-permute-start | bytes 3145736 | tf_op jit(solution)/shard_map/ppermute | solution.py:50
  566.8 28.4 %collective-permute-start.33 = (bf16[10,64,512]{2,1,0:T(8,128)(2,1)S(1)}, bf16[10,64,512]{2,1,0:T(8,128)(2,1)S(1)}, u32[]{:S(2)}, u32[]{:S(2)}) collective-permute-start(bf16[10,64,512]{2,1,0:T(8,128)(2,1)S(1)} %copy-done.93), channel_id=1, source_target_pairs={{0,1},{1,0},{2,3},{3,2},{4,5},{5,4},{6,7},{7,6},{8,9},{9,8},{10,11... | collective-permute-start | bytes 1966088 | tf_op jit(solution)/shard_map/ppermute | solution.py:50
  599.3 221.4 %all-gather.13.cloned.1.call-start = ((), (), s32[]{:S(2)}) async-start(), calls=%async_computation.5 | async-start | bytes 7667712 | tf_op jit(solution)/shard_map/all_gather | solution.py:834
  610.4 18.3 %collective-permute-start.38 = (bf16[1024,2048]{1,0:T(8,128)(2,1)}, bf16[1024,2048]{1,0:T(8,128)(2,1)S(1)}, u32[]{:S(2)}, u32[]{:S(2)}) collective-permute-start(bf16[1024,2048]{1,0:T(8,128)(2,1)} %add_convert_fusion.1), channel_id=1, source_target_pairs={{0,4},{4,0},{8,12},{12,8},{16,20},{20,16},{24,28},{28,24},{1,5},{5... | collective-permute-start | bytes 12582920 | tf_op jit(solution)/shard_map/ppermute | solution.py:50
  610.7 17.5 %collective-permute-start.39 = (bf16[80,2048]{1,0:T(8,128)(2,1)S(1)}, bf16[80,2048]{1,0:T(8,128)(2,1)S(1)}, u32[]{:S(2)}, u32[]{:S(2)}) collective-permute-start(bf16[80,2048]{1,0:T(8,128)(2,1)S(1)} %get-tuple-element.486), channel_id=1, source_target_pairs={{0,16},{4,20},{8,24},{12,28},{16,0},{20,4},{24,8},{28,12},{1,17},{... | collective-permute-start | bytes 983048 | tf_op jit(solution)/shard_map/ppermute | solution.py:50
  611.4 17.3 %collective-permute-start.40 = (bf16[80,2048]{1,0:T(8,128)(2,1)S(1)}, bf16[80,2048]{1,0:T(8,128)(2,1)S(1)}, u32[]{:S(2)}, u32[]{:S(2)}) collective-permute-start(bf16[80,2048]{1,0:T(8,128)(2,1)S(1)} %get-tuple-element.485), channel_id=1, source_target_pairs={{0,8},{4,12},{8,0},{12,4},{16,24},{20,28},{24,16},{28,20},{1,9},{5... | collective-permute-start | bytes 983048 | tf_op jit(solution)/shard_map/ppermute | solution.py:50
  632.5 50.6 %collective-permute-start.44 = (bf16[256,2048]{1,0:T(8,128)(2,1)S(1)}, bf16[256,2048]{1,0:T(8,128)(2,1)S(1)}, u32[]{:S(2)}, u32[]{:S(2)}) collective-permute-start(bf16[256,2048]{1,0:T(8,128)(2,1)S(1)} %get-tuple-element.305), channel_id=1, source_target_pairs={{0,8},{4,12},{8,0},{12,4},{16,24},{20,28},{24,16},{28,20},{1,9},{5... | collective-permute-start | bytes 3145736 | tf_op jit(solution)/shard_map/ppermute | solution.py:50
  633.9 49.2 %collective-permute-start.45 = (bf16[256,2048]{1,0:T(8,128)(2,1)S(1)}, bf16[256,2048]{1,0:T(8,128)(2,1)S(1)}, u32[]{:S(2)}, u32[]{:S(2)}) collective-permute-start(bf16[256,2048]{1,0:T(8,128)(2,1)S(1)} %get-tuple-element.306), channel_id=1, source_target_pairs={{0,16},{4,20},{8,24},{12,28},{16,0},{20,4},{24,8},{28,12},{1,17},{... | collective-permute-start | bytes 3145736 | tf_op jit(solution)/shard_map/ppermute | solution.py:50
  635.3 21.5 %collective-permute-start.41 = (bf16[512,512]{1,0:T(8,128)(2,1)S(1)}, bf16[512,512]{1,0:T(8,128)(2,1)S(1)}, u32[]{:S(2)}, u32[]{:S(2)}) collective-permute-start(bf16[512,512]{1,0:T(8,128)(2,1)S(1)} %get-tuple-element.441), channel_id=1, source_target_pairs={{0,1},{1,0},{2,3},{3,2},{4,5},{5,4},{6,7},{7,6},{8,9},{9,8},{10,11... | collective-permute-start | bytes 1572872 | tf_op jit(solution)/shard_map/ppermute | solution.py:36
  636.9 35.1 %collective-permute-start.42 = (bf16[512,512]{1,0:T(8,128)(2,1)S(1)}, bf16[512,512]{1,0:T(8,128)(2,1)S(1)}, u32[]{:S(2)}, u32[]{:S(2)}) collective-permute-start(bf16[512,512]{1,0:T(8,128)(2,1)S(1)} %get-tuple-element.442), channel_id=1, source_target_pairs={{0,2},{1,3},{2,0},{3,1},{4,6},{5,7},{6,4},{7,5},{8,10},{9,11},{10,... | collective-permute-start | bytes 1572872 | tf_op jit(solution)/shard_map/ppermute | solution.py:36
  637.1 45.9 %collective-permute-start.43 = (bf16[512,512]{1,0:T(8,128)(2,1)S(1)}, bf16[512,512]{1,0:T(8,128)(2,1)S(1)}, u32[]{:S(2)}, u32[]{:S(2)}) collective-permute-start(bf16[512,512]{1,0:T(8,128)(2,1)S(1)} %get-tuple-element.439), channel_id=1, source_target_pairs={{0,3},{1,2},{2,1},{3,0},{4,7},{5,6},{6,5},{7,4},{8,11},{9,10},{10,... | collective-permute-start | bytes 1572872 | tf_op jit(solution)/shard_map/ppermute | solution.py:36
  684.5 19.7 %collective-permute-start.49 = (bf16[128,2048]{1,0:T(8,128)(2,1)}, bf16[128,2048]{1,0:T(8,128)(2,1)}, u32[]{:S(2)}, u32[]{:S(2)}) collective-permute-start(bf16[128,2048]{1,0:T(8,128)(2,1)} %get-tuple-element.438), channel_id=1, source_target_pairs={{0,16},{4,20},{8,24},{12,28},{16,0},{20,4},{24,8},{28,12},{1,17},{... | collective-permute-start | bytes 1572872 | tf_op jit(solution)/shard_map/ppermute | solution.py:50
  685.7 18.5 %collective-permute-start.50 = (bf16[128,2048]{1,0:T(8,128)(2,1)}, bf16[128,2048]{1,0:T(8,128)(2,1)}, u32[]{:S(2)}, u32[]{:S(2)}) collective-permute-start(bf16[128,2048]{1,0:T(8,128)(2,1)} %get-tuple-element.437), channel_id=1, source_target_pairs={{0,8},{4,12},{8,0},{12,4},{16,24},{20,28},{24,16},{28,20},{1,9},{5... | collective-permute-start | bytes 1572872 | tf_op jit(solution)/shard_map/ppermute | solution.py:50
  688.3 11.7 %collective-permute-start.47 = (bf16[160,512]{1,0:T(8,128)(2,1)}, bf16[160,512]{1,0:T(8,128)(2,1)}, u32[]{:S(2)}, u32[]{:S(2)}) collective-permute-start(bf16[160,512]{1,0:T(8,128)(2,1)} %get-tuple-element.501), channel_id=1, source_target_pairs={{0,2},{1,3},{2,0},{3,1},{4,6},{5,7},{6,4},{7,5},{8,10},{9,11},{10,... | collective-permute-start | bytes 491528 | tf_op jit(solution)/shard_map/ppermute | solution.py:36
  690.3 13.8 %collective-permute-start.48 = (bf16[160,512]{1,0:T(8,128)(2,1)}, bf16[160,512]{1,0:T(8,128)(2,1)}, u32[]{:S(2)}, u32[]{:S(2)}) collective-permute-start(bf16[160,512]{1,0:T(8,128)(2,1)} %get-tuple-element.398), channel_id=1, source_target_pairs={{0,3},{1,2},{2,1},{3,0},{4,7},{5,6},{6,5},{7,4},{8,11},{9,10},{10,... | collective-permute-start | bytes 491528 | tf_op jit(solution)/shard_map/ppermute | solution.py:36
  695.6 29.3 %collective-permute-start.54 = (bf16[256,2048]{1,0:T(8,128)(2,1)S(1)}, bf16[256,2048]{1,0:T(8,128)(2,1)S(1)}, u32[]{:S(2)}, u32[]{:S(2)}) collective-permute-start(bf16[256,2048]{1,0:T(8,128)(2,1)S(1)} %copy-done.19), channel_id=1, source_target_pairs={{0,8},{4,12},{8,0},{12,4},{16,24},{20,28},{24,16},{28,20},{1,9},{5... | collective-permute-start | bytes 3145736 | tf_op jit(solution)/shard_map/ppermute | solution.py:50
  700.0 25.6 %collective-permute-start.55 = (bf16[256,2048]{1,0:T(8,128)(2,1)S(1)}, bf16[256,2048]{1,0:T(8,128)(2,1)S(1)}, u32[]{:S(2)}, u32[]{:S(2)}) collective-permute-start(bf16[256,2048]{1,0:T(8,128)(2,1)S(1)} %copy-done.17), channel_id=1, source_target_pairs={{0,16},{4,20},{8,24},{12,28},{16,0},{20,4},{24,8},{28,12},{1,17},{... | collective-permute-start | bytes 3145736 | tf_op jit(solution)/shard_map/ppermute | solution.py:50
  710.9 22.5 %collective-permute-start.51 = (bf16[256,1152]{1,0:T(8,128)(2,1)S(1)}, bf16[256,1152]{1,0:T(8,128)(2,1)S(1)}, u32[]{:S(2)}, u32[]{:S(2)}) collective-permute-start(bf16[256,1152]{1,0:T(8,128)(2,1)S(1)} %get-tuple-element.515), channel_id=1, source_target_pairs={{0,1},{1,0},{2,3},{3,2},{4,5},{5,4},{6,7},{7,6},{8,9},{9,8},{10,11... | collective-permute-start | bytes 1769480 | tf_op jit(solution)/shard_map/ppermute | solution.py:36
  713.2 39.2 %collective-permute-start.52 = (bf16[256,1152]{1,0:T(8,128)(2,1)S(1)}, bf16[256,1152]{1,0:T(8,128)(2,1)S(1)}, u32[]{:S(2)}, u32[]{:S(2)}) collective-permute-start(bf16[256,1152]{1,0:T(8,128)(2,1)S(1)} %get-tuple-element.516), channel_id=1, source_target_pairs={{0,2},{1,3},{2,0},{3,1},{4,6},{5,7},{6,4},{7,5},{8,10},{9,11},{10,... | collective-permute-start | bytes 1769480 | tf_op jit(solution)/shard_map/ppermute | solution.py:36
  713.4 50.9 %collective-permute-start.53 = (bf16[256,1152]{1,0:T(8,128)(2,1)S(1)}, bf16[256,1152]{1,0:T(8,128)(2,1)}, u32[]{:S(2)}, u32[]{:S(2)}) collective-permute-start(bf16[256,1152]{1,0:T(8,128)(2,1)S(1)} %get-tuple-element.514), channel_id=1, source_target_pairs={{0,3},{1,2},{2,1},{3,0},{4,7},{5,6},{6,5},{7,4},{8,11},{9,10},{10,... | collective-permute-start | bytes 1769480 | tf_op jit(solution)/shard_map/ppermute | solution.py:36
  774.3 18.2 %collective-permute-start.56 = (bf16[512,512]{1,0:T(8,128)(2,1)S(1)}, bf16[512,512]{1,0:T(8,128)(2,1)S(1)}, u32[]{:S(2)}, u32[]{:S(2)}) collective-permute-start(bf16[512,512]{1,0:T(8,128)(2,1)S(1)} %get-tuple-element.431), channel_id=1, source_target_pairs={{0,1},{1,0},{2,3},{3,2},{4,5},{5,4},{6,7},{7,6},{8,9},{9,8},{10,11... | collective-permute-start | bytes 1572872 | tf_op jit(solution)/shard_map/ppermute | solution.py:36
  774.4 36.5 %collective-permute-start.57 = (bf16[512,512]{1,0:T(8,128)(2,1)S(1)}, bf16[512,512]{1,0:T(8,128)(2,1)}, u32[]{:S(2)}, u32[]{:S(2)}) collective-permute-start(bf16[512,512]{1,0:T(8,128)(2,1)S(1)} %get-tuple-element.432), channel_id=1, source_target_pairs={{0,2},{1,3},{2,0},{3,1},{4,6},{5,7},{6,4},{7,5},{8,10},{9,11},{10,... | collective-permute-start | bytes 1572872 | tf_op jit(solution)/shard_map/ppermute | solution.py:36
  776.0 44.7 %collective-permute-start.58 = (bf16[512,512]{1,0:T(8,128)(2,1)S(1)}, bf16[512,512]{1,0:T(8,128)(2,1)}, u32[]{:S(2)}, u32[]{:S(2)}) collective-permute-start(bf16[512,512]{1,0:T(8,128)(2,1)S(1)} %get-tuple-element.429), channel_id=1, source_target_pairs={{0,3},{1,2},{2,1},{3,0},{4,7},{5,6},{6,5},{7,4},{8,11},{9,10},{10,... | collective-permute-start | bytes 1572872 | tf_op jit(solution)/shard_map/ppermute | solution.py:36
  (139 other events, 1288.5 us)
Sparse Core Ops, SparseCore 0:
  57.5 44.0 all-gather.6
  104.1 41.1 all-gather.8
  252.4 88.0 all-gather.10
  471.0 124.0 reduce-scatter.1
  599.4 100.3 all-gather.14
  767.4 46.5 all-gather.12

commit v4 on v3

--- a/solution.py
+++ b/solution.py
@@ -15,7 +15,6 @@
 QPG = QH // KVH
 HD = 64
 LEN = 1024
-HALF = LEN // 2
 
 epsilon = 1e-05
 rope_base = 10000.0
@@ -276,75 +275,129 @@
     return jnp.dot(left, right, preferred_element_type=full)
 
 
-def scores_of(key, query, start, first):
+BLOCK = LEN // 4
+PARTS = (((0, True),), ((0, False), (BLOCK, False), (2 * BLOCK, True)))
+
+
+def scores_of(key, query, lead):
     scores = mm(key, query)
-    if first is None:
+    if lead is None:
         return scores
     rows = lax.broadcasted_iota(jnp.int32, scores.shape, 0)
     cols = lax.broadcasted_iota(jnp.int32, scores.shape, 1)
-    return jnp.where(rows - cols <= start - first, scores, masked_score)
-
-
-PARTS = (((0, 0),), ((0, None), (HALF, HALF)))
-
-
-def attend_kernel(starts, q_ref, k_ref, v_ref, o_ref, sums_ref):
+    return jnp.where(rows - cols <= lead, scores, masked_score)
+
+
+def last_piece(starts, chunk):
+    early = starts[0] >= BLOCK
+    at = pl.multiple_of(jnp.where(early, BLOCK, 3 * BLOCK), BLOCK)
+    span = pl.multiple_of(jnp.where(early, 0, chunk), 128)
+    start = jnp.where(early, starts[0], starts[1])
+    flag = jnp.where(early, 1.0, 0.0).astype(full)
+    return early, pl.ds(at, BLOCK), pl.ds(span, chunk), start - at, (flag, 1.0 - flag)
+
+
+def rows_kept(array):
+    return array.astype(full).T.astype(low)
+
+
+def attend_kernel(starts, q_ref, k_ref, v_ref, o_ref, sums_ref, key_ref):
     chunk = q_ref.shape[2] // 2
-    scale = 1.0 / math.sqrt(HD)
-    key = k_ref[0].astype(full).T.astype(low)
-    for part, pieces in enumerate(PARTS):
-        span = pl.ds(part * chunk, chunk)
-        for head in range(QPG):
-            query = q_ref[head, :, span] * jnp.asarray(scale, low)
-            scores = [
-                scores_of(key[at : at + HALF], query, starts[part], first) for at, first in pieces
-            ]
-            peak = functools.reduce(
-                jnp.maximum, [jnp.max(s, axis=0, keepdims=True) for s in scores]
+    scale = jnp.asarray(1.0 / math.sqrt(HD), low)
+    key_ref[...] = rows_kept(k_ref[0])
+    early, keys, columns, lead, flags = last_piece(starts, chunk)
+    for head in range(QPG):
+        scores, peaks = [], []
+        for part, pieces in enumerate(PARTS):
+            query = q_ref[head, :, part * chunk : (part + 1) * chunk] * scale
+            scores.append(
+                [
+                    scores_of(key_ref[at : at + BLOCK], query, starts[part] - at if cut else None)
+                    for at, cut in pieces
+                ]
             )
-            total = jnp.zeros_like(peak)
-            result = jnp.zeros((HD, chunk), full)
-            for (at, _), s in zip(pieces, scores):
-                weights = jnp.exp(s - peak)
+            peaks.append(
+                functools.reduce(
+                    jnp.maximum, [jnp.max(s, axis=0, keepdims=True) for s in scores[-1]]
+                )
+            )
+        more = scores_of(key_ref[keys], q_ref[head, :, columns] * scale, lead)
+        peak = jnp.max(more, axis=0, keepdims=True)
+        peaks = [
+            jnp.maximum(peaks[0], jnp.where(early, peak, masked_score)),
+            jnp.maximum(peaks[1], jnp.where(early, masked_score, peak)),
+        ]
+        more = jnp.exp(more - jnp.where(early, peaks[0], peaks[1]))
+        more_total = jnp.sum(more, axis=0, keepdims=True)
+        more_result = mm(v_ref[0, :, keys], more.astype(low))
+        for part, pieces in enumerate(PARTS):
+            total = more_total * flags[part]
+            result = more_result * flags[part]
+            for (at, _), s in zip(pieces, scores[part]):
+                weights = jnp.exp(s - peaks[part])
                 total += jnp.sum(weights, axis=0, keepdims=True)
-                result += mm(v_ref[0, :, at : at + HALF], weights.astype(low))
+                result += mm(v_ref[0, :, at : at + BLOCK], weights.astype(low))
+            span = pl.ds(part * chunk, chunk)
             o_ref[head, :, span] = (result / total).astype(low)
-            sums_ref[0, head : head + 1, span] = peak + jnp.log(total)
+            sums_ref[0, head : head + 1, span] = peaks[part] + jnp.log(total)
 
 
 def attend_back_kernel(
-    starts, q_ref, k_ref, v_ref, g_ref, sums_ref, dq_ref, dk_ref, dv_ref, dk_acc, dv_acc
+    starts, q_ref, k_ref, v_ref, g_ref, sums_ref, dq_ref, dk_ref, dv_ref, dk_acc, dv_acc,
+    key_ref, value_ref
 ):
     chunk = q_ref.shape[2] // 2
     scale = 1.0 / math.sqrt(HD)
-    key = k_ref[0].astype(full).T.astype(low)
-    value = v_ref[0].astype(full).T.astype(low)
+    key_ref[...] = rows_kept(k_ref[0])
+    value_ref[...] = rows_kept(v_ref[0])
     dk_acc[...] = jnp.zeros_like(dk_acc)
     dv_acc[...] = jnp.zeros_like(dv_acc)
-    for part, pieces in enumerate(PARTS):
-        span = pl.ds(part * chunk, chunk)
-        for head in range(QPG):
+    early, keys, columns, lead, flags = last_piece(starts, chunk)
+
+    def products(at, query, grad, sums, lead):
+        probs = jnp.exp(scores_of(key_ref[at], query, lead) - sums)
+        return probs, probs * mm(value_ref[at], grad)
+
+    def store(at, probs, product, delta, query_rows, grad_rows):
+        score_grad = (product - probs * delta).astype(low)
+        dk_acc[at, :] += mm(score_grad, query_rows)
+        dv_acc[at, :] += mm(probs.astype(low), grad_rows)
+        return mm(k_ref[0, :, at], score_grad)
+
+    for head in range(QPG):
+        parts = []
+        for part, pieces in enumerate(PARTS):
+            span = pl.ds(part * chunk, chunk)
             query = q_ref[head, :, span] * jnp.asarray(scale, low)
             grad = g_ref[head, :, span]
-            query_rows = query.astype(full).T.astype(low)
-            grad_rows = grad.astype(full).T.astype(low)
             sums = sums_ref[0, head : head + 1, span]
-            delta = jnp.zeros((1, chunk), full)
-            kept = []
-            for at, first in pieces:
-                probs = jnp.exp(
-                    scores_of(key[at : at + HALF], query, starts[part], first) - sums
+            found = [
+                products(
+                    pl.ds(at, BLOCK), query, grad, sums, starts[part] - at if cut else None
                 )
-                product = probs * mm(value[at : at + HALF], grad)
-                delta += jnp.sum(product, axis=0, keepdims=True)
-                kept.append((probs, product))
-            dq = jnp.zeros((HD, chunk), full)
-            for (at, _), (probs, product) in zip(pieces, kept):
-                score_grad = (product - probs * delta).astype(low)
-                dq += mm(k_ref[0, :, at : at + HALF], score_grad)
-                dk_acc[at : at + HALF, :] += mm(score_grad, query_rows)
-                dv_acc[at : at + HALF, :] += mm(probs.astype(low), grad_rows)
-            dq_ref[head, :, span] = dq * scale
+                for at, cut in pieces
+            ]
+            delta = sum(jnp.sum(product, axis=0, keepdims=True) for _, product in found)
+            parts.append([found, delta, rows_kept(query), rows_kept(grad)])
+        probs, product = products(
+            keys,
+            q_ref[head, :, columns] * jnp.asarray(scale, low),
+            g_ref[head, :, columns],
+            sums_ref[0, head : head + 1, columns],
+            lead,
+        )
+        more = jnp.sum(product, axis=0, keepdims=True)
+        for part in range(2):
+            parts[part][1] += more * flags[part]
+        more = store(
+            keys, probs, product, *(jnp.where(early, a, b) for a, b in zip(parts[0][1:], parts[1][1:]))
+        )
+        for part, pieces in enumerate(PARTS):
+            found, delta, query_rows, grad_rows = parts[part]
+            dq = more * flags[part]
+            for (at, _), (probs, product) in zip(pieces, found):
+                dq += store(pl.ds(at, BLOCK), probs, product, delta, query_rows, grad_rows)
+            dq_ref[head, :, part * chunk : (part + 1) * chunk] = dq * scale
     dk_ref[0] = dk_acc[...].T
     dv_ref[0] = dv_acc[...].T
 
@@ -359,7 +412,7 @@
 def attend(starts, queries, keys, values):
     tokens = queries.shape[2]
     heads, whole, sums = attention_specs(tokens)
-    pairs = QH * (tokens // 2) * (LEN + HALF)
+    pairs = QH * (tokens // 2) * 5 * BLOCK
     return pl.pallas_call(
         attend_kernel,
         out_shape=(
@@ -371,6 +424,7 @@
             grid=(KVH,),
             in_specs=[heads, whole, whole],
             out_specs=[heads, sums],
+            scratch_shapes=[pltpu.VMEM((LEN, HD), low)],
         ),
         compiler_params=pltpu.CompilerParams(vmem_limit_bytes=40 << 20),
         cost_estimate=pl.CostEstimate(
@@ -382,7 +436,7 @@
 def attend_back(starts, queries, keys, values, grads, sums_in):
     tokens = queries.shape[2]
     heads, whole, sums = attention_specs(tokens)
-    pairs = QH * (tokens // 2) * (LEN + HALF)
+    pairs = QH * (tokens // 2) * 5 * BLOCK
     return pl.pallas_call(
         attend_back_kernel,
         out_shape=(
@@ -395,7 +449,7 @@
             grid=(KVH,),
             in_specs=[heads, whole, whole, heads, sums],
             out_specs=[heads, whole, whole],
-            scratch_shapes=[pltpu.VMEM((LEN, HD), full), pltpu.VMEM((LEN, HD), full)],
+            scratch_shapes=[pltpu.VMEM((LEN, HD), kind) for kind in (full, full, low, low)],
         ),
         compiler_params=pltpu.CompilerParams(vmem_limit_bytes=40 << 20),
         cost_estimate=pl.CostEstimate(
@@ -464,6 +518,33 @@
         compiler_params=pltpu.CompilerParams(vmem_limit_bytes=32 << 20),
         cost_estimate=pl.CostEstimate(flops=0, bytes_accessed=1 << 16, transcendentals=0),
     )(pack)
+
+
+def split_kernel(in_ref, query_out, key_out, value_out):
+    slots, width = query_out.shape[1], key_out.shape[0]
+    array = in_ref[...].astype(full)
+    query_out[...] = array[:, :slots]
+    key_out[...] = array[:, slots : slots + width].T
+    value_out[...] = array[:, slots + width : slots + 2 * width].T
+
+
+def split_projections(array, slots, rows):
+    width = KVH * HD
+    if slots % 128 or rows % 128:
+        array = array.astype(full)
+        return array[:, :slots], array[:, slots:][:, :width], array[:, slots + width :][:, :width]
+    turned = jax.ShapeDtypeStruct((width, array.shape[0]), full)
+    column = pl.BlockSpec((width, rows), lambda g: (0, g))
+    query, key, value = pl.pallas_call(
+        split_kernel,
+        out_shape=(jax.ShapeDtypeStruct((array.shape[0], slots), full), turned, turned),
+        grid=(array.shape[0] // rows,),
+        in_specs=[pl.BlockSpec((rows, array.shape[1]), lambda g: (g, 0))],
+        out_specs=[pl.BlockSpec((rows, slots), lambda g: (g, 0)), column, column],
+        compiler_params=pltpu.CompilerParams(vmem_limit_bytes=32 << 20),
+        cost_estimate=pl.CostEstimate(flops=0, bytes_accessed=1 << 16, transcendentals=0),
+    )(array)
+    return query, key.T, value.T
 
 
 def norm_backward(values, rms, gain, normed_grad):
@@ -806,7 +887,7 @@
     output_grad, got, out_relayed = order_split(
         order, [], output_grad, projection_sum.flying, out_relayed
     )
-    output_grad = jnp.pad(added(*output_grad), ((0, rows - heads_here), (0, 0)))
+    output_grad = lax.all_gather(added(*output_grad), "dp", axis=0, tiled=True)
     projection_total = projection_sum.last(*got)
     down_sum.fourth(*out_relayed)
 
@@ -830,25 +911,23 @@
     )
     pack, projection, flying = order_split(order, [pack], projection, down_sum.flying)
 
-    projection = jnp.concatenate([added(*projection), output_grad], 1)
-    projection = lax.all_gather(projection, "dp", axis=0, tiled=True)
+    projection = lax.all_gather(added(*projection), "dp", axis=0, tiled=True)
+    output_weight_grad = mm(select, output_grad)
     output = (middle + down_sum.last(*flying).astype(full)).astype(low)
     output = swap(by_feature(output), "mp")
     gate_weight_grad, up_weight_grad, down_weight_grad = widen(pack)
     input_gradient = by_tokens(input_gradient, full)
     got = order(
-        projection, gate_weight_grad, up_weight_grad, down_weight_grad, input_gradient, *output
-    )
-    projection, gate_weight_grad, up_weight_grad, down_weight_grad, input_gradient = got[:5]
+        gate_weight_grad, up_weight_grad, down_weight_grad, input_gradient, output_weight_grad,
+        *output
+    )
+    gate_weight_grad, up_weight_grad, down_weight_grad, input_gradient = got[:4]
+    output_weight_grad = got[4]
     output = by_tokens(got[5:], low)
-
-    widths = [slots, KVH * HD, KVH * HD, EXTRA]
-    cuts = [sum(widths[: k + 1]) for k in range(4)]
-    query_weight_grad, key_weight_grad, value_weight_grad, extra, output_grad = jnp.split(
-        projection, cuts, axis=1
-    )
-    output_grad = output_grad.reshape(groups, rows, -1)[:, :heads_here].reshape(QH * HD, -1)
-    output_weight_grad = mm(select, output_grad)
+    query_weight_grad, key_weight_grad, value_weight_grad = split_projections(
+        projection, slots, rows
+    )
+    extra = projection[:, slots + 2 * KVH * HD :]
     extra = extra.astype(full)
     own_share = lax.dynamic_slice_in_dim(extra, rank * share, share, 0)
     return (

time: 864 us -> 858 us (level)
  Pallas kernels: 93 us -> 84.1 us
  other arithmetic: 108 us -> 99.3 us
    unnamed x291 -> x281, local copies, waits for them, and re-layouts: 32.3 us -> 37.5 us
  transfers between devices with their start and end apart: 65 -> 66, of which waited for: 39 -> 41; matrix products, arithmetic and copies ran while one was open for 31% -> 34% of each run, Pallas kernels for 10% -> 9%
where the time goes in v4:
time: 858 us; the launch traced here: 850 us
  waiting for transfers between devices  308 us (36%)
  matrix products  179 us (21%)
  other arithmetic  99.3 us (12%)
  local copies, waits for them, and re-layouts  88.4 us (10%)
  Pallas kernels  84.1 us (10%)
  starting transfers between devices  73.8 us (9%)
  between operations  16.7 us (2%)
    ppermute x21, waiting for transfers between devices, swap(): lax.ppermute(pieces[k], axis, [(i, i ^ k) for i in range(n)])  159 us
    dot_general x20, matrix products, dot(): lax.dot_general(left, right, (((left_axis,), (right_axis,)), ((), ())), p...  118 us
    ppermute x32, waiting for transfers between devices, exchange(): return lax.ppermute(array, axis, [(i, i ^ mask) for i in range(n)])  92.3 us
    dot_general x8, matrix products, mm(): return jnp.dot(left, right, preferred_element_type=full)  60.9 us
    ppermute x3, waiting for transfers between devices, send(): lax.ppermute(up, self.axis, right)  49.2 us
    unnamed x281, local copies, waits for them, and re-layouts  37.5 us
    ppermute x32, starting transfers between devices, exchange(): return lax.ppermute(array, axis, [(i, i ^ mask) for i in range(n)])  31.7 us
    pallas_call x4, Pallas kernels, chip_sums(): pl.pallas_call(kernel, out_shape=[jax.ShapeDtypeStruct((len(places) * hal...  27.6 us
  transfers between devices with their start and end apart: 66, of which 41 were waited for; matrix products, arithmetic and copies ran while one was open for 34% of the time, Pallas kernels for 9%

profile of v4, /device:TPU:16, one launch (start us, length us, event | category | flops | bytes accessed | tf_op | source)
XLA Modules:
  0.0 849.6 jit_solution(1530959485089527754)
XLA Ops:
  13.1 3.4 constant_dynamic-slice_fusion.10
  27.1 3.6 iota_compare_fusion
  41.6 9.9 %collective-permute-done.4 = bf16[512,512]{1,0:T(8,128)(2,1)} collective-permute-done((bf16[512,512]{1,0:T(8,128)(2,1)}, bf16[512,512]{1,0:T(8,128)(2,1)}, u32[]{:S(2)}, u32[]{:S(2)}) %collective-permute-start.4) | collective-permute-done | bytes 524320 | tf_op jit(solution)/shard_map/ppermute | solution.py:49
  59.0 3.3 collective-permute-start.6
  63.9 14.8 %collective-permute-done.6 = bf16[160,512]{1,0:T(8,128)(2,1)S(1)} collective-permute-done((bf16[160,512]{1,0:T(8,128)(2,1)S(1)}, bf16[160,512]{1,0:T(8,128)(2,1)S(1)}, u32[]{:S(2)}, u32[]{:S(2)}) %collective-permute-start.6) | collective-permute-done | bytes 163872 | tf_op jit(solution)/shard_map/ppermute | solution.py:35
  78.7 13.9 %collective-permute-done.7 = bf16[160,512]{1,0:T(8,128)(2,1)S(1)} collective-permute-done((bf16[160,512]{1,0:T(8,128)(2,1)S(1)}, bf16[160,512]{1,0:T(8,128)(2,1)S(1)}, u32[]{:S(2)}, u32[]{:S(2)}) %collective-permute-start.7) | collective-permute-done | bytes 163872 | tf_op jit(solution)/shard_map/ppermute | solution.py:35
  106.5 5.5 fusion.84
  114.8 6.3 collective-permute-done.9
  126.2 14.6 %shard_map.246 = (bf16[20,64,512]{2,1,0:T(8,128)(2,1)S(1)}, f32[5,4,512]{2,1,0:T(4,128)S(1)}) custom-call(s32[2]{0:T(128)S(1)} %pad_add_fusion.2.starts, bf16[20,64,512]{2,1,0:T(8,128)(2,1)S(1)} %fusion.21.q_ref, bf16[5,64,1024]{2,1,0:T(8,128)(2,1)S(1)} %get-tuple-element.455.k_ref, bf16[5,64,1024]{2,1,0:T(8,128)(2,1)S(1)} %get-tuple-element.454.v_ref), custom_call_target="tpu_custom_call" | custom-call | flops 6553600 | bytes 1048576 | tf_op jit(solution)/shard_map/pallas_call | solution.py:416
  145.2 6.1 multiply_reduce_fusion
  154.0 5.3 collective-permute-done.11
  159.3 7.8 collective-permute-done.12
  172.1 4.4 collective-permute-start.16
  184.9 19.0 %collective-permute-done.15 = bf16[2048,384]{0,1:T(8,128)(2,1)} collective-permute-done((bf16[2048,384]{0,1:T(8,128)(2,1)}, bf16[2048,384]{0,1:T(8,128)(2,1)}, u32[]{:S(2)}, u32[]{:S(2)}) %collective-permute-start.15) | collective-permute-done | bytes 1572896 | tf_op jit(solution)/shard_map/ppermute | solution.py:79
  205.8 4.9 collective-permute-done.13
  213.8 5.2 collective-permute-start.20
  219.0 4.5 broadcast_in_dim.51
  223.5 3.2 bitcast_dynamic-update-slice_fusion.2
  237.8 9.2 %collective-permute-done.17 = bf16[256,2048]{1,0:T(8,128)(2,1)S(1)} collective-permute-done((bf16[256,2048]{1,0:T(8,128)(2,1)S(1)}, bf16[256,2048]{1,0:T(8,128)(2,1)S(1)}, u32[]{:S(2)}, u32[]{:S(2)}) %collective-permute-start.17) | collective-permute-done | bytes 1048608 | tf_op jit(solution)/shard_map/ppermute | solution.py:49
  259.1 30.2 %collective-permute-done.22 = bf16[2048,384]{0,1:T(8,128)(2,1)S(1)} collective-permute-done((bf16[2048,384]{0,1:T(8,128)(2,1)S(1)}, bf16[2048,384]{0,1:T(8,128)(2,1)S(1)}, u32[]{:S(2)}, u32[]{:S(2)}) %collective-permute-start.22) | collective-permute-done | bytes 1572896 | tf_op jit(solution)/shard_map/ppermute | solution.py:79
  289.3 3.3 add.511
  297.4 12.8 %fusion.86 = f32[2048,1024]{1,0:T(8,128)S(1)} fusion(bf16[2048,2048]{1,0:T(8,128)(2,1)} %copy-done.128, bf16[2048,1024]{0,1:T(8,128)(2,1)S(1)} %get-tuple-element.447), kind=kOutput, calls=%fused_computation.394 | convolution fusion | flops 8589934592 | bytes 20971520 | tf_op jit(solution)/shard_map/dot_general | solution.py:275
  310.2 3.2 copy-done.45
  314.9 12.0 %fusion.85 = f32[2048,1024]{1,0:T(8,128)S(1)} fusion(bf16[2048,2048]{1,0:T(8,128)(2,1)} %bitcast.31, bf16[2048,1024]{0,1:T(8,128)(2,1)S(1)} %get-tuple-element.447), kind=kOutput, calls=%fused_computation.393 | convolution fusion | flops 8589934592 | bytes 20971520 | tf_op jit(solution)/shard_map/dot_general | solution.py:275
  330.2 6.9 convolution_convert_fusion.2
  337.1 6.7 convolution_convert_fusion.3.mine_ref
  343.8 9.4 %constant_dynamic-slice_fusion.6 = (bf16[4,1,512,2048]{3,2,1,0:T(8,128)(2,1)}, bf16[4,1,512,2048]{3,2,1,0:T(8,128)(2,1)S(1)}) fusion(bf16[4,2,512,2048]{3,2,1,0:T(8,128)(2,1)} %bitcast.113, s32[]{:T(128)S(6)} %select_n.642, s32[]{:T(128)S(6)} %select_n.643), kind=kLoop, calls=%fused_computation.304 | loop fusion | bytes 33554440 | tf_op jit(solution)/shard_map/jit(dynamic_index_in_dim)/dynamic_slice | solution.py:745
  353.2 12.6 %multiply_convert_fusion.3 = (bf16[2048,512]{1,0:T(8,128)(2,1)S(1)}, bf16[2048,512]{1,0:T(8,128)(2,1)S(1)}) fusion(f32[2048,1024]{1,0:T(8,128)} %copy-done.45, bf16[2048,2048]{1,0:T(8,128)(2,1)S(1)} %bitcast.126, bf16[2048,128]{0,1:T(8,128)(2,1)S(1)} %get-tuple-element.446, bf16[2048,128]{0,1:T(8,128)(2,1)S(1)} %get-tuple-element.444, ...), kind=kOutput, calls=%fused_computation.50 | convolution fusion | flops 4316987392 | bytes 23068672 | tf_op jit(solution)/shard_map/dot_general | solution.py:275
  369.4 10.8 %convolution_convert_fusion.1 = bf16[2048,2048]{1,0:T(8,128)(2,1)} fusion(bf16[2048,1024]{0,1:T(8,128)(2,1)S(1)} %copy-done.116, bf16[2048,512]{1,0:T(8,128)(2,1)S(1)} %get-tuple-element.377, bf16[2048,512]{1,0:T(8,128)(2,1)S(1)} %get-tuple-element.376), kind=kOutput, calls=%fused_computation.16 | convolution fusion | flops 8602517504 | bytes 16777216 | tf_op jit(solution)/shard_map/dot_general | solution.py:27
  380.9 12.0 %multiply_convert_fusion.1 = (bf16[2048,512]{1,0:T(8,128)(2,1)S(1)}, bf16[2048,512]{1,0:T(8,128)(2,1)S(1)}) fusion(f32[2048,1024]{1,0:T(8,128)} %copy-done.44, bf16[2048,2048]{1,0:T(8,128)(2,1)} %bitcast.122, bf16[2048,128]{0,1:T(8,128)(2,1)S(1)} %get-tuple-element.446, bf16[2048,128]{0,1:T(8,128)(2,1)S(1)} %get-tuple-element.444, ...), kind=kOutput, calls=%fused_computation.47 | convolution fusion | flops 4316987392 | bytes 23068672 | tf_op jit(solution)/shard_map/dot_general | solution.py:275
  392.9 10.9 %convolution_convert_fusion.mine_ref = bf16[2048,2048]{1,0:T(8,128)(2,1)} fusion(bf16[2048,1024]{0,1:T(8,128)(2,1)S(1)} %copy-done.117, bf16[2048,512]{1,0:T(8,128)(2,1)S(1)} %get-tuple-element.375, bf16[2048,512]{1,0:T(8,128)(2,1)S(1)} %get-tuple-element.374), kind=kOutput, calls=%fused_computation.15 | convolution fusion | flops 8602517504 | bytes 16777216 | tf_op jit(solution)/shard_map/dot_general | solution.py:27
  404.5 11.0 %shard_map.247 = (bf16[512,2048]{1,0:T(8,128)(2,1)S(1)}, bf16[512,2048]{1,0:T(8,128)(2,1)S(1)}, bf16[1024,2048]{1,0:T(8,128)(2,1)S(1)}) custom-call(s32[8]{0:T(128)S(1)} %stack.97.index_ref, bf16[2048,2048]{1,0:T(8,128)(2,1)} %convolution_convert_fusion.mine_ref, bf16[2048,2048]{1,0:T(8,128)(2,1)} %collective-permute-done.24.got_ref), custom_call_target="tpu_custom_call" | custom-call | bytes 65536 | tf_op jit(solution)/shard_map/pallas_call | solution.py:169
  416.5 6.1 fusion.87
  422.6 7.2 add_convert_fusion.4.down_ref
  429.8 13.7 %fusion.88 = f32[2048,1024]{1,0:T(8,128)} fusion(bf16[2048,2048]{1,0:T(8,128)(2,1)} %copy-done.128, bf16[2048,1024]{1,0:T(8,128)(2,1)S(1)} %copy-done.57), kind=kOutput, calls=%fused_computation.396 | convolution fusion | flops 8589934592 | bytes 20971520 | tf_op jit(solution)/shard_map/dot_general | solution.py:27
  443.5 12.7 %add_convert_fusion.2.gate_ref.up_ref = bf16[2048,1024]{1,0:T(8,128)(2,1)S(1)} fusion(f32[2048,1024]{1,0:T(8,128)} %fusion.88, bf16[2048,2048]{1,0:T(8,128)(2,1)} %bitcast.31, bf16[2048,1024]{1,0:T(8,128)(2,1)S(1)} %pad_maximum_fusion.1), kind=kOutput, calls=%fused_computation.6 | convolution fusion | flops 8594128896 | bytes 25165824 | tf_op jit(solution)/shard_map/dot_general | solution.py:27
  456.2 7.0 collective-permute-done.25
  463.6 3.2 shard_map.250
  474.6 11.7 %shard_map.248 = (bf16[256,2048]{1,0:T(8,128)(2,1)S(1)}, bf16[256,2048]{1,0:T(8,128)(2,1)S(1)}, bf16[256,2048]{1,0:T(8,128)(2,1)S(1)}, bf16[256,2048]{1,0:T(8,128)(2,1)S(1)}, bf16[1024,2048]{1,0:T(8,128)(2,1)S(1)}) custom-call(s32[8]{0:T(128)S(1)} %stack.98.index_ref, bf16[2048,2048]{1,0:T(8,128)(2,1)} %convolution_convert_fusion.3.mine_ref, ...), custom_call_target="tpu_custom_call" | custom-call | bytes 65536 | tf_op jit(solution)/shard_map/pallas_call | solution.py:169
  486.3 10.4 %collective-permute-done.28 = bf16[256,2048]{1,0:T(8,128)(2,1)} collective-permute-done((bf16[256,2048]{1,0:T(8,128)(2,1)S(1)}, bf16[256,2048]{1,0:T(8,128)(2,1)}, u32[]{:S(2)}, u32[]{:S(2)}) %collective-permute-start.28) | collective-permute-done | bytes 1048608 | tf_op jit(solution)/shard_map/ppermute | solution.py:49
  496.9 3.8 add_convert_fusion.10
  511.5 6.7 convolution_convert_fusion.6
  518.3 25.1 %shard_map.249 = (f32[20,64,512]{2,1,0:T(8,128)S(1)}, f32[5,64,1024]{2,1,0:T(8,128)S(1)}, f32[5,64,1024]{2,1,0:T(8,128)S(1)}) custom-call(s32[2]{0:T(128)S(1)} %copy-done.17, bf16[20,64,512]{2,1,0:T(8,128)(2,1)S(1)} %copy-done.5, bf16[5,64,1024]{2,1,0:T(8,128)(2,1)S(1)} %copy-done.9, bf16[5,64,1024]{2,1,0:T(8,128)(2,1)S(1)} %copy-done.7, ...), custom_call_target="tpu_custom_call" | custom-call | flops 6553600 | bytes 1048576 | tf_op jit(solution)/shard_map/pallas_call | solution.py:440
  564.2 5.7 collective-permute-done.36
  570.6 18.9 %collective-permute-done.33 = bf16[10,64,512]{2,1,0:T(8,128)(2,1)S(1)} collective-permute-done((bf16[10,64,512]{2,1,0:T(8,128)(2,1)S(1)}, bf16[10,64,512]{2,1,0:T(8,128)(2,1)S(1)}, u32[]{:S(2)}, u32[]{:S(2)}) %collective-permute-start.33) | collective-permute-done | bytes 655392 | tf_op jit(solution)/shard_map/ppermute | solution.py:49
  602.6 5.2 add_convert_fusion.1
  613.2 5.1 fusion.24
  639.0 14.3 %collective-permute-done.41 = bf16[512,512]{1,0:T(8,128)(2,1)S(1)} collective-permute-done((bf16[512,512]{1,0:T(8,128)(2,1)S(1)}, bf16[512,512]{1,0:T(8,128)(2,1)S(1)}, u32[]{:S(2)}, u32[]{:S(2)}) %collective-permute-start.41) | collective-permute-done | bytes 524320 | tf_op jit(solution)/shard_map/ppermute | solution.py:35
  653.3 16.1 %collective-permute-done.42 = bf16[512,512]{1,0:T(8,128)(2,1)S(1)} collective-permute-done((bf16[512,512]{1,0:T(8,128)(2,1)S(1)}, bf16[512,512]{1,0:T(8,128)(2,1)S(1)}, u32[]{:S(2)}, u32[]{:S(2)}) %collective-permute-start.42) | collective-permute-done | bytes 524320 | tf_op jit(solution)/shard_map/ppermute | solution.py:35
  669.4 12.2 %collective-permute-done.43 = bf16[512,512]{1,0:T(8,128)(2,1)S(1)} collective-permute-done((bf16[512,512]{1,0:T(8,128)(2,1)S(1)}, bf16[512,512]{1,0:T(8,128)(2,1)S(1)}, u32[]{:S(2)}, u32[]{:S(2)}) %collective-permute-start.43) | collective-permute-done | bytes 524320 | tf_op jit(solution)/shard_map/ppermute | solution.py:35
  690.6 3.2 collective-permute-done.46
  698.5 3.4 collective-permute-done.48
  706.4 4.2 convolution_convert_fusion.7
  718.0 6.8 collective-permute-done.54
  726.0 10.5 %collective-permute-done.51 = bf16[256,1152]{1,0:T(8,128)(2,1)S(1)} collective-permute-done((bf16[256,1152]{1,0:T(8,128)(2,1)S(1)}, bf16[256,1152]{1,0:T(8,128)(2,1)S(1)}, u32[]{:S(2)}, u32[]{:S(2)}) %collective-permute-start.51) | collective-permute-done | bytes 589856 | tf_op jit(solution)/shard_map/ppermute | solution.py:35
  736.4 18.4 %collective-permute-done.52 = bf16[256,1152]{1,0:T(8,128)(2,1)S(1)} collective-permute-done((bf16[256,1152]{1,0:T(8,128)(2,1)S(1)}, bf16[256,1152]{1,0:T(8,128)(2,1)S(1)}, u32[]{:S(2)}, u32[]{:S(2)}) %collective-permute-start.52) | collective-permute-done | bytes 589856 | tf_op jit(solution)/shard_map/ppermute | solution.py:35
  755.7 12.0 %collective-permute-done.53 = bf16[256,1152]{1,0:T(8,128)(2,1)} collective-permute-done((bf16[256,1152]{1,0:T(8,128)(2,1)S(1)}, bf16[256,1152]{1,0:T(8,128)(2,1)}, u32[]{:S(2)}, u32[]{:S(2)}) %collective-permute-start.53) | collective-permute-done | bytes 589856 | tf_op jit(solution)/shard_map/ppermute | solution.py:35
  776.4 3.4 add_convert_fusion.6
  785.2 6.4 fusion.89
  791.5 5.3 copy-done.3
  796.9 8.6 %shard_map.253 = (f32[2048,1024]{1,0:T(8,128)}, f32[2048,1024]{1,0:T(8,128)}, f32[1024,2048]{1,0:T(8,128)}) custom-call(bf16[8,2048,384]{2,1,0:T(8,128)(2,1)S(1)} %bitcast.104), custom_call_target="tpu_custom_call" | custom-call | bytes 65536 | tf_op jit(solution)/shard_map/pallas_call | solution.py:512
  805.5 12.2 %collective-permute-done.57 = bf16[512,512]{1,0:T(8,128)(2,1)S(1)} collective-permute-done((bf16[512,512]{1,0:T(8,128)(2,1)S(1)}, bf16[512,512]{1,0:T(8,128)(2,1)S(1)}, u32[]{:S(2)}, u32[]{:S(2)}) %collective-permute-start.57) | collective-permute-done | bytes 524320 | tf_op jit(solution)/shard_map/ppermute | solution.py:35
  817.6 10.0 %collective-permute-done.58 = bf16[512,512]{1,0:T(8,128)(2,1)S(1)} collective-permute-done((bf16[512,512]{1,0:T(8,128)(2,1)S(1)}, bf16[512,512]{1,0:T(8,128)(2,1)S(1)}, u32[]{:S(2)}, u32[]{:S(2)}) %collective-permute-start.58) | collective-permute-done | bytes 524320 | tf_op jit(solution)/shard_map/ppermute | solution.py:35
  837.7 4.9 shard_map.254
  (570 shorter events, 252.2 us)
Async XLA Ops:
  7.2 99.3 %all-gather.8.cloned.1.call-start = ((), (), s32[]{:S(2)}) async-start(), calls=%async_computation.1 | async-start | bytes 5898240 | tf_op jit(solution)/shard_map/all_gather | solution.py:653
  9.6 31.8 %collective-permute-start = (bf16[264,384]{1,0:T(8,128)(2,1)}, bf16[264,384]{1,0:T(8,128)(2,1)}, u32[]{:S(2)}, u32[]{:S(2)}) collective-permute-start(bf16[264,384]{1,0:T(8,128)(2,1)} %pad_maximum_fusion.32), channel_id=1, source_target_pairs={{0,1},{1,0},{2,3},{3,2},{4,5},{5,4},{6,7},{7,6},{8,9},{9,8},{10,11... | collective-permute-start | bytes 608264 | tf_op jit(solution)/shard_map/ppermute | solution.py:35
  11.1 30.2 %collective-permute-start.1 = (bf16[264,384]{1,0:T(8,128)(2,1)}, bf16[264,384]{1,0:T(8,128)(2,1)}, u32[]{:S(2)}, u32[]{:S(2)}) collective-permute-start(bf16[264,384]{1,0:T(8,128)(2,1)} %pad_maximum_fusion.32), channel_id=1, source_target_pairs={{0,2},{1,3},{2,0},{3,1},{4,6},{5,7},{6,4},{7,5},{8,10},{9,11},{10,... | collective-permute-start | bytes 608264 | tf_op jit(solution)/shard_map/ppermute | solution.py:35
  11.5 29.9 %collective-permute-start.2 = (bf16[264,384]{1,0:T(8,128)(2,1)}, bf16[264,384]{1,0:T(8,128)(2,1)}, u32[]{:S(2)}, u32[]{:S(2)}) collective-permute-start(bf16[264,384]{1,0:T(8,128)(2,1)} %pad_maximum_fusion.32), channel_id=1, source_target_pairs={{0,3},{1,2},{2,1},{3,0},{4,7},{5,6},{6,5},{7,4},{8,11},{9,10},{10,... | collective-permute-start | bytes 608264 | tf_op jit(solution)/shard_map/ppermute | solution.py:35
  17.3 24.3 %collective-permute-start.3 = (bf16[512,512]{1,0:T(8,128)(2,1)}, bf16[512,512]{1,0:T(8,128)(2,1)}, u32[]{:S(2)}, u32[]{:S(2)}) collective-permute-start(bf16[512,512]{1,0:T(8,128)(2,1)} %pad_maximum_fusion.30), channel_id=1, source_target_pairs={{0,1},{1,0},{2,3},{3,2},{4,5},{5,4},{6,7},{7,6},{8,9},{9,8},{10,11... | collective-permute-start | bytes 1572872 | tf_op jit(solution)/shard_map/ppermute | solution.py:49
  20.6 30.9 %collective-permute-start.4 = (bf16[512,512]{1,0:T(8,128)(2,1)}, bf16[512,512]{1,0:T(8,128)(2,1)}, u32[]{:S(2)}, u32[]{:S(2)}) collective-permute-start(bf16[512,512]{1,0:T(8,128)(2,1)} %pad_maximum_fusion.31), channel_id=1, source_target_pairs={{0,2},{1,3},{2,0},{3,1},{4,6},{5,7},{6,4},{7,5},{8,10},{9,11},{10,... | collective-permute-start | bytes 1572872 | tf_op jit(solution)/shard_map/ppermute | solution.py:49
  57.4 87.9 %all-gather.10.cloned.1.call-start = ((), (), s32[]{:S(2)}) async-start(), calls=%async_computation.2 | async-start | bytes 5898240 | tf_op jit(solution)/shard_map/all_gather | solution.py:668
  57.4 37.9 %collective-permute-start.5 = (bf16[512,512]{1,0:T(8,128)(2,1)S(1)}, bf16[512,512]{1,0:T(8,128)(2,1)S(1)}, u32[]{:S(2)}, u32[]{:S(2)}) collective-permute-start(bf16[512,512]{1,0:T(8,128)(2,1)S(1)} %pad_maximum_fusion.24), channel_id=1, source_target_pairs={{0,3},{1,2},{2,1},{3,0},{4,7},{5,6},{6,5},{7,4},{8,11},{9,10},{10,... | collective-permute-start | bytes 1572872 | tf_op jit(solution)/shard_map/ppermute | solution.py:49
  59.0 19.7 %collective-permute-start.6 = (bf16[160,512]{1,0:T(8,128)(2,1)S(1)}, bf16[160,512]{1,0:T(8,128)(2,1)S(1)}, u32[]{:S(2)}, u32[]{:S(2)}) collective-permute-start(bf16[160,512]{1,0:T(8,128)(2,1)S(1)} %fusion.26), channel_id=1, source_target_pairs={{0,1},{1,0},{2,3},{3,2},{4,5},{5,4},{6,7},{7,6},{8,9},{9,8},{10,11... | collective-permute-start | bytes 491528 | tf_op jit(solution)/shard_map/ppermute | solution.py:35
  62.3 30.3 %collective-permute-start.7 = (bf16[160,512]{1,0:T(8,128)(2,1)S(1)}, bf16[160,512]{1,0:T(8,128)(2,1)S(1)}, u32[]{:S(2)}, u32[]{:S(2)}) collective-permute-start(bf16[160,512]{1,0:T(8,128)(2,1)S(1)} %fusion.26), channel_id=1, source_target_pairs={{0,2},{1,3},{2,0},{3,1},{4,6},{5,7},{6,4},{7,5},{8,10},{9,11},{10,... | collective-permute-start | bytes 491528 | tf_op jit(solution)/shard_map/ppermute | solution.py:35
  63.3 32.0 %collective-permute-start.8 = (bf16[160,512]{1,0:T(8,128)(2,1)S(1)}, bf16[160,512]{1,0:T(8,128)(2,1)S(1)}, u32[]{:S(2)}, u32[]{:S(2)}) collective-permute-start(bf16[160,512]{1,0:T(8,128)(2,1)S(1)} %fusion.26), channel_id=1, source_target_pairs={{0,3},{1,2},{2,1},{3,0},{4,7},{5,6},{6,5},{7,4},{8,11},{9,10},{10,... | collective-permute-start | bytes 491528 | tf_op jit(solution)/shard_map/ppermute | solution.py:35
  96.3 247.5 %all-gather.12.cloned.1.call-start = ((), (), s32[]{:S(2)}) async-start(), calls=%async_computation.3 | async-start | bytes 18874368 | tf_op jit(solution)/shard_map/all_gather | solution.py:720
  106.4 14.8 %collective-permute-start.9 = (bf16[10,64,512]{2,1,0:T(8,128)(2,1)S(1)}, bf16[10,64,512]{2,1,0:T(8,128)(2,1)}, u32[]{:S(2)}, u32[]{:S(2)}) collective-permute-start(bf16[10,64,512]{2,1,0:T(8,128)(2,1)S(1)} %pad_maximum_fusion.21), channel_id=1, source_target_pairs={{0,1},{1,0},{2,3},{3,2},{4,5},{5,4},{6,7},{7,6},{8,9},{9,8},{10,11... | collective-permute-start | bytes 1966088 | tf_op jit(solution)/shard_map/ppermute | solution.py:49
  121.1 32.9 %collective-permute-start.10 = (bf16[512,512]{1,0:T(8,128)(2,1)}, bf16[512,512]{1,0:T(8,128)(2,1)}, u32[]{:S(2)}, u32[]{:S(2)}) collective-permute-start(bf16[512,512]{1,0:T(8,128)(2,1)} %pad_maximum_fusion.26), channel_id=1, source_target_pairs={{0,1},{1,0},{2,3},{3,2},{4,5},{5,4},{6,7},{7,6},{8,9},{9,8},{10,11... | collective-permute-start | bytes 1572872 | tf_op jit(solution)/shard_map/ppermute | solution.py:35
  121.3 37.9 %collective-permute-start.11 = (bf16[512,512]{1,0:T(8,128)(2,1)}, bf16[512,512]{1,0:T(8,128)(2,1)}, u32[]{:S(2)}, u32[]{:S(2)}) collective-permute-start(bf16[512,512]{1,0:T(8,128)(2,1)} %pad_maximum_fusion.27), channel_id=1, source_target_pairs={{0,2},{1,3},{2,0},{3,1},{4,6},{5,7},{6,4},{7,5},{8,10},{9,11},{10,... | collective-permute-start | bytes 1572872 | tf_op jit(solution)/shard_map/ppermute | solution.py:35
  124.1 43.0 %collective-permute-start.12 = (bf16[512,512]{1,0:T(8,128)(2,1)}, bf16[512,512]{1,0:T(8,128)(2,1)}, u32[]{:S(2)}, u32[]{:S(2)}) collective-permute-start(bf16[512,512]{1,0:T(8,128)(2,1)} %pad_maximum_fusion.28), channel_id=1, source_target_pairs={{0,3},{1,2},{2,1},{3,0},{4,7},{5,6},{6,5},{7,4},{8,11},{9,10},{10,... | collective-permute-start | bytes 1572872 | tf_op jit(solution)/shard_map/ppermute | solution.py:35
  167.1 43.6 %collective-permute-start.13 = (bf16[512,2048]{1,0:T(8,128)(2,1)}, bf16[512,2048]{1,0:T(8,128)(2,1)}, u32[]{:S(2)}, u32[]{:S(2)}) collective-permute-start(bf16[512,2048]{1,0:T(8,128)(2,1)} %multiply_convert_fusion.4), channel_id=1, source_target_pairs={{0,8},{4,12},{8,0},{12,4},{16,24},{20,28},{24,16},{28,20},{1,9},{5... | collective-permute-start | bytes 6291464 | tf_op jit(solution)/shard_map/ppermute | solution.py:49
  168.6 43.3 %collective-permute-start.14 = (bf16[512,2048]{1,0:T(8,128)(2,1)}, bf16[512,2048]{1,0:T(8,128)(2,1)}, u32[]{:S(2)}, u32[]{:S(2)}) collective-permute-start(bf16[512,2048]{1,0:T(8,128)(2,1)} %multiply_convert_fusion.4), channel_id=1, source_target_pairs={{0,16},{4,20},{8,24},{12,28},{16,0},{20,4},{24,8},{28,12},{1,17},{... | collective-permute-start | bytes 6291464 | tf_op jit(solution)/shard_map/ppermute | solution.py:49
  170.2 33.7 %collective-permute-start.15 = (bf16[2048,384]{0,1:T(8,128)(2,1)}, bf16[2048,384]{0,1:T(8,128)(2,1)}, u32[]{:S(2)}, u32[]{:S(2)}) collective-permute-start(bf16[2048,384]{0,1:T(8,128)(2,1)} %pad_maximum_fusion.7), channel_id=1, source_target_pairs={{0,1},{1,2},{2,3},{4,5},{5,6},{6,7},{8,9},{9,10},{10,11},{12,13},{... | collective-permute-start | bytes 4718600 | tf_op jit(solution)/shard_map/ppermute | solution.py:79
  172.1 33.7 %collective-permute-start.16 = (bf16[2048,384]{0,1:T(8,128)(2,1)}, bf16[2048,384]{0,1:T(8,128)(2,1)}, u32[]{:S(2)}, u32[]{:S(2)}) collective-permute-start(bf16[2048,384]{0,1:T(8,128)(2,1)} %pad_maximum_fusion.7), channel_id=1, source_target_pairs={{3,2},{2,1},{1,0},{7,6},{6,5},{5,4},{11,10},{10,9},{9,8},{15,14},{... | collective-permute-start | bytes 4718600 | tf_op jit(solution)/shard_map/ppermute | solution.py:79
  211.9 37.9 %collective-permute-start.19 = (bf16[2048,384]{0,1:T(8,128)(2,1)}, bf16[2048,384]{0,1:T(8,128)(2,1)S(1)}, u32[]{:S(2)}, u32[]{:S(2)}) collective-permute-start(bf16[2048,384]{0,1:T(8,128)(2,1)} %collective-permute-done.15), channel_id=1, source_target_pairs={{1,2},{2,3},{5,6},{6,7},{9,10},{10,11},{13,14},{14,15},{17,18},{18... | collective-permute-start | bytes 4718600 | tf_op jit(solution)/shard_map/ppermute | solution.py:79
  213.8 36.9 %collective-permute-start.20 = (bf16[2048,384]{0,1:T(8,128)(2,1)}, bf16[2048,384]{0,1:T(8,128)(2,1)}, u32[]{:S(2)}, u32[]{:S(2)}) collective-permute-start(bf16[2048,384]{0,1:T(8,128)(2,1)} %collective-permute-done.16), channel_id=1, source_target_pairs={{2,1},{1,0},{6,5},{5,4},{10,9},{9,8},{14,13},{13,12},{18,17},{17,1... | collective-permute-start | bytes 4718600 | tf_op jit(solution)/shard_map/ppermute | solution.py:79
  227.9 19.1 %collective-permute-start.17 = (bf16[256,2048]{1,0:T(8,128)(2,1)S(1)}, bf16[256,2048]{1,0:T(8,128)(2,1)S(1)}, u32[]{:S(2)}, u32[]{:S(2)}) collective-permute-start(bf16[256,2048]{1,0:T(8,128)(2,1)S(1)} %slice.424), channel_id=1, source_target_pairs={{0,16},{4,20},{8,24},{12,28},{16,0},{20,4},{24,8},{28,12},{1,17},{... | collective-permute-start | bytes 3145736 | tf_op jit(solution)/shard_map/ppermute | solution.py:49
  230.9 18.9 %collective-permute-start.18 = (bf16[256,2048]{1,0:T(8,128)(2,1)S(1)}, bf16[256,2048]{1,0:T(8,128)(2,1)S(1)}, u32[]{:S(2)}, u32[]{:S(2)}) collective-permute-start(bf16[256,2048]{1,0:T(8,128)(2,1)S(1)} %slice.425), channel_id=1, source_target_pairs={{0,8},{4,12},{8,0},{12,4},{16,24},{20,28},{24,16},{28,20},{1,9},{5... | collective-permute-start | bytes 3145736 | tf_op jit(solution)/shard_map/ppermute | solution.py:49
  250.8 344.9 %reduce-scatter.2.cloned.1.call-start = ((), (), s32[]{:S(2)}) async-start(), calls=%async_computation.4 | async-start | bytes 7864320 | tf_op jit(solution)/shard_map/reduce_scatter | solution.py:778
  253.5 35.9 %collective-permute-start.21 = (bf16[2048,2048]{1,0:T(8,128)(2,1)}, bf16[2048,2048]{1,0:T(8,128)(2,1)S(1)}, u32[]{:S(2)}, u32[]{:S(2)}) collective-permute-start(bf16[2048,2048]{1,0:T(8,128)(2,1)} %bitcast.31), channel_id=1, source_target_pairs={{0,4},{4,0},{8,12},{12,8},{16,20},{20,16},{24,28},{28,24},{1,5},{5... | collective-permute-start | bytes 25165832 | tf_op jit(solution)/shard_map/ppermute | solution.py:49
  253.5 35.9 %collective-permute-start.22 = (bf16[2048,384]{0,1:T(8,128)(2,1)S(1)}, bf16[2048,384]{0,1:T(8,128)(2,1)S(1)}, u32[]{:S(2)}, u32[]{:S(2)}) collective-permute-start(bf16[2048,384]{0,1:T(8,128)(2,1)S(1)} %collective-permute-done.19), channel_id=1, source_target_pairs={{2,3},{6,7},{10,11},{14,15},{18,19},{22,23},{26,27},{30,31}} | collective-permute-start | bytes 4718600 | tf_op jit(solution)/shard_map/ppermute | solution.py:79
  254.8 34.5 %collective-permute-start.23 = (bf16[2048,384]{0,1:T(8,128)(2,1)}, bf16[2048,384]{0,1:T(8,128)(2,1)S(1)}, u32[]{:S(2)}, u32[]{:S(2)}) collective-permute-start(bf16[2048,384]{0,1:T(8,128)(2,1)} %collective-permute-done.20), channel_id=1, source_target_pairs={{1,0},{5,4},{9,8},{13,12},{17,16},{21,20},{25,24},{29,28}} | collective-permute-start | bytes 4718600 | tf_op jit(solution)/shard_map/ppermute | solution.py:79
  380.2 24.2 %collective-permute-start.24 = (bf16[2048,2048]{1,0:T(8,128)(2,1)}, bf16[2048,2048]{1,0:T(8,128)(2,1)}, u32[]{:S(2)}, u32[]{:S(2)}) collective-permute-start(bf16[2048,2048]{1,0:T(8,128)(2,1)} %convolution_convert_fusion.1), channel_id=1, source_target_pairs={{0,4},{4,0},{8,12},{12,8},{16,20},{20,16},{24,28},{28,24},{1,5},{5... | collective-permute-start | bytes 25165832 | tf_op jit(solution)/shard_map/ppermute | solution.py:49
  380.3 75.8 %collective-permute-start.27 = (bf16[2048,2048]{1,0:T(8,128)(2,1)}, bf16[2048,2048]{1,0:T(8,128)(2,1)}, u32[]{:S(2)}, u32[]{:S(2)}) collective-permute-start(bf16[2048,2048]{1,0:T(8,128)(2,1)} %convolution_convert_fusion.2), channel_id=1, source_target_pairs={{0,4},{4,0},{8,12},{12,8},{16,20},{20,16},{24,28},{28,24},{1,5},{5... | collective-permute-start | bytes 25165832 | tf_op jit(solution)/shard_map/ppermute | solution.py:49
  415.4 47.8 %collective-permute-start.25 = (bf16[512,2048]{1,0:T(8,128)(2,1)S(1)}, bf16[512,2048]{1,0:T(8,128)(2,1)}, u32[]{:S(2)}, u32[]{:S(2)}) collective-permute-start(bf16[512,2048]{1,0:T(8,128)(2,1)S(1)} %get-tuple-element.260), channel_id=1, source_target_pairs={{0,8},{4,12},{8,0},{12,4},{16,24},{20,28},{24,16},{28,20},{1,9},{5... | collective-permute-start | bytes 6291464 | tf_op jit(solution)/shard_map/ppermute | solution.py:49
  416.2 47.4 %collective-permute-start.26 = (bf16[512,2048]{1,0:T(8,128)(2,1)S(1)}, bf16[512,2048]{1,0:T(8,128)(2,1)}, u32[]{:S(2)}, u32[]{:S(2)}) collective-permute-start(bf16[512,2048]{1,0:T(8,128)(2,1)S(1)} %get-tuple-element.261), channel_id=1, source_target_pairs={{0,16},{4,20},{8,24},{12,28},{16,0},{20,4},{24,8},{28,12},{1,17},{... | collective-permute-start | bytes 6291464 | tf_op jit(solution)/shard_map/ppermute | solution.py:49
  469.5 298.1 %all-gather.18.cloned.1.call-start = ((), (), s32[]{:S(2)}) async-start(), calls=%async_computation.7 | async-start | bytes 14155776 | tf_op jit(solution)/shard_map/all_gather | solution.py:824
  472.6 24.1 %collective-permute-start.28 = (bf16[256,2048]{1,0:T(8,128)(2,1)S(1)}, bf16[256,2048]{1,0:T(8,128)(2,1)}, u32[]{:S(2)}, u32[]{:S(2)}) collective-permute-start(bf16[256,2048]{1,0:T(8,128)(2,1)S(1)} %get-tuple-element.385), channel_id=1, source_target_pairs={{0,16},{4,20},{8,24},{12,28},{16,0},{20,4},{24,8},{28,12},{1,17},{... | collective-permute-start | bytes 3145736 | tf_op jit(solution)/shard_map/ppermute | solution.py:49
  473.0 23.8 %collective-permute-start.29 = (bf16[256,2048]{1,0:T(8,128)(2,1)S(1)}, bf16[256,2048]{1,0:T(8,128)(2,1)}, u32[]{:S(2)}, u32[]{:S(2)}) collective-permute-start(bf16[256,2048]{1,0:T(8,128)(2,1)S(1)} %get-tuple-element.384), channel_id=1, source_target_pairs={{0,8},{4,12},{8,0},{12,4},{16,24},{20,28},{24,16},{28,20},{1,9},{5... | collective-permute-start | bytes 3145736 | tf_op jit(solution)/shard_map/ppermute | solution.py:49
  508.3 41.9 %collective-permute-start.32 = (bf16[640,2048]{1,0:T(8,128)(2,1)S(1)}, bf16[640,2048]{1,0:T(8,128)(2,1)S(1)}, u32[]{:S(2)}, u32[]{:S(2)}) collective-permute-start(bf16[640,2048]{1,0:T(8,128)(2,1)S(1)} %convolution_convert_fusion.4), channel_id=1, source_target_pairs={{0,4},{4,0},{8,12},{12,8},{16,20},{20,16},{24,28},{28,24},{1,5},{5... | collective-permute-start | bytes 7864328 | tf_op jit(solution)/shard_map/ppermute | solution.py:49
  508.5 41.7 %collective-permute-start.30 = (bf16[256,2048]{1,0:T(8,128)(2,1)S(1)}, bf16[256,2048]{1,0:T(8,128)(2,1)S(1)}, u32[]{:S(2)}, u32[]{:S(2)}) collective-permute-start(bf16[256,2048]{1,0:T(8,128)(2,1)S(1)} %get-tuple-element.276), channel_id=1, source_target_pairs={{0,8},{4,12},{8,0},{12,4},{16,24},{20,28},{24,16},{28,20},{1,9},{5... | collective-permute-start | bytes 3145736 | tf_op jit(solution)/shard_map/ppermute | solution.py:49
  510.0 40.2 %collective-permute-start.31 = (bf16[256,2048]{1,0:T(8,128)(2,1)S(1)}, bf16[256,2048]{1,0:T(8,128)(2,1)S(1)}, u32[]{:S(2)}, u32[]{:S(2)}) collective-permute-start(bf16[256,2048]{1,0:T(8,128)(2,1)S(1)} %get-tuple-element.277), channel_id=1, source_target_pairs={{0,16},{4,20},{8,24},{12,28},{16,0},{20,4},{24,8},{28,12},{1,17},{... | collective-permute-start | bytes 3145736 | tf_op jit(solution)/shard_map/ppermute | solution.py:49
  552.2 17.7 %collective-permute-start.36 = (bf16[160,2048]{1,0:T(8,128)(2,1)S(1)}, bf16[160,2048]{1,0:T(8,128)(2,1)S(1)}, u32[]{:S(2)}, u32[]{:S(2)}) collective-permute-start(bf16[160,2048]{1,0:T(8,128)(2,1)S(1)} %get-tuple-element.288), channel_id=1, source_target_pairs={{0,8},{4,12},{8,0},{12,4},{16,24},{20,28},{24,16},{28,20},{1,9},{5... | collective-permute-start | bytes 1966088 | tf_op jit(solution)/shard_map/ppermute | solution.py:49
  552.9 17.6 %collective-permute-start.37 = (bf16[160,2048]{1,0:T(8,128)(2,1)S(1)}, bf16[160,2048]{1,0:T(8,128)(2,1)S(1)}, u32[]{:S(2)}, u32[]{:S(2)}) collective-permute-start(bf16[160,2048]{1,0:T(8,128)(2,1)S(1)} %get-tuple-element.289), channel_id=1, source_target_pairs={{0,16},{4,20},{8,24},{12,28},{16,0},{20,4},{24,8},{28,12},{1,17},{... | collective-permute-start | bytes 1966088 | tf_op jit(solution)/shard_map/ppermute | solution.py:49
  554.2 37.4 %collective-permute-start.34 = (bf16[256,2048]{1,0:T(8,128)(2,1)S(1)}, bf16[256,2048]{1,0:T(8,128)(2,1)S(1)}, u32[]{:S(2)}, u32[]{:S(2)}) collective-permute-start(bf16[256,2048]{1,0:T(8,128)(2,1)S(1)} %get-tuple-element.381), channel_id=1, source_target_pairs={{0,16},{4,20},{8,24},{12,28},{16,0},{20,4},{24,8},{28,12},{1,17},{... | collective-permute-start | bytes 3145736 | tf_op jit(solution)/shard_map/ppermute | solution.py:49
  555.9 36.7 %collective-permute-start.35 = (bf16[256,2048]{1,0:T(8,128)(2,1)S(1)}, bf16[256,2048]{1,0:T(8,128)(2,1)}, u32[]{:S(2)}, u32[]{:S(2)}) collective-permute-start(bf16[256,2048]{1,0:T(8,128)(2,1)S(1)} %get-tuple-element.380), channel_id=1, source_target_pairs={{0,8},{4,12},{8,0},{12,4},{16,24},{20,28},{24,16},{28,20},{1,9},{5... | collective-permute-start | bytes 3145736 | tf_op jit(solution)/shard_map/ppermute | solution.py:49
  558.1 31.4 %collective-permute-start.33 = (bf16[10,64,512]{2,1,0:T(8,128)(2,1)S(1)}, bf16[10,64,512]{2,1,0:T(8,128)(2,1)S(1)}, u32[]{:S(2)}, u32[]{:S(2)}) collective-permute-start(bf16[10,64,512]{2,1,0:T(8,128)(2,1)S(1)} %select_convert_fusion), channel_id=1, source_target_pairs={{0,1},{1,0},{2,3},{3,2},{4,5},{5,4},{6,7},{7,6},{8,9},{9,8},{10,11... | collective-permute-start | bytes 1966088 | tf_op jit(solution)/shard_map/ppermute | solution.py:49
  595.7 189.5 %all-gather.14.cloned.1.call-start = ((), (), s32[]{:S(2)}) async-start(), calls=%async_computation.5 | async-start | bytes 1474560 | tf_op jit(solution)/shard_map/all_gather | solution.py:890
  607.8 20.2 %collective-permute-start.38 = (bf16[1024,2048]{1,0:T(8,128)(2,1)}, bf16[1024,2048]{1,0:T(8,128)(2,1)S(1)}, u32[]{:S(2)}, u32[]{:S(2)}) collective-permute-start(bf16[1024,2048]{1,0:T(8,128)(2,1)} %add_convert_fusion.1), channel_id=1, source_target_pairs={{0,4},{4,0},{8,12},{12,8},{16,20},{20,16},{24,28},{28,24},{1,5},{5... | collective-permute-start | bytes 12582920 | tf_op jit(solution)/shard_map/ppermute | solution.py:49
  608.9 17.7 %collective-permute-start.39 = (bf16[80,2048]{1,0:T(8,128)(2,1)}, bf16[80,2048]{1,0:T(8,128)(2,1)}, u32[]{:S(2)}, u32[]{:S(2)}) collective-permute-start(bf16[80,2048]{1,0:T(8,128)(2,1)} %get-tuple-element.451), channel_id=1, source_target_pairs={{0,16},{4,20},{8,24},{12,28},{16,0},{20,4},{24,8},{28,12},{1,17},{... | collective-permute-start | bytes 983048 | tf_op jit(solution)/shard_map/ppermute | solution.py:49
  610.3 17.6 %collective-permute-start.40 = (bf16[80,2048]{1,0:T(8,128)(2,1)}, bf16[80,2048]{1,0:T(8,128)(2,1)}, u32[]{:S(2)}, u32[]{:S(2)}) collective-permute-start(bf16[80,2048]{1,0:T(8,128)(2,1)} %get-tuple-element.450), channel_id=1, source_target_pairs={{0,8},{4,12},{8,0},{12,4},{16,24},{20,28},{24,16},{28,20},{1,9},{5... | collective-permute-start | bytes 983048 | tf_op jit(solution)/shard_map/ppermute | solution.py:49
  631.0 50.6 %collective-permute-start.44 = (bf16[256,2048]{1,0:T(8,128)(2,1)S(1)}, bf16[256,2048]{1,0:T(8,128)(2,1)S(1)}, u32[]{:S(2)}, u32[]{:S(2)}) collective-permute-start(bf16[256,2048]{1,0:T(8,128)(2,1)S(1)} %get-tuple-element.308), channel_id=1, source_target_pairs={{0,8},{4,12},{8,0},{12,4},{16,24},{20,28},{24,16},{28,20},{1,9},{5... | collective-permute-start | bytes 3145736 | tf_op jit(solution)/shard_map/ppermute | solution.py:49
  632.6 49.1 %collective-permute-start.45 = (bf16[256,2048]{1,0:T(8,128)(2,1)S(1)}, bf16[256,2048]{1,0:T(8,128)(2,1)S(1)}, u32[]{:S(2)}, u32[]{:S(2)}) collective-permute-start(bf16[256,2048]{1,0:T(8,128)(2,1)S(1)} %get-tuple-element.309), channel_id=1, source_target_pairs={{0,16},{4,20},{8,24},{12,28},{16,0},{20,4},{24,8},{28,12},{1,17},{... | collective-permute-start | bytes 3145736 | tf_op jit(solution)/shard_map/ppermute | solution.py:49
  634.1 19.3 %collective-permute-start.41 = (bf16[512,512]{1,0:T(8,128)(2,1)S(1)}, bf16[512,512]{1,0:T(8,128)(2,1)S(1)}, u32[]{:S(2)}, u32[]{:S(2)}) collective-permute-start(bf16[512,512]{1,0:T(8,128)(2,1)S(1)} %get-tuple-element.406), channel_id=1, source_target_pairs={{0,1},{1,0},{2,3},{3,2},{4,5},{5,4},{6,7},{7,6},{8,9},{9,8},{10,11... | collective-permute-start | bytes 1572872 | tf_op jit(solution)/shard_map/ppermute | solution.py:35
  634.5 34.9 %collective-permute-start.42 = (bf16[512,512]{1,0:T(8,128)(2,1)S(1)}, bf16[512,512]{1,0:T(8,128)(2,1)S(1)}, u32[]{:S(2)}, u32[]{:S(2)}) collective-permute-start(bf16[512,512]{1,0:T(8,128)(2,1)S(1)} %get-tuple-element.407), channel_id=1, source_target_pairs={{0,2},{1,3},{2,0},{3,1},{4,6},{5,7},{6,4},{7,5},{8,10},{9,11},{10,... | collective-permute-start | bytes 1572872 | tf_op jit(solution)/shard_map/ppermute | solution.py:35
  634.5 47.1 %collective-permute-start.43 = (bf16[512,512]{1,0:T(8,128)(2,1)S(1)}, bf16[512,512]{1,0:T(8,128)(2,1)S(1)}, u32[]{:S(2)}, u32[]{:S(2)}) collective-permute-start(bf16[512,512]{1,0:T(8,128)(2,1)S(1)} %get-tuple-element.404), channel_id=1, source_target_pairs={{0,3},{1,2},{2,1},{3,0},{4,7},{5,6},{6,5},{7,4},{8,11},{9,10},{10,... | collective-permute-start | bytes 1572872 | tf_op jit(solution)/shard_map/ppermute | solution.py:35
  683.1 19.8 %collective-permute-start.49 = (bf16[128,2048]{1,0:T(8,128)(2,1)}, bf16[128,2048]{1,0:T(8,128)(2,1)}, u32[]{:S(2)}, u32[]{:S(2)}) collective-permute-start(bf16[128,2048]{1,0:T(8,128)(2,1)} %get-tuple-element.403), channel_id=1, source_target_pairs={{0,16},{4,20},{8,24},{12,28},{16,0},{20,4},{24,8},{28,12},{1,17},{... | collective-permute-start | bytes 1572872 | tf_op jit(solution)/shard_map/ppermute | solution.py:49
  684.5 18.3 %collective-permute-start.50 = (bf16[128,2048]{1,0:T(8,128)(2,1)}, bf16[128,2048]{1,0:T(8,128)(2,1)}, u32[]{:S(2)}, u32[]{:S(2)}) collective-permute-start(bf16[128,2048]{1,0:T(8,128)(2,1)} %get-tuple-element.402), channel_id=1, source_target_pairs={{0,8},{4,12},{8,0},{12,4},{16,24},{20,28},{24,16},{28,20},{1,9},{5... | collective-permute-start | bytes 1572872 | tf_op jit(solution)/shard_map/ppermute | solution.py:49
  687.8 14.1 %collective-permute-start.48 = (bf16[160,512]{1,0:T(8,128)(2,1)}, bf16[160,512]{1,0:T(8,128)(2,1)S(1)}, u32[]{:S(2)}, u32[]{:S(2)}) collective-permute-start(bf16[160,512]{1,0:T(8,128)(2,1)} %get-tuple-element.365), channel_id=1, source_target_pairs={{0,3},{1,2},{2,1},{3,0},{4,7},{5,6},{6,5},{7,4},{8,11},{9,10},{10,... | collective-permute-start | bytes 491528 | tf_op jit(solution)/shard_map/ppermute | solution.py:35
  693.9 30.9 %collective-permute-start.54 = (bf16[256,2048]{1,0:T(8,128)(2,1)S(1)}, bf16[256,2048]{1,0:T(8,128)(2,1)}, u32[]{:S(2)}, u32[]{:S(2)}) collective-permute-start(bf16[256,2048]{1,0:T(8,128)(2,1)S(1)} %copy-done.21), channel_id=1, source_target_pairs={{0,8},{4,12},{8,0},{12,4},{16,24},{20,28},{24,16},{28,20},{1,9},{5... | collective-permute-start | bytes 3145736 | tf_op jit(solution)/shard_map/ppermute | solution.py:49
  697.9 28.1 %collective-permute-start.55 = (bf16[256,2048]{1,0:T(8,128)(2,1)S(1)}, bf16[256,2048]{1,0:T(8,128)(2,1)}, u32[]{:S(2)}, u32[]{:S(2)}) collective-permute-start(bf16[256,2048]{1,0:T(8,128)(2,1)S(1)} %copy-done.19), channel_id=1, source_target_pairs={{0,16},{4,20},{8,24},{12,28},{16,0},{20,4},{24,8},{28,12},{1,17},{... | collective-permute-start | bytes 3145736 | tf_op jit(solution)/shard_map/ppermute | solution.py:49
  710.6 122.1 %all-gather.16.cloned.1.call-start = ((), (), s32[]{:S(2)}) async-start(), calls=%async_computation.6 | async-start | bytes 5308416 | tf_op jit(solution)/shard_map/all_gather | solution.py:914
  714.5 21.9 %collective-permute-start.51 = (bf16[256,1152]{1,0:T(8,128)(2,1)S(1)}, bf16[256,1152]{1,0:T(8,128)(2,1)S(1)}, u32[]{:S(2)}, u32[]{:S(2)}) collective-permute-start(bf16[256,1152]{1,0:T(8,128)(2,1)S(1)} %get-tuple-element.480), channel_id=1, source_target_pairs={{0,1},{1,0},{2,3},{3,2},{4,5},{5,4},{6,7},{7,6},{8,9},{9,8},{10,11... | collective-permute-start | bytes 1769480 | tf_op jit(solution)/shard_map/ppermute | solution.py:35
  715.2 39.7 %collective-permute-start.52 = (bf16[256,1152]{1,0:T(8,128)(2,1)S(1)}, bf16[256,1152]{1,0:T(8,128)(2,1)S(1)}, u32[]{:S(2)}, u32[]{:S(2)}) collective-permute-start(bf16[256,1152]{1,0:T(8,128)(2,1)S(1)} %get-tuple-element.481), channel_id=1, source_target_pairs={{0,2},{1,3},{2,0},{3,1},{4,6},{5,7},{6,4},{7,5},{8,10},{9,11},{10,... | collective-permute-start | bytes 1769480 | tf_op jit(solution)/shard_map/ppermute | solution.py:35
  715.8 51.8 %collective-permute-start.53 = (bf16[256,1152]{1,0:T(8,128)(2,1)S(1)}, bf16[256,1152]{1,0:T(8,128)(2,1)}, u32[]{:S(2)}, u32[]{:S(2)}) collective-permute-start(bf16[256,1152]{1,0:T(8,128)(2,1)S(1)} %get-tuple-element.479), channel_id=1, source_target_pairs={{0,3},{1,2},{2,1},{3,0},{4,7},{5,6},{6,5},{7,4},{8,11},{9,10},{10,... | collective-permute-start | bytes 1769480 | tf_op jit(solution)/shard_map/ppermute | solution.py:35
  781.7 23.8 %collective-permute-start.56 = (bf16[512,512]{1,0:T(8,128)(2,1)}, bf16[512,512]{1,0:T(8,128)(2,1)S(1)}, u32[]{:S(2)}, u32[]{:S(2)}) collective-permute-start(bf16[512,512]{1,0:T(8,128)(2,1)} %get-tuple-element.396), channel_id=1, source_target_pairs={{0,1},{1,0},{2,3},{3,2},{4,5},{5,4},{6,7},{7,6},{8,9},{9,8},{10,11... | collective-permute-start | bytes 1572872 | tf_op jit(solution)/shard_map/ppermute | solution.py:35
  781.7 35.9 %collective-permute-start.57 = (bf16[512,512]{1,0:T(8,128)(2,1)S(1)}, bf16[512,512]{1,0:T(8,128)(2,1)S(1)}, u32[]{:S(2)}, u32[]{:S(2)}) collective-permute-start(bf16[512,512]{1,0:T(8,128)(2,1)S(1)} %get-tuple-element.397), channel_id=1, source_target_pairs={{0,2},{1,3},{2,0},{3,1},{4,6},{5,7},{6,4},{7,5},{8,10},{9,11},{10,... | collective-permute-start | bytes 1572872 | tf_op jit(solution)/shard_map/ppermute | solution.py:35
  782.8 44.8 %collective-permute-start.58 = (bf16[512,512]{1,0:T(8,128)(2,1)S(1)}, bf16[512,512]{1,0:T(8,128)(2,1)S(1)}, u32[]{:S(2)}, u32[]{:S(2)}) collective-permute-start(bf16[512,512]{1,0:T(8,128)(2,1)S(1)} %get-tuple-element.394), channel_id=1, source_target_pairs={{0,3},{1,2},{2,1},{3,0},{4,7},{5,6},{6,5},{7,4},{8,11},{9,10},{10,... | collective-permute-start | bytes 1572872 | tf_op jit(solution)/shard_map/ppermute | solution.py:35
  (135 other events, 1200.0 us)
Sparse Core Ops, SparseCore 0:
  57.5 44.0 all-gather.7
  104.1 41.1 all-gather.9
  250.9 88.0 all-gather.11
  469.7 125.9 reduce-scatter.1
  597.4 100.9 all-gather.17
  710.7 24.6 all-gather.13
  770.5 37.9 all-gather.15

commit v5 on v4

--- a/solution.py
+++ b/solution.py
@@ -458,6 +458,58 @@
     )(starts, queries, keys, values, grads, sums_in)
 
 
+def gates_back(hidden_grad, raised):
+    half = raised.shape[1] // 2
+    gate, up = raised[:, :half], raised[:, half:]
+    sigma = jax.nn.sigmoid(gate)
+    gate_grad = hidden_grad * up * sigma * (1.0 + gate * (1.0 - sigma))
+    return gate_grad.astype(low), (hidden_grad * gate * sigma).astype(low)
+
+
+def units_back_whole(cotangent, raised, down, wide):
+    grad = jnp.concatenate(gates_back(mm(cotangent, down), raised), 1)
+    return grad, dot(grad, wide, 1, 1).astype(low)
+
+
+def units_back_kernel(core, cot_ref, raised_ref, down_ref, wide_ref, grad_ref, out_ref):
+    half = down_ref.shape[1]
+    gate_grad, up_grad = gates_back(mm(cot_ref[0, 0], down_ref[...]), raised_ref[...])
+    grad_ref[:, :half] = gate_grad
+    grad_ref[:, half:] = up_grad
+    out_ref[...] = dot(grad_ref[...], wide_ref[...], 1, 1).astype(low)
+
+
+def units_back(cotangent, core, raised, down, wide):
+    rows, columns = raised.shape[0] // 4, raised.shape[1]
+    width = cotangent.shape[1]
+    once = lambda array: pl.BlockSpec(
+        array.shape, lambda g, core: (0, 0), pipeline_mode=pl.Buffered(1)
+    )
+    return pl.pallas_call(
+        units_back_kernel,
+        out_shape=(
+            jax.ShapeDtypeStruct(raised.shape, low),
+            jax.ShapeDtypeStruct((4 * rows, width), low),
+        ),
+        grid_spec=pltpu.PrefetchScalarGridSpec(
+            num_scalar_prefetch=1,
+            grid=(4,),
+            in_specs=[
+                pl.BlockSpec((1, 1, rows, width), lambda g, core: (g, core[0], 0, 0)),
+                pl.BlockSpec((rows, columns), lambda g, core: (g, 0)),
+                once(down),
+                once(wide),
+            ],
+            out_specs=[
+                pl.BlockSpec((rows, columns), lambda g, core: (g, 0)),
+                pl.BlockSpec((rows, width), lambda g, core: (g, 0)),
+            ],
+        ),
+        compiler_params=pltpu.CompilerParams(vmem_limit_bytes=44 << 20),
+        cost_estimate=pl.CostEstimate(flops=0, bytes_accessed=1 << 16, transcendentals=0),
+    )(core.astype(jnp.int32).reshape(1), cotangent.reshape(4, 2, rows, width), raised, down, wide)
+
+
 def by_ranks(wide, down, rank, parts):
     rows, units = wide.shape[0], wide.shape[1] // (2 * parts)
     place = lambda r: (rank - r) % parts
@@ -738,35 +790,34 @@
     down_terms, raised, hidden, (cotangent_full,) = order_split(
         order, [], down_terms, raised, hidden, [cotangent_full]
     )
-    def cores(array, at):
-        if not cube:
-            return array
-        array = array.reshape(4, 2, mine, D)
-        return lax.dynamic_index_in_dim(array, at, 1, keepdims=False).reshape(4 * mine, D)
-
-    cot = [cores(cotangent_full, at) for at in ((group % 2, 1 - group % 2) if cube else (0,))]
-
-    def back(part, v):
-        hidden_grad = mm(part, down_here)
-        gate, up = v[:, :half], v[:, half:]
-        sigma = jax.nn.sigmoid(gate)
-        gate_grad = hidden_grad * up * sigma * (1.0 + gate * (1.0 - sigma))
-        return jnp.concatenate([gate_grad.astype(low), (hidden_grad * gate * sigma).astype(low)], 1)
-
-    grads = [back(cot[-1], raised[-1])]
-    other = dot(grads[0], wide, 1, 1).astype(low)
+
+    core = group % 2
+    if cube:
+        back = lambda at, v: units_back(cotangent_full, at, v, down_here, wide)
+    else:
+        back = lambda at, v: units_back_whole(cotangent_full, v, down_here, wide)
+    grad, other = back(1 - core, raised[-1])
+    grads = [grad]
     other, grads[0], *raised = order(other, grads[0], *raised)
 
     second_sum = Collect(other, "dp", groups, group)
     own = other
     if len(raised) > 1:
-        grads.insert(0, back(cot[0], raised[0]))
-        own = dot(grads[0], wide, 1, 1).astype(low)
+        grad, own = back(core, raised[0])
+        grads.insert(0, grad)
     own, *grads, hidden, got = order_split(order, [own, *grads], hidden, second_sum.flying)
 
     second_sum.second(own, *got)
     wide_grad = sum(dot(part, grad, 0, 0) for part, grad in zip(second.parts, grads)).astype(low)
-    down_grad = sum(dot(part, h, 0, 0) for part, h in zip(cot, hidden)).astype(low)
+    if cube:
+        shape = (4, 1, mine, half)
+        first, last = (h.reshape(shape) for h in hidden)
+        hidden_full = jnp.concatenate(
+            [jnp.where(core == 0, first, last), jnp.where(core == 0, last, first)], 1
+        ).reshape(2 * 4 * mine, half)
+    else:
+        hidden_full = hidden[0]
+    down_grad = dot(cotangent_full, hidden_full, 0, 0).astype(low)
     down_sum = Collect(down_terms[-1], "dp", groups, group)
     down_grad, wide_grad, got, flying = order_split(
         order, [down_grad, wide_grad], second_sum.flying, down_sum.flying

time: 858 us -> 844 us (0.984)
  matrix products: 179 us -> 128 us
  Pallas kernels: 84.1 us -> 124 us
    pallas_call x0 -> x2, Pallas kernels: none -> 39.6 us  [units_back(): pl.pallas_call(units_back_kernel, out_shape=(jax.ShapeDtypeStruct(raised....]
    dot_general x8 -> x6, matrix products: 60.9 us -> 32.7 us  [mm(): return jnp.dot(left, right, preferred_element_type=full)]
    dot_general x20 -> x17, matrix products: 118 us -> 95.5 us  [dot(): lax.dot_general(left, right, (((left_axis,), (right_axis,)), ((), ())), p...]
    unnamed x281 -> x278, local copies, waits for them, and re-layouts: 37.5 us -> 47.9 us
  transfers between devices with their start and end apart: 66 -> 66, of which waited for: 41 -> 40; matrix products, arithmetic and copies ran while one was open for 34% -> 31% of each run, Pallas kernels for 9% -> 12%
where the time goes in v5:
time: 844 us; the launch traced here: 836 us
  waiting for transfers between devices  306 us (36%)
  matrix products  128 us (15%)
  Pallas kernels  124 us (15%)
  other arithmetic  98.7 us (12%)
  local copies, waits for them, and re-layouts  90.1 us (11%)
  starting transfers between devices  71.7 us (8%)
  between operations  16.6 us (2%)
    ppermute x21, waiting for transfers between devices, swap(): lax.ppermute(pieces[k], axis, [(i, i ^ k) for i in range(n)])  159 us
    dot_general x17, matrix products, dot(): lax.dot_general(left, right, (((left_axis,), (right_axis,)), ((), ())), p...  95.5 us
    ppermute x32, waiting for transfers between devices, exchange(): return lax.ppermute(array, axis, [(i, i ^ mask) for i in range(n)])  91.3 us
    ppermute x3, waiting for transfers between devices, send(): lax.ppermute(up, self.axis, right)  49.5 us
    unnamed x278, local copies, waits for them, and re-layouts  47.9 us
    pallas_call x2, Pallas kernels, units_back(): pl.pallas_call(units_back_kernel, out_shape=(jax.ShapeDtypeStruct(raised....  39.6 us
    dot_general x6, matrix products, mm(): return jnp.dot(left, right, preferred_element_type=full)  32.7 us
    ppermute x32, starting transfers between devices, exchange(): return lax.ppermute(array, axis, [(i, i ^ mask) for i in range(n)])  30 us
  transfers between devices with their start and end apart: 66, of which 40 were waited for; matrix products, arithmetic and copies ran while one was open for 31% of the time, Pallas kernels for 12%

profile of v5, /device:TPU:16, one launch (start us, length us, event | category | flops | bytes accessed | tf_op | source)
XLA Modules:
  0.0 835.7 jit_solution(11454662937484660015)
XLA Ops:
  13.1 3.3 constant_dynamic-slice_fusion.8
  25.5 3.6 iota_compare_fusion
  41.5 9.9 %collective-permute-done.4 = bf16[512,512]{1,0:T(8,128)(2,1)} collective-permute-done((bf16[512,512]{1,0:T(8,128)(2,1)}, bf16[512,512]{1,0:T(8,128)(2,1)}, u32[]{:S(2)}, u32[]{:S(2)}) %collective-permute-start.4) | collective-permute-done | bytes 524320 | tf_op jit(solution)/shard_map/ppermute | solution.py:49
  59.0 3.3 collective-permute-start.6
  63.9 14.8 %collective-permute-done.6 = bf16[160,512]{1,0:T(8,128)(2,1)S(1)} collective-permute-done((bf16[160,512]{1,0:T(8,128)(2,1)S(1)}, bf16[160,512]{1,0:T(8,128)(2,1)S(1)}, u32[]{:S(2)}, u32[]{:S(2)}) %collective-permute-start.6) | collective-permute-done | bytes 163872 | tf_op jit(solution)/shard_map/ppermute | solution.py:35
  78.7 13.9 %collective-permute-done.7 = bf16[160,512]{1,0:T(8,128)(2,1)S(1)} collective-permute-done((bf16[160,512]{1,0:T(8,128)(2,1)S(1)}, bf16[160,512]{1,0:T(8,128)(2,1)S(1)}, u32[]{:S(2)}, u32[]{:S(2)}) %collective-permute-start.7) | collective-permute-done | bytes 163872 | tf_op jit(solution)/shard_map/ppermute | solution.py:35
  106.4 5.5 fusion.82
  114.8 6.3 collective-permute-done.9
  126.1 14.6 %shard_map.246 = (bf16[20,64,512]{2,1,0:T(8,128)(2,1)S(1)}, f32[5,4,512]{2,1,0:T(4,128)S(1)}) custom-call(s32[2]{0:T(128)S(1)} %pad_add_fusion.2.starts, bf16[20,64,512]{2,1,0:T(8,128)(2,1)S(1)} %fusion.21.q_ref, bf16[5,64,1024]{2,1,0:T(8,128)(2,1)S(1)} %get-tuple-element.459.k_ref, bf16[5,64,1024]{2,1,0:T(8,128)(2,1)S(1)} %get-tuple-element.458.v_ref), custom_call_target="tpu_custom_call" | custom-call | flops 6553600 | bytes 1048576 | tf_op jit(solution)/shard_map/pallas_call | solution.py:416
  145.2 6.1 multiply_reduce_fusion
  154.0 5.2 collective-permute-done.11
  159.2 7.8 collective-permute-done.12
  172.0 3.9 collective-permute-start.16
  184.3 19.5 %collective-permute-done.15 = bf16[2048,384]{1,0:T(8,128)(2,1)} collective-permute-done((bf16[2048,384]{1,0:T(8,128)(2,1)}, bf16[2048,384]{1,0:T(8,128)(2,1)}, u32[]{:S(2)}, u32[]{:S(2)}) %collective-permute-start.15) | collective-permute-done | bytes 1572896 | tf_op jit(solution)/shard_map/ppermute | solution.py:79
  205.8 4.9 collective-permute-done.13
  213.8 5.2 collective-permute-start.20
  218.9 4.5 broadcast_in_dim.51
  223.4 3.2 bitcast_dynamic-update-slice_fusion.2
  231.4 3.2 bitcast_dynamic-update-slice_fusion.1
  234.6 3.2 bitcast_dynamic-update-slice_fusion
  237.7 9.2 %collective-permute-done.17 = bf16[256,2048]{1,0:T(8,128)(2,1)S(1)} collective-permute-done((bf16[256,2048]{1,0:T(8,128)(2,1)S(1)}, bf16[256,2048]{1,0:T(8,128)(2,1)S(1)}, u32[]{:S(2)}, u32[]{:S(2)}) %collective-permute-start.17) | collective-permute-done | bytes 1048608 | tf_op jit(solution)/shard_map/ppermute | solution.py:49
  259.4 30.0 %collective-permute-done.22 = bf16[2048,384]{1,0:T(8,128)(2,1)S(1)} collective-permute-done((bf16[2048,384]{1,0:T(8,128)(2,1)S(1)}, bf16[2048,384]{1,0:T(8,128)(2,1)S(1)}, u32[]{:S(2)}, u32[]{:S(2)}) %collective-permute-start.22) | collective-permute-done | bytes 1572896 | tf_op jit(solution)/shard_map/ppermute | solution.py:79
  289.3 3.1 add.492
  299.8 9.1 %fusion.84.raised_ref = f32[2048,1024]{1,0:T(8,128)S(1)} fusion(bf16[2048,2048]{1,0:T(8,128)(2,1)S(1)} %collective-permute-done.21, bf16[2048,1024]{1,0:T(8,128)(2,1)S(1)} %get-tuple-element.451.wide_ref), kind=kOutput, calls=%fused_computation.383 | convolution fusion | flops 8589934592 | bytes 20971520 | tf_op jit(solution)/shard_map/dot_general | solution.py:275
  308.9 3.3 copy-done.33
  313.9 12.0 %fusion.83.raised_ref = f32[2048,1024]{1,0:T(8,128)S(1)} fusion(bf16[2048,2048]{1,0:T(8,128)(2,1)} %bitcast.32, bf16[2048,1024]{1,0:T(8,128)(2,1)S(1)} %get-tuple-element.451.wide_ref), kind=kOutput, calls=%fused_computation.382 | convolution fusion | flops 8589934592 | bytes 20971520 | tf_op jit(solution)/shard_map/dot_general | solution.py:275
  326.0 3.2 copy-done.32
  330.7 6.8 convolution_convert_fusion
  337.5 6.9 convolution_convert_fusion.1.mine_ref
  346.0 19.6 %shard_map.247 = (bf16[2048,1024]{1,0:T(8,128)(2,1)S(1)}, bf16[2048,2048]{1,0:T(8,128)(2,1)}) custom-call(s32[1]{0:T(128)} %bitcast.34.core, bf16[4,2,512,2048]{3,2,1,0:T(8,128)(2,1)} %bitcast.108, f32[2048,1024]{1,0:T(8,128)} %copy-done.33, bf16[2048,512]{1,0:T(8,128)(2,1)S(1)} %copy-done.3, bf16[2048,1024]{1,0:T(8,128)(2,1)} %copy-done.34), custom_call_target="tpu_custom_call" | custom-call | bytes 65536 | tf_op jit(solution)/shard_map/pallas_call | solution.py:488
  369.8 20.0 %shard_map.248 = (bf16[2048,1024]{1,0:T(8,128)(2,1)S(1)}, bf16[2048,2048]{1,0:T(8,128)(2,1)}) custom-call(s32[1]{0:T(128)} %bitcast.29.core, bf16[4,2,512,2048]{3,2,1,0:T(8,128)(2,1)} %bitcast.109, f32[2048,1024]{1,0:T(8,128)} %copy-done.32, bf16[2048,512]{1,0:T(8,128)(2,1)S(1)} %copy-done.4, bf16[2048,1024]{1,0:T(8,128)(2,1)} %copy-done.34), custom_call_target="tpu_custom_call" | custom-call | bytes 65536 | tf_op jit(solution)/shard_map/pallas_call | solution.py:488
  389.9 10.4 %shard_map.249 = (bf16[512,2048]{1,0:T(8,128)(2,1)S(1)}, bf16[512,2048]{1,0:T(8,128)(2,1)S(1)}, bf16[1024,2048]{1,0:T(8,128)(2,1)S(1)}) custom-call(s32[8]{0:T(128)S(1)} %stack.97.index_ref, bf16[2048,2048]{1,0:T(8,128)(2,1)} %get-tuple-element.261.mine_ref, bf16[2048,2048]{1,0:T(8,128)(2,1)} %collective-permute-done.24.got_ref), custom_call_target="tpu_custom_call" | custom-call | bytes 65536 | tf_op jit(solution)/shard_map/pallas_call | solution.py:169
  404.5 13.5 %fusion.85 = f32[2048,1024]{1,0:T(8,128)} fusion(bf16[2048,2048]{1,0:T(8,128)(2,1)} %copy-done.131, bf16[2048,1024]{1,0:T(8,128)(2,1)S(1)} %copy-done.21), kind=kOutput, calls=%fused_computation.384 | convolution fusion | flops 8589934592 | bytes 20971520 | tf_op jit(solution)/shard_map/dot_general | solution.py:27
  417.9 12.4 %convolution_convert_fusion.5.down_ref = bf16[2048,512]{1,0:T(8,128)(2,1)S(1)} fusion(bf16[4096,2048]{1,0:T(8,128)(2,1)} %all-gather.12.cloned.1.call-done, bf16[4096,512]{1,0:T(8,128)(2,1)S(1)} %bitcast.128), kind=kOutput, calls=%fused_computation.48 | convolution fusion | flops 8590983168 | bytes 23068672 | tf_op jit(solution)/shard_map/dot_general | solution.py:27
  430.4 12.9 %add_convert_fusion.2.gate_ref.up_ref = bf16[2048,1024]{1,0:T(8,128)(2,1)S(1)} fusion(f32[2048,1024]{1,0:T(8,128)} %fusion.85, bf16[2048,2048]{1,0:T(8,128)(2,1)} %bitcast.32, bf16[2048,1024]{1,0:T(8,128)(2,1)S(1)} %get-tuple-element.266), kind=kOutput, calls=%fused_computation.6 | convolution fusion | flops 8594128896 | bytes 25165824 | tf_op jit(solution)/shard_map/dot_general | solution.py:27
  443.3 4.6 collective-permute-done.25
  450.5 3.2 shard_map.252
  456.5 4.1 add_convert_fusion.10
  461.7 12.2 %shard_map.250 = (bf16[256,2048]{1,0:T(8,128)(2,1)S(1)}, bf16[256,2048]{1,0:T(8,128)(2,1)S(1)}, bf16[256,2048]{1,0:T(8,128)(2,1)S(1)}, bf16[256,2048]{1,0:T(8,128)(2,1)S(1)}, bf16[1024,2048]{1,0:T(8,128)(2,1)S(1)}) custom-call(s32[8]{0:T(128)S(1)} %stack.98.index_ref, bf16[2048,2048]{1,0:T(8,128)(2,1)} %convolution_convert_fusion.1.mine_ref, ...), custom_call_target="tpu_custom_call" | custom-call | bytes 65536 | tf_op jit(solution)/shard_map/pallas_call | solution.py:169
  474.0 11.2 %collective-permute-done.28 = bf16[256,2048]{1,0:T(8,128)(2,1)} collective-permute-done((bf16[256,2048]{1,0:T(8,128)(2,1)}, bf16[256,2048]{1,0:T(8,128)(2,1)}, u32[]{:S(2)}, u32[]{:S(2)}) %collective-permute-start.28) | collective-permute-done | bytes 1048608 | tf_op jit(solution)/shard_map/ppermute | solution.py:49
  485.2 3.1 add_convert_fusion.9
  498.5 6.7 convolution_convert_fusion.4
  505.2 25.3 %shard_map.251 = (f32[20,64,512]{2,1,0:T(8,128)S(1)}, f32[5,64,1024]{2,1,0:T(8,128)S(1)}, f32[5,64,1024]{2,1,0:T(8,128)S(1)}) custom-call(s32[2]{0:T(128)S(1)} %copy-done.19, bf16[20,64,512]{2,1,0:T(8,128)(2,1)S(1)} %copy-done.7, bf16[5,64,1024]{2,1,0:T(8,128)(2,1)S(1)} %copy-done.11, bf16[5,64,1024]{2,1,0:T(8,128)(2,1)S(1)} %copy-done.9, ...), custom_call_target="tpu_custom_call" | custom-call | flops 6553600 | bytes 1048576 | tf_op jit(solution)/shard_map/pallas_call | solution.py:440
  551.3 5.7 collective-permute-done.36
  558.3 18.3 %collective-permute-done.33 = bf16[10,64,512]{2,1,0:T(8,128)(2,1)S(1)} collective-permute-done((bf16[10,64,512]{2,1,0:T(8,128)(2,1)S(1)}, bf16[10,64,512]{2,1,0:T(8,128)(2,1)S(1)}, u32[]{:S(2)}, u32[]{:S(2)}) %collective-permute-start.33) | collective-permute-done | bytes 655392 | tf_op jit(solution)/shard_map/ppermute | solution.py:49
  588.6 5.3 add_convert_fusion.1
  599.2 5.1 fusion.24
  625.1 14.3 %collective-permute-done.41 = bf16[512,512]{1,0:T(8,128)(2,1)S(1)} collective-permute-done((bf16[512,512]{1,0:T(8,128)(2,1)S(1)}, bf16[512,512]{1,0:T(8,128)(2,1)S(1)}, u32[]{:S(2)}, u32[]{:S(2)}) %collective-permute-start.41) | collective-permute-done | bytes 524320 | tf_op jit(solution)/shard_map/ppermute | solution.py:35
  639.4 16.1 %collective-permute-done.42 = bf16[512,512]{1,0:T(8,128)(2,1)S(1)} collective-permute-done((bf16[512,512]{1,0:T(8,128)(2,1)S(1)}, bf16[512,512]{1,0:T(8,128)(2,1)S(1)}, u32[]{:S(2)}, u32[]{:S(2)}) %collective-permute-start.42) | collective-permute-done | bytes 524320 | tf_op jit(solution)/shard_map/ppermute | solution.py:35
  655.5 12.2 %collective-permute-done.43 = bf16[512,512]{1,0:T(8,128)(2,1)S(1)} collective-permute-done((bf16[512,512]{1,0:T(8,128)(2,1)S(1)}, bf16[512,512]{1,0:T(8,128)(2,1)S(1)}, u32[]{:S(2)}, u32[]{:S(2)}) %collective-permute-start.43) | collective-permute-done | bytes 524320 | tf_op jit(solution)/shard_map/ppermute | solution.py:35
  676.7 3.2 collective-permute-done.46
  684.5 3.4 collective-permute-done.48
  692.5 4.2 convolution_convert_fusion.6
  704.1 6.8 collective-permute-done.54
  712.1 10.4 %collective-permute-done.51 = bf16[256,1152]{1,0:T(8,128)(2,1)S(1)} collective-permute-done((bf16[256,1152]{1,0:T(8,128)(2,1)S(1)}, bf16[256,1152]{1,0:T(8,128)(2,1)S(1)}, u32[]{:S(2)}, u32[]{:S(2)}) %collective-permute-start.51) | collective-permute-done | bytes 589856 | tf_op jit(solution)/shard_map/ppermute | solution.py:35
  722.5 18.4 %collective-permute-done.52 = bf16[256,1152]{1,0:T(8,128)(2,1)S(1)} collective-permute-done((bf16[256,1152]{1,0:T(8,128)(2,1)S(1)}, bf16[256,1152]{1,0:T(8,128)(2,1)S(1)}, u32[]{:S(2)}, u32[]{:S(2)}) %collective-permute-start.52) | collective-permute-done | bytes 589856 | tf_op jit(solution)/shard_map/ppermute | solution.py:35
  741.7 12.0 %collective-permute-done.53 = bf16[256,1152]{1,0:T(8,128)(2,1)} collective-permute-done((bf16[256,1152]{1,0:T(8,128)(2,1)S(1)}, bf16[256,1152]{1,0:T(8,128)(2,1)}, u32[]{:S(2)}, u32[]{:S(2)}) %collective-permute-start.53) | collective-permute-done | bytes 589856 | tf_op jit(solution)/shard_map/ppermute | solution.py:35
  762.4 3.4 add_convert_fusion.5
  771.2 6.4 fusion.86
  777.6 5.3 copy-done.5
  783.0 8.6 %shard_map.255 = (f32[2048,1024]{1,0:T(8,128)}, f32[2048,1024]{1,0:T(8,128)}, f32[1024,2048]{1,0:T(8,128)}) custom-call(bf16[8,2048,384]{2,1,0:T(8,128)(2,1)S(1)} %bitcast.104), custom_call_target="tpu_custom_call" | custom-call | bytes 65536 | tf_op jit(solution)/shard_map/pallas_call | solution.py:564
  791.5 12.1 %collective-permute-done.57 = bf16[512,512]{1,0:T(8,128)(2,1)S(1)} collective-permute-done((bf16[512,512]{1,0:T(8,128)(2,1)S(1)}, bf16[512,512]{1,0:T(8,128)(2,1)S(1)}, u32[]{:S(2)}, u32[]{:S(2)}) %collective-permute-start.57) | collective-permute-done | bytes 524320 | tf_op jit(solution)/shard_map/ppermute | solution.py:35
  803.7 10.0 %collective-permute-done.58 = bf16[512,512]{1,0:T(8,128)(2,1)S(1)} collective-permute-done((bf16[512,512]{1,0:T(8,128)(2,1)S(1)}, bf16[512,512]{1,0:T(8,128)(2,1)S(1)}, u32[]{:S(2)}, u32[]{:S(2)}) %collective-permute-start.58) | collective-permute-done | bytes 524320 | tf_op jit(solution)/shard_map/ppermute | solution.py:35
  823.7 4.9 shard_map.256
  (562 shorter events, 248.3 us)
Async XLA Ops:
  7.2 99.2 %all-gather.8.cloned.1.call-start = ((), (), s32[]{:S(2)}) async-start(), calls=%async_computation.1 | async-start | bytes 5898240 | tf_op jit(solution)/shard_map/all_gather | solution.py:705
  9.6 31.7 %collective-permute-start = (bf16[264,384]{1,0:T(8,128)(2,1)}, bf16[264,384]{1,0:T(8,128)(2,1)}, u32[]{:S(2)}, u32[]{:S(2)}) collective-permute-start(bf16[264,384]{1,0:T(8,128)(2,1)} %pad_maximum_fusion.31), channel_id=1, source_target_pairs={{0,1},{1,0},{2,3},{3,2},{4,5},{5,4},{6,7},{7,6},{8,9},{9,8},{10,11... | collective-permute-start | bytes 608264 | tf_op jit(solution)/shard_map/ppermute | solution.py:35
  11.1 30.1 %collective-permute-start.1 = (bf16[264,384]{1,0:T(8,128)(2,1)}, bf16[264,384]{1,0:T(8,128)(2,1)}, u32[]{:S(2)}, u32[]{:S(2)}) collective-permute-start(bf16[264,384]{1,0:T(8,128)(2,1)} %pad_maximum_fusion.31), channel_id=1, source_target_pairs={{0,2},{1,3},{2,0},{3,1},{4,6},{5,7},{6,4},{7,5},{8,10},{9,11},{10,... | collective-permute-start | bytes 608264 | tf_op jit(solution)/shard_map/ppermute | solution.py:35
  11.5 29.8 %collective-permute-start.2 = (bf16[264,384]{1,0:T(8,128)(2,1)}, bf16[264,384]{1,0:T(8,128)(2,1)}, u32[]{:S(2)}, u32[]{:S(2)}) collective-permute-start(bf16[264,384]{1,0:T(8,128)(2,1)} %pad_maximum_fusion.31), channel_id=1, source_target_pairs={{0,3},{1,2},{2,1},{3,0},{4,7},{5,6},{6,5},{7,4},{8,11},{9,10},{10,... | collective-permute-start | bytes 608264 | tf_op jit(solution)/shard_map/ppermute | solution.py:35
  17.2 24.3 %collective-permute-start.3 = (bf16[512,512]{1,0:T(8,128)(2,1)}, bf16[512,512]{1,0:T(8,128)(2,1)}, u32[]{:S(2)}, u32[]{:S(2)}) collective-permute-start(bf16[512,512]{1,0:T(8,128)(2,1)} %pad_maximum_fusion.29), channel_id=1, source_target_pairs={{0,1},{1,0},{2,3},{3,2},{4,5},{5,4},{6,7},{7,6},{8,9},{9,8},{10,11... | collective-permute-start | bytes 1572872 | tf_op jit(solution)/shard_map/ppermute | solution.py:49
  20.5 31.0 %collective-permute-start.4 = (bf16[512,512]{1,0:T(8,128)(2,1)}, bf16[512,512]{1,0:T(8,128)(2,1)}, u32[]{:S(2)}, u32[]{:S(2)}) collective-permute-start(bf16[512,512]{1,0:T(8,128)(2,1)} %pad_maximum_fusion.30), channel_id=1, source_target_pairs={{0,2},{1,3},{2,0},{3,1},{4,6},{5,7},{6,4},{7,5},{8,10},{9,11},{10,... | collective-permute-start | bytes 1572872 | tf_op jit(solution)/shard_map/ppermute | solution.py:49
  57.4 87.9 %all-gather.10.cloned.1.call-start = ((), (), s32[]{:S(2)}) async-start(), calls=%async_computation.2 | async-start | bytes 5898240 | tf_op jit(solution)/shard_map/all_gather | solution.py:720
  57.4 37.9 %collective-permute-start.5 = (bf16[512,512]{1,0:T(8,128)(2,1)S(1)}, bf16[512,512]{1,0:T(8,128)(2,1)S(1)}, u32[]{:S(2)}, u32[]{:S(2)}) collective-permute-start(bf16[512,512]{1,0:T(8,128)(2,1)S(1)} %pad_maximum_fusion.23), channel_id=1, source_target_pairs={{0,3},{1,2},{2,1},{3,0},{4,7},{5,6},{6,5},{7,4},{8,11},{9,10},{10,... | collective-permute-start | bytes 1572872 | tf_op jit(solution)/shard_map/ppermute | solution.py:49
  59.0 19.7 %collective-permute-start.6 = (bf16[160,512]{1,0:T(8,128)(2,1)S(1)}, bf16[160,512]{1,0:T(8,128)(2,1)S(1)}, u32[]{:S(2)}, u32[]{:S(2)}) collective-permute-start(bf16[160,512]{1,0:T(8,128)(2,1)S(1)} %fusion.26), channel_id=1, source_target_pairs={{0,1},{1,0},{2,3},{3,2},{4,5},{5,4},{6,7},{7,6},{8,9},{9,8},{10,11... | collective-permute-start | bytes 491528 | tf_op jit(solution)/shard_map/ppermute | solution.py:35
  62.3 30.3 %collective-permute-start.7 = (bf16[160,512]{1,0:T(8,128)(2,1)S(1)}, bf16[160,512]{1,0:T(8,128)(2,1)S(1)}, u32[]{:S(2)}, u32[]{:S(2)}) collective-permute-start(bf16[160,512]{1,0:T(8,128)(2,1)S(1)} %fusion.26), channel_id=1, source_target_pairs={{0,2},{1,3},{2,0},{3,1},{4,6},{5,7},{6,4},{7,5},{8,10},{9,11},{10,... | collective-permute-start | bytes 491528 | tf_op jit(solution)/shard_map/ppermute | solution.py:35
  63.3 32.0 %collective-permute-start.8 = (bf16[160,512]{1,0:T(8,128)(2,1)S(1)}, bf16[160,512]{1,0:T(8,128)(2,1)S(1)}, u32[]{:S(2)}, u32[]{:S(2)}) collective-permute-start(bf16[160,512]{1,0:T(8,128)(2,1)S(1)} %fusion.26), channel_id=1, source_target_pairs={{0,3},{1,2},{2,1},{3,0},{4,7},{5,6},{6,5},{7,4},{8,11},{9,10},{10,... | collective-permute-start | bytes 491528 | tf_op jit(solution)/shard_map/ppermute | solution.py:35
  96.3 248.1 %all-gather.12.cloned.1.call-start = ((), (), s32[]{:S(2)}) async-start(), calls=%async_computation.3 | async-start | bytes 18874368 | tf_op jit(solution)/shard_map/all_gather | solution.py:772
  106.3 14.8 %collective-permute-start.9 = (bf16[10,64,512]{2,1,0:T(8,128)(2,1)S(1)}, bf16[10,64,512]{2,1,0:T(8,128)(2,1)}, u32[]{:S(2)}, u32[]{:S(2)}) collective-permute-start(bf16[10,64,512]{2,1,0:T(8,128)(2,1)S(1)} %pad_maximum_fusion.20), channel_id=1, source_target_pairs={{0,1},{1,0},{2,3},{3,2},{4,5},{5,4},{6,7},{7,6},{8,9},{9,8},{10,11... | collective-permute-start | bytes 1966088 | tf_op jit(solution)/shard_map/ppermute | solution.py:49
  121.0 33.0 %collective-permute-start.10 = (bf16[512,512]{1,0:T(8,128)(2,1)}, bf16[512,512]{1,0:T(8,128)(2,1)}, u32[]{:S(2)}, u32[]{:S(2)}) collective-permute-start(bf16[512,512]{1,0:T(8,128)(2,1)} %pad_maximum_fusion.25), channel_id=1, source_target_pairs={{0,1},{1,0},{2,3},{3,2},{4,5},{5,4},{6,7},{7,6},{8,9},{9,8},{10,11... | collective-permute-start | bytes 1572872 | tf_op jit(solution)/shard_map/ppermute | solution.py:35
  121.3 37.9 %collective-permute-start.11 = (bf16[512,512]{1,0:T(8,128)(2,1)}, bf16[512,512]{1,0:T(8,128)(2,1)}, u32[]{:S(2)}, u32[]{:S(2)}) collective-permute-start(bf16[512,512]{1,0:T(8,128)(2,1)} %pad_maximum_fusion.26), channel_id=1, source_target_pairs={{0,2},{1,3},{2,0},{3,1},{4,6},{5,7},{6,4},{7,5},{8,10},{9,11},{10,... | collective-permute-start | bytes 1572872 | tf_op jit(solution)/shard_map/ppermute | solution.py:35
  124.0 43.0 %collective-permute-start.12 = (bf16[512,512]{1,0:T(8,128)(2,1)}, bf16[512,512]{1,0:T(8,128)(2,1)}, u32[]{:S(2)}, u32[]{:S(2)}) collective-permute-start(bf16[512,512]{1,0:T(8,128)(2,1)} %pad_maximum_fusion.27), channel_id=1, source_target_pairs={{0,3},{1,2},{2,1},{3,0},{4,7},{5,6},{6,5},{7,4},{8,11},{9,10},{10,... | collective-permute-start | bytes 1572872 | tf_op jit(solution)/shard_map/ppermute | solution.py:35
  167.0 43.6 %collective-permute-start.13 = (bf16[512,2048]{1,0:T(8,128)(2,1)}, bf16[512,2048]{1,0:T(8,128)(2,1)}, u32[]{:S(2)}, u32[]{:S(2)}) collective-permute-start(bf16[512,2048]{1,0:T(8,128)(2,1)} %multiply_convert_fusion), channel_id=1, source_target_pairs={{0,8},{4,12},{8,0},{12,4},{16,24},{20,28},{24,16},{28,20},{1,9},{5... | collective-permute-start | bytes 6291464 | tf_op jit(solution)/shard_map/ppermute | solution.py:49
  168.5 43.3 %collective-permute-start.14 = (bf16[512,2048]{1,0:T(8,128)(2,1)}, bf16[512,2048]{1,0:T(8,128)(2,1)}, u32[]{:S(2)}, u32[]{:S(2)}) collective-permute-start(bf16[512,2048]{1,0:T(8,128)(2,1)} %multiply_convert_fusion), channel_id=1, source_target_pairs={{0,16},{4,20},{8,24},{12,28},{16,0},{20,4},{24,8},{28,12},{1,17},{... | collective-permute-start | bytes 6291464 | tf_op jit(solution)/shard_map/ppermute | solution.py:49
  170.1 33.7 %collective-permute-start.15 = (bf16[2048,384]{1,0:T(8,128)(2,1)}, bf16[2048,384]{1,0:T(8,128)(2,1)}, u32[]{:S(2)}, u32[]{:S(2)}) collective-permute-start(bf16[2048,384]{1,0:T(8,128)(2,1)} %pad_maximum_fusion.6), channel_id=1, source_target_pairs={{0,1},{1,2},{2,3},{4,5},{5,6},{6,7},{8,9},{9,10},{10,11},{12,13},{... | collective-permute-start | bytes 4718600 | tf_op jit(solution)/shard_map/ppermute | solution.py:79
  172.0 33.8 %collective-permute-start.16 = (bf16[2048,384]{1,0:T(8,128)(2,1)}, bf16[2048,384]{1,0:T(8,128)(2,1)}, u32[]{:S(2)}, u32[]{:S(2)}) collective-permute-start(bf16[2048,384]{1,0:T(8,128)(2,1)} %pad_maximum_fusion.6), channel_id=1, source_target_pairs={{3,2},{2,1},{1,0},{7,6},{6,5},{5,4},{11,10},{10,9},{9,8},{15,14},{... | collective-permute-start | bytes 4718600 | tf_op jit(solution)/shard_map/ppermute | solution.py:79
  211.8 37.9 %collective-permute-start.19 = (bf16[2048,384]{1,0:T(8,128)(2,1)}, bf16[2048,384]{1,0:T(8,128)(2,1)S(1)}, u32[]{:S(2)}, u32[]{:S(2)}) collective-permute-start(bf16[2048,384]{1,0:T(8,128)(2,1)} %collective-permute-done.15), channel_id=1, source_target_pairs={{1,2},{2,3},{5,6},{6,7},{9,10},{10,11},{13,14},{14,15},{17,18},{18... | collective-permute-start | bytes 4718600 | tf_op jit(solution)/shard_map/ppermute | solution.py:79
  213.8 37.0 %collective-permute-start.20 = (bf16[2048,384]{1,0:T(8,128)(2,1)}, bf16[2048,384]{1,0:T(8,128)(2,1)}, u32[]{:S(2)}, u32[]{:S(2)}) collective-permute-start(bf16[2048,384]{1,0:T(8,128)(2,1)} %collective-permute-done.16), channel_id=1, source_target_pairs={{2,1},{1,0},{6,5},{5,4},{10,9},{9,8},{14,13},{13,12},{18,17},{17,1... | collective-permute-start | bytes 4718600 | tf_op jit(solution)/shard_map/ppermute | solution.py:79
  227.9 19.1 %collective-permute-start.17 = (bf16[256,2048]{1,0:T(8,128)(2,1)S(1)}, bf16[256,2048]{1,0:T(8,128)(2,1)S(1)}, u32[]{:S(2)}, u32[]{:S(2)}) collective-permute-start(bf16[256,2048]{1,0:T(8,128)(2,1)S(1)} %slice.412), channel_id=1, source_target_pairs={{0,16},{4,20},{8,24},{12,28},{16,0},{20,4},{24,8},{28,12},{1,17},{... | collective-permute-start | bytes 3145736 | tf_op jit(solution)/shard_map/ppermute | solution.py:49
  230.9 18.9 %collective-permute-start.18 = (bf16[256,2048]{1,0:T(8,128)(2,1)S(1)}, bf16[256,2048]{1,0:T(8,128)(2,1)S(1)}, u32[]{:S(2)}, u32[]{:S(2)}) collective-permute-start(bf16[256,2048]{1,0:T(8,128)(2,1)S(1)} %slice.413), channel_id=1, source_target_pairs={{0,8},{4,12},{8,0},{12,4},{16,24},{20,28},{24,16},{28,20},{1,9},{5... | collective-permute-start | bytes 3145736 | tf_op jit(solution)/shard_map/ppermute | solution.py:49
  250.7 331.2 %reduce-scatter.2.cloned.1.call-start = ((), (), s32[]{:S(2)}) async-start(), calls=%async_computation.4 | async-start | bytes 7864320 | tf_op jit(solution)/shard_map/reduce_scatter | solution.py:829
  253.5 35.9 %collective-permute-start.21 = (bf16[2048,2048]{1,0:T(8,128)(2,1)}, bf16[2048,2048]{1,0:T(8,128)(2,1)S(1)}, u32[]{:S(2)}, u32[]{:S(2)}) collective-permute-start(bf16[2048,2048]{1,0:T(8,128)(2,1)} %bitcast.32), channel_id=1, source_target_pairs={{0,4},{4,0},{8,12},{12,8},{16,20},{20,16},{24,28},{28,24},{1,5},{5... | collective-permute-start | bytes 25165832 | tf_op jit(solution)/shard_map/ppermute | solution.py:49
  253.5 35.9 %collective-permute-start.22 = (bf16[2048,384]{1,0:T(8,128)(2,1)S(1)}, bf16[2048,384]{1,0:T(8,128)(2,1)S(1)}, u32[]{:S(2)}, u32[]{:S(2)}) collective-permute-start(bf16[2048,384]{1,0:T(8,128)(2,1)S(1)} %collective-permute-done.19), channel_id=1, source_target_pairs={{2,3},{6,7},{10,11},{14,15},{18,19},{22,23},{26,27},{30,31}} | collective-permute-start | bytes 4718600 | tf_op jit(solution)/shard_map/ppermute | solution.py:79
  254.8 34.5 %collective-permute-start.23 = (bf16[2048,384]{1,0:T(8,128)(2,1)}, bf16[2048,384]{1,0:T(8,128)(2,1)S(1)}, u32[]{:S(2)}, u32[]{:S(2)}) collective-permute-start(bf16[2048,384]{1,0:T(8,128)(2,1)} %collective-permute-done.20), channel_id=1, source_target_pairs={{1,0},{5,4},{9,8},{13,12},{17,16},{21,20},{25,24},{29,28}} | collective-permute-start | bytes 4718600 | tf_op jit(solution)/shard_map/ppermute | solution.py:79
  367.6 22.2 %collective-permute-start.24 = (bf16[2048,2048]{1,0:T(8,128)(2,1)}, bf16[2048,2048]{1,0:T(8,128)(2,1)}, u32[]{:S(2)}, u32[]{:S(2)}) collective-permute-start(bf16[2048,2048]{1,0:T(8,128)(2,1)} %get-tuple-element.260), channel_id=1, source_target_pairs={{0,4},{4,0},{8,12},{12,8},{16,20},{20,16},{24,28},{28,24},{1,5},{5... | collective-permute-start | bytes 25165832 | tf_op jit(solution)/shard_map/ppermute | solution.py:49
  367.6 75.6 %collective-permute-start.27 = (bf16[2048,2048]{1,0:T(8,128)(2,1)}, bf16[2048,2048]{1,0:T(8,128)(2,1)}, u32[]{:S(2)}, u32[]{:S(2)}) collective-permute-start(bf16[2048,2048]{1,0:T(8,128)(2,1)} %convolution_convert_fusion), channel_id=1, source_target_pairs={{0,4},{4,0},{8,12},{12,8},{16,20},{20,16},{24,28},{28,24},{1,5},{5... | collective-permute-start | bytes 25165832 | tf_op jit(solution)/shard_map/ppermute | solution.py:49
  400.3 47.6 %collective-permute-start.25 = (bf16[512,2048]{1,0:T(8,128)(2,1)S(1)}, bf16[512,2048]{1,0:T(8,128)(2,1)S(1)}, u32[]{:S(2)}, u32[]{:S(2)}) collective-permute-start(bf16[512,2048]{1,0:T(8,128)(2,1)S(1)} %get-tuple-element.268), channel_id=1, source_target_pairs={{0,8},{4,12},{8,0},{12,4},{16,24},{20,28},{24,16},{28,20},{1,9},{5... | collective-permute-start | bytes 6291464 | tf_op jit(solution)/shard_map/ppermute | solution.py:49
  401.1 47.2 %collective-permute-start.26 = (bf16[512,2048]{1,0:T(8,128)(2,1)S(1)}, bf16[512,2048]{1,0:T(8,128)(2,1)S(1)}, u32[]{:S(2)}, u32[]{:S(2)}) collective-permute-start(bf16[512,2048]{1,0:T(8,128)(2,1)S(1)} %get-tuple-element.269), channel_id=1, source_target_pairs={{0,16},{4,20},{8,24},{12,28},{16,0},{20,4},{24,8},{28,12},{1,17},{... | collective-permute-start | bytes 6291464 | tf_op jit(solution)/shard_map/ppermute | solution.py:49
  456.5 297.2 %all-gather.18.cloned.1.call-start = ((), (), s32[]{:S(2)}) async-start(), calls=%async_computation.7 | async-start | bytes 14155776 | tf_op jit(solution)/shard_map/all_gather | solution.py:875
  460.6 24.5 %collective-permute-start.28 = (bf16[256,2048]{1,0:T(8,128)(2,1)}, bf16[256,2048]{1,0:T(8,128)(2,1)}, u32[]{:S(2)}, u32[]{:S(2)}) collective-permute-start(bf16[256,2048]{1,0:T(8,128)(2,1)} %get-tuple-element.387), channel_id=1, source_target_pairs={{0,16},{4,20},{8,24},{12,28},{16,0},{20,4},{24,8},{28,12},{1,17},{... | collective-permute-start | bytes 3145736 | tf_op jit(solution)/shard_map/ppermute | solution.py:49
  461.1 24.1 %collective-permute-start.29 = (bf16[256,2048]{1,0:T(8,128)(2,1)S(1)}, bf16[256,2048]{1,0:T(8,128)(2,1)}, u32[]{:S(2)}, u32[]{:S(2)}) collective-permute-start(bf16[256,2048]{1,0:T(8,128)(2,1)S(1)} %get-tuple-element.386), channel_id=1, source_target_pairs={{0,8},{4,12},{8,0},{12,4},{16,24},{20,28},{24,16},{28,20},{1,9},{5... | collective-permute-start | bytes 3145736 | tf_op jit(solution)/shard_map/ppermute | solution.py:49
  496.0 41.3 %collective-permute-start.32 = (bf16[640,2048]{1,0:T(8,128)(2,1)S(1)}, bf16[640,2048]{1,0:T(8,128)(2,1)S(1)}, u32[]{:S(2)}, u32[]{:S(2)}) collective-permute-start(bf16[640,2048]{1,0:T(8,128)(2,1)S(1)} %convolution_convert_fusion.2), channel_id=1, source_target_pairs={{0,4},{4,0},{8,12},{12,8},{16,20},{20,16},{24,28},{28,24},{1,5},{5... | collective-permute-start | bytes 7864328 | tf_op jit(solution)/shard_map/ppermute | solution.py:49
  496.1 41.2 %collective-permute-start.30 = (bf16[256,2048]{1,0:T(8,128)(2,1)S(1)}, bf16[256,2048]{1,0:T(8,128)(2,1)S(1)}, u32[]{:S(2)}, u32[]{:S(2)}) collective-permute-start(bf16[256,2048]{1,0:T(8,128)(2,1)S(1)} %get-tuple-element.284), channel_id=1, source_target_pairs={{0,8},{4,12},{8,0},{12,4},{16,24},{20,28},{24,16},{28,20},{1,9},{5... | collective-permute-start | bytes 3145736 | tf_op jit(solution)/shard_map/ppermute | solution.py:49
  497.0 40.4 %collective-permute-start.31 = (bf16[256,2048]{1,0:T(8,128)(2,1)S(1)}, bf16[256,2048]{1,0:T(8,128)(2,1)S(1)}, u32[]{:S(2)}, u32[]{:S(2)}) collective-permute-start(bf16[256,2048]{1,0:T(8,128)(2,1)S(1)} %get-tuple-element.285), channel_id=1, source_target_pairs={{0,16},{4,20},{8,24},{12,28},{16,0},{20,4},{24,8},{28,12},{1,17},{... | collective-permute-start | bytes 3145736 | tf_op jit(solution)/shard_map/ppermute | solution.py:49
  539.3 17.7 %collective-permute-start.36 = (bf16[160,2048]{1,0:T(8,128)(2,1)S(1)}, bf16[160,2048]{1,0:T(8,128)(2,1)S(1)}, u32[]{:S(2)}, u32[]{:S(2)}) collective-permute-start(bf16[160,2048]{1,0:T(8,128)(2,1)S(1)} %get-tuple-element.296), channel_id=1, source_target_pairs={{0,8},{4,12},{8,0},{12,4},{16,24},{20,28},{24,16},{28,20},{1,9},{5... | collective-permute-start | bytes 1966088 | tf_op jit(solution)/shard_map/ppermute | solution.py:49
  540.6 17.6 %collective-permute-start.37 = (bf16[160,2048]{1,0:T(8,128)(2,1)S(1)}, bf16[160,2048]{1,0:T(8,128)(2,1)S(1)}, u32[]{:S(2)}, u32[]{:S(2)}) collective-permute-start(bf16[160,2048]{1,0:T(8,128)(2,1)S(1)} %get-tuple-element.297), channel_id=1, source_target_pairs={{0,16},{4,20},{8,24},{12,28},{16,0},{20,4},{24,8},{28,12},{1,17},{... | collective-permute-start | bytes 1966088 | tf_op jit(solution)/shard_map/ppermute | solution.py:49
  542.1 37.3 %collective-permute-start.34 = (bf16[256,2048]{1,0:T(8,128)(2,1)S(1)}, bf16[256,2048]{1,0:T(8,128)(2,1)S(1)}, u32[]{:S(2)}, u32[]{:S(2)}) collective-permute-start(bf16[256,2048]{1,0:T(8,128)(2,1)S(1)} %get-tuple-element.383), channel_id=1, source_target_pairs={{0,16},{4,20},{8,24},{12,28},{16,0},{20,4},{24,8},{28,12},{1,17},{... | collective-permute-start | bytes 3145736 | tf_op jit(solution)/shard_map/ppermute | solution.py:49
  543.6 36.7 %collective-permute-start.35 = (bf16[256,2048]{1,0:T(8,128)(2,1)S(1)}, bf16[256,2048]{1,0:T(8,128)(2,1)}, u32[]{:S(2)}, u32[]{:S(2)}) collective-permute-start(bf16[256,2048]{1,0:T(8,128)(2,1)S(1)} %get-tuple-element.382), channel_id=1, source_target_pairs={{0,8},{4,12},{8,0},{12,4},{16,24},{20,28},{24,16},{28,20},{1,9},{5... | collective-permute-start | bytes 3145736 | tf_op jit(solution)/shard_map/ppermute | solution.py:49
  545.2 31.4 %collective-permute-start.33 = (bf16[10,64,512]{2,1,0:T(8,128)(2,1)S(1)}, bf16[10,64,512]{2,1,0:T(8,128)(2,1)S(1)}, u32[]{:S(2)}, u32[]{:S(2)}) collective-permute-start(bf16[10,64,512]{2,1,0:T(8,128)(2,1)S(1)} %select_convert_fusion), channel_id=1, source_target_pairs={{0,1},{1,0},{2,3},{3,2},{4,5},{5,4},{6,7},{7,6},{8,9},{9,8},{10,11... | collective-permute-start | bytes 1966088 | tf_op jit(solution)/shard_map/ppermute | solution.py:49
  582.0 189.3 %all-gather.14.cloned.1.call-start = ((), (), s32[]{:S(2)}) async-start(), calls=%async_computation.5 | async-start | bytes 1474560 | tf_op jit(solution)/shard_map/all_gather | solution.py:941
  593.9 20.2 %collective-permute-start.38 = (bf16[1024,2048]{1,0:T(8,128)(2,1)}, bf16[1024,2048]{1,0:T(8,128)(2,1)S(1)}, u32[]{:S(2)}, u32[]{:S(2)}) collective-permute-start(bf16[1024,2048]{1,0:T(8,128)(2,1)} %add_convert_fusion.1), channel_id=1, source_target_pairs={{0,4},{4,0},{8,12},{12,8},{16,20},{20,16},{24,28},{28,24},{1,5},{5... | collective-permute-start | bytes 12582920 | tf_op jit(solution)/shard_map/ppermute | solution.py:49
  594.9 17.7 %collective-permute-start.39 = (bf16[80,2048]{1,0:T(8,128)(2,1)}, bf16[80,2048]{1,0:T(8,128)(2,1)}, u32[]{:S(2)}, u32[]{:S(2)}) collective-permute-start(bf16[80,2048]{1,0:T(8,128)(2,1)} %get-tuple-element.455), channel_id=1, source_target_pairs={{0,16},{4,20},{8,24},{12,28},{16,0},{20,4},{24,8},{28,12},{1,17},{... | collective-permute-start | bytes 983048 | tf_op jit(solution)/shard_map/ppermute | solution.py:49
  596.4 17.6 %collective-permute-start.40 = (bf16[80,2048]{1,0:T(8,128)(2,1)}, bf16[80,2048]{1,0:T(8,128)(2,1)}, u32[]{:S(2)}, u32[]{:S(2)}) collective-permute-start(bf16[80,2048]{1,0:T(8,128)(2,1)} %get-tuple-element.454), channel_id=1, source_target_pairs={{0,8},{4,12},{8,0},{12,4},{16,24},{20,28},{24,16},{28,20},{1,9},{5... | collective-permute-start | bytes 983048 | tf_op jit(solution)/shard_map/ppermute | solution.py:49
  617.1 50.6 %collective-permute-start.44 = (bf16[256,2048]{1,0:T(8,128)(2,1)S(1)}, bf16[256,2048]{1,0:T(8,128)(2,1)S(1)}, u32[]{:S(2)}, u32[]{:S(2)}) collective-permute-start(bf16[256,2048]{1,0:T(8,128)(2,1)S(1)} %get-tuple-element.316), channel_id=1, source_target_pairs={{0,8},{4,12},{8,0},{12,4},{16,24},{20,28},{24,16},{28,20},{1,9},{5... | collective-permute-start | bytes 3145736 | tf_op jit(solution)/shard_map/ppermute | solution.py:49
  618.6 49.1 %collective-permute-start.45 = (bf16[256,2048]{1,0:T(8,128)(2,1)S(1)}, bf16[256,2048]{1,0:T(8,128)(2,1)S(1)}, u32[]{:S(2)}, u32[]{:S(2)}) collective-permute-start(bf16[256,2048]{1,0:T(8,128)(2,1)S(1)} %get-tuple-element.317), channel_id=1, source_target_pairs={{0,16},{4,20},{8,24},{12,28},{16,0},{20,4},{24,8},{28,12},{1,17},{... | collective-permute-start | bytes 3145736 | tf_op jit(solution)/shard_map/ppermute | solution.py:49
  620.1 19.3 %collective-permute-start.41 = (bf16[512,512]{1,0:T(8,128)(2,1)S(1)}, bf16[512,512]{1,0:T(8,128)(2,1)S(1)}, u32[]{:S(2)}, u32[]{:S(2)}) collective-permute-start(bf16[512,512]{1,0:T(8,128)(2,1)S(1)} %get-tuple-element.410), channel_id=1, source_target_pairs={{0,1},{1,0},{2,3},{3,2},{4,5},{5,4},{6,7},{7,6},{8,9},{9,8},{10,11... | collective-permute-start | bytes 1572872 | tf_op jit(solution)/shard_map/ppermute | solution.py:35
  620.6 34.9 %collective-permute-start.42 = (bf16[512,512]{1,0:T(8,128)(2,1)S(1)}, bf16[512,512]{1,0:T(8,128)(2,1)S(1)}, u32[]{:S(2)}, u32[]{:S(2)}) collective-permute-start(bf16[512,512]{1,0:T(8,128)(2,1)S(1)} %get-tuple-element.411), channel_id=1, source_target_pairs={{0,2},{1,3},{2,0},{3,1},{4,6},{5,7},{6,4},{7,5},{8,10},{9,11},{10,... | collective-permute-start | bytes 1572872 | tf_op jit(solution)/shard_map/ppermute | solution.py:35
  620.6 47.1 %collective-permute-start.43 = (bf16[512,512]{1,0:T(8,128)(2,1)S(1)}, bf16[512,512]{1,0:T(8,128)(2,1)S(1)}, u32[]{:S(2)}, u32[]{:S(2)}) collective-permute-start(bf16[512,512]{1,0:T(8,128)(2,1)S(1)} %get-tuple-element.408), channel_id=1, source_target_pairs={{0,3},{1,2},{2,1},{3,0},{4,7},{5,6},{6,5},{7,4},{8,11},{9,10},{10,... | collective-permute-start | bytes 1572872 | tf_op jit(solution)/shard_map/ppermute | solution.py:35
  669.2 19.7 %collective-permute-start.49 = (bf16[128,2048]{1,0:T(8,128)(2,1)}, bf16[128,2048]{1,0:T(8,128)(2,1)}, u32[]{:S(2)}, u32[]{:S(2)}) collective-permute-start(bf16[128,2048]{1,0:T(8,128)(2,1)} %get-tuple-element.407), channel_id=1, source_target_pairs={{0,16},{4,20},{8,24},{12,28},{16,0},{20,4},{24,8},{28,12},{1,17},{... | collective-permute-start | bytes 1572872 | tf_op jit(solution)/shard_map/ppermute | solution.py:49
  670.6 18.3 %collective-permute-start.50 = (bf16[128,2048]{1,0:T(8,128)(2,1)}, bf16[128,2048]{1,0:T(8,128)(2,1)}, u32[]{:S(2)}, u32[]{:S(2)}) collective-permute-start(bf16[128,2048]{1,0:T(8,128)(2,1)} %get-tuple-element.406), channel_id=1, source_target_pairs={{0,8},{4,12},{8,0},{12,4},{16,24},{20,28},{24,16},{28,20},{1,9},{5... | collective-permute-start | bytes 1572872 | tf_op jit(solution)/shard_map/ppermute | solution.py:49
  673.9 14.1 %collective-permute-start.48 = (bf16[160,512]{1,0:T(8,128)(2,1)}, bf16[160,512]{1,0:T(8,128)(2,1)S(1)}, u32[]{:S(2)}, u32[]{:S(2)}) collective-permute-start(bf16[160,512]{1,0:T(8,128)(2,1)} %get-tuple-element.373), channel_id=1, source_target_pairs={{0,3},{1,2},{2,1},{3,0},{4,7},{5,6},{6,5},{7,4},{8,11},{9,10},{10,... | collective-permute-start | bytes 491528 | tf_op jit(solution)/shard_map/ppermute | solution.py:35
  679.9 30.9 %collective-permute-start.54 = (bf16[256,2048]{1,0:T(8,128)(2,1)S(1)}, bf16[256,2048]{1,0:T(8,128)(2,1)}, u32[]{:S(2)}, u32[]{:S(2)}) collective-permute-start(bf16[256,2048]{1,0:T(8,128)(2,1)S(1)} %copy-done.25), channel_id=1, source_target_pairs={{0,8},{4,12},{8,0},{12,4},{16,24},{20,28},{24,16},{28,20},{1,9},{5... | collective-permute-start | bytes 3145736 | tf_op jit(solution)/shard_map/ppermute | solution.py:49
  684.0 28.1 %collective-permute-start.55 = (bf16[256,2048]{1,0:T(8,128)(2,1)S(1)}, bf16[256,2048]{1,0:T(8,128)(2,1)}, u32[]{:S(2)}, u32[]{:S(2)}) collective-permute-start(bf16[256,2048]{1,0:T(8,128)(2,1)S(1)} %copy-done.23), channel_id=1, source_target_pairs={{0,16},{4,20},{8,24},{12,28},{16,0},{20,4},{24,8},{28,12},{1,17},{... | collective-permute-start | bytes 3145736 | tf_op jit(solution)/shard_map/ppermute | solution.py:49
  696.7 122.1 %all-gather.16.cloned.1.call-start = ((), (), s32[]{:S(2)}) async-start(), calls=%async_computation.6 | async-start | bytes 5308416 | tf_op jit(solution)/shard_map/all_gather | solution.py:965
  700.6 21.9 %collective-permute-start.51 = (bf16[256,1152]{1,0:T(8,128)(2,1)S(1)}, bf16[256,1152]{1,0:T(8,128)(2,1)S(1)}, u32[]{:S(2)}, u32[]{:S(2)}) collective-permute-start(bf16[256,1152]{1,0:T(8,128)(2,1)S(1)} %get-tuple-element.484), channel_id=1, source_target_pairs={{0,1},{1,0},{2,3},{3,2},{4,5},{5,4},{6,7},{7,6},{8,9},{9,8},{10,11... | collective-permute-start | bytes 1769480 | tf_op jit(solution)/shard_map/ppermute | solution.py:35
  701.4 39.5 %collective-permute-start.52 = (bf16[256,1152]{1,0:T(8,128)(2,1)S(1)}, bf16[256,1152]{1,0:T(8,128)(2,1)S(1)}, u32[]{:S(2)}, u32[]{:S(2)}) collective-permute-start(bf16[256,1152]{1,0:T(8,128)(2,1)S(1)} %get-tuple-element.485), channel_id=1, source_target_pairs={{0,2},{1,3},{2,0},{3,1},{4,6},{5,7},{6,4},{7,5},{8,10},{9,11},{10,... | collective-permute-start | bytes 1769480 | tf_op jit(solution)/shard_map/ppermute | solution.py:35
  701.9 51.9 %collective-permute-start.53 = (bf16[256,1152]{1,0:T(8,128)(2,1)S(1)}, bf16[256,1152]{1,0:T(8,128)(2,1)}, u32[]{:S(2)}, u32[]{:S(2)}) collective-permute-start(bf16[256,1152]{1,0:T(8,128)(2,1)S(1)} %get-tuple-element.483), channel_id=1, source_target_pairs={{0,3},{1,2},{2,1},{3,0},{4,7},{5,6},{6,5},{7,4},{8,11},{9,10},{10,... | collective-permute-start | bytes 1769480 | tf_op jit(solution)/shard_map/ppermute | solution.py:35
  767.7 23.8 %collective-permute-start.56 = (bf16[512,512]{1,0:T(8,128)(2,1)}, bf16[512,512]{1,0:T(8,128)(2,1)S(1)}, u32[]{:S(2)}, u32[]{:S(2)}) collective-permute-start(bf16[512,512]{1,0:T(8,128)(2,1)} %get-tuple-element.400), channel_id=1, source_target_pairs={{0,1},{1,0},{2,3},{3,2},{4,5},{5,4},{6,7},{7,6},{8,9},{9,8},{10,11... | collective-permute-start | bytes 1572872 | tf_op jit(solution)/shard_map/ppermute | solution.py:35
  767.7 35.9 %collective-permute-start.57 = (bf16[512,512]{1,0:T(8,128)(2,1)S(1)}, bf16[512,512]{1,0:T(8,128)(2,1)S(1)}, u32[]{:S(2)}, u32[]{:S(2)}) collective-permute-start(bf16[512,512]{1,0:T(8,128)(2,1)S(1)} %get-tuple-element.401), channel_id=1, source_target_pairs={{0,2},{1,3},{2,0},{3,1},{4,6},{5,7},{6,4},{7,5},{8,10},{9,11},{10,... | collective-permute-start | bytes 1572872 | tf_op jit(solution)/shard_map/ppermute | solution.py:35
  768.8 44.8 %collective-permute-start.58 = (bf16[512,512]{1,0:T(8,128)(2,1)S(1)}, bf16[512,512]{1,0:T(8,128)(2,1)S(1)}, u32[]{:S(2)}, u32[]{:S(2)}) collective-permute-start(bf16[512,512]{1,0:T(8,128)(2,1)S(1)} %get-tuple-element.398), channel_id=1, source_target_pairs={{0,3},{1,2},{2,1},{3,0},{4,7},{5,6},{6,5},{7,4},{8,11},{9,10},{10,... | collective-permute-start | bytes 1572872 | tf_op jit(solution)/shard_map/ppermute | solution.py:35
  (134 other events, 1185.0 us)
Sparse Core Ops, SparseCore 0:
  57.5 44.0 all-gather.7
  104.1 41.1 all-gather.9
  250.9 88.0 all-gather.11
  456.6 125.2 reduce-scatter.1
  583.7 100.8 all-gather.17
  696.8 24.7 all-gather.13
  756.6 37.9 all-gather.15

commit v6 on v5

--- a/solution.py
+++ b/solution.py
@@ -458,6 +458,27 @@
     )(starts, queries, keys, values, grads, sums_in)
 
 
+def compact_kernel(*refs):
+    *pieces, select_ref, out_ref = refs
+    rows, slots = out_ref.shape[0], pieces[0].shape[1]
+    out_ref[...] = sum(
+        mm(piece[:rows, :], select_ref[k * slots : (k + 1) * slots, :])
+        for k, piece in enumerate(pieces)
+    ).astype(low)
+
+
+def compact(pieces, select, rows):
+    if pieces[0].shape[1] % 128:
+        joined = jnp.concatenate([piece[:rows] for piece in pieces], axis=1)
+        return mm(joined, select).astype(low)
+    return pl.pallas_call(
+        compact_kernel,
+        out_shape=jax.ShapeDtypeStruct((rows, select.shape[1]), low),
+        compiler_params=pltpu.CompilerParams(vmem_limit_bytes=32 << 20),
+        cost_estimate=pl.CostEstimate(flops=0, bytes_accessed=1 << 16, transcendentals=0),
+    )(*pieces, select)
+
+
 def gates_back(hidden_grad, raised):
     half = raised.shape[1] // 2
     gate, up = raised[:, :half], raised[:, half:]
@@ -696,16 +717,14 @@
     inputs = got[7 + 2 * parts :]
 
     inputs.append(exchange(late, "mp", parts - 1, parts))
-    output_slice = swap([output_slice] * parts, "mp")
     gains = by_rank([piece[rows:].reshape(4, -1)[:, :share] for piece in query_slice], rank)
     gains = jnp.concatenate(gains, 1).astype(full)
     attention_gain_all, feedforward_gain_all = gains[0] + gains[2], gains[1] + gains[3]
-    query_slice = jnp.concatenate([piece[:rows] for piece in query_slice], axis=1)
-    query_slice = mm(query_slice, select_near).astype(low)
+    query_slice = compact(query_slice, select_near, rows)
     query_all = lax.all_gather(query_slice, "dp", axis=0, tiled=True)
-    got = order(*inputs, *output_slice)
-    inputs, output_slice = got[:parts], got[parts:]
-
+    *inputs, output_slice = order(*inputs, output_slice)
+
+    output_slice = swap([output_slice] * parts, "mp")
     inputs = jnp.concatenate(by_rank(inputs, rank), axis=1).astype(full)
     first_rms = lax.rsqrt(jnp.mean(inputs * inputs, axis=1, keepdims=True) + epsilon)
     normed = (inputs * first_rms * attention_gain_all).astype(low)
@@ -713,7 +732,7 @@
     values_mine = dot(value_weight, normed, 0, 1).astype(low).reshape(KVH, HD, mine)
     turned_keys, key_pull = jax.vjp(lambda v, g: turn(v, g, cosine, sine), keys, key_gain)
     pair_mine = jnp.concatenate([turned_keys.astype(low), values_mine], 0)
-    pair_mine, normed = order(pair_mine, normed)
+    pair_mine, normed, *output_slice = order(pair_mine, normed, *output_slice)
 
     near_pairs = [pair_mine] + [exchange(pair_mine, "mp", k, parts) for k in range(1, ring)]
     output_slice = jnp.concatenate(by_rank(output_slice, rank), axis=1)

time: 844 us -> 837 us (level)
    ppermute x21, waiting for transfers between devices: 159 us -> 127 us  [swap(): lax.ppermute(pieces[k], axis, [(i, i ^ k) for i in range(n)])]
    ppermute x32, waiting for transfers between devices: 91.3 us -> 106 us  [exchange(): return lax.ppermute(array, axis, [(i, i ^ mask) for i in range(n)])]
    dot_general x6 -> x5, matrix products: 32.7 us -> 30.6 us  [mm(): return jnp.dot(left, right, preferred_element_type=full)]
    unnamed x278 -> x288, local copies, waits for them, and re-layouts: 47.9 us -> 48 us
  transfers between devices with their start and end apart: 66 -> 66, of which waited for: 40 -> 40; matrix products, arithmetic and copies ran while one was open for 31% -> 32% of each run, Pallas kernels for 12% -> 12%
where the time goes in v6:
time: 837 us; the launch traced here: 827 us
  waiting for transfers between devices  300 us (36%)
  matrix products  127 us (15%)
  Pallas kernels  126 us (15%)
  other arithmetic  101 us (12%)
  local copies, waits for them, and re-layouts  84.7 us (10%)
  starting transfers between devices  71.8 us (9%)
  between operations  16.6 us (2%)
    ppermute x21, waiting for transfers between devices, swap(): lax.ppermute(pieces[k], axis, [(i, i ^ k) for i in range(n)])  127 us
    ppermute x32, waiting for transfers between devices, exchange(): return lax.ppermute(array, axis, [(i, i ^ mask) for i in range(n)])  106 us
    dot_general x17, matrix products, dot(): lax.dot_general(left, right, (((left_axis,), (right_axis,)), ((), ())), p...  96.4 us
    ppermute x3, waiting for transfers between devices, send(): lax.ppermute(up, self.axis, right)  50.8 us
    unnamed x288, local copies, waits for them, and re-layouts  48 us
    pallas_call x2, Pallas kernels, units_back(): pl.pallas_call(units_back_kernel, out_shape=(jax.ShapeDtypeStruct(raised....  39.6 us
    ppermute x32, starting transfers between devices, exchange(): return lax.ppermute(array, axis, [(i, i ^ mask) for i in range(n)])  30.6 us
    dot_general x5, matrix products, mm(): return jnp.dot(left, right, preferred_element_type=full)  30.6 us
  transfers between devices with their start and end apart: 66, of which 40 were waited for; matrix products, arithmetic and copies ran while one was open for 32% of the time, Pallas kernels for 12%

profile of v6, /device:TPU:16, one launch (start us, length us, event | category | flops | bytes accessed | tf_op | source)
XLA Modules:
  0.0 827.5 jit_solution(7195356248708260499)
XLA Ops:
  12.4 3.4 constant_dynamic-slice_fusion.8
  25.8 3.6 iota_compare_fusion
  40.1 3.6 fusion.26
  46.1 4.6 collective-permute-done.4
  54.9 22.0 %collective-permute-done.5 = bf16[512,512]{1,0:T(8,128)(2,1)S(1)} collective-permute-done((bf16[512,512]{1,0:T(8,128)(2,1)S(1)}, bf16[512,512]{1,0:T(8,128)(2,1)S(1)}, u32[]{:S(2)}, u32[]{:S(2)}) %collective-permute-start.5) | collective-permute-done | bytes 524320 | tf_op jit(solution)/shard_map/ppermute | solution.py:49
  97.2 5.5 fusion.74
  105.6 4.4 collective-permute-done.9
  110.3 3.3 collective-permute-start.11
  115.2 14.6 %shard_map.247 = (bf16[20,64,512]{2,1,0:T(8,128)(2,1)S(1)}, f32[5,4,512]{2,1,0:T(4,128)S(1)}) custom-call(s32[2]{0:T(128)S(1)} %pad_add_fusion.2.starts, bf16[20,64,512]{2,1,0:T(8,128)(2,1)S(1)} %fusion.21.q_ref, bf16[5,64,1024]{2,1,0:T(8,128)(2,1)S(1)} %get-tuple-element.461.k_ref, bf16[5,64,1024]{2,1,0:T(8,128)(2,1)S(1)} %get-tuple-element.460.v_ref), custom_call_target="tpu_custom_call" | custom-call | flops 6553600 | bytes 1048576 | tf_op jit(solution)/shard_map/pallas_call | solution.py:416
  131.5 9.4 %all-gather.10.cloned.1.call-done = bf16[1280,2048]{1,0:T(8,128)(2,1)} async-done(((bf16[160,2048]{1,0:T(8,128)(2,1)}), bf16[1280,2048]{1,0:T(8,128)(2,1)}) %all-gather.10.cloned.1.call-update) | async-done | bytes 5242896 | tf_op jit(solution)/shard_map/all_gather | solution.py:739
  140.9 6.1 multiply_reduce_fusion
  149.7 7.1 collective-permute-done.12
  161.7 4.4 collective-permute-start.16
  174.5 20.8 %collective-permute-done.15 = bf16[2048,384]{1,0:T(8,128)(2,1)} collective-permute-done((bf16[2048,384]{1,0:T(8,128)(2,1)}, bf16[2048,384]{1,0:T(8,128)(2,1)}, u32[]{:S(2)}, u32[]{:S(2)}) %collective-permute-start.15) | collective-permute-done | bytes 1572896 | tf_op jit(solution)/shard_map/ppermute | solution.py:79
  196.4 5.0 collective-permute-done.13
  204.5 5.2 collective-permute-start.20
  209.7 4.5 broadcast_in_dim.51
  214.2 3.2 bitcast_dynamic-update-slice_fusion.2
  222.1 3.2 bitcast_dynamic-update-slice_fusion.1
  225.3 3.2 bitcast_dynamic-update-slice_fusion
  228.4 10.5 %collective-permute-done.17 = bf16[256,2048]{1,0:T(8,128)(2,1)S(1)} collective-permute-done((bf16[256,2048]{1,0:T(8,128)(2,1)S(1)}, bf16[256,2048]{1,0:T(8,128)(2,1)S(1)}, u32[]{:S(2)}, u32[]{:S(2)}) %collective-permute-start.17) | collective-permute-done | bytes 1048608 | tf_op jit(solution)/shard_map/ppermute | solution.py:49
  251.1 30.0 %collective-permute-done.22 = bf16[2048,384]{1,0:T(8,128)(2,1)S(1)} collective-permute-done((bf16[2048,384]{1,0:T(8,128)(2,1)S(1)}, bf16[2048,384]{1,0:T(8,128)(2,1)S(1)}, u32[]{:S(2)}, u32[]{:S(2)}) %collective-permute-start.22) | collective-permute-done | bytes 1572896 | tf_op jit(solution)/shard_map/ppermute | solution.py:79
  281.1 3.1 add.492
  291.6 9.1 %fusion.76.raised_ref = f32[2048,1024]{1,0:T(8,128)S(1)} fusion(bf16[2048,2048]{1,0:T(8,128)(2,1)S(1)} %collective-permute-done.21, bf16[2048,1024]{1,0:T(8,128)(2,1)S(1)} %get-tuple-element.453.wide_ref), kind=kOutput, calls=%fused_computation.374 | convolution fusion | flops 8589934592 | bytes 20971520 | tf_op jit(solution)/shard_map/dot_general | solution.py:275
  300.7 3.3 copy-done.34
  305.7 12.0 %fusion.75.raised_ref = f32[2048,1024]{1,0:T(8,128)S(1)} fusion(bf16[2048,2048]{1,0:T(8,128)(2,1)} %bitcast.32, bf16[2048,1024]{1,0:T(8,128)(2,1)S(1)} %get-tuple-element.453.wide_ref), kind=kOutput, calls=%fused_computation.373 | convolution fusion | flops 8589934592 | bytes 20971520 | tf_op jit(solution)/shard_map/dot_general | solution.py:275
  317.7 3.2 copy-done.33
  322.4 6.8 convolution_convert_fusion
  329.2 6.9 convolution_convert_fusion.1.mine_ref
  337.7 19.6 %shard_map.248 = (bf16[2048,1024]{1,0:T(8,128)(2,1)S(1)}, bf16[2048,2048]{1,0:T(8,128)(2,1)}) custom-call(s32[1]{0:T(128)} %bitcast.34.core, bf16[4,2,512,2048]{3,2,1,0:T(8,128)(2,1)} %bitcast.107, f32[2048,1024]{1,0:T(8,128)} %copy-done.34, bf16[2048,512]{1,0:T(8,128)(2,1)S(1)} %copy-done.3, bf16[2048,1024]{1,0:T(8,128)(2,1)} %copy-done.35), custom_call_target="tpu_custom_call" | custom-call | bytes 65536 | tf_op jit(solution)/shard_map/pallas_call | solution.py:509
  361.6 20.0 %shard_map.249 = (bf16[2048,1024]{1,0:T(8,128)(2,1)S(1)}, bf16[2048,2048]{1,0:T(8,128)(2,1)}) custom-call(s32[1]{0:T(128)} %bitcast.29.core, bf16[4,2,512,2048]{3,2,1,0:T(8,128)(2,1)} %bitcast.108, f32[2048,1024]{1,0:T(8,128)} %copy-done.33, bf16[2048,512]{1,0:T(8,128)(2,1)S(1)} %copy-done.4, bf16[2048,1024]{1,0:T(8,128)(2,1)} %copy-done.35), custom_call_target="tpu_custom_call" | custom-call | bytes 65536 | tf_op jit(solution)/shard_map/pallas_call | solution.py:509
  381.6 10.4 %shard_map.250 = (bf16[512,2048]{1,0:T(8,128)(2,1)S(1)}, bf16[512,2048]{1,0:T(8,128)(2,1)S(1)}, bf16[1024,2048]{1,0:T(8,128)(2,1)S(1)}) custom-call(s32[8]{0:T(128)S(1)} %stack.97.index_ref, bf16[2048,2048]{1,0:T(8,128)(2,1)} %get-tuple-element.263.mine_ref, bf16[2048,2048]{1,0:T(8,128)(2,1)} %collective-permute-done.24.got_ref), custom_call_target="tpu_custom_call" | custom-call | bytes 65536 | tf_op jit(solution)/shard_map/pallas_call | solution.py:169
  396.2 13.5 %fusion.77 = f32[2048,1024]{1,0:T(8,128)} fusion(bf16[2048,2048]{1,0:T(8,128)(2,1)} %copy-done.136, bf16[2048,1024]{1,0:T(8,128)(2,1)S(1)} %copy-done.22), kind=kOutput, calls=%fused_computation.375 | convolution fusion | flops 8589934592 | bytes 20971520 | tf_op jit(solution)/shard_map/dot_general | solution.py:27
  409.7 12.4 %convolution_convert_fusion.5.down_ref = bf16[2048,512]{1,0:T(8,128)(2,1)S(1)} fusion(bf16[4096,2048]{1,0:T(8,128)(2,1)} %all-gather.12.cloned.1.call-done, bf16[4096,512]{1,0:T(8,128)(2,1)S(1)} %bitcast.127), kind=kOutput, calls=%fused_computation.48 | convolution fusion | flops 8590983168 | bytes 23068672 | tf_op jit(solution)/shard_map/dot_general | solution.py:27
  422.1 12.9 %add_convert_fusion.2.gate_ref.up_ref = bf16[2048,1024]{1,0:T(8,128)(2,1)S(1)} fusion(f32[2048,1024]{1,0:T(8,128)} %fusion.77, bf16[2048,2048]{1,0:T(8,128)(2,1)} %bitcast.32, bf16[2048,1024]{1,0:T(8,128)(2,1)S(1)} %get-tuple-element.268), kind=kOutput, calls=%fused_computation.6 | convolution fusion | flops 8594128896 | bytes 25165824 | tf_op jit(solution)/shard_map/dot_general | solution.py:27
  435.0 4.6 collective-permute-done.25
  442.2 3.2 shard_map.253
  448.3 4.1 add_convert_fusion.10
  453.7 12.2 %shard_map.251 = (bf16[256,2048]{1,0:T(8,128)(2,1)S(1)}, bf16[256,2048]{1,0:T(8,128)(2,1)S(1)}, bf16[256,2048]{1,0:T(8,128)(2,1)S(1)}, bf16[256,2048]{1,0:T(8,128)(2,1)S(1)}, bf16[1024,2048]{1,0:T(8,128)(2,1)S(1)}) custom-call(s32[8]{0:T(128)S(1)} %stack.98.index_ref, bf16[2048,2048]{1,0:T(8,128)(2,1)} %convolution_convert_fusion.1.mine_ref, ...), custom_call_target="tpu_custom_call" | custom-call | bytes 65536 | tf_op jit(solution)/shard_map/pallas_call | solution.py:169
  465.9 10.9 %collective-permute-done.28 = bf16[256,2048]{1,0:T(8,128)(2,1)} collective-permute-done((bf16[256,2048]{1,0:T(8,128)(2,1)}, bf16[256,2048]{1,0:T(8,128)(2,1)}, u32[]{:S(2)}, u32[]{:S(2)}) %collective-permute-start.28) | collective-permute-done | bytes 1048608 | tf_op jit(solution)/shard_map/ppermute | solution.py:49
  488.4 6.7 convolution_convert_fusion.4
  495.1 25.3 %shard_map.252 = (f32[20,64,512]{2,1,0:T(8,128)S(1)}, f32[5,64,1024]{2,1,0:T(8,128)S(1)}, f32[5,64,1024]{2,1,0:T(8,128)S(1)}) custom-call(s32[2]{0:T(128)S(1)} %copy-done.20, bf16[20,64,512]{2,1,0:T(8,128)(2,1)S(1)} %copy-done.8, bf16[5,64,1024]{2,1,0:T(8,128)(2,1)S(1)} %copy-done.12, bf16[5,64,1024]{2,1,0:T(8,128)(2,1)S(1)} %copy-done.10, ...), custom_call_target="tpu_custom_call" | custom-call | flops 6553600 | bytes 1048576 | tf_op jit(solution)/shard_map/pallas_call | solution.py:440
  541.7 5.2 collective-permute-done.36
  548.2 18.9 %collective-permute-done.33 = bf16[10,64,512]{2,1,0:T(8,128)(2,1)S(1)} collective-permute-done((bf16[10,64,512]{2,1,0:T(8,128)(2,1)S(1)}, bf16[10,64,512]{2,1,0:T(8,128)(2,1)S(1)}, u32[]{:S(2)}, u32[]{:S(2)}) %collective-permute-start.33) | collective-permute-done | bytes 655392 | tf_op jit(solution)/shard_map/ppermute | solution.py:49
  570.3 3.3 reduce-scatter.2.cloned.1.call-done
  580.1 5.3 add_convert_fusion.1
  590.1 5.1 fusion.24
  612.1 3.1 collective-permute-start.43
  616.6 14.6 %collective-permute-done.41 = bf16[512,512]{1,0:T(8,128)(2,1)S(1)} collective-permute-done((bf16[512,512]{1,0:T(8,128)(2,1)S(1)}, bf16[512,512]{1,0:T(8,128)(2,1)S(1)}, u32[]{:S(2)}, u32[]{:S(2)}) %collective-permute-start.41) | collective-permute-done | bytes 524320 | tf_op jit(solution)/shard_map/ppermute | solution.py:35
  631.2 15.7 %collective-permute-done.42 = bf16[512,512]{1,0:T(8,128)(2,1)S(1)} collective-permute-done((bf16[512,512]{1,0:T(8,128)(2,1)S(1)}, bf16[512,512]{1,0:T(8,128)(2,1)S(1)}, u32[]{:S(2)}, u32[]{:S(2)}) %collective-permute-start.42) | collective-permute-done | bytes 524320 | tf_op jit(solution)/shard_map/ppermute | solution.py:35
  646.8 12.8 %collective-permute-done.43 = bf16[512,512]{1,0:T(8,128)(2,1)S(1)} collective-permute-done((bf16[512,512]{1,0:T(8,128)(2,1)S(1)}, bf16[512,512]{1,0:T(8,128)(2,1)S(1)}, u32[]{:S(2)}, u32[]{:S(2)}) %collective-permute-start.43) | collective-permute-done | bytes 524320 | tf_op jit(solution)/shard_map/ppermute | solution.py:35
  668.1 3.3 collective-permute-done.46
  683.7 4.2 convolution_convert_fusion.6
  695.3 6.9 collective-permute-done.54
  703.4 10.8 %collective-permute-done.51 = bf16[256,1152]{1,0:T(8,128)(2,1)S(1)} collective-permute-done((bf16[256,1152]{1,0:T(8,128)(2,1)S(1)}, bf16[256,1152]{1,0:T(8,128)(2,1)S(1)}, u32[]{:S(2)}, u32[]{:S(2)}) %collective-permute-start.51) | collective-permute-done | bytes 589856 | tf_op jit(solution)/shard_map/ppermute | solution.py:35
  714.3 18.2 %collective-permute-done.52 = bf16[256,1152]{1,0:T(8,128)(2,1)S(1)} collective-permute-done((bf16[256,1152]{1,0:T(8,128)(2,1)S(1)}, bf16[256,1152]{1,0:T(8,128)(2,1)S(1)}, u32[]{:S(2)}, u32[]{:S(2)}) %collective-permute-start.52) | collective-permute-done | bytes 589856 | tf_op jit(solution)/shard_map/ppermute | solution.py:35
  733.3 12.0 %collective-permute-done.53 = bf16[256,1152]{1,0:T(8,128)(2,1)} collective-permute-done((bf16[256,1152]{1,0:T(8,128)(2,1)S(1)}, bf16[256,1152]{1,0:T(8,128)(2,1)}, u32[]{:S(2)}, u32[]{:S(2)}) %collective-permute-start.53) | collective-permute-done | bytes 589856 | tf_op jit(solution)/shard_map/ppermute | solution.py:35
  753.9 3.5 add_convert_fusion.5
  762.9 6.4 fusion.78
  769.3 5.3 copy-done.6
  774.6 8.6 %shard_map.256 = (f32[2048,1024]{1,0:T(8,128)}, f32[2048,1024]{1,0:T(8,128)}, f32[1024,2048]{1,0:T(8,128)}) custom-call(bf16[8,2048,384]{2,1,0:T(8,128)(2,1)S(1)} %bitcast.103), custom_call_target="tpu_custom_call" | custom-call | bytes 65536 | tf_op jit(solution)/shard_map/pallas_call | solution.py:585
  783.2 11.9 %collective-permute-done.57 = bf16[512,512]{1,0:T(8,128)(2,1)S(1)} collective-permute-done((bf16[512,512]{1,0:T(8,128)(2,1)S(1)}, bf16[512,512]{1,0:T(8,128)(2,1)S(1)}, u32[]{:S(2)}, u32[]{:S(2)}) %collective-permute-start.57) | collective-permute-done | bytes 524320 | tf_op jit(solution)/shard_map/ppermute | solution.py:35
  795.1 10.4 %collective-permute-done.58 = bf16[512,512]{1,0:T(8,128)(2,1)S(1)} collective-permute-done((bf16[512,512]{1,0:T(8,128)(2,1)S(1)}, bf16[512,512]{1,0:T(8,128)(2,1)S(1)}, u32[]{:S(2)}, u32[]{:S(2)}) %collective-permute-start.58) | collective-permute-done | bytes 524320 | tf_op jit(solution)/shard_map/ppermute | solution.py:35
  815.5 4.9 shard_map.257
  (568 shorter events, 243.0 us)
Async XLA Ops:
  7.2 90.1 %all-gather.8.cloned.1.call-start = ((), (), s32[]{:S(2)}) async-start(), calls=%async_computation.1 | async-start | bytes 5898240 | tf_op jit(solution)/shard_map/all_gather | solution.py:724
  8.9 37.2 %collective-permute-start = (bf16[264,384]{1,0:T(8,128)(2,1)S(1)}, bf16[264,384]{1,0:T(8,128)(2,1)S(1)}, u32[]{:S(2)}, u32[]{:S(2)}) collective-permute-start(bf16[264,384]{1,0:T(8,128)(2,1)S(1)} %pad_maximum_fusion.31.refs_0_), channel_id=1, source_target_pairs={{0,1},{1,0},{2,3},{3,2},{4,5},{5,4},{6,7},{7,6},{8,9},{9,8},{10,11... | collective-permute-start | bytes 608264 | tf_op jit(solution)/shard_map/ppermute | solution.py:35
  10.5 35.5 %collective-permute-start.1 = (bf16[264,384]{1,0:T(8,128)(2,1)S(1)}, bf16[264,384]{1,0:T(8,128)(2,1)S(1)}, u32[]{:S(2)}, u32[]{:S(2)}) collective-permute-start(bf16[264,384]{1,0:T(8,128)(2,1)S(1)} %pad_maximum_fusion.31.refs_0_), channel_id=1, source_target_pairs={{0,2},{1,3},{2,0},{3,1},{4,6},{5,7},{6,4},{7,5},{8,10},{9,11},{10,... | collective-permute-start | bytes 608264 | tf_op jit(solution)/shard_map/ppermute | solution.py:35
  10.9 35.2 %collective-permute-start.2 = (bf16[264,384]{1,0:T(8,128)(2,1)S(1)}, bf16[264,384]{1,0:T(8,128)(2,1)S(1)}, u32[]{:S(2)}, u32[]{:S(2)}) collective-permute-start(bf16[264,384]{1,0:T(8,128)(2,1)S(1)} %pad_maximum_fusion.31.refs_0_), channel_id=1, source_target_pairs={{0,3},{1,2},{2,1},{3,0},{4,7},{5,6},{6,5},{7,4},{8,11},{9,10},{10,... | collective-permute-start | bytes 608264 | tf_op jit(solution)/shard_map/ppermute | solution.py:35
  16.7 29.3 %collective-permute-start.3 = (bf16[512,512]{1,0:T(8,128)(2,1)}, bf16[512,512]{1,0:T(8,128)(2,1)}, u32[]{:S(2)}, u32[]{:S(2)}) collective-permute-start(bf16[512,512]{1,0:T(8,128)(2,1)} %pad_maximum_fusion.29), channel_id=1, source_target_pairs={{0,1},{1,0},{2,3},{3,2},{4,5},{5,4},{6,7},{7,6},{8,9},{9,8},{10,11... | collective-permute-start | bytes 1572872 | tf_op jit(solution)/shard_map/ppermute | solution.py:49
  20.0 30.6 %collective-permute-start.4 = (bf16[512,512]{1,0:T(8,128)(2,1)}, bf16[512,512]{1,0:T(8,128)(2,1)}, u32[]{:S(2)}, u32[]{:S(2)}) collective-permute-start(bf16[512,512]{1,0:T(8,128)(2,1)} %pad_maximum_fusion.30), channel_id=1, source_target_pairs={{0,2},{1,3},{2,0},{3,1},{4,6},{5,7},{6,4},{7,5},{8,10},{9,11},{10,... | collective-permute-start | bytes 1572872 | tf_op jit(solution)/shard_map/ppermute | solution.py:49
  53.0 87.9 %all-gather.10.cloned.1.call-start = ((), (), s32[]{:S(2)}) async-start(), calls=%async_computation.2 | async-start | bytes 5898240 | tf_op jit(solution)/shard_map/all_gather | solution.py:739
  53.1 23.8 %collective-permute-start.5 = (bf16[512,512]{1,0:T(8,128)(2,1)S(1)}, bf16[512,512]{1,0:T(8,128)(2,1)S(1)}, u32[]{:S(2)}, u32[]{:S(2)}) collective-permute-start(bf16[512,512]{1,0:T(8,128)(2,1)S(1)} %copy-done.105), channel_id=1, source_target_pairs={{0,3},{1,2},{2,1},{3,0},{4,7},{5,6},{6,5},{7,4},{8,11},{9,10},{10,... | collective-permute-start | bytes 1572872 | tf_op jit(solution)/shard_map/ppermute | solution.py:49
  76.9 12.8 %collective-permute-start.7 = (bf16[160,512]{1,0:T(8,128)(2,1)}, bf16[160,512]{1,0:T(8,128)(2,1)S(1)}, u32[]{:S(2)}, u32[]{:S(2)}) collective-permute-start(bf16[160,512]{1,0:T(8,128)(2,1)} %fusion.26), channel_id=1, source_target_pairs={{0,2},{1,3},{2,0},{3,1},{4,6},{5,7},{6,4},{7,5},{8,10},{9,11},{10,... | collective-permute-start | bytes 491528 | tf_op jit(solution)/shard_map/ppermute | solution.py:35
  80.0 12.8 %collective-permute-start.8 = (bf16[160,512]{1,0:T(8,128)(2,1)}, bf16[160,512]{1,0:T(8,128)(2,1)S(1)}, u32[]{:S(2)}, u32[]{:S(2)}) collective-permute-start(bf16[160,512]{1,0:T(8,128)(2,1)} %fusion.26), channel_id=1, source_target_pairs={{0,3},{1,2},{2,1},{3,0},{4,7},{5,6},{6,5},{7,4},{8,11},{9,10},{10,... | collective-permute-start | bytes 491528 | tf_op jit(solution)/shard_map/ppermute | solution.py:35
  94.6 241.5 %all-gather.12.cloned.1.call-start = ((), (), s32[]{:S(2)}) async-start(), calls=%async_computation.3 | async-start | bytes 18874368 | tf_op jit(solution)/shard_map/all_gather | solution.py:791
  94.9 15.1 %collective-permute-start.9 = (bf16[10,64,512]{2,1,0:T(8,128)(2,1)S(1)}, bf16[10,64,512]{2,1,0:T(8,128)(2,1)}, u32[]{:S(2)}, u32[]{:S(2)}) collective-permute-start(bf16[10,64,512]{2,1,0:T(8,128)(2,1)S(1)} %pad_maximum_fusion.20), channel_id=1, source_target_pairs={{0,1},{1,0},{2,3},{3,2},{4,5},{5,4},{6,7},{7,6},{8,9},{9,8},{10,11... | collective-permute-start | bytes 1966088 | tf_op jit(solution)/shard_map/ppermute | solution.py:49
  110.0 39.6 %collective-permute-start.10 = (bf16[512,512]{1,0:T(8,128)(2,1)}, bf16[512,512]{1,0:T(8,128)(2,1)}, u32[]{:S(2)}, u32[]{:S(2)}) collective-permute-start(bf16[512,512]{1,0:T(8,128)(2,1)} %pad_maximum_fusion.25), channel_id=1, source_target_pairs={{0,1},{1,0},{2,3},{3,2},{4,5},{5,4},{6,7},{7,6},{8,9},{9,8},{10,11... | collective-permute-start | bytes 1572872 | tf_op jit(solution)/shard_map/ppermute | solution.py:35
  110.3 39.3 %collective-permute-start.11 = (bf16[512,512]{1,0:T(8,128)(2,1)}, bf16[512,512]{1,0:T(8,128)(2,1)}, u32[]{:S(2)}, u32[]{:S(2)}) collective-permute-start(bf16[512,512]{1,0:T(8,128)(2,1)} %pad_maximum_fusion.26), channel_id=1, source_target_pairs={{0,2},{1,3},{2,0},{3,1},{4,6},{5,7},{6,4},{7,5},{8,10},{9,11},{10,... | collective-permute-start | bytes 1572872 | tf_op jit(solution)/shard_map/ppermute | solution.py:35
  113.6 43.1 %collective-permute-start.12 = (bf16[512,512]{1,0:T(8,128)(2,1)}, bf16[512,512]{1,0:T(8,128)(2,1)}, u32[]{:S(2)}, u32[]{:S(2)}) collective-permute-start(bf16[512,512]{1,0:T(8,128)(2,1)} %pad_maximum_fusion.27), channel_id=1, source_target_pairs={{0,3},{1,2},{2,1},{3,0},{4,7},{5,6},{6,5},{7,4},{8,11},{9,10},{10,... | collective-permute-start | bytes 1572872 | tf_op jit(solution)/shard_map/ppermute | solution.py:35
  156.7 44.7 %collective-permute-start.13 = (bf16[512,2048]{1,0:T(8,128)(2,1)}, bf16[512,2048]{1,0:T(8,128)(2,1)}, u32[]{:S(2)}, u32[]{:S(2)}) collective-permute-start(bf16[512,2048]{1,0:T(8,128)(2,1)} %multiply_convert_fusion), channel_id=1, source_target_pairs={{0,8},{4,12},{8,0},{12,4},{16,24},{20,28},{24,16},{28,20},{1,9},{5... | collective-permute-start | bytes 6291464 | tf_op jit(solution)/shard_map/ppermute | solution.py:49
  158.2 44.4 %collective-permute-start.14 = (bf16[512,2048]{1,0:T(8,128)(2,1)}, bf16[512,2048]{1,0:T(8,128)(2,1)}, u32[]{:S(2)}, u32[]{:S(2)}) collective-permute-start(bf16[512,2048]{1,0:T(8,128)(2,1)} %multiply_convert_fusion), channel_id=1, source_target_pairs={{0,16},{4,20},{8,24},{12,28},{16,0},{20,4},{24,8},{28,12},{1,17},{... | collective-permute-start | bytes 6291464 | tf_op jit(solution)/shard_map/ppermute | solution.py:49
  159.7 35.5 %collective-permute-start.15 = (bf16[2048,384]{1,0:T(8,128)(2,1)}, bf16[2048,384]{1,0:T(8,128)(2,1)}, u32[]{:S(2)}, u32[]{:S(2)}) collective-permute-start(bf16[2048,384]{1,0:T(8,128)(2,1)} %pad_maximum_fusion.6), channel_id=1, source_target_pairs={{0,1},{1,2},{2,3},{4,5},{5,6},{6,7},{8,9},{9,10},{10,11},{12,13},{... | collective-permute-start | bytes 4718600 | tf_op jit(solution)/shard_map/ppermute | solution.py:79
  161.7 34.8 %collective-permute-start.16 = (bf16[2048,384]{1,0:T(8,128)(2,1)}, bf16[2048,384]{1,0:T(8,128)(2,1)}, u32[]{:S(2)}, u32[]{:S(2)}) collective-permute-start(bf16[2048,384]{1,0:T(8,128)(2,1)} %pad_maximum_fusion.6), channel_id=1, source_target_pairs={{3,2},{2,1},{1,0},{7,6},{6,5},{5,4},{11,10},{10,9},{9,8},{15,14},{... | collective-permute-start | bytes 4718600 | tf_op jit(solution)/shard_map/ppermute | solution.py:79
  202.6 38.9 %collective-permute-start.19 = (bf16[2048,384]{1,0:T(8,128)(2,1)}, bf16[2048,384]{1,0:T(8,128)(2,1)S(1)}, u32[]{:S(2)}, u32[]{:S(2)}) collective-permute-start(bf16[2048,384]{1,0:T(8,128)(2,1)} %collective-permute-done.15), channel_id=1, source_target_pairs={{1,2},{2,3},{5,6},{6,7},{9,10},{10,11},{13,14},{14,15},{17,18},{18... | collective-permute-start | bytes 4718600 | tf_op jit(solution)/shard_map/ppermute | solution.py:79
  204.5 38.0 %collective-permute-start.20 = (bf16[2048,384]{1,0:T(8,128)(2,1)}, bf16[2048,384]{1,0:T(8,128)(2,1)}, u32[]{:S(2)}, u32[]{:S(2)}) collective-permute-start(bf16[2048,384]{1,0:T(8,128)(2,1)} %collective-permute-done.16), channel_id=1, source_target_pairs={{2,1},{1,0},{6,5},{5,4},{10,9},{9,8},{14,13},{13,12},{18,17},{17,1... | collective-permute-start | bytes 4718600 | tf_op jit(solution)/shard_map/ppermute | solution.py:79
  218.6 20.3 %collective-permute-start.17 = (bf16[256,2048]{1,0:T(8,128)(2,1)S(1)}, bf16[256,2048]{1,0:T(8,128)(2,1)S(1)}, u32[]{:S(2)}, u32[]{:S(2)}) collective-permute-start(bf16[256,2048]{1,0:T(8,128)(2,1)S(1)} %slice.396), channel_id=1, source_target_pairs={{0,16},{4,20},{8,24},{12,28},{16,0},{20,4},{24,8},{28,12},{1,17},{... | collective-permute-start | bytes 3145736 | tf_op jit(solution)/shard_map/ppermute | solution.py:49
  221.5 20.0 %collective-permute-start.18 = (bf16[256,2048]{1,0:T(8,128)(2,1)S(1)}, bf16[256,2048]{1,0:T(8,128)(2,1)S(1)}, u32[]{:S(2)}, u32[]{:S(2)}) collective-permute-start(bf16[256,2048]{1,0:T(8,128)(2,1)S(1)} %slice.397), channel_id=1, source_target_pairs={{0,8},{4,12},{8,0},{12,4},{16,24},{20,28},{24,16},{28,20},{1,9},{5... | collective-permute-start | bytes 3145736 | tf_op jit(solution)/shard_map/ppermute | solution.py:49
  242.5 331.2 %reduce-scatter.2.cloned.1.call-start = ((), (), s32[]{:S(2)}) async-start(), calls=%async_computation.4 | async-start | bytes 7864320 | tf_op jit(solution)/shard_map/reduce_scatter | solution.py:848
  245.2 35.9 %collective-permute-start.21 = (bf16[2048,2048]{1,0:T(8,128)(2,1)}, bf16[2048,2048]{1,0:T(8,128)(2,1)S(1)}, u32[]{:S(2)}, u32[]{:S(2)}) collective-permute-start(bf16[2048,2048]{1,0:T(8,128)(2,1)} %bitcast.32), channel_id=1, source_target_pairs={{0,4},{4,0},{8,12},{12,8},{16,20},{20,16},{24,28},{28,24},{1,5},{5... | collective-permute-start | bytes 25165832 | tf_op jit(solution)/shard_map/ppermute | solution.py:49
  245.2 35.9 %collective-permute-start.22 = (bf16[2048,384]{1,0:T(8,128)(2,1)S(1)}, bf16[2048,384]{1,0:T(8,128)(2,1)S(1)}, u32[]{:S(2)}, u32[]{:S(2)}) collective-permute-start(bf16[2048,384]{1,0:T(8,128)(2,1)S(1)} %collective-permute-done.19), channel_id=1, source_target_pairs={{2,3},{6,7},{10,11},{14,15},{18,19},{22,23},{26,27},{30,31}} | collective-permute-start | bytes 4718600 | tf_op jit(solution)/shard_map/ppermute | solution.py:79
  246.6 34.5 %collective-permute-start.23 = (bf16[2048,384]{1,0:T(8,128)(2,1)}, bf16[2048,384]{1,0:T(8,128)(2,1)S(1)}, u32[]{:S(2)}, u32[]{:S(2)}) collective-permute-start(bf16[2048,384]{1,0:T(8,128)(2,1)} %collective-permute-done.20), channel_id=1, source_target_pairs={{1,0},{5,4},{9,8},{13,12},{17,16},{21,20},{25,24},{29,28}} | collective-permute-start | bytes 4718600 | tf_op jit(solution)/shard_map/ppermute | solution.py:79
  359.4 22.2 %collective-permute-start.24 = (bf16[2048,2048]{1,0:T(8,128)(2,1)}, bf16[2048,2048]{1,0:T(8,128)(2,1)}, u32[]{:S(2)}, u32[]{:S(2)}) collective-permute-start(bf16[2048,2048]{1,0:T(8,128)(2,1)} %get-tuple-element.262), channel_id=1, source_target_pairs={{0,4},{4,0},{8,12},{12,8},{16,20},{20,16},{24,28},{28,24},{1,5},{5... | collective-permute-start | bytes 25165832 | tf_op jit(solution)/shard_map/ppermute | solution.py:49
  359.4 75.6 %collective-permute-start.27 = (bf16[2048,2048]{1,0:T(8,128)(2,1)}, bf16[2048,2048]{1,0:T(8,128)(2,1)}, u32[]{:S(2)}, u32[]{:S(2)}) collective-permute-start(bf16[2048,2048]{1,0:T(8,128)(2,1)} %convolution_convert_fusion), channel_id=1, source_target_pairs={{0,4},{4,0},{8,12},{12,8},{16,20},{20,16},{24,28},{28,24},{1,5},{5... | collective-permute-start | bytes 25165832 | tf_op jit(solution)/shard_map/ppermute | solution.py:49
  392.0 47.6 %collective-permute-start.25 = (bf16[512,2048]{1,0:T(8,128)(2,1)S(1)}, bf16[512,2048]{1,0:T(8,128)(2,1)S(1)}, u32[]{:S(2)}, u32[]{:S(2)}) collective-permute-start(bf16[512,2048]{1,0:T(8,128)(2,1)S(1)} %get-tuple-element.270), channel_id=1, source_target_pairs={{0,8},{4,12},{8,0},{12,4},{16,24},{20,28},{24,16},{28,20},{1,9},{5... | collective-permute-start | bytes 6291464 | tf_op jit(solution)/shard_map/ppermute | solution.py:49
  392.9 47.2 %collective-permute-start.26 = (bf16[512,2048]{1,0:T(8,128)(2,1)S(1)}, bf16[512,2048]{1,0:T(8,128)(2,1)S(1)}, u32[]{:S(2)}, u32[]{:S(2)}) collective-permute-start(bf16[512,2048]{1,0:T(8,128)(2,1)S(1)} %get-tuple-element.271), channel_id=1, source_target_pairs={{0,16},{4,20},{8,24},{12,28},{16,0},{20,4},{24,8},{28,12},{1,17},{... | collective-permute-start | bytes 6291464 | tf_op jit(solution)/shard_map/ppermute | solution.py:49
  448.2 297.0 %all-gather.18.cloned.1.call-start = ((), (), s32[]{:S(2)}) async-start(), calls=%async_computation.7 | async-start | bytes 14155776 | tf_op jit(solution)/shard_map/all_gather | solution.py:894
  452.4 24.5 %collective-permute-start.28 = (bf16[256,2048]{1,0:T(8,128)(2,1)}, bf16[256,2048]{1,0:T(8,128)(2,1)}, u32[]{:S(2)}, u32[]{:S(2)}) collective-permute-start(bf16[256,2048]{1,0:T(8,128)(2,1)} %get-tuple-element.389), channel_id=1, source_target_pairs={{0,16},{4,20},{8,24},{12,28},{16,0},{20,4},{24,8},{28,12},{1,17},{... | collective-permute-start | bytes 3145736 | tf_op jit(solution)/shard_map/ppermute | solution.py:49
  452.9 24.0 %collective-permute-start.29 = (bf16[256,2048]{1,0:T(8,128)(2,1)S(1)}, bf16[256,2048]{1,0:T(8,128)(2,1)}, u32[]{:S(2)}, u32[]{:S(2)}) collective-permute-start(bf16[256,2048]{1,0:T(8,128)(2,1)S(1)} %get-tuple-element.388), channel_id=1, source_target_pairs={{0,8},{4,12},{8,0},{12,4},{16,24},{20,28},{24,16},{28,20},{1,9},{5... | collective-permute-start | bytes 3145736 | tf_op jit(solution)/shard_map/ppermute | solution.py:49
  486.0 41.2 %collective-permute-start.32 = (bf16[640,2048]{1,0:T(8,128)(2,1)S(1)}, bf16[640,2048]{1,0:T(8,128)(2,1)S(1)}, u32[]{:S(2)}, u32[]{:S(2)}) collective-permute-start(bf16[640,2048]{1,0:T(8,128)(2,1)S(1)} %convolution_convert_fusion.2), channel_id=1, source_target_pairs={{0,4},{4,0},{8,12},{12,8},{16,20},{20,16},{24,28},{28,24},{1,5},{5... | collective-permute-start | bytes 7864328 | tf_op jit(solution)/shard_map/ppermute | solution.py:49
  486.1 41.2 %collective-permute-start.30 = (bf16[256,2048]{1,0:T(8,128)(2,1)S(1)}, bf16[256,2048]{1,0:T(8,128)(2,1)S(1)}, u32[]{:S(2)}, u32[]{:S(2)}) collective-permute-start(bf16[256,2048]{1,0:T(8,128)(2,1)S(1)} %get-tuple-element.286), channel_id=1, source_target_pairs={{0,8},{4,12},{8,0},{12,4},{16,24},{20,28},{24,16},{28,20},{1,9},{5... | collective-permute-start | bytes 3145736 | tf_op jit(solution)/shard_map/ppermute | solution.py:49
  486.9 40.4 %collective-permute-start.31 = (bf16[256,2048]{1,0:T(8,128)(2,1)S(1)}, bf16[256,2048]{1,0:T(8,128)(2,1)S(1)}, u32[]{:S(2)}, u32[]{:S(2)}) collective-permute-start(bf16[256,2048]{1,0:T(8,128)(2,1)S(1)} %get-tuple-element.287), channel_id=1, source_target_pairs={{0,16},{4,20},{8,24},{12,28},{16,0},{20,4},{24,8},{28,12},{1,17},{... | collective-permute-start | bytes 3145736 | tf_op jit(solution)/shard_map/ppermute | solution.py:49
  529.3 17.7 %collective-permute-start.36 = (bf16[160,2048]{1,0:T(8,128)(2,1)S(1)}, bf16[160,2048]{1,0:T(8,128)(2,1)S(1)}, u32[]{:S(2)}, u32[]{:S(2)}) collective-permute-start(bf16[160,2048]{1,0:T(8,128)(2,1)S(1)} %get-tuple-element.298), channel_id=1, source_target_pairs={{0,8},{4,12},{8,0},{12,4},{16,24},{20,28},{24,16},{28,20},{1,9},{5... | collective-permute-start | bytes 1966088 | tf_op jit(solution)/shard_map/ppermute | solution.py:49
  530.6 17.7 %collective-permute-start.37 = (bf16[160,2048]{1,0:T(8,128)(2,1)S(1)}, bf16[160,2048]{1,0:T(8,128)(2,1)S(1)}, u32[]{:S(2)}, u32[]{:S(2)}) collective-permute-start(bf16[160,2048]{1,0:T(8,128)(2,1)S(1)} %get-tuple-element.299), channel_id=1, source_target_pairs={{0,16},{4,20},{8,24},{12,28},{16,0},{20,4},{24,8},{28,12},{1,17},{... | collective-permute-start | bytes 1966088 | tf_op jit(solution)/shard_map/ppermute | solution.py:49
  532.0 37.4 %collective-permute-start.34 = (bf16[256,2048]{1,0:T(8,128)(2,1)S(1)}, bf16[256,2048]{1,0:T(8,128)(2,1)S(1)}, u32[]{:S(2)}, u32[]{:S(2)}) collective-permute-start(bf16[256,2048]{1,0:T(8,128)(2,1)S(1)} %get-tuple-element.385), channel_id=1, source_target_pairs={{0,16},{4,20},{8,24},{12,28},{16,0},{20,4},{24,8},{28,12},{1,17},{... | collective-permute-start | bytes 3145736 | tf_op jit(solution)/shard_map/ppermute | solution.py:49
  533.6 36.7 %collective-permute-start.35 = (bf16[256,2048]{1,0:T(8,128)(2,1)S(1)}, bf16[256,2048]{1,0:T(8,128)(2,1)}, u32[]{:S(2)}, u32[]{:S(2)}) collective-permute-start(bf16[256,2048]{1,0:T(8,128)(2,1)S(1)} %get-tuple-element.384), channel_id=1, source_target_pairs={{0,8},{4,12},{8,0},{12,4},{16,24},{20,28},{24,16},{28,20},{1,9},{5... | collective-permute-start | bytes 3145736 | tf_op jit(solution)/shard_map/ppermute | solution.py:49
  535.9 31.3 %collective-permute-start.33 = (bf16[10,64,512]{2,1,0:T(8,128)(2,1)S(1)}, bf16[10,64,512]{2,1,0:T(8,128)(2,1)S(1)}, u32[]{:S(2)}, u32[]{:S(2)}) collective-permute-start(bf16[10,64,512]{2,1,0:T(8,128)(2,1)S(1)} %copy-done.100), channel_id=1, source_target_pairs={{0,1},{1,0},{2,3},{3,2},{4,5},{5,4},{6,7},{7,6},{8,9},{9,8},{10,11... | collective-permute-start | bytes 1966088 | tf_op jit(solution)/shard_map/ppermute | solution.py:49
  573.7 189.2 %all-gather.14.cloned.1.call-start = ((), (), s32[]{:S(2)}) async-start(), calls=%async_computation.5 | async-start | bytes 1474560 | tf_op jit(solution)/shard_map/all_gather | solution.py:960
  585.5 19.8 %collective-permute-start.38 = (bf16[1024,2048]{1,0:T(8,128)(2,1)}, bf16[1024,2048]{1,0:T(8,128)(2,1)S(1)}, u32[]{:S(2)}, u32[]{:S(2)}) collective-permute-start(bf16[1024,2048]{1,0:T(8,128)(2,1)} %add_convert_fusion.1), channel_id=1, source_target_pairs={{0,4},{4,0},{8,12},{12,8},{16,20},{20,16},{24,28},{28,24},{1,5},{5... | collective-permute-start | bytes 12582920 | tf_op jit(solution)/shard_map/ppermute | solution.py:49
  585.7 17.5 %collective-permute-start.39 = (bf16[80,2048]{1,0:T(8,128)(2,1)S(1)}, bf16[80,2048]{1,0:T(8,128)(2,1)S(1)}, u32[]{:S(2)}, u32[]{:S(2)}) collective-permute-start(bf16[80,2048]{1,0:T(8,128)(2,1)S(1)} %get-tuple-element.457), channel_id=1, source_target_pairs={{0,16},{4,20},{8,24},{12,28},{16,0},{20,4},{24,8},{28,12},{1,17},{... | collective-permute-start | bytes 983048 | tf_op jit(solution)/shard_map/ppermute | solution.py:49
  587.2 17.3 %collective-permute-start.40 = (bf16[80,2048]{1,0:T(8,128)(2,1)S(1)}, bf16[80,2048]{1,0:T(8,128)(2,1)S(1)}, u32[]{:S(2)}, u32[]{:S(2)}) collective-permute-start(bf16[80,2048]{1,0:T(8,128)(2,1)S(1)} %get-tuple-element.456), channel_id=1, source_target_pairs={{0,8},{4,12},{8,0},{12,4},{16,24},{20,28},{24,16},{28,20},{1,9},{5... | collective-permute-start | bytes 983048 | tf_op jit(solution)/shard_map/ppermute | solution.py:49
  608.4 51.3 %collective-permute-start.44 = (bf16[256,2048]{1,0:T(8,128)(2,1)S(1)}, bf16[256,2048]{1,0:T(8,128)(2,1)S(1)}, u32[]{:S(2)}, u32[]{:S(2)}) collective-permute-start(bf16[256,2048]{1,0:T(8,128)(2,1)S(1)} %get-tuple-element.318), channel_id=1, source_target_pairs={{0,8},{4,12},{8,0},{12,4},{16,24},{20,28},{24,16},{28,20},{1,9},{5... | collective-permute-start | bytes 3145736 | tf_op jit(solution)/shard_map/ppermute | solution.py:49
  609.9 49.7 %collective-permute-start.45 = (bf16[256,2048]{1,0:T(8,128)(2,1)S(1)}, bf16[256,2048]{1,0:T(8,128)(2,1)S(1)}, u32[]{:S(2)}, u32[]{:S(2)}) collective-permute-start(bf16[256,2048]{1,0:T(8,128)(2,1)S(1)} %get-tuple-element.319), channel_id=1, source_target_pairs={{0,16},{4,20},{8,24},{12,28},{16,0},{20,4},{24,8},{28,12},{1,17},{... | collective-permute-start | bytes 3145736 | tf_op jit(solution)/shard_map/ppermute | solution.py:49
  611.7 19.5 %collective-permute-start.41 = (bf16[512,512]{1,0:T(8,128)(2,1)S(1)}, bf16[512,512]{1,0:T(8,128)(2,1)S(1)}, u32[]{:S(2)}, u32[]{:S(2)}) collective-permute-start(bf16[512,512]{1,0:T(8,128)(2,1)S(1)} %get-tuple-element.412), channel_id=1, source_target_pairs={{0,1},{1,0},{2,3},{3,2},{4,5},{5,4},{6,7},{7,6},{8,9},{9,8},{10,11... | collective-permute-start | bytes 1572872 | tf_op jit(solution)/shard_map/ppermute | solution.py:35
  612.1 34.7 %collective-permute-start.42 = (bf16[512,512]{1,0:T(8,128)(2,1)S(1)}, bf16[512,512]{1,0:T(8,128)(2,1)S(1)}, u32[]{:S(2)}, u32[]{:S(2)}) collective-permute-start(bf16[512,512]{1,0:T(8,128)(2,1)S(1)} %get-tuple-element.413), channel_id=1, source_target_pairs={{0,2},{1,3},{2,0},{3,1},{4,6},{5,7},{6,4},{7,5},{8,10},{9,11},{10,... | collective-permute-start | bytes 1572872 | tf_op jit(solution)/shard_map/ppermute | solution.py:35
  612.1 47.5 %collective-permute-start.43 = (bf16[512,512]{1,0:T(8,128)(2,1)S(1)}, bf16[512,512]{1,0:T(8,128)(2,1)S(1)}, u32[]{:S(2)}, u32[]{:S(2)}) collective-permute-start(bf16[512,512]{1,0:T(8,128)(2,1)S(1)} %get-tuple-element.410), channel_id=1, source_target_pairs={{0,3},{1,2},{2,1},{3,0},{4,7},{5,6},{6,5},{7,4},{8,11},{9,10},{10,... | collective-permute-start | bytes 1572872 | tf_op jit(solution)/shard_map/ppermute | solution.py:35
  661.1 19.1 %collective-permute-start.49 = (bf16[128,2048]{1,0:T(8,128)(2,1)}, bf16[128,2048]{1,0:T(8,128)(2,1)}, u32[]{:S(2)}, u32[]{:S(2)}) collective-permute-start(bf16[128,2048]{1,0:T(8,128)(2,1)} %get-tuple-element.409), channel_id=1, source_target_pairs={{0,16},{4,20},{8,24},{12,28},{16,0},{20,4},{24,8},{28,12},{1,17},{... | collective-permute-start | bytes 1572872 | tf_op jit(solution)/shard_map/ppermute | solution.py:49
  662.0 18.1 %collective-permute-start.50 = (bf16[128,2048]{1,0:T(8,128)(2,1)}, bf16[128,2048]{1,0:T(8,128)(2,1)}, u32[]{:S(2)}, u32[]{:S(2)}) collective-permute-start(bf16[128,2048]{1,0:T(8,128)(2,1)} %get-tuple-element.408), channel_id=1, source_target_pairs={{0,8},{4,12},{8,0},{12,4},{16,24},{20,28},{24,16},{28,20},{1,9},{5... | collective-permute-start | bytes 1572872 | tf_op jit(solution)/shard_map/ppermute | solution.py:49
  664.3 11.2 %collective-permute-start.47 = (bf16[160,512]{1,0:T(8,128)(2,1)}, bf16[160,512]{1,0:T(8,128)(2,1)S(1)}, u32[]{:S(2)}, u32[]{:S(2)}) collective-permute-start(bf16[160,512]{1,0:T(8,128)(2,1)} %get-tuple-element.472), channel_id=1, source_target_pairs={{0,2},{1,3},{2,0},{3,1},{4,6},{5,7},{6,4},{7,5},{8,10},{9,11},{10,... | collective-permute-start | bytes 491528 | tf_op jit(solution)/shard_map/ppermute | solution.py:35
  665.3 14.2 %collective-permute-start.48 = (bf16[160,512]{1,0:T(8,128)(2,1)}, bf16[160,512]{1,0:T(8,128)(2,1)S(1)}, u32[]{:S(2)}, u32[]{:S(2)}) collective-permute-start(bf16[160,512]{1,0:T(8,128)(2,1)} %get-tuple-element.375), channel_id=1, source_target_pairs={{0,3},{1,2},{2,1},{3,0},{4,7},{5,6},{6,5},{7,4},{8,11},{9,10},{10,... | collective-permute-start | bytes 491528 | tf_op jit(solution)/shard_map/ppermute | solution.py:35
  671.5 30.8 %collective-permute-start.54 = (bf16[256,2048]{1,0:T(8,128)(2,1)S(1)}, bf16[256,2048]{1,0:T(8,128)(2,1)}, u32[]{:S(2)}, u32[]{:S(2)}) collective-permute-start(bf16[256,2048]{1,0:T(8,128)(2,1)S(1)} %copy-done.26), channel_id=1, source_target_pairs={{0,8},{4,12},{8,0},{12,4},{16,24},{20,28},{24,16},{28,20},{1,9},{5... | collective-permute-start | bytes 3145736 | tf_op jit(solution)/shard_map/ppermute | solution.py:49
  675.5 28.0 %collective-permute-start.55 = (bf16[256,2048]{1,0:T(8,128)(2,1)S(1)}, bf16[256,2048]{1,0:T(8,128)(2,1)}, u32[]{:S(2)}, u32[]{:S(2)}) collective-permute-start(bf16[256,2048]{1,0:T(8,128)(2,1)S(1)} %copy-done.24), channel_id=1, source_target_pairs={{0,16},{4,20},{8,24},{12,28},{16,0},{20,4},{24,8},{28,12},{1,17},{... | collective-permute-start | bytes 3145736 | tf_op jit(solution)/shard_map/ppermute | solution.py:49
  687.9 122.6 %all-gather.16.cloned.1.call-start = ((), (), s32[]{:S(2)}) async-start(), calls=%async_computation.6 | async-start | bytes 5308416 | tf_op jit(solution)/shard_map/all_gather | solution.py:984
  691.8 22.4 %collective-permute-start.51 = (bf16[256,1152]{1,0:T(8,128)(2,1)S(1)}, bf16[256,1152]{1,0:T(8,128)(2,1)S(1)}, u32[]{:S(2)}, u32[]{:S(2)}) collective-permute-start(bf16[256,1152]{1,0:T(8,128)(2,1)S(1)} %get-tuple-element.486), channel_id=1, source_target_pairs={{0,1},{1,0},{2,3},{3,2},{4,5},{5,4},{6,7},{7,6},{8,9},{9,8},{10,11... | collective-permute-start | bytes 1769480 | tf_op jit(solution)/shard_map/ppermute | solution.py:35
  692.6 39.8 %collective-permute-start.52 = (bf16[256,1152]{1,0:T(8,128)(2,1)S(1)}, bf16[256,1152]{1,0:T(8,128)(2,1)S(1)}, u32[]{:S(2)}, u32[]{:S(2)}) collective-permute-start(bf16[256,1152]{1,0:T(8,128)(2,1)S(1)} %get-tuple-element.487), channel_id=1, source_target_pairs={{0,2},{1,3},{2,0},{3,1},{4,6},{5,7},{6,4},{7,5},{8,10},{9,11},{10,... | collective-permute-start | bytes 1769480 | tf_op jit(solution)/shard_map/ppermute | solution.py:35
  693.4 51.9 %collective-permute-start.53 = (bf16[256,1152]{1,0:T(8,128)(2,1)S(1)}, bf16[256,1152]{1,0:T(8,128)(2,1)}, u32[]{:S(2)}, u32[]{:S(2)}) collective-permute-start(bf16[256,1152]{1,0:T(8,128)(2,1)S(1)} %get-tuple-element.485), channel_id=1, source_target_pairs={{0,3},{1,2},{2,1},{3,0},{4,7},{5,6},{6,5},{7,4},{8,11},{9,10},{10,... | collective-permute-start | bytes 1769480 | tf_op jit(solution)/shard_map/ppermute | solution.py:35
  759.4 23.8 %collective-permute-start.56 = (bf16[512,512]{1,0:T(8,128)(2,1)}, bf16[512,512]{1,0:T(8,128)(2,1)S(1)}, u32[]{:S(2)}, u32[]{:S(2)}) collective-permute-start(bf16[512,512]{1,0:T(8,128)(2,1)} %get-tuple-element.402), channel_id=1, source_target_pairs={{0,1},{1,0},{2,3},{3,2},{4,5},{5,4},{6,7},{7,6},{8,9},{9,8},{10,11... | collective-permute-start | bytes 1572872 | tf_op jit(solution)/shard_map/ppermute | solution.py:35
  759.4 35.7 %collective-permute-start.57 = (bf16[512,512]{1,0:T(8,128)(2,1)S(1)}, bf16[512,512]{1,0:T(8,128)(2,1)S(1)}, u32[]{:S(2)}, u32[]{:S(2)}) collective-permute-start(bf16[512,512]{1,0:T(8,128)(2,1)S(1)} %get-tuple-element.403), channel_id=1, source_target_pairs={{0,2},{1,3},{2,0},{3,1},{4,6},{5,7},{6,4},{7,5},{8,10},{9,11},{10,... | collective-permute-start | bytes 1572872 | tf_op jit(solution)/shard_map/ppermute | solution.py:35
  760.2 45.2 %collective-permute-start.58 = (bf16[512,512]{1,0:T(8,128)(2,1)S(1)}, bf16[512,512]{1,0:T(8,128)(2,1)S(1)}, u32[]{:S(2)}, u32[]{:S(2)}) collective-permute-start(bf16[512,512]{1,0:T(8,128)(2,1)S(1)} %get-tuple-element.400), channel_id=1, source_target_pairs={{0,3},{1,2},{2,1},{3,0},{4,7},{5,6},{6,5},{7,4},{8,11},{9,10},{10,... | collective-permute-start | bytes 1572872 | tf_op jit(solution)/shard_map/ppermute | solution.py:35
  (139 other events, 1244.8 us)
Sparse Core Ops, SparseCore 0:
  53.1 44.0 all-gather.7
  99.7 41.1 all-gather.9
  242.6 88.0 all-gather.11
  448.3 125.2 reduce-scatter.1
  575.4 99.6 all-gather.17
  688.1 25.6 all-gather.13
  748.1 38.7 all-gather.15

commit v7 on v6

--- a/solution.py
+++ b/solution.py
@@ -979,24 +979,31 @@
         ],
         "mp",
     )
-    pack, projection, flying = order_split(order, [pack], projection, down_sum.flying)
+    input_gradient = by_tokens(input_gradient, full)
+    pack, input_gradient, projection, flying = order_split(
+        order, [pack, input_gradient], projection, down_sum.flying
+    )
 
     projection = lax.all_gather(added(*projection), "dp", axis=0, tiled=True)
     output_weight_grad = mm(select, output_grad)
     output = (middle + down_sum.last(*flying).astype(full)).astype(low)
     output = swap(by_feature(output), "mp")
     gate_weight_grad, up_weight_grad, down_weight_grad = widen(pack)
-    input_gradient = by_tokens(input_gradient, full)
-    got = order(
-        gate_weight_grad, up_weight_grad, down_weight_grad, input_gradient, output_weight_grad,
-        *output
-    )
-    gate_weight_grad, up_weight_grad, down_weight_grad, input_gradient = got[:4]
-    output_weight_grad = got[4]
-    output = by_tokens(got[5:], low)
     query_weight_grad, key_weight_grad, value_weight_grad = split_projections(
         projection, slots, rows
     )
+    (
+        query_weight_grad, key_weight_grad, value_weight_grad, gate_weight_grad, up_weight_grad,
+        down_weight_grad, output_weight_grad, output,
+    ) = order_split(
+        order,
+        [
+            query_weight_grad, key_weight_grad, value_weight_grad, gate_weight_grad,
+            up_weight_grad, down_weight_grad, output_weight_grad,
+        ],
+        output,
+    )
+    output = by_tokens(output, low)
     extra = projection[:, slots + 2 * KVH * HD :]
     extra = extra.astype(full)
     own_share = lax.dynamic_slice_in_dim(extra, rank * share, share, 0)

time: 837 us -> 821 us (0.981)
  waiting for transfers between devices: 300 us -> 285 us
    ppermute x21, waiting for transfers between devices: 127 us -> 99 us  [swap(): lax.ppermute(pieces[k], axis, [(i, i ^ k) for i in range(n)])]
    all_gather x1, waiting for transfers between devices: 0.01 us -> 8.86 us  [on_device(): projection = lax.all_gather(added(*projection), 'dp', axis=0, tiled=True)]
    unnamed x288 -> x278, local copies, waits for them, and re-layouts: 48 us -> 44.6 us
  transfers between devices with their start and end apart: 66 -> 66, of which waited for: 40 -> 37; matrix products, arithmetic and copies ran while one was open for 32% -> 32% of each run, Pallas kernels for 12% -> 13%
where the time goes in v7:
time: 821 us; the launch traced here: 812 us
  waiting for transfers between devices  285 us (35%)
  Pallas kernels  130 us (16%)
  matrix products  127 us (15%)
  other arithmetic  97.9 us (12%)
  local copies, waits for them, and re-layouts  80.4 us (10%)
  starting transfers between devices  74.1 us (9%)
  between operations  16.6 us (2%)
    ppermute x32, waiting for transfers between devices, exchange(): return lax.ppermute(array, axis, [(i, i ^ mask) for i in range(n)])  111 us
    ppermute x21, waiting for transfers between devices, swap(): lax.ppermute(pieces[k], axis, [(i, i ^ k) for i in range(n)])  99 us
    dot_general x17, matrix products, dot(): lax.dot_general(left, right, (((left_axis,), (right_axis,)), ((), ())), p...  96.5 us
    ppermute x3, waiting for transfers between devices, send(): lax.ppermute(up, self.axis, right)  50.8 us
    unnamed x278, local copies, waits for them, and re-layouts  44.6 us
    pallas_call x2, Pallas kernels, units_back(): pl.pallas_call(units_back_kernel, out_shape=(jax.ShapeDtypeStruct(raised....  39.6 us
    pallas_call x4, Pallas kernels, chip_sums(): pl.pallas_call(kernel, out_shape=[jax.ShapeDtypeStruct((len(places) * hal...  31 us
    dot_general x5, matrix products, mm(): return jnp.dot(left, right, preferred_element_type=full)  30.6 us
  transfers between devices with their start and end apart: 66, of which 37 were waited for; matrix products, arithmetic and copies ran while one was open for 32% of the time, Pallas kernels for 13%

profile of v7, /device:TPU:16, one launch (start us, length us, event | category | flops | bytes accessed | tf_op | source)
XLA Modules:
  0.0 811.5 jit_solution(12870126479185327935)
XLA Ops:
  12.4 3.4 constant_dynamic-slice_fusion.8
  25.8 3.6 iota_compare_fusion
  40.1 3.6 fusion.26
  46.1 4.5 collective-permute-done.4
  54.9 22.0 %collective-permute-done.5 = bf16[512,512]{1,0:T(8,128)(2,1)S(1)} collective-permute-done((bf16[512,512]{1,0:T(8,128)(2,1)S(1)}, bf16[512,512]{1,0:T(8,128)(2,1)S(1)}, u32[]{:S(2)}, u32[]{:S(2)}) %collective-permute-start.5) | collective-permute-done | bytes 524320 | tf_op jit(solution)/shard_map/ppermute | solution.py:49
  97.2 5.5 fusion.74
  105.6 4.4 collective-permute-done.9
  110.3 3.3 collective-permute-start.11
  115.2 14.6 %shard_map.247 = (bf16[20,64,512]{2,1,0:T(8,128)(2,1)S(1)}, f32[5,4,512]{2,1,0:T(4,128)S(1)}) custom-call(s32[2]{0:T(128)S(1)} %pad_add_fusion.2.starts, bf16[20,64,512]{2,1,0:T(8,128)(2,1)S(1)} %fusion.21.q_ref, bf16[5,64,1024]{2,1,0:T(8,128)(2,1)S(1)} %get-tuple-element.467.k_ref, bf16[5,64,1024]{2,1,0:T(8,128)(2,1)S(1)} %get-tuple-element.466.v_ref), custom_call_target="tpu_custom_call" | custom-call | flops 6553600 | bytes 1048576 | tf_op jit(solution)/shard_map/pallas_call | solution.py:416
  131.5 9.4 %all-gather.10.cloned.1.call-done = bf16[1280,2048]{1,0:T(8,128)(2,1)} async-done(((bf16[160,2048]{1,0:T(8,128)(2,1)}), bf16[1280,2048]{1,0:T(8,128)(2,1)}) %all-gather.10.cloned.1.call-update) | async-done | bytes 5242896 | tf_op jit(solution)/shard_map/all_gather | solution.py:739
  140.9 6.1 multiply_reduce_fusion
  149.7 7.1 collective-permute-done.12
  161.7 4.4 collective-permute-start.16
  174.4 20.8 %collective-permute-done.15 = bf16[2048,384]{1,0:T(8,128)(2,1)} collective-permute-done((bf16[2048,384]{1,0:T(8,128)(2,1)}, bf16[2048,384]{1,0:T(8,128)(2,1)}, u32[]{:S(2)}, u32[]{:S(2)}) %collective-permute-start.15) | collective-permute-done | bytes 1572896 | tf_op jit(solution)/shard_map/ppermute | solution.py:79
  196.4 5.0 collective-permute-done.13
  204.5 5.2 collective-permute-start.20
  209.7 4.5 broadcast_in_dim.51
  214.2 3.2 bitcast_dynamic-update-slice_fusion.2
  222.1 3.2 bitcast_dynamic-update-slice_fusion.1
  228.4 10.5 %collective-permute-done.17 = bf16[256,2048]{1,0:T(8,128)(2,1)S(1)} collective-permute-done((bf16[256,2048]{1,0:T(8,128)(2,1)S(1)}, bf16[256,2048]{1,0:T(8,128)(2,1)S(1)}, u32[]{:S(2)}, u32[]{:S(2)}) %collective-permute-start.17) | collective-permute-done | bytes 1048608 | tf_op jit(solution)/shard_map/ppermute | solution.py:49
  251.1 30.0 %collective-permute-done.22 = bf16[2048,384]{1,0:T(8,128)(2,1)S(1)} collective-permute-done((bf16[2048,384]{1,0:T(8,128)(2,1)S(1)}, bf16[2048,384]{1,0:T(8,128)(2,1)S(1)}, u32[]{:S(2)}, u32[]{:S(2)}) %collective-permute-start.22) | collective-permute-done | bytes 1572896 | tf_op jit(solution)/shard_map/ppermute | solution.py:79
  291.6 9.1 %fusion.76.raised_ref = f32[2048,1024]{1,0:T(8,128)S(1)} fusion(bf16[2048,2048]{1,0:T(8,128)(2,1)S(1)} %collective-permute-done.21, bf16[2048,1024]{1,0:T(8,128)(2,1)S(1)} %get-tuple-element.459.wide_ref), kind=kOutput, calls=%fused_computation.374 | convolution fusion | flops 8589934592 | bytes 20971520 | tf_op jit(solution)/shard_map/dot_general | solution.py:275
  300.7 3.3 copy-done.32
  305.7 12.0 %fusion.75.raised_ref = f32[2048,1024]{1,0:T(8,128)S(1)} fusion(bf16[2048,2048]{1,0:T(8,128)(2,1)} %bitcast.32, bf16[2048,1024]{1,0:T(8,128)(2,1)S(1)} %get-tuple-element.459.wide_ref), kind=kOutput, calls=%fused_computation.373 | convolution fusion | flops 8589934592 | bytes 20971520 | tf_op jit(solution)/shard_map/dot_general | solution.py:275
  317.7 3.2 copy-done.31
  322.4 6.8 convolution_convert_fusion
  329.3 6.9 convolution_convert_fusion.1.mine_ref
  337.7 19.6 %shard_map.248 = (bf16[2048,1024]{1,0:T(8,128)(2,1)S(1)}, bf16[2048,2048]{1,0:T(8,128)(2,1)}) custom-call(s32[1]{0:T(128)} %bitcast.34.core, bf16[4,2,512,2048]{3,2,1,0:T(8,128)(2,1)} %bitcast.107, f32[2048,1024]{1,0:T(8,128)} %copy-done.32, bf16[2048,512]{1,0:T(8,128)(2,1)S(1)} %copy-done.3, bf16[2048,1024]{1,0:T(8,128)(2,1)} %copy-done.33), custom_call_target="tpu_custom_call" | custom-call | bytes 65536 | tf_op jit(solution)/shard_map/pallas_call | solution.py:509
  361.6 20.0 %shard_map.249 = (bf16[2048,1024]{1,0:T(8,128)(2,1)S(1)}, bf16[2048,2048]{1,0:T(8,128)(2,1)}) custom-call(s32[1]{0:T(128)} %bitcast.29.core, bf16[4,2,512,2048]{3,2,1,0:T(8,128)(2,1)} %bitcast.108, f32[2048,1024]{1,0:T(8,128)} %copy-done.31, bf16[2048,512]{1,0:T(8,128)(2,1)S(1)} %copy-done.4, bf16[2048,1024]{1,0:T(8,128)(2,1)} %copy-done.33), custom_call_target="tpu_custom_call" | custom-call | bytes 65536 | tf_op jit(solution)/shard_map/pallas_call | solution.py:509
  381.6 10.4 %shard_map.250 = (bf16[512,2048]{1,0:T(8,128)(2,1)S(1)}, bf16[512,2048]{1,0:T(8,128)(2,1)S(1)}, bf16[1024,2048]{1,0:T(8,128)(2,1)S(1)}) custom-call(s32[8]{0:T(128)S(1)} %stack.97.index_ref, bf16[2048,2048]{1,0:T(8,128)(2,1)} %get-tuple-element.266.mine_ref, bf16[2048,2048]{1,0:T(8,128)(2,1)} %collective-permute-done.24.got_ref), custom_call_target="tpu_custom_call" | custom-call | bytes 65536 | tf_op jit(solution)/shard_map/pallas_call | solution.py:169
  396.2 13.5 %fusion.77 = f32[2048,1024]{1,0:T(8,128)} fusion(bf16[2048,2048]{1,0:T(8,128)(2,1)} %copy-done.131, bf16[2048,1024]{1,0:T(8,128)(2,1)S(1)} %copy-done.20), kind=kOutput, calls=%fused_computation.375 | convolution fusion | flops 8589934592 | bytes 20971520 | tf_op jit(solution)/shard_map/dot_general | solution.py:27
  409.7 12.4 %convolution_convert_fusion.5.down_ref = bf16[2048,512]{1,0:T(8,128)(2,1)S(1)} fusion(bf16[4096,2048]{1,0:T(8,128)(2,1)} %all-gather.12.cloned.1.call-done, bf16[4096,512]{1,0:T(8,128)(2,1)S(1)} %bitcast.127), kind=kOutput, calls=%fused_computation.48 | convolution fusion | flops 8590983168 | bytes 23068672 | tf_op jit(solution)/shard_map/dot_general | solution.py:27
  422.2 12.9 %add_convert_fusion.2.gate_ref.up_ref = bf16[2048,1024]{1,0:T(8,128)(2,1)S(1)} fusion(f32[2048,1024]{1,0:T(8,128)} %fusion.77, bf16[2048,2048]{1,0:T(8,128)(2,1)} %bitcast.32, bf16[2048,1024]{1,0:T(8,128)(2,1)S(1)} %get-tuple-element.271), kind=kOutput, calls=%fused_computation.6 | convolution fusion | flops 8594128896 | bytes 25165824 | tf_op jit(solution)/shard_map/dot_general | solution.py:27
  435.0 4.6 collective-permute-done.25
  442.3 3.2 shard_map.253
  448.3 4.1 add_convert_fusion.10
  453.7 12.2 %shard_map.251 = (bf16[256,2048]{1,0:T(8,128)(2,1)S(1)}, bf16[256,2048]{1,0:T(8,128)(2,1)S(1)}, bf16[256,2048]{1,0:T(8,128)(2,1)S(1)}, bf16[256,2048]{1,0:T(8,128)(2,1)S(1)}, bf16[1024,2048]{1,0:T(8,128)(2,1)S(1)}) custom-call(s32[8]{0:T(128)S(1)} %stack.98.index_ref, bf16[2048,2048]{1,0:T(8,128)(2,1)} %convolution_convert_fusion.1.mine_ref, ...), custom_call_target="tpu_custom_call" | custom-call | bytes 65536 | tf_op jit(solution)/shard_map/pallas_call | solution.py:169
  466.0 11.0 %collective-permute-done.28 = bf16[256,2048]{1,0:T(8,128)(2,1)} collective-permute-done((bf16[256,2048]{1,0:T(8,128)(2,1)}, bf16[256,2048]{1,0:T(8,128)(2,1)}, u32[]{:S(2)}, u32[]{:S(2)}) %collective-permute-start.28) | collective-permute-done | bytes 1048608 | tf_op jit(solution)/shard_map/ppermute | solution.py:49
  488.4 6.7 convolution_convert_fusion.4
  495.1 25.3 %shard_map.252 = (f32[20,64,512]{2,1,0:T(8,128)S(1)}, f32[5,64,1024]{2,1,0:T(8,128)S(1)}, f32[5,64,1024]{2,1,0:T(8,128)S(1)}) custom-call(s32[2]{0:T(128)S(1)} %copy-done.18, bf16[20,64,512]{2,1,0:T(8,128)(2,1)S(1)} %copy-done.8, bf16[5,64,1024]{2,1,0:T(8,128)(2,1)S(1)} %copy-done.12, bf16[5,64,1024]{2,1,0:T(8,128)(2,1)S(1)} %copy-done.10, ...), custom_call_target="tpu_custom_call" | custom-call | flops 6553600 | bytes 1048576 | tf_op jit(solution)/shard_map/pallas_call | solution.py:440
  541.7 5.3 collective-permute-done.36
  548.3 18.9 %collective-permute-done.33 = bf16[10,64,512]{2,1,0:T(8,128)(2,1)S(1)} collective-permute-done((bf16[10,64,512]{2,1,0:T(8,128)(2,1)S(1)}, bf16[10,64,512]{2,1,0:T(8,128)(2,1)S(1)}, u32[]{:S(2)}, u32[]{:S(2)}) %collective-permute-start.33) | collective-permute-done | bytes 655392 | tf_op jit(solution)/shard_map/ppermute | solution.py:49
  570.4 3.3 reduce-scatter.2.cloned.1.call-done
  582.1 5.3 add_convert_fusion.1
  596.8 5.1 fusion.24
  610.3 6.5 shard_map.255
  623.1 15.4 %collective-permute-done.41 = bf16[512,512]{1,0:T(8,128)(2,1)S(1)} collective-permute-done((bf16[512,512]{1,0:T(8,128)(2,1)S(1)}, bf16[512,512]{1,0:T(8,128)(2,1)S(1)}, u32[]{:S(2)}, u32[]{:S(2)}) %collective-permute-start.41) | collective-permute-done | bytes 524320 | tf_op jit(solution)/shard_map/ppermute | solution.py:35
  641.0 12.1 %collective-permute-done.42 = bf16[512,512]{1,0:T(8,128)(2,1)S(1)} collective-permute-done((bf16[512,512]{1,0:T(8,128)(2,1)S(1)}, bf16[512,512]{1,0:T(8,128)(2,1)S(1)}, u32[]{:S(2)}, u32[]{:S(2)}) %collective-permute-start.42) | collective-permute-done | bytes 524320 | tf_op jit(solution)/shard_map/ppermute | solution.py:35
  653.0 3.9 collective-permute-start.47
  656.9 19.3 %collective-permute-done.43 = bf16[512,512]{1,0:T(8,128)(2,1)S(1)} collective-permute-done((bf16[512,512]{1,0:T(8,128)(2,1)S(1)}, bf16[512,512]{1,0:T(8,128)(2,1)S(1)}, u32[]{:S(2)}, u32[]{:S(2)}) %collective-permute-start.43) | collective-permute-done | bytes 524320 | tf_op jit(solution)/shard_map/ppermute | solution.py:35
  682.9 8.7 %collective-permute-done.49 = bf16[128,2048]{1,0:T(8,128)(2,1)S(1)} collective-permute-done((bf16[128,2048]{1,0:T(8,128)(2,1)S(1)}, bf16[128,2048]{1,0:T(8,128)(2,1)S(1)}, u32[]{:S(2)}, u32[]{:S(2)}) %collective-permute-start.49) | collective-permute-done | bytes 524320 | tf_op jit(solution)/shard_map/ppermute | solution.py:49
  696.1 3.4 convolution_convert_fusion.6
  699.9 3.5 collective-permute-start.52
  706.3 5.4 collective-permute-done.54
  711.7 11.0 %collective-permute-done.51 = bf16[256,1152]{1,0:T(8,128)(2,1)S(1)} collective-permute-done((bf16[256,1152]{1,0:T(8,128)(2,1)S(1)}, bf16[256,1152]{1,0:T(8,128)(2,1)S(1)}, u32[]{:S(2)}, u32[]{:S(2)}) %collective-permute-start.51) | collective-permute-done | bytes 589856 | tf_op jit(solution)/shard_map/ppermute | solution.py:35
  722.8 15.9 %collective-permute-done.52 = bf16[256,1152]{1,0:T(8,128)(2,1)S(1)} collective-permute-done((bf16[256,1152]{1,0:T(8,128)(2,1)S(1)}, bf16[256,1152]{1,0:T(8,128)(2,1)S(1)}, u32[]{:S(2)}, u32[]{:S(2)}) %collective-permute-start.52) | collective-permute-done | bytes 589856 | tf_op jit(solution)/shard_map/ppermute | solution.py:35
  739.5 7.6 collective-permute-done.53
  749.7 3.9 add_convert_fusion.5
  758.9 6.4 fusion.78
  765.2 4.6 copy-done.6
  769.8 8.8 %shard_map.257 = (f32[2048,1024]{1,0:T(8,128)}, f32[2048,1024]{1,0:T(8,128)}, f32[1024,2048]{1,0:T(8,128)}) custom-call(bf16[8,2048,384]{2,1,0:T(8,128)(2,1)S(1)} %bitcast.103), custom_call_target="tpu_custom_call" | custom-call | bytes 65536 | tf_op jit(solution)/shard_map/pallas_call | solution.py:585
  778.6 8.9 %all-gather.14.cloned.1.call-done.in_ref = bf16[2048,1152]{1,0:T(8,128)(2,1)} async-done(((bf16[256,1152]{1,0:T(8,128)(2,1)}), bf16[2048,1152]{1,0:T(8,128)(2,1)}) %all-gather.14.cloned.1.call-update) | async-done | bytes 4718608 | tf_op jit(solution)/shard_map/all_gather | solution.py:987
  789.8 4.9 shard_map.256
  794.7 5.6 collective-permute-done.58
  (558 shorter events, 230.2 us)
Async XLA Ops:
  7.2 90.1 %all-gather.8.cloned.1.call-start = ((), (), s32[]{:S(2)}) async-start(), calls=%async_computation.1 | async-start | bytes 5898240 | tf_op jit(solution)/shard_map/all_gather | solution.py:724
  8.9 37.2 %collective-permute-start = (bf16[264,384]{1,0:T(8,128)(2,1)S(1)}, bf16[264,384]{1,0:T(8,128)(2,1)S(1)}, u32[]{:S(2)}, u32[]{:S(2)}) collective-permute-start(bf16[264,384]{1,0:T(8,128)(2,1)S(1)} %pad_maximum_fusion.31.refs_0_), channel_id=1, source_target_pairs={{0,1},{1,0},{2,3},{3,2},{4,5},{5,4},{6,7},{7,6},{8,9},{9,8},{10,11... | collective-permute-start | bytes 608264 | tf_op jit(solution)/shard_map/ppermute | solution.py:35
  10.5 35.5 %collective-permute-start.1 = (bf16[264,384]{1,0:T(8,128)(2,1)S(1)}, bf16[264,384]{1,0:T(8,128)(2,1)S(1)}, u32[]{:S(2)}, u32[]{:S(2)}) collective-permute-start(bf16[264,384]{1,0:T(8,128)(2,1)S(1)} %pad_maximum_fusion.31.refs_0_), channel_id=1, source_target_pairs={{0,2},{1,3},{2,0},{3,1},{4,6},{5,7},{6,4},{7,5},{8,10},{9,11},{10,... | collective-permute-start | bytes 608264 | tf_op jit(solution)/shard_map/ppermute | solution.py:35
  10.9 35.2 %collective-permute-start.2 = (bf16[264,384]{1,0:T(8,128)(2,1)S(1)}, bf16[264,384]{1,0:T(8,128)(2,1)S(1)}, u32[]{:S(2)}, u32[]{:S(2)}) collective-permute-start(bf16[264,384]{1,0:T(8,128)(2,1)S(1)} %pad_maximum_fusion.31.refs_0_), channel_id=1, source_target_pairs={{0,3},{1,2},{2,1},{3,0},{4,7},{5,6},{6,5},{7,4},{8,11},{9,10},{10,... | collective-permute-start | bytes 608264 | tf_op jit(solution)/shard_map/ppermute | solution.py:35
  16.7 29.4 %collective-permute-start.3 = (bf16[512,512]{1,0:T(8,128)(2,1)}, bf16[512,512]{1,0:T(8,128)(2,1)}, u32[]{:S(2)}, u32[]{:S(2)}) collective-permute-start(bf16[512,512]{1,0:T(8,128)(2,1)} %pad_maximum_fusion.29), channel_id=1, source_target_pairs={{0,1},{1,0},{2,3},{3,2},{4,5},{5,4},{6,7},{7,6},{8,9},{9,8},{10,11... | collective-permute-start | bytes 1572872 | tf_op jit(solution)/shard_map/ppermute | solution.py:49
  20.0 30.6 %collective-permute-start.4 = (bf16[512,512]{1,0:T(8,128)(2,1)}, bf16[512,512]{1,0:T(8,128)(2,1)}, u32[]{:S(2)}, u32[]{:S(2)}) collective-permute-start(bf16[512,512]{1,0:T(8,128)(2,1)} %pad_maximum_fusion.30), channel_id=1, source_target_pairs={{0,2},{1,3},{2,0},{3,1},{4,6},{5,7},{6,4},{7,5},{8,10},{9,11},{10,... | collective-permute-start | bytes 1572872 | tf_op jit(solution)/shard_map/ppermute | solution.py:49
  53.0 87.9 %all-gather.10.cloned.1.call-start = ((), (), s32[]{:S(2)}) async-start(), calls=%async_computation.2 | async-start | bytes 5898240 | tf_op jit(solution)/shard_map/all_gather | solution.py:739
  53.1 23.8 %collective-permute-start.5 = (bf16[512,512]{1,0:T(8,128)(2,1)S(1)}, bf16[512,512]{1,0:T(8,128)(2,1)S(1)}, u32[]{:S(2)}, u32[]{:S(2)}) collective-permute-start(bf16[512,512]{1,0:T(8,128)(2,1)S(1)} %copy-done.107), channel_id=1, source_target_pairs={{0,3},{1,2},{2,1},{3,0},{4,7},{5,6},{6,5},{7,4},{8,11},{9,10},{10,... | collective-permute-start | bytes 1572872 | tf_op jit(solution)/shard_map/ppermute | solution.py:49
  76.9 12.8 %collective-permute-start.7 = (bf16[160,512]{1,0:T(8,128)(2,1)}, bf16[160,512]{1,0:T(8,128)(2,1)S(1)}, u32[]{:S(2)}, u32[]{:S(2)}) collective-permute-start(bf16[160,512]{1,0:T(8,128)(2,1)} %fusion.26), channel_id=1, source_target_pairs={{0,2},{1,3},{2,0},{3,1},{4,6},{5,7},{6,4},{7,5},{8,10},{9,11},{10,... | collective-permute-start | bytes 491528 | tf_op jit(solution)/shard_map/ppermute | solution.py:35
  80.0 12.8 %collective-permute-start.8 = (bf16[160,512]{1,0:T(8,128)(2,1)}, bf16[160,512]{1,0:T(8,128)(2,1)S(1)}, u32[]{:S(2)}, u32[]{:S(2)}) collective-permute-start(bf16[160,512]{1,0:T(8,128)(2,1)} %fusion.26), channel_id=1, source_target_pairs={{0,3},{1,2},{2,1},{3,0},{4,7},{5,6},{6,5},{7,4},{8,11},{9,10},{10,... | collective-permute-start | bytes 491528 | tf_op jit(solution)/shard_map/ppermute | solution.py:35
  94.6 241.5 %all-gather.12.cloned.1.call-start = ((), (), s32[]{:S(2)}) async-start(), calls=%async_computation.3 | async-start | bytes 18874368 | tf_op jit(solution)/shard_map/all_gather | solution.py:791
  94.9 15.1 %collective-permute-start.9 = (bf16[10,64,512]{2,1,0:T(8,128)(2,1)S(1)}, bf16[10,64,512]{2,1,0:T(8,128)(2,1)}, u32[]{:S(2)}, u32[]{:S(2)}) collective-permute-start(bf16[10,64,512]{2,1,0:T(8,128)(2,1)S(1)} %pad_maximum_fusion.20), channel_id=1, source_target_pairs={{0,1},{1,0},{2,3},{3,2},{4,5},{5,4},{6,7},{7,6},{8,9},{9,8},{10,11... | collective-permute-start | bytes 1966088 | tf_op jit(solution)/shard_map/ppermute | solution.py:49
  110.0 39.6 %collective-permute-start.10 = (bf16[512,512]{1,0:T(8,128)(2,1)}, bf16[512,512]{1,0:T(8,128)(2,1)}, u32[]{:S(2)}, u32[]{:S(2)}) collective-permute-start(bf16[512,512]{1,0:T(8,128)(2,1)} %pad_maximum_fusion.25), channel_id=1, source_target_pairs={{0,1},{1,0},{2,3},{3,2},{4,5},{5,4},{6,7},{7,6},{8,9},{9,8},{10,11... | collective-permute-start | bytes 1572872 | tf_op jit(solution)/shard_map/ppermute | solution.py:35
  110.3 39.3 %collective-permute-start.11 = (bf16[512,512]{1,0:T(8,128)(2,1)}, bf16[512,512]{1,0:T(8,128)(2,1)}, u32[]{:S(2)}, u32[]{:S(2)}) collective-permute-start(bf16[512,512]{1,0:T(8,128)(2,1)} %pad_maximum_fusion.26), channel_id=1, source_target_pairs={{0,2},{1,3},{2,0},{3,1},{4,6},{5,7},{6,4},{7,5},{8,10},{9,11},{10,... | collective-permute-start | bytes 1572872 | tf_op jit(solution)/shard_map/ppermute | solution.py:35
  113.6 43.1 %collective-permute-start.12 = (bf16[512,512]{1,0:T(8,128)(2,1)}, bf16[512,512]{1,0:T(8,128)(2,1)}, u32[]{:S(2)}, u32[]{:S(2)}) collective-permute-start(bf16[512,512]{1,0:T(8,128)(2,1)} %pad_maximum_fusion.27), channel_id=1, source_target_pairs={{0,3},{1,2},{2,1},{3,0},{4,7},{5,6},{6,5},{7,4},{8,11},{9,10},{10,... | collective-permute-start | bytes 1572872 | tf_op jit(solution)/shard_map/ppermute | solution.py:35
  156.7 44.7 %collective-permute-start.13 = (bf16[512,2048]{1,0:T(8,128)(2,1)}, bf16[512,2048]{1,0:T(8,128)(2,1)}, u32[]{:S(2)}, u32[]{:S(2)}) collective-permute-start(bf16[512,2048]{1,0:T(8,128)(2,1)} %multiply_convert_fusion), channel_id=1, source_target_pairs={{0,8},{4,12},{8,0},{12,4},{16,24},{20,28},{24,16},{28,20},{1,9},{5... | collective-permute-start | bytes 6291464 | tf_op jit(solution)/shard_map/ppermute | solution.py:49
  158.2 44.4 %collective-permute-start.14 = (bf16[512,2048]{1,0:T(8,128)(2,1)}, bf16[512,2048]{1,0:T(8,128)(2,1)}, u32[]{:S(2)}, u32[]{:S(2)}) collective-permute-start(bf16[512,2048]{1,0:T(8,128)(2,1)} %multiply_convert_fusion), channel_id=1, source_target_pairs={{0,16},{4,20},{8,24},{12,28},{16,0},{20,4},{24,8},{28,12},{1,17},{... | collective-permute-start | bytes 6291464 | tf_op jit(solution)/shard_map/ppermute | solution.py:49
  159.7 35.5 %collective-permute-start.15 = (bf16[2048,384]{1,0:T(8,128)(2,1)}, bf16[2048,384]{1,0:T(8,128)(2,1)}, u32[]{:S(2)}, u32[]{:S(2)}) collective-permute-start(bf16[2048,384]{1,0:T(8,128)(2,1)} %pad_maximum_fusion.6), channel_id=1, source_target_pairs={{0,1},{1,2},{2,3},{4,5},{5,6},{6,7},{8,9},{9,10},{10,11},{12,13},{... | collective-permute-start | bytes 4718600 | tf_op jit(solution)/shard_map/ppermute | solution.py:79
  161.7 34.8 %collective-permute-start.16 = (bf16[2048,384]{1,0:T(8,128)(2,1)}, bf16[2048,384]{1,0:T(8,128)(2,1)}, u32[]{:S(2)}, u32[]{:S(2)}) collective-permute-start(bf16[2048,384]{1,0:T(8,128)(2,1)} %pad_maximum_fusion.6), channel_id=1, source_target_pairs={{3,2},{2,1},{1,0},{7,6},{6,5},{5,4},{11,10},{10,9},{9,8},{15,14},{... | collective-permute-start | bytes 4718600 | tf_op jit(solution)/shard_map/ppermute | solution.py:79
  202.6 38.9 %collective-permute-start.19 = (bf16[2048,384]{1,0:T(8,128)(2,1)}, bf16[2048,384]{1,0:T(8,128)(2,1)S(1)}, u32[]{:S(2)}, u32[]{:S(2)}) collective-permute-start(bf16[2048,384]{1,0:T(8,128)(2,1)} %collective-permute-done.15), channel_id=1, source_target_pairs={{1,2},{2,3},{5,6},{6,7},{9,10},{10,11},{13,14},{14,15},{17,18},{18... | collective-permute-start | bytes 4718600 | tf_op jit(solution)/shard_map/ppermute | solution.py:79
  204.5 38.0 %collective-permute-start.20 = (bf16[2048,384]{1,0:T(8,128)(2,1)}, bf16[2048,384]{1,0:T(8,128)(2,1)}, u32[]{:S(2)}, u32[]{:S(2)}) collective-permute-start(bf16[2048,384]{1,0:T(8,128)(2,1)} %collective-permute-done.16), channel_id=1, source_target_pairs={{2,1},{1,0},{6,5},{5,4},{10,9},{9,8},{14,13},{13,12},{18,17},{17,1... | collective-permute-start | bytes 4718600 | tf_op jit(solution)/shard_map/ppermute | solution.py:79
  218.6 20.3 %collective-permute-start.17 = (bf16[256,2048]{1,0:T(8,128)(2,1)S(1)}, bf16[256,2048]{1,0:T(8,128)(2,1)S(1)}, u32[]{:S(2)}, u32[]{:S(2)}) collective-permute-start(bf16[256,2048]{1,0:T(8,128)(2,1)S(1)} %slice.396), channel_id=1, source_target_pairs={{0,16},{4,20},{8,24},{12,28},{16,0},{20,4},{24,8},{28,12},{1,17},{... | collective-permute-start | bytes 3145736 | tf_op jit(solution)/shard_map/ppermute | solution.py:49
  221.5 20.0 %collective-permute-start.18 = (bf16[256,2048]{1,0:T(8,128)(2,1)S(1)}, bf16[256,2048]{1,0:T(8,128)(2,1)S(1)}, u32[]{:S(2)}, u32[]{:S(2)}) collective-permute-start(bf16[256,2048]{1,0:T(8,128)(2,1)S(1)} %slice.397), channel_id=1, source_target_pairs={{0,8},{4,12},{8,0},{12,4},{16,24},{20,28},{24,16},{28,20},{1,9},{5... | collective-permute-start | bytes 3145736 | tf_op jit(solution)/shard_map/ppermute | solution.py:49
  242.5 331.2 %reduce-scatter.2.cloned.1.call-start = ((), (), s32[]{:S(2)}) async-start(), calls=%async_computation.4 | async-start | bytes 7864320 | tf_op jit(solution)/shard_map/reduce_scatter | solution.py:848
  245.2 35.9 %collective-permute-start.21 = (bf16[2048,2048]{1,0:T(8,128)(2,1)}, bf16[2048,2048]{1,0:T(8,128)(2,1)S(1)}, u32[]{:S(2)}, u32[]{:S(2)}) collective-permute-start(bf16[2048,2048]{1,0:T(8,128)(2,1)} %bitcast.32), channel_id=1, source_target_pairs={{0,4},{4,0},{8,12},{12,8},{16,20},{20,16},{24,28},{28,24},{1,5},{5... | collective-permute-start | bytes 25165832 | tf_op jit(solution)/shard_map/ppermute | solution.py:49
  245.2 35.9 %collective-permute-start.22 = (bf16[2048,384]{1,0:T(8,128)(2,1)S(1)}, bf16[2048,384]{1,0:T(8,128)(2,1)S(1)}, u32[]{:S(2)}, u32[]{:S(2)}) collective-permute-start(bf16[2048,384]{1,0:T(8,128)(2,1)S(1)} %collective-permute-done.19), channel_id=1, source_target_pairs={{2,3},{6,7},{10,11},{14,15},{18,19},{22,23},{26,27},{30,31}} | collective-permute-start | bytes 4718600 | tf_op jit(solution)/shard_map/ppermute | solution.py:79
  246.6 34.5 %collective-permute-start.23 = (bf16[2048,384]{1,0:T(8,128)(2,1)}, bf16[2048,384]{1,0:T(8,128)(2,1)S(1)}, u32[]{:S(2)}, u32[]{:S(2)}) collective-permute-start(bf16[2048,384]{1,0:T(8,128)(2,1)} %collective-permute-done.20), channel_id=1, source_target_pairs={{1,0},{5,4},{9,8},{13,12},{17,16},{21,20},{25,24},{29,28}} | collective-permute-start | bytes 4718600 | tf_op jit(solution)/shard_map/ppermute | solution.py:79
  359.4 22.2 %collective-permute-start.24 = (bf16[2048,2048]{1,0:T(8,128)(2,1)}, bf16[2048,2048]{1,0:T(8,128)(2,1)}, u32[]{:S(2)}, u32[]{:S(2)}) collective-permute-start(bf16[2048,2048]{1,0:T(8,128)(2,1)} %get-tuple-element.265), channel_id=1, source_target_pairs={{0,4},{4,0},{8,12},{12,8},{16,20},{20,16},{24,28},{28,24},{1,5},{5... | collective-permute-start | bytes 25165832 | tf_op jit(solution)/shard_map/ppermute | solution.py:49
  359.4 75.6 %collective-permute-start.27 = (bf16[2048,2048]{1,0:T(8,128)(2,1)}, bf16[2048,2048]{1,0:T(8,128)(2,1)}, u32[]{:S(2)}, u32[]{:S(2)}) collective-permute-start(bf16[2048,2048]{1,0:T(8,128)(2,1)} %convolution_convert_fusion), channel_id=1, source_target_pairs={{0,4},{4,0},{8,12},{12,8},{16,20},{20,16},{24,28},{28,24},{1,5},{5... | collective-permute-start | bytes 25165832 | tf_op jit(solution)/shard_map/ppermute | solution.py:49
  392.0 47.6 %collective-permute-start.25 = (bf16[512,2048]{1,0:T(8,128)(2,1)S(1)}, bf16[512,2048]{1,0:T(8,128)(2,1)S(1)}, u32[]{:S(2)}, u32[]{:S(2)}) collective-permute-start(bf16[512,2048]{1,0:T(8,128)(2,1)S(1)} %get-tuple-element.273), channel_id=1, source_target_pairs={{0,8},{4,12},{8,0},{12,4},{16,24},{20,28},{24,16},{28,20},{1,9},{5... | collective-permute-start | bytes 6291464 | tf_op jit(solution)/shard_map/ppermute | solution.py:49
  392.9 47.2 %collective-permute-start.26 = (bf16[512,2048]{1,0:T(8,128)(2,1)S(1)}, bf16[512,2048]{1,0:T(8,128)(2,1)S(1)}, u32[]{:S(2)}, u32[]{:S(2)}) collective-permute-start(bf16[512,2048]{1,0:T(8,128)(2,1)S(1)} %get-tuple-element.274), channel_id=1, source_target_pairs={{0,16},{4,20},{8,24},{12,28},{16,0},{20,4},{24,8},{28,12},{1,17},{... | collective-permute-start | bytes 6291464 | tf_op jit(solution)/shard_map/ppermute | solution.py:49
  448.2 298.9 %all-gather.18.cloned.1.call-start = ((), (), s32[]{:S(2)}) async-start(), calls=%async_computation.7 | async-start | bytes 14155776 | tf_op jit(solution)/shard_map/all_gather | solution.py:894
  452.4 24.5 %collective-permute-start.28 = (bf16[256,2048]{1,0:T(8,128)(2,1)}, bf16[256,2048]{1,0:T(8,128)(2,1)}, u32[]{:S(2)}, u32[]{:S(2)}) collective-permute-start(bf16[256,2048]{1,0:T(8,128)(2,1)} %get-tuple-element.395), channel_id=1, source_target_pairs={{0,16},{4,20},{8,24},{12,28},{16,0},{20,4},{24,8},{28,12},{1,17},{... | collective-permute-start | bytes 3145736 | tf_op jit(solution)/shard_map/ppermute | solution.py:49
  453.0 24.0 %collective-permute-start.29 = (bf16[256,2048]{1,0:T(8,128)(2,1)S(1)}, bf16[256,2048]{1,0:T(8,128)(2,1)}, u32[]{:S(2)}, u32[]{:S(2)}) collective-permute-start(bf16[256,2048]{1,0:T(8,128)(2,1)S(1)} %get-tuple-element.394), channel_id=1, source_target_pairs={{0,8},{4,12},{8,0},{12,4},{16,24},{20,28},{24,16},{28,20},{1,9},{5... | collective-permute-start | bytes 3145736 | tf_op jit(solution)/shard_map/ppermute | solution.py:49
  486.1 41.3 %collective-permute-start.32 = (bf16[640,2048]{1,0:T(8,128)(2,1)S(1)}, bf16[640,2048]{1,0:T(8,128)(2,1)S(1)}, u32[]{:S(2)}, u32[]{:S(2)}) collective-permute-start(bf16[640,2048]{1,0:T(8,128)(2,1)S(1)} %convolution_convert_fusion.2), channel_id=1, source_target_pairs={{0,4},{4,0},{8,12},{12,8},{16,20},{20,16},{24,28},{28,24},{1,5},{5... | collective-permute-start | bytes 7864328 | tf_op jit(solution)/shard_map/ppermute | solution.py:49
  486.1 41.2 %collective-permute-start.30 = (bf16[256,2048]{1,0:T(8,128)(2,1)S(1)}, bf16[256,2048]{1,0:T(8,128)(2,1)S(1)}, u32[]{:S(2)}, u32[]{:S(2)}) collective-permute-start(bf16[256,2048]{1,0:T(8,128)(2,1)S(1)} %get-tuple-element.289), channel_id=1, source_target_pairs={{0,8},{4,12},{8,0},{12,4},{16,24},{20,28},{24,16},{28,20},{1,9},{5... | collective-permute-start | bytes 3145736 | tf_op jit(solution)/shard_map/ppermute | solution.py:49
  486.9 40.4 %collective-permute-start.31 = (bf16[256,2048]{1,0:T(8,128)(2,1)S(1)}, bf16[256,2048]{1,0:T(8,128)(2,1)S(1)}, u32[]{:S(2)}, u32[]{:S(2)}) collective-permute-start(bf16[256,2048]{1,0:T(8,128)(2,1)S(1)} %get-tuple-element.290), channel_id=1, source_target_pairs={{0,16},{4,20},{8,24},{12,28},{16,0},{20,4},{24,8},{28,12},{1,17},{... | collective-permute-start | bytes 3145736 | tf_op jit(solution)/shard_map/ppermute | solution.py:49
  529.3 17.7 %collective-permute-start.36 = (bf16[160,2048]{1,0:T(8,128)(2,1)S(1)}, bf16[160,2048]{1,0:T(8,128)(2,1)S(1)}, u32[]{:S(2)}, u32[]{:S(2)}) collective-permute-start(bf16[160,2048]{1,0:T(8,128)(2,1)S(1)} %get-tuple-element.301), channel_id=1, source_target_pairs={{0,8},{4,12},{8,0},{12,4},{16,24},{20,28},{24,16},{28,20},{1,9},{5... | collective-permute-start | bytes 1966088 | tf_op jit(solution)/shard_map/ppermute | solution.py:49
  530.6 17.6 %collective-permute-start.37 = (bf16[160,2048]{1,0:T(8,128)(2,1)S(1)}, bf16[160,2048]{1,0:T(8,128)(2,1)S(1)}, u32[]{:S(2)}, u32[]{:S(2)}) collective-permute-start(bf16[160,2048]{1,0:T(8,128)(2,1)S(1)} %get-tuple-element.302), channel_id=1, source_target_pairs={{0,16},{4,20},{8,24},{12,28},{16,0},{20,4},{24,8},{28,12},{1,17},{... | collective-permute-start | bytes 1966088 | tf_op jit(solution)/shard_map/ppermute | solution.py:49
  532.0 37.4 %collective-permute-start.34 = (bf16[256,2048]{1,0:T(8,128)(2,1)S(1)}, bf16[256,2048]{1,0:T(8,128)(2,1)S(1)}, u32[]{:S(2)}, u32[]{:S(2)}) collective-permute-start(bf16[256,2048]{1,0:T(8,128)(2,1)S(1)} %get-tuple-element.391), channel_id=1, source_target_pairs={{0,16},{4,20},{8,24},{12,28},{16,0},{20,4},{24,8},{28,12},{1,17},{... | collective-permute-start | bytes 3145736 | tf_op jit(solution)/shard_map/ppermute | solution.py:49
  533.6 36.7 %collective-permute-start.35 = (bf16[256,2048]{1,0:T(8,128)(2,1)S(1)}, bf16[256,2048]{1,0:T(8,128)(2,1)}, u32[]{:S(2)}, u32[]{:S(2)}) collective-permute-start(bf16[256,2048]{1,0:T(8,128)(2,1)S(1)} %get-tuple-element.390), channel_id=1, source_target_pairs={{0,8},{4,12},{8,0},{12,4},{16,24},{20,28},{24,16},{28,20},{1,9},{5... | collective-permute-start | bytes 3145736 | tf_op jit(solution)/shard_map/ppermute | solution.py:49
  535.9 31.3 %collective-permute-start.33 = (bf16[10,64,512]{2,1,0:T(8,128)(2,1)S(1)}, bf16[10,64,512]{2,1,0:T(8,128)(2,1)S(1)}, u32[]{:S(2)}, u32[]{:S(2)}) collective-permute-start(bf16[10,64,512]{2,1,0:T(8,128)(2,1)S(1)} %copy-done.103), channel_id=1, source_target_pairs={{0,1},{1,0},{2,3},{3,2},{4,5},{5,4},{6,7},{7,6},{8,9},{9,8},{10,11... | collective-permute-start | bytes 1966088 | tf_op jit(solution)/shard_map/ppermute | solution.py:49
  573.7 185.1 %all-gather.16.cloned.1.call-start = ((), (), s32[]{:S(2)}) async-start(), calls=%async_computation.6 | async-start | bytes 1474560 | tf_op jit(solution)/shard_map/all_gather | solution.py:960
  587.5 22.8 %collective-permute-start.38 = (bf16[1024,2048]{1,0:T(8,128)(2,1)}, bf16[1024,2048]{1,0:T(8,128)(2,1)}, u32[]{:S(2)}, u32[]{:S(2)}) collective-permute-start(bf16[1024,2048]{1,0:T(8,128)(2,1)} %add_convert_fusion.1), channel_id=1, source_target_pairs={{0,4},{4,0},{8,12},{12,8},{16,20},{20,16},{24,28},{28,24},{1,5},{5... | collective-permute-start | bytes 12582920 | tf_op jit(solution)/shard_map/ppermute | solution.py:49
  591.5 17.5 %collective-permute-start.39 = (bf16[80,2048]{1,0:T(8,128)(2,1)S(1)}, bf16[80,2048]{1,0:T(8,128)(2,1)S(1)}, u32[]{:S(2)}, u32[]{:S(2)}) collective-permute-start(bf16[80,2048]{1,0:T(8,128)(2,1)S(1)} %get-tuple-element.463), channel_id=1, source_target_pairs={{0,16},{4,20},{8,24},{12,28},{16,0},{20,4},{24,8},{28,12},{1,17},{... | collective-permute-start | bytes 983048 | tf_op jit(solution)/shard_map/ppermute | solution.py:49
  593.0 17.2 %collective-permute-start.40 = (bf16[80,2048]{1,0:T(8,128)(2,1)S(1)}, bf16[80,2048]{1,0:T(8,128)(2,1)S(1)}, u32[]{:S(2)}, u32[]{:S(2)}) collective-permute-start(bf16[80,2048]{1,0:T(8,128)(2,1)S(1)} %get-tuple-element.462), channel_id=1, source_target_pairs={{0,8},{4,12},{8,0},{12,4},{16,24},{20,28},{24,16},{28,20},{1,9},{5... | collective-permute-start | bytes 983048 | tf_op jit(solution)/shard_map/ppermute | solution.py:49
  616.8 59.4 %collective-permute-start.44 = (bf16[256,2048]{1,0:T(8,128)(2,1)S(1)}, bf16[256,2048]{1,0:T(8,128)(2,1)S(1)}, u32[]{:S(2)}, u32[]{:S(2)}) collective-permute-start(bf16[256,2048]{1,0:T(8,128)(2,1)S(1)} %get-tuple-element.320), channel_id=1, source_target_pairs={{0,8},{4,12},{8,0},{12,4},{16,24},{20,28},{24,16},{28,20},{1,9},{5... | collective-permute-start | bytes 3145736 | tf_op jit(solution)/shard_map/ppermute | solution.py:49
  617.5 58.7 %collective-permute-start.45 = (bf16[256,2048]{1,0:T(8,128)(2,1)S(1)}, bf16[256,2048]{1,0:T(8,128)(2,1)S(1)}, u32[]{:S(2)}, u32[]{:S(2)}) collective-permute-start(bf16[256,2048]{1,0:T(8,128)(2,1)S(1)} %get-tuple-element.321), channel_id=1, source_target_pairs={{0,16},{4,20},{8,24},{12,28},{16,0},{20,4},{24,8},{28,12},{1,17},{... | collective-permute-start | bytes 3145736 | tf_op jit(solution)/shard_map/ppermute | solution.py:49
  619.0 19.4 %collective-permute-start.41 = (bf16[512,512]{1,0:T(8,128)(2,1)S(1)}, bf16[512,512]{1,0:T(8,128)(2,1)S(1)}, u32[]{:S(2)}, u32[]{:S(2)}) collective-permute-start(bf16[512,512]{1,0:T(8,128)(2,1)S(1)} %get-tuple-element.418), channel_id=1, source_target_pairs={{0,1},{1,0},{2,3},{3,2},{4,5},{5,4},{6,7},{7,6},{8,9},{9,8},{10,11... | collective-permute-start | bytes 1572872 | tf_op jit(solution)/shard_map/ppermute | solution.py:35
  619.6 33.4 %collective-permute-start.42 = (bf16[512,512]{1,0:T(8,128)(2,1)S(1)}, bf16[512,512]{1,0:T(8,128)(2,1)S(1)}, u32[]{:S(2)}, u32[]{:S(2)}) collective-permute-start(bf16[512,512]{1,0:T(8,128)(2,1)S(1)} %get-tuple-element.419), channel_id=1, source_target_pairs={{0,2},{1,3},{2,0},{3,1},{4,6},{5,7},{6,4},{7,5},{8,10},{9,11},{10,... | collective-permute-start | bytes 1572872 | tf_op jit(solution)/shard_map/ppermute | solution.py:35
  619.6 56.6 %collective-permute-start.43 = (bf16[512,512]{1,0:T(8,128)(2,1)S(1)}, bf16[512,512]{1,0:T(8,128)(2,1)S(1)}, u32[]{:S(2)}, u32[]{:S(2)}) collective-permute-start(bf16[512,512]{1,0:T(8,128)(2,1)S(1)} %get-tuple-element.416), channel_id=1, source_target_pairs={{0,3},{1,2},{2,1},{3,0},{4,7},{5,6},{6,5},{7,4},{8,11},{9,10},{10,... | collective-permute-start | bytes 1572872 | tf_op jit(solution)/shard_map/ppermute | solution.py:35
  638.5 41.5 %collective-permute-start.46 = (bf16[160,512]{1,0:T(8,128)(2,1)S(1)}, bf16[160,512]{1,0:T(8,128)(2,1)S(1)}, u32[]{:S(2)}, u32[]{:S(2)}) collective-permute-start(bf16[160,512]{1,0:T(8,128)(2,1)S(1)} %get-tuple-element.480), channel_id=1, source_target_pairs={{0,1},{1,0},{2,3},{3,2},{4,5},{5,4},{6,7},{7,6},{8,9},{9,8},{10,11... | collective-permute-start | bytes 491528 | tf_op jit(solution)/shard_map/ppermute | solution.py:35
  653.0 28.5 %collective-permute-start.47 = (bf16[160,512]{1,0:T(8,128)(2,1)S(1)}, bf16[160,512]{1,0:T(8,128)(2,1)S(1)}, u32[]{:S(2)}, u32[]{:S(2)}) collective-permute-start(bf16[160,512]{1,0:T(8,128)(2,1)S(1)} %get-tuple-element.478), channel_id=1, source_target_pairs={{0,2},{1,3},{2,0},{3,1},{4,6},{5,7},{6,4},{7,5},{8,10},{9,11},{10,... | collective-permute-start | bytes 491528 | tf_op jit(solution)/shard_map/ppermute | solution.py:35
  676.6 14.9 %collective-permute-start.49 = (bf16[128,2048]{1,0:T(8,128)(2,1)S(1)}, bf16[128,2048]{1,0:T(8,128)(2,1)S(1)}, u32[]{:S(2)}, u32[]{:S(2)}) collective-permute-start(bf16[128,2048]{1,0:T(8,128)(2,1)S(1)} %get-tuple-element.413), channel_id=1, source_target_pairs={{0,16},{4,20},{8,24},{12,28},{16,0},{20,4},{24,8},{28,12},{1,17},{... | collective-permute-start | bytes 1572872 | tf_op jit(solution)/shard_map/ppermute | solution.py:49
  677.4 14.9 %collective-permute-start.50 = (bf16[128,2048]{1,0:T(8,128)(2,1)S(1)}, bf16[128,2048]{1,0:T(8,128)(2,1)S(1)}, u32[]{:S(2)}, u32[]{:S(2)}) collective-permute-start(bf16[128,2048]{1,0:T(8,128)(2,1)S(1)} %get-tuple-element.412), channel_id=1, source_target_pairs={{0,8},{4,12},{8,0},{12,4},{16,24},{20,28},{24,16},{28,20},{1,9},{5... | collective-permute-start | bytes 1572872 | tf_op jit(solution)/shard_map/ppermute | solution.py:49
  680.8 30.9 %collective-permute-start.54 = (bf16[256,2048]{1,0:T(8,128)(2,1)S(1)}, bf16[256,2048]{1,0:T(8,128)(2,1)}, u32[]{:S(2)}, u32[]{:S(2)}) collective-permute-start(bf16[256,2048]{1,0:T(8,128)(2,1)S(1)} %copy-done.24), channel_id=1, source_target_pairs={{0,8},{4,12},{8,0},{12,4},{16,24},{20,28},{24,16},{28,20},{1,9},{5... | collective-permute-start | bytes 3145736 | tf_op jit(solution)/shard_map/ppermute | solution.py:49
  681.8 30.0 %collective-permute-start.55 = (bf16[256,2048]{1,0:T(8,128)(2,1)S(1)}, bf16[256,2048]{1,0:T(8,128)(2,1)}, u32[]{:S(2)}, u32[]{:S(2)}) collective-permute-start(bf16[256,2048]{1,0:T(8,128)(2,1)S(1)} %copy-done.22), channel_id=1, source_target_pairs={{0,16},{4,20},{8,24},{12,28},{16,0},{20,4},{24,8},{28,12},{1,17},{... | collective-permute-start | bytes 3145736 | tf_op jit(solution)/shard_map/ppermute | solution.py:49
  696.0 91.5 %all-gather.14.cloned.1.call-start = ((), (), s32[]{:S(2)}) async-start(), calls=%async_computation.5 | async-start | bytes 5308416 | tf_op jit(solution)/shard_map/all_gather | solution.py:987
  699.8 23.0 %collective-permute-start.51 = (bf16[256,1152]{1,0:T(8,128)(2,1)S(1)}, bf16[256,1152]{1,0:T(8,128)(2,1)S(1)}, u32[]{:S(2)}, u32[]{:S(2)}) collective-permute-start(bf16[256,1152]{1,0:T(8,128)(2,1)S(1)} %get-tuple-element.492), channel_id=1, source_target_pairs={{0,1},{1,0},{2,3},{3,2},{4,5},{5,4},{6,7},{7,6},{8,9},{9,8},{10,11... | collective-permute-start | bytes 1769480 | tf_op jit(solution)/shard_map/ppermute | solution.py:35
  699.9 38.8 %collective-permute-start.52 = (bf16[256,1152]{1,0:T(8,128)(2,1)S(1)}, bf16[256,1152]{1,0:T(8,128)(2,1)S(1)}, u32[]{:S(2)}, u32[]{:S(2)}) collective-permute-start(bf16[256,1152]{1,0:T(8,128)(2,1)S(1)} %get-tuple-element.493), channel_id=1, source_target_pairs={{0,2},{1,3},{2,0},{3,1},{4,6},{5,7},{6,4},{7,5},{8,10},{9,11},{10,... | collective-permute-start | bytes 1769480 | tf_op jit(solution)/shard_map/ppermute | solution.py:35
  703.3 43.8 %collective-permute-start.53 = (bf16[256,1152]{1,0:T(8,128)(2,1)S(1)}, bf16[256,1152]{1,0:T(8,128)(2,1)}, u32[]{:S(2)}, u32[]{:S(2)}) collective-permute-start(bf16[256,1152]{1,0:T(8,128)(2,1)S(1)} %get-tuple-element.491), channel_id=1, source_target_pairs={{0,3},{1,2},{2,1},{3,0},{4,7},{5,6},{6,5},{7,4},{8,11},{9,10},{10,... | collective-permute-start | bytes 1769480 | tf_op jit(solution)/shard_map/ppermute | solution.py:35
  755.4 39.4 %collective-permute-start.56 = (bf16[512,512]{1,0:T(8,128)(2,1)}, bf16[512,512]{1,0:T(8,128)(2,1)S(1)}, u32[]{:S(2)}, u32[]{:S(2)}) collective-permute-start(bf16[512,512]{1,0:T(8,128)(2,1)} %get-tuple-element.408), channel_id=1, source_target_pairs={{0,1},{1,0},{2,3},{3,2},{4,5},{5,4},{6,7},{7,6},{8,9},{9,8},{10,11... | collective-permute-start | bytes 1572872 | tf_op jit(solution)/shard_map/ppermute | solution.py:35
  755.4 39.4 %collective-permute-start.57 = (bf16[512,512]{1,0:T(8,128)(2,1)S(1)}, bf16[512,512]{1,0:T(8,128)(2,1)S(1)}, u32[]{:S(2)}, u32[]{:S(2)}) collective-permute-start(bf16[512,512]{1,0:T(8,128)(2,1)S(1)} %get-tuple-element.409), channel_id=1, source_target_pairs={{0,2},{1,3},{2,0},{3,1},{4,6},{5,7},{6,4},{7,5},{8,10},{9,11},{10,... | collective-permute-start | bytes 1572872 | tf_op jit(solution)/shard_map/ppermute | solution.py:35
  757.3 43.1 %collective-permute-start.58 = (bf16[512,512]{1,0:T(8,128)(2,1)S(1)}, bf16[512,512]{1,0:T(8,128)(2,1)S(1)}, u32[]{:S(2)}, u32[]{:S(2)}) collective-permute-start(bf16[512,512]{1,0:T(8,128)(2,1)S(1)} %get-tuple-element.406), channel_id=1, source_target_pairs={{0,3},{1,2},{2,1},{3,0},{4,7},{5,6},{6,5},{7,4},{8,11},{9,10},{10,... | collective-permute-start | bytes 1572872 | tf_op jit(solution)/shard_map/ppermute | solution.py:35
  (134 other events, 1148.6 us)
Sparse Core Ops, SparseCore 0:
  53.1 44.0 all-gather.7
  99.7 41.1 all-gather.9
  242.6 88.0 all-gather.11
  448.4 125.2 reduce-scatter.1
  575.4 101.6 all-gather.17
  696.1 25.7 all-gather.15
  749.8 37.6 all-gather.13
